TPU v7x, 32 devices: a whole 2x2x4 slice. The times are simulated.
32 devices in a mesh: ctx: 4 (over y, x), fsdp: 8 (over z, core).
Axes of the slice: x: 2, y: 2, z: 4, core: 2. Of those that a mesh axis runs over, the one named last changes fastest.
Arguments:
- tokens: bfloat16 [8, 2048, 576], P('fsdp', 'ctx'), may hold values from -6 to 6
- positions: int32 [8, 2048], P('fsdp', 'ctx'), may hold values from 0 to 2047, as said below
- query_weight: bfloat16 [2, 576, 576], P(None, 'fsdp'), may hold values from -0.25 to 0.25
- key_matrix: bfloat16 [2, 576, 192], P(None, 'fsdp'), may hold values from -0.25 to 0.25
- value_weight: bfloat16 [2, 576, 192], P(None, 'fsdp'), may hold values from -0.25 to 0.25
- out_weight: bfloat16 [2, 576, 576], P(None, 'fsdp'), may hold values from -1 to 1
- gate_weight: bfloat16 [2, 576, 1536], P(None, 'fsdp'), may hold values from -0.25 to 0.25
- up_weight: bfloat16 [2, 576, 1536], P(None, 'fsdp'), may hold values from -0.25 to 0.25
- down_weight: bfloat16 [2, 1536, 576], P(None, 'fsdp'), may hold values from -0.15625 to 0.15625
- attn_gain: bfloat16 [2, 576], P(None, 'fsdp'), may hold values from 0.5 to 1.5
- mlp_gain: bfloat16 [2, 576], P(None, 'fsdp'), may hold values from 0.5 to 1.5
- cotangent: bfloat16 [8, 2048, 576], P('fsdp', 'ctx'), may hold values from -6 to 6
Outputs:
- layer_out: bfloat16 [8, 2048, 576], P('fsdp', 'ctx')
- input_grad: float32 [8, 2048, 576], P('fsdp', 'ctx')
- grad_query: float32 [2, 576, 576], P(None, 'fsdp')
- grad_key: float32 [2, 576, 192], P(None, 'fsdp')
- grad_value: float32 [2, 576, 192], P(None, 'fsdp')
- grad_out: float32 [2, 576, 576], P(None, 'fsdp')
- grad_gate: float32 [2, 576, 1536], P(None, 'fsdp')
- grad_up: float32 [2, 576, 1536], P(None, 'fsdp')
- grad_down: float32 [2, 1536, 576], P(None, 'fsdp')
- grad_attn_gain: float32 [2, 576], P(None, 'fsdp')
- grad_mlp_gain: float32 [2, 576], P(None, 'fsdp')
Inputs may be any that keep to these rules, and one draw needn't show every extreme that they name: `positions`: A token's position is 0 where a document begins and one more than the previous token's otherwise; every sequence begins a document at its first token; sequence 0 is one document of 2048 tokens.
All inputs are finite; a program needn't handle non-finite values.
Results may differ from a plain program's by a relative error of at most 0.028.
Values may be sent and summed in bfloat16 or wider, within the bound.
No kernel may reach another device: no remote copies, remote signals or barrier semaphores. Data moves between devices by JAX's collectives and lax.ppermute only.
A program may use at most 192 MiB of HBM per device.

v0:
```python
import jax
import jax.numpy as jnp
from jax import lax
from jax.sharding import PartitionSpec as P

HEADS = 9
KV_HEADS = 3
HD = 64
LAYERS = 2


epsilon = 1e-05
theta = 100000.0
log_two_e = 1.4426950408889634
mask_filler = -1e30


def shifted(block, axis, distance):
    devices = range(lax.axis_size(axis))
    route = [((i - distance) % len(devices), i) for i in devices]
    return lax.ppermute(block, axis, route)


def rms_norm(hidden, gain):
    scale = lax.rsqrt(jnp.mean(hidden * hidden, axis=-1, keepdims=True) + epsilon)
    return hidden * scale * gain


def rope_tables(positions, head_size):
    half = head_size // 2
    freq = theta ** (-(jnp.arange(half, dtype=jnp.float32) * 2.0 / head_size))
    angle = positions.astype(jnp.float32)[..., None] * freq
    return (jnp.cos(angle), jnp.sin(angle))


def rotate(values, cosine, sine):
    half = values.shape[-1] // 2
    first = values[..., :half]
    second = values[..., half:]
    cosine = cosine[..., None, :]
    sine = sine[..., None, :]
    return jnp.concatenate(
        [first * cosine - second * sine, second * cosine + first * sine], axis=-1
    )


def project(input_tokens, weight_matrix):
    return jnp.einsum(
        "vnk,kp->vnp", input_tokens, weight_matrix, preferred_element_type=jnp.float32
    )


def project_back(gradient_tree, weight_matrix):
    return jnp.einsum(
        "qzy,gy->qzg", gradient_tree, weight_matrix, preferred_element_type=jnp.float32
    )


def outer_sum(input_tokens, gradient_tree):
    return jnp.einsum(
        "cwu,cwf->uf", input_tokens, gradient_tree, preferred_element_type=jnp.float32
    )


def to_rows(stat):
    return jnp.transpose(stat, (0, 3, 1, 2))


def body(
    tokens,
    positions,
    query_weight,
    key_matrix,
    value_weight,
    out_weight,
    gate_weight,
    up_weight,
    down_weight,
    attn_gain,
    mlp_gain,
    cotangent,
):
    cycle_size = lax.axis_size("ctx")
    cycle_rank = lax.axis_index("ctx")
    sequence_count, block, width = tokens.shape
    kv_heads = KV_HEADS
    group = HEADS // KV_HEADS
    head_size = HD
    cosine, sine = rope_tables(positions, head_size)
    row_index = cycle_rank * block + jnp.arange(block, dtype=jnp.int32)
    doc_start = row_index[None, :] - positions
    key_offsets = jnp.arange(block, dtype=jnp.int32)

    def block_scores(queries, key_in, source):
        key_index = source * block + key_offsets
        visible = (key_index[None, None, :] <= row_index[None, :, None]) & (
            key_index[None, None, :] >= doc_start[:, :, None]
        )
        visible = visible[:, None, None]
        raw = jnp.einsum("sqgjd,skgd->sgjqk", queries, key_in, preferred_element_type=jnp.float32)
        scaled = jnp.where(visible, raw * (0.125 * log_two_e), mask_filler)
        return (scaled, visible)

    def attend(queries, key_rows, value_rows):
        stat_shape = (sequence_count, kv_heads, group, block)

        def absorb(state, moving, source):
            numerator, row_total, row_top = state
            scaled, visible = block_scores(queries, moving[0], source)
            new_top = jnp.maximum(row_top, jnp.floor(jnp.max(scaled, axis=-1)))
            probs = jnp.where(visible, jnp.exp2(scaled - new_top[..., None]), 0.0)
            factor = jnp.exp2(row_top - new_top)
            row_total = row_total * factor + jnp.sum(probs, axis=-1)
            numerator = numerator * to_rows(factor)[..., None] + jnp.einsum(
                "sgjqk,skgd->sqgjd",
                probs.astype(jnp.bfloat16),
                moving[1],
                preferred_element_type=jnp.float32,
            )
            return (numerator, row_total, new_top)

        starting_carry = (
            jnp.zeros((sequence_count, block, kv_heads, group, head_size), jnp.float32),
            jnp.zeros(stat_shape, jnp.float32),
            jnp.full(stat_shape, mask_filler, jnp.float32),
        )
        state = absorb(starting_carry, (key_rows, value_rows), cycle_rank)
        stored = ()

        def turn(step, carry):
            state, moving, stored = carry
            moving = shifted((moving[0], moving[1]), "ctx", -1)
            source = (cycle_rank + step) % cycle_size
            state = absorb(state, moving, source)
            return (state, moving, stored)

        state, moving, stored = lax.fori_loop(
            1, cycle_size, turn, (state, (key_rows, value_rows), stored)
        )
        return (state, stored)

    def pass_grads(travel):
        return (
            shifted(travel[0].astype(jnp.bfloat16), "ctx", -1).astype(jnp.float32),
            shifted(travel[1].astype(jnp.bfloat16), "ctx", -1).astype(jnp.float32),
        )

    def backward_layer(grad_out, full, kept):
        (
            query_full,
            key_full,
            value_full,
            out_full,
            gate_full,
            up_full,
            down_full,
            first_gain,
            second_gain,
        ) = full
        (
            hidden,
            normed_low,
            queries,
            key_rows,
            value_low,
            attention,
            row_total,
            row_top,
            attn_low,
            middle,
            mixed_low,
            gate,
            upward,
            inner,
            stored,
        ) = kept
        down_in = grad_out.astype(jnp.bfloat16)
        grad_down = outer_sum(inner, down_in)
        d_inner = project_back(down_in, down_full)
        unused, pull_gate = jax.vjp(
            lambda gate_in, up_in: jax.nn.silu(gate_in) * up_in, gate, upward
        )
        d_gate, d_up = pull_gate(d_inner)
        d_gate = d_gate.astype(jnp.bfloat16)
        d_up = d_up.astype(jnp.bfloat16)
        grad_gate = outer_sum(mixed_low, d_gate)
        grad_up = outer_sum(mixed_low, d_up)
        d_mixed = project_back(d_gate, gate_full) + project_back(d_up, up_full)
        unused, pull_second = jax.vjp(rms_norm, middle, second_gain.astype(jnp.float32))
        d_middle, grad_second = pull_second(d_mixed)
        grad_mid = grad_out + d_middle
        mid_low = grad_mid.astype(jnp.bfloat16)
        grad_out_proj = outer_sum(attn_low, mid_low)
        d_attention = project_back(mid_low, out_full).reshape(
            sequence_count, block, kv_heads, group, head_size
        )
        totals = to_rows(row_total)
        delta = jnp.sum(d_attention * attention, axis=-1) / totals
        d_numer = (d_attention / totals[..., None]).astype(jnp.bfloat16)
        delta_cols = jnp.transpose(delta, (0, 2, 3, 1))

        def contrib(moving, source):
            key_in, value_in = moving
            scaled, visible = block_scores(queries, key_in, source)
            probs = jnp.where(visible, jnp.exp2(scaled - row_top[..., None]), 0.0)
            d_probs = jnp.einsum(
                "sqgjd,skgd->sgjqk", d_numer, value_in, preferred_element_type=jnp.float32
            )
            d_score = (probs * (d_probs - delta_cols[..., None])).astype(jnp.bfloat16)
            d_query = (
                jnp.einsum("sgjqk,skgd->sqgjd", d_score, key_in, preferred_element_type=jnp.float32)
                * 0.125
            )
            d_key = (
                jnp.einsum(
                    "sgjqk,sqgjd->skgd", d_score, queries, preferred_element_type=jnp.float32
                )
                * 0.125
            )
            d_value = jnp.einsum(
                "sgjqk,sqgjd->skgd",
                probs.astype(jnp.bfloat16),
                d_numer,
                preferred_element_type=jnp.float32,
            )
            return (d_query, (d_key, d_value))

        d_query, travel = contrib((key_rows, value_low), cycle_rank)

        def turn_back(step, carry):
            d_query, moving, travel = carry
            moving = shifted((moving[0], moving[1]), "ctx", -1)
            travel = pass_grads(travel)
            source = (cycle_rank + step) % cycle_size
            parts = contrib(moving, source)
            travel = (travel[0] + parts[1][0], travel[1] + parts[1][1])
            return (d_query + parts[0], moving, travel)

        d_query, moving, travel = lax.fori_loop(
            1, cycle_size, turn_back, (d_query, (key_rows, value_low), travel)
        )
        travel = pass_grads(travel)
        dq_low = (
            rotate(d_query.reshape(sequence_count, block, HEADS, head_size), cosine, -sine)
            .astype(jnp.bfloat16)
            .reshape(sequence_count, block, HEADS * head_size)
        )
        dk_low = (
            rotate(travel[0], cosine, -sine)
            .astype(jnp.bfloat16)
            .reshape(sequence_count, block, kv_heads * head_size)
        )
        dv_low = travel[1].astype(jnp.bfloat16).reshape(sequence_count, block, kv_heads * head_size)
        grad_query = outer_sum(normed_low, dq_low)
        grad_key = outer_sum(normed_low, dk_low)
        grad_value = outer_sum(normed_low, dv_low)
        normed_gradient = (
            project_back(dq_low, query_full)
            + project_back(dk_low, key_full)
            + project_back(dv_low, value_full)
        )
        unused, pull_first = jax.vjp(rms_norm, hidden, first_gain.astype(jnp.float32))
        d_hidden, grad_first = pull_first(normed_gradient)
        grad_in = grad_mid + d_hidden
        return (
            grad_in,
            (
                grad_query,
                grad_key,
                grad_value,
                grad_out_proj,
                grad_gate,
                grad_up,
                grad_down,
                grad_first,
                grad_second,
            ),
        )

    hidden = tokens.astype(jnp.float32)
    saved = []
    fulls = []
    for index in range(LAYERS):
        full = (
            lax.all_gather(query_weight[index], "fsdp", axis=0, tiled=True),
            lax.all_gather(key_matrix[index], "fsdp", axis=0, tiled=True),
            lax.all_gather(value_weight[index], "fsdp", axis=0, tiled=True),
            lax.all_gather(out_weight[index], "fsdp", axis=0, tiled=True),
            lax.all_gather(gate_weight[index], "fsdp", axis=0, tiled=True),
            lax.all_gather(up_weight[index], "fsdp", axis=0, tiled=True),
            lax.all_gather(down_weight[index], "fsdp", axis=0, tiled=True),
            lax.all_gather(attn_gain[index], "fsdp", axis=0, tiled=True),
            lax.all_gather(mlp_gain[index], "fsdp", axis=0, tiled=True),
        )
        (
            forward_query_full,
            forward_key_full,
            forward_value_full,
            forward_out_full,
            forward_gate_full,
            forward_up_full,
            forward_down_full,
            forward_first_gain,
            forward_second_gain,
        ) = full
        forward_normed_low = rms_norm(hidden, forward_first_gain.astype(jnp.float32)).astype(
            jnp.bfloat16
        )
        query_pre = project(forward_normed_low, forward_query_full)
        key_pre = project(forward_normed_low, forward_key_full)
        forward_value_low = (
            project(forward_normed_low, forward_value_full)
            .astype(jnp.bfloat16)
            .reshape(sequence_count, block, kv_heads, head_size)
        )
        forward_queries = rotate(
            query_pre.reshape(sequence_count, block, HEADS, head_size), cosine, sine
        ).astype(jnp.bfloat16)
        forward_queries = forward_queries.reshape(sequence_count, block, kv_heads, group, head_size)
        forward_key_rows = rotate(
            key_pre.reshape(sequence_count, block, kv_heads, head_size), cosine, sine
        ).astype(jnp.bfloat16)
        forward_state, forward_stored = attend(forward_queries, forward_key_rows, forward_value_low)
        forward_numerator, forward_row_total, forward_row_top = forward_state
        forward_attention = forward_numerator / to_rows(forward_row_total)[..., None]
        forward_attn_low = forward_attention.reshape(
            sequence_count, block, HEADS * head_size
        ).astype(jnp.bfloat16)
        forward_middle = hidden + project(forward_attn_low, forward_out_full)
        forward_mixed_low = rms_norm(
            forward_middle, forward_second_gain.astype(jnp.float32)
        ).astype(jnp.bfloat16)
        forward_gate = project(forward_mixed_low, forward_gate_full)
        forward_upward = project(forward_mixed_low, forward_up_full)
        forward_inner = (jax.nn.silu(forward_gate) * forward_upward).astype(jnp.bfloat16)
        output = forward_middle + project(forward_inner, forward_down_full)
        forward_kept = (
            hidden,
            forward_normed_low,
            forward_queries,
            forward_key_rows,
            forward_value_low,
            forward_attention,
            forward_row_total,
            forward_row_top,
            forward_attn_low,
            forward_middle,
            forward_mixed_low,
            forward_gate,
            forward_upward,
            forward_inner,
            forward_stored,
        )
        hidden = output
        kept = forward_kept
        saved.append(kept)
        fulls.append(full)
    layer_out = hidden.astype(jnp.bfloat16)
    grad = cotangent.astype(jnp.float32)
    layer_grads = [None] * LAYERS
    for index in reversed(range(LAYERS)):
        full = (
            lax.all_gather(query_weight[index], "fsdp", axis=0, tiled=True),
            lax.all_gather(key_matrix[index], "fsdp", axis=0, tiled=True),
            lax.all_gather(value_weight[index], "fsdp", axis=0, tiled=True),
            lax.all_gather(out_weight[index], "fsdp", axis=0, tiled=True),
            lax.all_gather(gate_weight[index], "fsdp", axis=0, tiled=True),
            lax.all_gather(up_weight[index], "fsdp", axis=0, tiled=True),
            lax.all_gather(down_weight[index], "fsdp", axis=0, tiled=True),
            lax.all_gather(attn_gain[index], "fsdp", axis=0, tiled=True),
            lax.all_gather(mlp_gain[index], "fsdp", axis=0, tiled=True),
        )
        grad, gradient_tree = backward_layer(grad, full, saved[index])
        layer_grads[index] = (
            lax.psum(
                lax.psum_scatter(
                    gradient_tree[0].astype(jnp.bfloat16), "fsdp", scatter_dimension=0, tiled=True
                ),
                "ctx",
            ).astype(jnp.float32),
            lax.psum(
                lax.psum_scatter(
                    gradient_tree[1].astype(jnp.bfloat16), "fsdp", scatter_dimension=0, tiled=True
                ),
                "ctx",
            ).astype(jnp.float32),
            lax.psum(
                lax.psum_scatter(
                    gradient_tree[2].astype(jnp.bfloat16), "fsdp", scatter_dimension=0, tiled=True
                ),
                "ctx",
            ).astype(jnp.float32),
            lax.psum(
                lax.psum_scatter(
                    gradient_tree[3].astype(jnp.bfloat16), "fsdp", scatter_dimension=0, tiled=True
                ),
                "ctx",
            ).astype(jnp.float32),
            lax.psum(
                lax.psum_scatter(
                    gradient_tree[4].astype(jnp.bfloat16), "fsdp", scatter_dimension=0, tiled=True
                ),
                "ctx",
            ).astype(jnp.float32),
            lax.psum(
                lax.psum_scatter(
                    gradient_tree[5].astype(jnp.bfloat16), "fsdp", scatter_dimension=0, tiled=True
                ),
                "ctx",
            ).astype(jnp.float32),
            lax.psum(
                lax.psum_scatter(
                    gradient_tree[6].astype(jnp.bfloat16), "fsdp", scatter_dimension=0, tiled=True
                ),
                "ctx",
            ).astype(jnp.float32),
            lax.psum(
                lax.psum_scatter(
                    gradient_tree[7].astype(jnp.bfloat16), "fsdp", scatter_dimension=0, tiled=True
                ),
                "ctx",
            ).astype(jnp.float32),
            lax.psum(
                lax.psum_scatter(
                    gradient_tree[8].astype(jnp.bfloat16), "fsdp", scatter_dimension=0, tiled=True
                ),
                "ctx",
            ).astype(jnp.float32),
        )
    results = tuple(
        (
            jnp.stack([layer_grads[index][position] for index in range(LAYERS)])
            for position in range(9)
        )
    )
    return (
        layer_out,
        grad,
        results[0],
        results[1],
        results[2],
        results[3],
        results[4],
        results[5],
        results[6],
        results[7],
        results[8],
    )


def solution(mesh):
    return jax.shard_map(
        body,
        mesh=mesh,
        in_specs=(
            P("fsdp", "ctx", None),
            P("fsdp", "ctx"),
            P(None, "fsdp", None),
            P(None, "fsdp", None),
            P(None, "fsdp", None),
            P(None, "fsdp", None),
            P(None, "fsdp", None),
            P(None, "fsdp", None),
            P(None, "fsdp", None),
            P(None, "fsdp"),
            P(None, "fsdp"),
            P("fsdp", "ctx", None),
        ),
        out_specs=(
            P("fsdp", "ctx", None),
            P("fsdp", "ctx", None),
            P(None, "fsdp", None),
            P(None, "fsdp", None),
            P(None, "fsdp", None),
            P(None, "fsdp", None),
            P(None, "fsdp", None),
            P(None, "fsdp", None),
            P(None, "fsdp", None),
            P(None, "fsdp"),
            P(None, "fsdp"),
        ),
        check_vma=False,
    )
```

profile of v0, /device:TPU:0, one launch (start us, length us, event | category | flops | bytes accessed | tf_op | source)
XLA Modules:
  0.0 1102.2 jit_solution(13683435469610822054)
XLA Ops:
  16.1 18.9 %all-reduce.13 = (bf16[576]{0:T(1024)(128)(2,1)S(1)}, bf16[576]{0:T(1024)(128)(2,1)S(1)}, bf16[576]{0:T(1024)(128)(2,1)S(1)}, bf16[576]{0:T(1024)(128)(2,1)S(1)}) all-reduce(bf16[576]{0:T(1024)(128)(2,1)S(1)} %dynamic-update-slice, bf16[576]{0:T(1024)(128)(2,1)S(1)} %dynamic-update-slice.1, ...), channel_id=2, replica_groups=mesh['ctx'=4,'fsdp'=8] {'fsdp'}, use_global_device_ids=true, to_apply=%add | all-reduce | flops 2304 | bytes 9216
  35.9 15.6 %all-gather.2 = bf16[1,576,576]{2,1,0:T(8,128)(2,1)S(1)} all-gather(bf16[1,72,576]{2,1,0:T(8,128)(2,1)S(1)} %get-tuple-element.1503), channel_id=4, replica_groups=mesh['ctx'=4,'fsdp'=8] {'fsdp'}, dimensions={1}, use_global_device_ids=true | all-gather | bytes 746496 | tf_op jit(solution)/shard_map/all_gather | solution.py:285
  52.6 15.5 %all-gather.1 = bf16[1,576,192]{2,1,0:T(8,128)(2,1)S(1)} all-gather(bf16[1,72,192]{2,1,0:T(8,128)(2,1)S(1)} %get-tuple-element.1505), channel_id=3, replica_groups=mesh['ctx'=4,'fsdp'=8] {'fsdp'}, dimensions={1}, use_global_device_ids=true | all-gather | bytes 248832 | tf_op jit(solution)/shard_map/all_gather | solution.py:286
  76.7 15.3 %all-gather.3 = bf16[1,576,192]{2,1,0:T(8,128)(2,1)S(1)} all-gather(bf16[1,72,192]{2,1,0:T(8,128)(2,1)S(1)} %get-tuple-element.1507), channel_id=5, replica_groups=mesh['ctx'=4,'fsdp'=8] {'fsdp'}, dimensions={1}, use_global_device_ids=true | all-gather | bytes 248832 | tf_op jit(solution)/shard_map/all_gather | solution.py:287
  96.4 17.1 %all-gather.4 = bf16[1,576,576]{2,1,0:T(8,128)(2,1)} all-gather(bf16[1,72,576]{2,1,0:T(8,128)(2,1)S(1)} %get-tuple-element.1501), channel_id=6, replica_groups=mesh['ctx'=4,'fsdp'=8] {'fsdp'}, dimensions={1}, use_global_device_ids=true | all-gather | bytes 746496 | tf_op jit(solution)/shard_map/all_gather | solution.py:288
  117.5 47.9 %while.96 = (s32[]{:T(128)}, f32[1,512,3,3,64]{1,4,3,2,0:T(8,128)S(1)}, f32[1,3,3,512]{3,2,1,0:T(4,128)S(1)}, f32[1,3,3,512]{3,2,1,0:T(4,128)S(1)}, bf16[1,512,3...) while((s32[]{:T(128)}, ...), condition=%wide.region_6.7_spmd.clone, body=%wide.region_3.6_spmd.clone.sunk | while | flops 640774144 | bytes 35367272 | solution.py:137
  120.9 4.4 collective-permute-done
  137.3 5.0 collective-permute-done
  168.4 18.2 %all-gather.11 = bf16[1,576,576]{2,1,0:T(8,128)(2,1)S(1)} all-gather(bf16[1,72,576]{2,1,0:T(8,128)(2,1)S(1)} %copy-done.102), channel_id=13, replica_groups=mesh['ctx'=4,'fsdp'=8] {'fsdp'}, dimensions={1}, use_global_device_ids=true | all-gather | bytes 746496 | tf_op jit(solution)/shard_map/all_gather | solution.py:285
  187.8 14.3 %all-gather.10 = bf16[1,576,192]{2,1,0:T(8,128)(2,1)S(1)} all-gather(bf16[1,72,192]{2,1,0:T(8,128)(2,1)S(1)} %copy-done.106), channel_id=12, replica_groups=mesh['ctx'=4,'fsdp'=8] {'fsdp'}, dimensions={1}, use_global_device_ids=true | all-gather | bytes 248832 | tf_op jit(solution)/shard_map/all_gather | solution.py:286
  202.9 14.3 %all-gather.12 = bf16[1,576,192]{2,1,0:T(8,128)(2,1)S(1)} all-gather(bf16[1,72,192]{2,1,0:T(8,128)(2,1)S(1)} %copy-done.107), channel_id=14, replica_groups=mesh['ctx'=4,'fsdp'=8] {'fsdp'}, dimensions={1}, use_global_device_ids=true | all-gather | bytes 248832 | tf_op jit(solution)/shard_map/all_gather | solution.py:287
  217.2 17.0 %all-gather.13 = bf16[1,576,576]{2,1,0:T(8,128)(2,1)} all-gather(bf16[1,72,576]{2,1,0:T(8,128)(2,1)S(1)} %copy-done.103), channel_id=15, replica_groups=mesh['ctx'=4,'fsdp'=8] {'fsdp'}, dimensions={1}, use_global_device_ids=true | all-gather | bytes 746496 | tf_op jit(solution)/shard_map/all_gather | solution.py:288
  234.4 4.7 fusion.194
  239.1 6.4 multiply_convert_fusion.3
  261.8 50.0 %while.97 = (s32[]{:T(128)}, f32[1,512,3,3,64]{1,4,3,2,0:T(8,128)}, f32[1,3,3,512]{3,2,1,0:T(4,128)S(1)}, f32[1,3,3,512]{3,2,1,0:T(4,128)S(1)}, bf16[1,512,3,64]...) while((s32[]{:T(128)}, f32[1,512,3,3,64]{1,4,3,2,0:T(8,128)}, ...), condition=%wide.region_14.15_spmd.clone, body=%wide.region_11.14_spmd.clone.sunk | while | flops 640774144 | bytes 44804512 | solution.py:137
  265.7 4.9 collective-permute-done.2
  282.9 5.0 collective-permute-done.2
  314.7 5.0 fusion.182
  319.7 4.7 fusion.172
  324.5 6.5 fusion.166
  350.6 77.6 %while.98 = (s32[]{:T(128)}, f32[1,512,3,3,64]{1,4,3,2,0:T(8,128)S(1)}, bf16[1,512,3,64]{1,3,2,0:T(8,128)(2,1)}, bf16[1,512,3,64]{1,3,2,0:T(8,128)(2,1)}, bf16[1...) while((s32[]{:T(128)}, ...), condition=%wide.region_19.20_spmd.clone, body=%wide.region_18.19_spmd.clone.sunk | while | flops 1545044992 | bytes 55706092 | solution.py:239
  362.4 4.9 fusion.464
  373.7 4.5 convert_add_fusion.10
  387.5 4.9 fusion.464
  398.8 4.5 convert_add_fusion.10
  412.4 4.9 fusion.464
  423.7 4.5 convert_add_fusion.10
  455.7 5.0 fusion.151
  465.1 66.1 %while.99 = (s32[]{:T(128)}, f32[1,512,3,3,64]{1,4,3,2,0:T(8,128)S(1)}, bf16[1,512,3,64]{1,3,2,0:T(8,128)(2,1)}, bf16[1,512,3,64]{1,3,2,0:T(8,128)(2,1)}, bf16[1...) while((s32[]{:T(128)}, ...), condition=%wide.region_24.25_spmd.clone, body=%wide.region_23.24_spmd.clone.sunk | while | flops 1545044992 | bytes 55853604 | solution.py:239
  482.8 4.5 convert_add_fusion.12
  504.8 4.5 convert_add_fusion.12
  526.7 4.5 convert_add_fusion.12
  561.8 4.1 convolution_convert_fusion
  567.2 4.2 convolution_convert_fusion.1
  585.5 14.0 %all-reduce.12 = (bf16[576]{0:T(1024)(128)(2,1)S(1)}, bf16[576]{0:T(1024)(128)(2,1)S(1)}, bf16[576]{0:T(1024)(128)(2,1)S(1)}, bf16[576]{0:T(1024)(128)(2,1)S(1)}) all-reduce(bf16[576]{0:T(1024)(128)(2,1)S(1)} %copy-done.134, bf16[576]{0:T(1024)(128)(2,1)S(1)} %get-tuple-element.1337, ...), channel_id=35, replica_groups=mesh['ctx'=4,'fsdp'=8] {'fsdp'}, use_global_device_ids=true, to_apply=%region_58.59.clone | all-reduce | flops 2304 | bytes 9216
  600.7 27.6 %reduce-scatter.27.cloned.1.call-done = bf16[72,192]{1,0:T(8,128)(2,1)} async-done(((bf16[576,192]{1,0:T(8,128)(2,1)}), bf16[72,192]{1,0:T(8,128)(2,1)}) %reduce-scatter.27.cloned.1.call-update) | async-done | bytes 27664 | tf_op jit(solution)/shard_map/reduce_scatter | solution.py:388
  628.4 32.1 %reduce-scatter.49.cloned.1.call-done = bf16[72,576]{1,0:T(8,128)(2,1)} async-done(((bf16[576,576]{1,0:T(8,128)(2,1)}), bf16[72,576]{1,0:T(8,128)(2,1)}) %reduce-scatter.49.cloned.1.call-update) | async-done | bytes 82960
  660.4 32.8 %reduce-scatter.45.cloned.1.call-done = bf16[72,576]{1,0:T(8,128)(2,1)} async-done(((bf16[576,576]{1,0:T(8,128)(2,1)}), bf16[72,576]{1,0:T(8,128)(2,1)}) %reduce-scatter.45.cloned.1.call-update) | async-done | bytes 82960
  693.2 32.2 %reduce-scatter.47.cloned.1.call-done = bf16[72,576]{1,0:T(8,128)(2,1)} async-done(((bf16[576,576]{1,0:T(8,128)(2,1)}), bf16[72,576]{1,0:T(8,128)(2,1)}) %reduce-scatter.47.cloned.1.call-update) | async-done | bytes 82960
  725.4 32.7 %reduce-scatter.43.cloned.1.call-done = bf16[72,576]{1,0:T(8,128)(2,1)} async-done(((bf16[576,576]{1,0:T(8,128)(2,1)}), bf16[72,576]{1,0:T(8,128)(2,1)}) %reduce-scatter.43.cloned.1.call-update) | async-done | bytes 82960
  758.2 35.4 %reduce-scatter.37.cloned.1.call-done = bf16[72,1536]{1,0:T(8,128)(2,1)} async-done(((bf16[576,1536]{1,0:T(8,128)(2,1)}), bf16[72,1536]{1,0:T(8,128)(2,1)}) %reduce-scatter.37.cloned.1.call-update) | async-done | bytes 221200 | tf_op jit(solution)/shard_map/reduce_scatter | solution.py:406
  793.5 35.2 %reduce-scatter.33.cloned.1.call-done = bf16[72,1536]{1,0:T(8,128)(2,1)} async-done(((bf16[576,1536]{1,0:T(8,128)(2,1)}), bf16[72,1536]{1,0:T(8,128)(2,1)}) %reduce-scatter.33.cloned.1.call-update) | async-done | bytes 221200 | tf_op jit(solution)/shard_map/reduce_scatter | solution.py:400
  828.7 35.8 %reduce-scatter.41.cloned.1.call-done = bf16[192,576]{1,0:T(8,128)(2,1)} async-done(((bf16[1536,576]{1,0:T(8,128)(2,1)}), bf16[192,576]{1,0:T(8,128)(2,1)}) %reduce-scatter.41.cloned.1.call-update) | async-done | bytes 221200 | tf_op jit(solution)/shard_map/reduce_scatter | solution.py:412
  864.5 36.2 %reduce-scatter.39.cloned.1.call-done = bf16[192,576]{1,0:T(8,128)(2,1)} async-done(((bf16[1536,576]{1,0:T(8,128)(2,1)}), bf16[192,576]{1,0:T(8,128)(2,1)}) %reduce-scatter.39.cloned.1.call-update) | async-done | bytes 221200 | tf_op jit(solution)/shard_map/reduce_scatter | solution.py:412
  900.7 35.5 %reduce-scatter.31.cloned.1.call-done = bf16[72,1536]{1,0:T(8,128)(2,1)} async-done(((bf16[576,1536]{1,0:T(8,128)(2,1)}), bf16[72,1536]{1,0:T(8,128)(2,1)}) %reduce-scatter.31.cloned.1.call-update) | async-done | bytes 221200 | tf_op jit(solution)/shard_map/reduce_scatter | solution.py:400
  936.2 35.2 %reduce-scatter.35.cloned.1.call-done = bf16[72,1536]{1,0:T(8,128)(2,1)} async-done(((bf16[576,1536]{1,0:T(8,128)(2,1)}), bf16[72,1536]{1,0:T(8,128)(2,1)}) %reduce-scatter.35.cloned.1.call-update) | async-done | bytes 221200 | tf_op jit(solution)/shard_map/reduce_scatter | solution.py:406
  976.9 41.2 %all-reduce.19.cloned.1.call-done = (bf16[1,72,192]{2,1,0:T(8,128)(2,1)}, bf16[1,72,192]{2,1,0:T(8,128)(2,1)}, bf16[1,72,192]{2,1,0:T(8,128)(2,1)}, bf16[1,72,19...) async-done(((bf16[1,72,192]{2,1,0:T(8,128)(2,1)}, bf16[1,72,192]{2,1,0:T(8,128)(2,1)}, ...) | async-done | bytes 111184 | tf_op jit(solution)/shard_map/psum | solution.py:381
  1023.5 65.8 %all-reduce.21.cloned.1.call-done = (bf16[1,72,576]{2,1,0:T(8,128)(2,1)}, bf16[1,72,576]{2,1,0:T(8,128)(2,1)}, bf16[1,72,576]{2,1,0:T(8,128)(2,1)}, bf16[1,72,57...) async-done(((bf16[1,72,576]{2,1,0:T(8,128)(2,1)}, ...) | async-done | bytes 1658896 | tf_op jit(solution)/shard_map/psum | solution.py:375
  (721 shorter events, 343.1 us)
Async XLA Ops:
  7.2 227.2 %all-gather.25.cloned.1.call-start = ((), (), s32[]{:S(2)}) async-start(), calls=%async_computation.24 | async-start | bytes 1990656 | tf_op jit(solution)/shard_map/all_gather | solution.py:289
  9.2 230.0 %all-gather.27.cloned.1.call-start = ((), (), s32[]{:S(2)}) async-start(), calls=%async_computation.25 | async-start | bytes 1990656 | tf_op jit(solution)/shard_map/all_gather | solution.py:290
  11.2 234.4 %all-gather.29.cloned.1.call-start = ((), (), s32[]{:S(2)}) async-start(), calls=%async_computation.26 | async-start | bytes 2211840 | tf_op jit(solution)/shard_map/all_gather | solution.py:291
  12.1 302.7 %all-gather.33.cloned.1.call-start = ((), (), s32[]{:S(2)}) async-start(), calls=%async_computation.28 | async-start | bytes 1990656 | tf_op jit(solution)/shard_map/all_gather | solution.py:290
  12.6 307.1 %all-gather.35.cloned.1.call-start = ((), (), s32[]{:S(2)}) async-start(), calls=%async_computation.29 | async-start | bytes 2211840 | tf_op jit(solution)/shard_map/all_gather | solution.py:291
  13.2 311.2 %all-gather.31.cloned.1.call-start = ((), (), s32[]{:S(2)}) async-start(), calls=%async_computation.27 | async-start | bytes 1990656 | tf_op jit(solution)/shard_map/all_gather | solution.py:289
  13.8 586.9 %reduce-scatter.25.cloned.1.call-start = ((), (), s32[]{:S(2)}) async-start(), calls=%async_computation.15 | async-start | bytes 331776 | tf_op jit(solution)/shard_map/reduce_scatter | solution.py:382
  117.5 7.8 collective-permute-start
  120.1 9.7 collective-permute-start.1
  133.6 8.8 collective-permute-start
  137.0 9.8 collective-permute-start.1
  154.0 7.6 collective-permute-start.1
  261.8 8.9 collective-permute-start.2
  265.4 9.7 collective-permute-start.3
  279.2 8.7 collective-permute-start.2
  282.6 9.8 collective-permute-start.3
  299.9 7.7 collective-permute-start.3
  351.0 9.1 collective-permute-start.4
  354.4 8.0 collective-permute-start.5
  354.5 16.1 %collective-permute-start.6 = (bf16[1,512,3,64]{1,3,2,0:T(8,128)(2,1)}, bf16[1,512,3,64]{1,3,2,0:T(8,128)(2,1)}, u32[]{:S(2)}, u32[]{:S(2)}) collective-permute-start(bf16[1,512,3,64]{1,3,2,0:T(8,128)(2,1)} %get-tuple-element.1967), channel_id=1, source_target_pairs={{8,0},{16,8},{24,16},{0,24},{9,1},{17,9},{25,17},{1,25},{10,2},{18... | collective-permute-start | bytes 589832 | tf_op jit(solution)/shard_map/while/body/eval_jaxpr/ppermute | solution.py:21
  356.4 17.3 %collective-permute-start.7 = (bf16[1,512,3,64]{1,3,2,0:T(8,128)(2,1)}, bf16[1,512,3,64]{1,3,2,0:T(8,128)(2,1)}, u32[]{:S(2)}, u32[]{:S(2)}) collective-permute-start(bf16[1,512,3,64]{1,3,2,0:T(8,128)(2,1)} %get-tuple-element.1968), channel_id=1, source_target_pairs={{8,0},{16,8},{24,16},{0,24},{9,1},{17,9},{25,17},{1,25},{10,2},{18... | collective-permute-start | bytes 589832 | tf_op jit(solution)/shard_map/while/body/eval_jaxpr/ppermute | solution.py:21
  378.3 6.8 collective-permute-start.4
  381.6 14.1 %collective-permute-start.6 = (bf16[1,512,3,64]{1,3,2,0:T(8,128)(2,1)}, bf16[1,512,3,64]{1,3,2,0:T(8,128)(2,1)}, u32[]{:S(2)}, u32[]{:S(2)}) collective-permute-start(bf16[1,512,3,64]{1,3,2,0:T(8,128)(2,1)} %get-tuple-element.1967), channel_id=1, source_target_pairs={{8,0},{16,8},{24,16},{0,24},{9,1},{17,9},{25,17},{1,25},{10,2},{18... | collective-permute-start | bytes 589832 | tf_op jit(solution)/shard_map/while/body/eval_jaxpr/ppermute | solution.py:21
  383.5 15.3 %collective-permute-start.7 = (bf16[1,512,3,64]{1,3,2,0:T(8,128)(2,1)}, bf16[1,512,3,64]{1,3,2,0:T(8,128)(2,1)}, u32[]{:S(2)}, u32[]{:S(2)}) collective-permute-start(bf16[1,512,3,64]{1,3,2,0:T(8,128)(2,1)} %get-tuple-element.1968), channel_id=1, source_target_pairs={{8,0},{16,8},{24,16},{0,24},{9,1},{17,9},{25,17},{1,25},{10,2},{18... | collective-permute-start | bytes 589832 | tf_op jit(solution)/shard_map/while/body/eval_jaxpr/ppermute | solution.py:21
  406.4 14.1 %collective-permute-start.6 = (bf16[1,512,3,64]{1,3,2,0:T(8,128)(2,1)}, bf16[1,512,3,64]{1,3,2,0:T(8,128)(2,1)}, u32[]{:S(2)}, u32[]{:S(2)}) collective-permute-start(bf16[1,512,3,64]{1,3,2,0:T(8,128)(2,1)} %get-tuple-element.1967), channel_id=1, source_target_pairs={{8,0},{16,8},{24,16},{0,24},{9,1},{17,9},{25,17},{1,25},{10,2},{18... | collective-permute-start | bytes 589832 | tf_op jit(solution)/shard_map/while/body/eval_jaxpr/ppermute | solution.py:21
  408.4 15.3 %collective-permute-start.7 = (bf16[1,512,3,64]{1,3,2,0:T(8,128)(2,1)}, bf16[1,512,3,64]{1,3,2,0:T(8,128)(2,1)}, u32[]{:S(2)}, u32[]{:S(2)}) collective-permute-start(bf16[1,512,3,64]{1,3,2,0:T(8,128)(2,1)} %get-tuple-element.1968), channel_id=1, source_target_pairs={{8,0},{16,8},{24,16},{0,24},{9,1},{17,9},{25,17},{1,25},{10,2},{18... | collective-permute-start | bytes 589832 | tf_op jit(solution)/shard_map/while/body/eval_jaxpr/ppermute | solution.py:21
  465.1 135.6 %reduce-scatter.29.cloned.1.call-start = ((), (), s32[]{:S(2)}) async-start(), calls=%async_computation.17 | async-start | bytes 331776 | tf_op jit(solution)/shard_map/reduce_scatter | solution.py:388
  468.5 12.1 %collective-permute-start.10 = (bf16[1,512,3,64]{1,3,2,0:T(8,128)(2,1)}, bf16[1,512,3,64]{1,3,2,0:T(8,128)(2,1)S(1)}, u32[]{:S(2)}, u32[]{:S(2)}) collective-permute-start(bf16[1,512,3,64]{1,3,2,0:T(8,128)(2,1)} %get-tuple-element.2021), channel_id=1, source_target_pairs={{8,0},{16,8},{24,16},{0,24},{9,1},{17,9},{25,17},{1,25},{10,2},{18... | collective-permute-start | bytes 589832 | tf_op jit(solution)/shard_map/while/body/eval_jaxpr/ppermute | solution.py:21
  470.4 12.4 %collective-permute-start.11 = (bf16[1,512,3,64]{1,3,2,0:T(8,128)(2,1)}, bf16[1,512,3,64]{1,3,2,0:T(8,128)(2,1)}, u32[]{:S(2)}, u32[]{:S(2)}) collective-permute-start(bf16[1,512,3,64]{1,3,2,0:T(8,128)(2,1)} %get-tuple-element.2022), channel_id=1, source_target_pairs={{8,0},{16,8},{24,16},{0,24},{9,1},{17,9},{25,17},{1,25},{10,2},{18... | collective-permute-start | bytes 589832 | tf_op jit(solution)/shard_map/while/body/eval_jaxpr/ppermute | solution.py:21
  490.4 12.1 %collective-permute-start.10 = (bf16[1,512,3,64]{1,3,2,0:T(8,128)(2,1)}, bf16[1,512,3,64]{1,3,2,0:T(8,128)(2,1)S(1)}, u32[]{:S(2)}, u32[]{:S(2)}) collective-permute-start(bf16[1,512,3,64]{1,3,2,0:T(8,128)(2,1)} %get-tuple-element.2021), channel_id=1, source_target_pairs={{8,0},{16,8},{24,16},{0,24},{9,1},{17,9},{25,17},{1,25},{10,2},{18... | collective-permute-start | bytes 589832 | tf_op jit(solution)/shard_map/while/body/eval_jaxpr/ppermute | solution.py:21
  492.3 12.4 %collective-permute-start.11 = (bf16[1,512,3,64]{1,3,2,0:T(8,128)(2,1)}, bf16[1,512,3,64]{1,3,2,0:T(8,128)(2,1)}, u32[]{:S(2)}, u32[]{:S(2)}) collective-permute-start(bf16[1,512,3,64]{1,3,2,0:T(8,128)(2,1)} %get-tuple-element.2022), channel_id=1, source_target_pairs={{8,0},{16,8},{24,16},{0,24},{9,1},{17,9},{25,17},{1,25},{10,2},{18... | collective-permute-start | bytes 589832 | tf_op jit(solution)/shard_map/while/body/eval_jaxpr/ppermute | solution.py:21
  512.3 12.1 %collective-permute-start.10 = (bf16[1,512,3,64]{1,3,2,0:T(8,128)(2,1)}, bf16[1,512,3,64]{1,3,2,0:T(8,128)(2,1)S(1)}, u32[]{:S(2)}, u32[]{:S(2)}) collective-permute-start(bf16[1,512,3,64]{1,3,2,0:T(8,128)(2,1)} %get-tuple-element.2021), channel_id=1, source_target_pairs={{8,0},{16,8},{24,16},{0,24},{9,1},{17,9},{25,17},{1,25},{10,2},{18... | collective-permute-start | bytes 589832 | tf_op jit(solution)/shard_map/while/body/eval_jaxpr/ppermute | solution.py:21
  514.3 12.4 %collective-permute-start.11 = (bf16[1,512,3,64]{1,3,2,0:T(8,128)(2,1)}, bf16[1,512,3,64]{1,3,2,0:T(8,128)(2,1)}, u32[]{:S(2)}, u32[]{:S(2)}) collective-permute-start(bf16[1,512,3,64]{1,3,2,0:T(8,128)(2,1)} %get-tuple-element.2022), channel_id=1, source_target_pairs={{8,0},{16,8},{24,16},{0,24},{9,1},{17,9},{25,17},{1,25},{10,2},{18... | collective-permute-start | bytes 589832 | tf_op jit(solution)/shard_map/while/body/eval_jaxpr/ppermute | solution.py:21
  534.3 6.7 collective-permute-start.15
  536.6 64.2 %reduce-scatter.23.cloned.1.call-start = ((), (), s32[]{:S(2)}) async-start(), calls=%async_computation.14 | async-start | bytes 331776 | tf_op jit(solution)/shard_map/reduce_scatter | solution.py:382
  541.0 87.3 %reduce-scatter.27.cloned.1.call-start = ((), (), s32[]{:S(2)}) async-start(), calls=%async_computation.16 | async-start | bytes 331776 | tf_op jit(solution)/shard_map/reduce_scatter | solution.py:388
  543.2 117.2 %reduce-scatter.49.cloned.1.call-start = ((), (), s32[]{:S(2)}) async-start(), calls=%async_computation.33 | async-start | bytes 829440
  545.9 147.3 %reduce-scatter.45.cloned.1.call-start = ((), (), s32[]{:S(2)}) async-start(), calls=%async_computation.31 | async-start | bytes 829440
  548.8 176.6 %reduce-scatter.47.cloned.1.call-start = ((), (), s32[]{:S(2)}) async-start(), calls=%async_computation.32 | async-start | bytes 829440
  550.4 207.7 %reduce-scatter.43.cloned.1.call-start = ((), (), s32[]{:S(2)}) async-start(), calls=%async_computation.30 | async-start | bytes 829440
  553.0 240.5 %reduce-scatter.37.cloned.1.call-start = ((), (), s32[]{:S(2)}) async-start(), calls=%async_computation.21 | async-start | bytes 1990656 | tf_op jit(solution)/shard_map/reduce_scatter | solution.py:406
  556.9 271.8 %reduce-scatter.33.cloned.1.call-start = ((), (), s32[]{:S(2)}) async-start(), calls=%async_computation.19 | async-start | bytes 1990656 | tf_op jit(solution)/shard_map/reduce_scatter | solution.py:400
  560.7 303.8 %reduce-scatter.41.cloned.1.call-start = ((), (), s32[]{:S(2)}) async-start(), calls=%async_computation.23 | async-start | bytes 2211840 | tf_op jit(solution)/shard_map/reduce_scatter | solution.py:412
  565.9 334.8 %reduce-scatter.39.cloned.1.call-start = ((), (), s32[]{:S(2)}) async-start(), calls=%async_computation.22 | async-start | bytes 2211840 | tf_op jit(solution)/shard_map/reduce_scatter | solution.py:412
  571.4 364.8 %reduce-scatter.31.cloned.1.call-start = ((), (), s32[]{:S(2)}) async-start(), calls=%async_computation.18 | async-start | bytes 1990656 | tf_op jit(solution)/shard_map/reduce_scatter | solution.py:400
  576.1 395.2 %reduce-scatter.35.cloned.1.call-start = ((), (), s32[]{:S(2)}) async-start(), calls=%async_computation.20 | async-start | bytes 1990656 | tf_op jit(solution)/shard_map/reduce_scatter | solution.py:406
  580.0 438.1 %all-reduce.19.cloned.1.call-start = ((), (), s32[]{:S(2)}) async-start(), calls=%async_computation.34 | async-start | bytes 299008 | tf_op jit(solution)/shard_map/psum | solution.py:381
  628.3 460.9 %all-reduce.21.cloned.1.call-start = ((), (), s32[]{:S(2)}) async-start(), calls=%async_computation.35 | async-start | bytes 3489792 | tf_op jit(solution)/shard_map/psum | solution.py:375
  (186 other events, 2132.9 us)
Sparse Core Ops, SparseCore 0:
  10.2 31.5 all-gather.24
  43.4 27.2 all-gather.26
  73.0 30.2 all-gather.28
  104.7 26.1 all-gather.32
  132.9 27.5 all-gather.34
  162.0 31.0 all-gather.30
  465.2 30.1 reduce-scatter.24
  536.7 29.1 reduce-scatter.28
  568.7 28.6 reduce-scatter.22
  599.6 28.6 reduce-scatter.26
  630.6 29.7 reduce-scatter.48
  663.3 29.8 reduce-scatter.44
  695.5 29.8 reduce-scatter.46
  728.3 29.8 reduce-scatter.42
  760.3 33.1 reduce-scatter.36
  795.7 32.9 reduce-scatter.32
  830.9 33.5 reduce-scatter.40
  866.8 33.8 reduce-scatter.38
  903.0 33.1 reduce-scatter.30
  938.4 32.9 reduce-scatter.34
  976.1 41.8 all-reduce.18
  1023.1 66.1 all-reduce.20
where the time goes:
time: 1110 us; the launch traced here: 1100 us
  waiting for transfers between devices  524 us (47%)
  matrix products  241 us (22%)
  blocking collectives  160 us (14%)
  starting transfers between devices  59 us (5%)
  local copies, waits for them, and re-layouts  51 us (5%)
  other arithmetic  46.7 us (4%)
  between operations  18.1 us (2%)
    unnamed x26, waiting for transfers between devices  132 us
    reduce_scatter x2, waiting for transfers between devices, body(): lax.psum_scatter(gradient_tree[6].astype(jnp.bfloat16), 'fsdp', scatter_d...  72 us
    reduce_scatter x2, waiting for transfers between devices, body(): lax.psum_scatter(gradient_tree[4].astype(jnp.bfloat16), 'fsdp', scatter_d...  70.7 us
    reduce_scatter x2, waiting for transfers between devices, body(): lax.psum_scatter(gradient_tree[5].astype(jnp.bfloat16), 'fsdp', scatter_d...  70.5 us
    psum x1, waiting for transfers between devices, body(): lax.psum(lax.psum_scatter(gradient_tree[0].astype(jnp.bfloat16), 'fsdp',...  65.8 us
    ppermute x40, starting transfers between devices, shifted(): return lax.ppermute(block, axis, route)  57.8 us
    ppermute x40, waiting for transfers between devices, shifted(): return lax.ppermute(block, axis, route)  45 us
    psum x1, waiting for transfers between devices, body(): lax.psum(lax.psum_scatter(gradient_tree[1].astype(jnp.bfloat16), 'fsdp',...  41.2 us
  transfers between devices with their start and end apart: 62, of which 34 were waited for; matrix products, arithmetic and copies ran while one was open for 23% of the time, Pallas kernels for 0%

commit v1 on v0

v1 whole, which is shorter than its diff:
```python
import jax
import jax.numpy as jnp
from jax import lax
from jax.experimental import pallas as pl
from jax.experimental.pallas import tpu as pltpu
from jax.sharding import PartitionSpec as P

HEADS = 9
KV_HEADS = 3
HD = 64
LAYERS = 2


epsilon = 1e-05
theta = 100000.0
log_two_e = 1.4426950408889634
mask_filler = -1e30


def flip(block, axis, mask):
    route = [(i, i ^ mask) for i in range(lax.axis_size(axis))]
    return lax.ppermute(block, axis, route)


def swap_halves(x):
    half = x.shape[1] // 2
    return jnp.concatenate(
        [x[:, :half], flip(x[:, half:], "ctx", lax.axis_size("ctx") - 1)], axis=1
    )


def tied(first, *then):
    return lax.optimization_barrier((first, then))[0]


def low(x):
    return x.astype(jnp.bfloat16)


def wide(x):
    return x.astype(jnp.float32)


PIECE = 384
VMEM_LIMIT = 48 * 1024 * 1024


def fold_down(shard):
    rows = shard.shape[0]
    right = shard[:, PIECE:]
    tall = jnp.concatenate(
        [shard[:, :PIECE], jnp.concatenate([right[: rows // 2], right[rows // 2 :]], axis=1)],
        axis=0,
    )
    return jnp.concatenate(jnp.split(tall, 4, axis=0), axis=1)


def unfold_down(folded):
    tall = jnp.concatenate(jnp.split(folded, 4, axis=-1), axis=-2)
    rows = tall.shape[-2] * 2 // 3
    left = tall[..., :rows, :]
    rest = tall[..., rows:, :]
    right = jnp.concatenate(jnp.split(rest, 2, axis=-1), axis=-2)
    return jnp.concatenate([left, right], axis=-1)


def assemble_kernel(count, own, own_flip, mine, theirs, out, sems):
    j = lax.axis_index("ctx")
    f = lax.axis_index("fsdp")
    copies = []

    def copy(src, dst):
        made = pltpu.make_async_copy(src, dst, sems.at[len(copies)])
        made.start()
        copies.append(made)

    copy(own, out.at[:, f])
    copy(own_flip, out.at[:, f ^ 1])
    for core, pieces in ((0, mine), (1, theirs)):
        for jrel in range(4):
            for zrel in range(1, 4):
                row = f ^ (core + 2 * zrel)
                column = pl.multiple_of((j ^ jrel) * PIECE, 128)
                copy(
                    pieces.at[jrel * 3 + zrel - 1],
                    out.at[:, row, :, pl.ds(column, PIECE)],
                )
    for made in copies:
        made.wait()


def assemble(own, own_flip, mine, theirs):
    count, rows, columns = own.shape
    fsdp = lax.axis_size("fsdp")
    return pl.pallas_call(
        lambda *refs: assemble_kernel(count, *refs),
        out_shape=jax.ShapeDtypeStruct((count, fsdp, rows, columns), own.dtype),
        in_specs=[pl.BlockSpec(memory_space=pl.ANY)] * 4,
        out_specs=pl.BlockSpec(memory_space=pltpu.VMEM),
        scratch_shapes=[pltpu.SemaphoreType.DMA((26,))],
        compiler_params=pltpu.CompilerParams(vmem_limit_bytes=VMEM_LIMIT),
        name="assemble",
    )(own, own_flip, mine, theirs)


def gather_line(own):
    j = lax.axis_index("ctx")
    piece = lax.dynamic_slice_in_dim(own, j * PIECE, PIECE, axis=2)
    return jnp.stack([flip(piece, "fsdp", 2 * k) for k in (1, 2, 3)])


def gather_rest(own, line):
    count, rows, columns = own.shape
    by_x = flip(line, "ctx", 1)
    by_y = flip(line, "ctx", 2)
    diag = jnp.concatenate([flip(by_x[:2], "ctx", 2), flip(by_y[2:], "ctx", 1)])
    mine = jnp.concatenate([line, by_x, by_y, diag])
    theirs = flip(mine, "fsdp", 1)
    own_flip = flip(own, "fsdp", 1)
    whole = assemble(own, own_flip, mine, theirs)
    return whole.reshape(count, -1, columns)


def gather_plain(own):
    return lax.all_gather(own, "fsdp", axis=1, tiled=True)


def scatter_kernel(whole, keep, send, sems):
    j = lax.axis_index("ctx")
    f = lax.axis_index("fsdp")
    copies = []
    for core, pieces in ((0, keep), (1, send)):
        for jrel in range(4):
            for zrel in range(4):
                row = f ^ (core + 2 * zrel)
                column = pl.multiple_of((j ^ jrel) * PIECE, 128)
                made = pltpu.make_async_copy(
                    whole.at[:, row, :, pl.ds(column, PIECE)],
                    pieces.at[jrel, zrel],
                    sems.at[len(copies)],
                )
                made.start()
                copies.append(made)
    for made in copies:
        made.wait()


def cut(whole):
    count, fsdp, rows, columns = whole.shape
    piece = jax.ShapeDtypeStruct((4, 4, count, rows, PIECE), whole.dtype)
    return pl.pallas_call(
        scatter_kernel,
        out_shape=(piece, piece),
        in_specs=[pl.BlockSpec(memory_space=pltpu.VMEM)],
        out_specs=[pl.BlockSpec(memory_space=pl.ANY)] * 2,
        scratch_shapes=[pltpu.SemaphoreType.DMA((32,))],
        compiler_params=pltpu.CompilerParams(vmem_limit_bytes=VMEM_LIMIT),
        name="cut",
    )(whole)


def reduce_fast(whole):
    keep, send = cut(whole)
    total = wide(keep) + wide(flip(send, "fsdp", 1))
    a = total[:, :2]
    b = total[:, 2:]
    x1 = wide(flip(low(jnp.stack([a[1], a[3]])), "ctx", 1))
    y1 = wide(flip(low(jnp.stack([b[2], b[3]])), "ctx", 2))
    a0, a2 = a[0] + x1[0], a[2] + x1[1]
    b0, b1 = b[0] + y1[0], b[1] + y1[1]
    a0 = a0 + wide(flip(low(a2), "ctx", 2))
    b0 = b0 + wide(flip(low(b1), "ctx", 1))
    return (
        a0[0]
        + wide(flip(low(a0[1]), "fsdp", 2))
        + wide(flip(low(b0[0]), "fsdp", 4))
        + wide(flip(low(b0[1]), "fsdp", 6))
    )


def spread_fast(piece):
    j = lax.axis_index("ctx")
    own = low(piece)
    parts = [own] + [flip(own, "ctx", k) for k in (1, 2, 3)]
    for bit in (1, 2):
        odd = (j & bit) != 0
        parts = [jnp.where(odd, parts[i ^ bit], parts[i]) for i in range(4)]
    return wide(jnp.concatenate(parts, axis=2))


def reduce_line(whole):
    part = lax.psum_scatter(whole, "fsdp", scatter_dimension=0, tiled=True)
    rows, columns = part.shape
    count = columns // (4 * PIECE)
    j = lax.axis_index("ctx")

    def piece(k):
        return jnp.stack(
            [
                lax.dynamic_slice_in_dim(part, m * 4 * PIECE + (j ^ k) * PIECE, PIECE, axis=1)
                for m in range(count)
            ]
        )

    return sum((wide(flip(piece(k), "ctx", k)) for k in (1, 2, 3)), wide(piece(0)))


def reduce_plain(whole):
    part = lax.psum_scatter(whole, "fsdp", scatter_dimension=1, tiled=True)
    return wide(lax.psum(part, "ctx"))


def dot_nn(a, b):
    return jnp.dot(a, b, preferred_element_type=jnp.float32)


def dot_nt(a, b):
    return lax.dot_general(a, b, (((1,), (1,)), ((), ())), preferred_element_type=jnp.float32)


def chunks_of(source, slots):
    return (2 * source, 2 * slots - 1 - 2 * source)


def stack_heads(ref, dst, half):
    group = HEADS // KV_HEADS
    for g in range(KV_HEADS):
        for part in range(2):
            for i in range(group):
                h = g * group + i
                dst[g, part, i * half : (i + 1) * half] = ref[
                    part * half : (part + 1) * half, h * HD : (h + 1) * HD
                ]


def thrice(row):
    return jnp.concatenate([row] * (HEADS // KV_HEADS), axis=1)


def attend_kernel(slots, *refs):
    q_ref, start_ref = refs[:2]
    kv_refs = refs[2 : 2 + slots]
    o_ref, lse_ref, qs, ks, vt, top_s, acc_s, ot = refs[2 + slots :]
    rank = lax.axis_index("ctx")
    half = q_ref.shape[0] // 2
    group = HEADS // KV_HEADS
    wide_cols = group * half
    stack_heads(q_ref, qs, half)
    ones = jnp.ones((16, half), jnp.bfloat16)
    for k in range(slots):
        values_t = low(jnp.transpose(wide(kv_refs[k][:, 128:])))
        for g in range(KV_HEADS):
            row = KV_HEADS * HD - 128 + g * HD
            for part in range(2):
                rows = slice(part * half, (part + 1) * half)
                ks[k, g, part] = kv_refs[k][rows, g * HD : (g + 1) * HD]
                vt[k, g, part, :HD] = values_t[row : row + HD, rows]
                vt[k, g, part, HD:] = ones
    lse_ref[...] = jnp.zeros_like(lse_ref)
    mine = chunks_of(rank, slots)

    def one_group(g, carry):
        for part in range(2):
            cols = slice(part * half, (part + 1) * half)
            start = thrice(start_ref[:, cols])
            q = qs[g, part]

            def scores(k, other, first):
                s = dot_nt(ks[k, g, other], q)
                key = lax.broadcasted_iota(jnp.int32, s.shape, 0)
                visible = key >= start - first
                return s, key, visible

            s, key, visible = scores(0, part, mine[part] * half)
            query = thrice(lax.broadcasted_iota(jnp.int32, (half, half), 1))
            s = jnp.where(visible & (key <= query), s, mask_filler)
            top = jnp.floor(jnp.max(s, axis=0, keepdims=True))
            top_s[...] = top
            acc_s[...] = dot_nn(vt[0, g, part], low(jnp.exp2(s - top)))

            def tile(k, other, chunk):
                @pl.when(chunk < mine[part])
                def _():
                    s, _, visible = scores(k, other, chunk * half)
                    s = jnp.where(visible, s, mask_filler)
                    old = top_s[...]
                    top = jnp.maximum(old, jnp.floor(jnp.max(s, axis=0, keepdims=True)))
                    top_s[...] = top
                    acc_s[...] = acc_s[...] * jnp.exp2(old - top) + dot_nn(
                        vt[k, g, other], low(jnp.exp2(s - top))
                    )

            tile(0, 1 - part, mine[1 - part])

            def slot(k, carry):
                theirs = chunks_of(rank ^ k, slots)
                for other in range(2):
                    tile(k, other, theirs[other])
                return carry

            lax.fori_loop(1, slots, slot, 0)
            total = acc_s[HD : HD + 1]
            out = acc_s[:HD] / total
            level = top_s[...] + jnp.log2(total)
            for i in range(group):
                inner = slice(i * half, (i + 1) * half)
                ot[g, i, :, cols] = out[:, inner]
                lse_ref[pl.ds(g * group + i, 1), cols] = level[:, inner]
        return carry

    lax.fori_loop(0, KV_HEADS, one_group, 0)
    o_ref[...] = low(jnp.transpose(ot[...].reshape(HEADS * HD, 2 * half)))


def attend(q, start, kvs):
    block = q.shape[0]
    half = block // 2
    slots = len(kvs)
    group = HEADS // KV_HEADS
    vmem = pl.BlockSpec(memory_space=pltpu.VMEM)
    return pl.pallas_call(
        lambda *refs: attend_kernel(slots, *refs),
        out_shape=(
            jax.ShapeDtypeStruct((block, HEADS * HD), jnp.bfloat16),
            jax.ShapeDtypeStruct((16, block), jnp.float32),
        ),
        in_specs=[vmem] * (2 + slots),
        out_specs=[vmem] * 2,
        scratch_shapes=[
            pltpu.VMEM((KV_HEADS, 2, group * half, HD), jnp.bfloat16),
            pltpu.VMEM((slots, KV_HEADS, 2, half, HD), jnp.bfloat16),
            pltpu.VMEM((slots, KV_HEADS, 2, HD + 16, half), jnp.bfloat16),
            pltpu.VMEM((1, group * half), jnp.float32),
            pltpu.VMEM((HD + 16, group * half), jnp.float32),
            pltpu.VMEM((KV_HEADS, group, HD, block), jnp.float32),
        ],
        compiler_params=pltpu.CompilerParams(vmem_limit_bytes=VMEM_LIMIT),
        cost_estimate=pl.CostEstimate(flops=15_000_000_000, bytes_accessed=4_000_000, transcendentals=0),
        name="attend",
    )(q, start, *kvs)


def attend_back_kernel(slots, *refs):
    q_ref, o_ref, do_ref, lse_ref, start_ref = refs[:5]
    kv_refs = refs[5 : 5 + slots]
    dq_ref = refs[5 + slots]
    dkv_refs = refs[6 + slots : 6 + 2 * slots]
    qs, dos, ks, kt, vs, dk_s, dv_s, dqt_s, delta_s, dqt_all = refs[6 + 2 * slots :]
    rank = lax.axis_index("ctx")
    half = q_ref.shape[0] // 2
    group = HEADS // KV_HEADS
    stack_heads(q_ref, qs, half)
    stack_heads(do_ref, dos, half)
    for k in range(slots):
        keys_t = low(jnp.transpose(wide(kv_refs[k][:, : 2 * 128])))
        for g in range(KV_HEADS):
            for part in range(2):
                rows = slice(part * half, (part + 1) * half)
                ks[k, g, part] = kv_refs[k][rows, g * HD : (g + 1) * HD]
                kt[k, g, part] = keys_t[g * HD : (g + 1) * HD, rows]
                vs[k, g, part] = kv_refs[k][rows, (KV_HEADS + g) * HD : (KV_HEADS + g + 1) * HD]
    product = wide(do_ref[...]) * wide(o_ref[...])
    coarse = low(product)
    fine = low(product - wide(coarse))
    shape = (16, HEADS * HD)
    owner = lax.div(lax.broadcasted_iota(jnp.int32, shape, 1), HD)
    pick = jnp.where(owner == lax.broadcasted_iota(jnp.int32, shape, 0), 1.0, 0.0)
    pick = pick.astype(jnp.bfloat16)
    delta_s[...] = dot_nt(pick, coarse) + dot_nt(pick, fine)
    dk_s[...] = jnp.zeros_like(dk_s)
    dv_s[...] = jnp.zeros_like(dv_s)
    mine = chunks_of(rank, slots)

    def one_group(g, carry):
        for part in range(2):
            cols = slice(part * half, (part + 1) * half)
            start = thrice(start_ref[:, cols])
            heads = [pl.ds(g * group + i, 1) for i in range(group)]
            lse = jnp.concatenate([lse_ref[h, cols] for h in heads], axis=1)
            delta = jnp.concatenate([delta_s[h, cols] for h in heads], axis=1)

            def tile(k, other, first, diagonal):
                q = qs[g, part]
                do = dos[g, part]
                s = dot_nt(ks[k, g, other], q)
                key = lax.broadcasted_iota(jnp.int32, s.shape, 0)
                visible = key >= start - first
                if diagonal:
                    query = thrice(lax.broadcasted_iota(jnp.int32, (half, half), 1))
                    visible = visible & (key <= query)
                p = jnp.where(visible, jnp.exp2(s - lse), 0.0)
                dv = dot_nn(low(p), do)
                dp = dot_nt(vs[k, g, other], do)
                ds = low(p * (dp - delta))
                dk_s[k, g, other] += dot_nn(ds, q)
                dv_s[k, g, other] += dv
                dq = dot_nn(kt[k, g, other], ds)
                if diagonal:
                    dqt_s[...] = dq
                else:
                    dqt_s[...] += dq

            tile(0, part, mine[part] * half, True)

            @pl.when(mine[1 - part] < mine[part])
            def _():
                tile(0, 1 - part, mine[1 - part] * half, False)

            def slot(k, carry):
                theirs = chunks_of(rank ^ k, slots)
                for other in range(2):

                    @pl.when(theirs[other] < mine[part])
                    def _():
                        tile(k, other, theirs[other] * half, False)

                return carry

            lax.fori_loop(1, slots, slot, 0)
            for i in range(group):
                dqt_all[g, i, :, cols] = dqt_s[:, i * half : (i + 1) * half]
        return carry

    lax.fori_loop(0, KV_HEADS, one_group, 0)
    dq_ref[...] = jnp.transpose(dqt_all[...].reshape(HEADS * HD, 2 * half)) * 0.125
    for k in range(slots):
        for part in range(2):
            dkv = jnp.concatenate(
                [dk_s[k, g, part] * (1.0 / log_two_e) for g in range(KV_HEADS)]
                + [dv_s[k, g, part] for g in range(KV_HEADS)],
                axis=1,
            )
            dkv_refs[k][part * half : (part + 1) * half] = dkv.astype(dkv_refs[k].dtype)


def attend_back(q, o, do, lse, start_row, kvs):
    block = q.shape[0]
    half = block // 2
    slots = len(kvs)
    group = HEADS // KV_HEADS
    vmem = pl.BlockSpec(memory_space=pltpu.VMEM)
    pair = lambda kind: jax.ShapeDtypeStruct((block, 2 * KV_HEADS * HD), kind)
    return pl.pallas_call(
        lambda *refs: attend_back_kernel(slots, *refs),
        out_shape=(
            jax.ShapeDtypeStruct((block, HEADS * HD), jnp.float32),
            pair(jnp.float32),
            *[pair(jnp.bfloat16)] * (slots - 1),
        ),
        in_specs=[vmem] * (5 + slots),
        out_specs=[vmem] * (1 + slots),
        scratch_shapes=[
            pltpu.VMEM((KV_HEADS, 2, group * half, HD), jnp.bfloat16),
            pltpu.VMEM((KV_HEADS, 2, group * half, HD), jnp.bfloat16),
            pltpu.VMEM((slots, KV_HEADS, 2, half, HD), jnp.bfloat16),
            pltpu.VMEM((slots, KV_HEADS, 2, HD, half), jnp.bfloat16),
            pltpu.VMEM((slots, KV_HEADS, 2, half, HD), jnp.bfloat16),
            pltpu.VMEM((slots, KV_HEADS, 2, half, HD), jnp.float32),
            pltpu.VMEM((slots, KV_HEADS, 2, half, HD), jnp.float32),
            pltpu.VMEM((HD, group * half), jnp.float32),
            pltpu.VMEM((16, block), jnp.float32),
            pltpu.VMEM((KV_HEADS, group, HD, block), jnp.float32),
        ],
        compiler_params=pltpu.CompilerParams(vmem_limit_bytes=VMEM_LIMIT),
        cost_estimate=pl.CostEstimate(flops=20_000_000_000, bytes_accessed=4_000_000, transcendentals=0),
        name="attend_back",
    )(q, o, do, lse, start_row, *kvs)


def rms_norm(hidden, gain):
    scale = lax.rsqrt(jnp.mean(hidden * hidden, axis=-1, keepdims=True) + epsilon)
    return hidden * scale * gain


def rope_tables(positions, head_size):
    half = head_size // 2
    freq = theta ** (-(jnp.arange(half, dtype=jnp.float32) * 2.0 / head_size))
    angle = positions.astype(jnp.float32)[..., None] * freq
    return (jnp.cos(angle), jnp.sin(angle))


def rotate(values, cosine, sine):
    half = values.shape[-1] // 2
    first = values[..., :half]
    second = values[..., half:]
    cosine = cosine[..., None, :]
    sine = sine[..., None, :]
    return jnp.concatenate(
        [first * cosine - second * sine, second * cosine + first * sine], axis=-1
    )


def project(input_tokens, weight_matrix):
    return jnp.einsum(
        "vnk,kp->vnp", input_tokens, weight_matrix, preferred_element_type=jnp.float32
    )


def project_back(gradient_tree, weight_matrix):
    return jnp.einsum(
        "qzy,gy->qzg", gradient_tree, weight_matrix, preferred_element_type=jnp.float32
    )


def outer_sum(input_tokens, gradient_tree):
    return jnp.einsum(
        "cwu,cwf->uf", input_tokens, gradient_tree, preferred_element_type=jnp.float32
    )


def body(
    tokens,
    positions,
    query_weight,
    key_matrix,
    value_weight,
    out_weight,
    gate_weight,
    up_weight,
    down_weight,
    attn_gain,
    mlp_gain,
    cotangent,
):
    cycle_size = lax.axis_size("ctx")
    cycle_rank = lax.axis_index("ctx")
    sequence_count, block, width = tokens.shape
    kv_heads = KV_HEADS
    group = HEADS // KV_HEADS
    head_size = HD
    tokens = swap_halves(tokens)
    positions = swap_halves(positions)
    cosine, sine = rope_tables(positions, head_size)
    half = block // 2
    first_row, second_row = chunks_of(cycle_rank, cycle_size)
    offsets = jnp.arange(half, dtype=jnp.int32)
    row_index = jnp.concatenate([first_row * half + offsets, second_row * half + offsets])
    doc_start = row_index[None, :] - positions

    def backward_layer(grad_out, full, kept):
        (
            query_full,
            key_full,
            value_full,
            out_full,
            gate_full,
            up_full,
            down_full,
            first_gain,
            second_gain,
        ) = full
        (
            hidden,
            normed_low,
            queries,
            kvs,
            lse,
            attn_low,
            middle,
            mixed_low,
            gate,
            upward,
            inner,
        ) = kept
        down_in = grad_out.astype(jnp.bfloat16)
        grad_down = outer_sum(inner, down_in)
        d_inner = project_back(down_in, down_full)
        unused, pull_gate = jax.vjp(
            lambda gate_in, up_in: jax.nn.silu(gate_in) * up_in, gate, upward
        )
        d_gate, d_up = pull_gate(d_inner)
        d_gate = d_gate.astype(jnp.bfloat16)
        d_up = d_up.astype(jnp.bfloat16)
        grad_gate = outer_sum(mixed_low, d_gate)
        grad_up = outer_sum(mixed_low, d_up)
        d_mixed = project_back(d_gate, gate_full) + project_back(d_up, up_full)
        unused, pull_second = jax.vjp(rms_norm, middle, second_gain.astype(jnp.float32))
        d_middle, grad_second = pull_second(d_mixed)
        grad_mid = grad_out + d_middle
        mid_low = grad_mid.astype(jnp.bfloat16)
        grad_out_proj = outer_sum(attn_low, mid_low)
        d_attention = low(project_back(mid_low, out_full)[0])
        d_query, *d_pairs = attend_back(
            queries, attn_low[0], d_attention, lse, doc_start, kvs
        )
        d_pair = d_pairs[0]
        for k, part in enumerate(d_pairs[1:]):
            d_pair = d_pair + wide(flip(part, "ctx", k + 1))
        travel = (
            d_pair[:, : kv_heads * head_size].reshape(1, block, kv_heads, head_size),
            d_pair[:, kv_heads * head_size :],
        )
        dq_low = (
            rotate(d_query.reshape(sequence_count, block, HEADS, head_size), cosine, -sine)
            .astype(jnp.bfloat16)
            .reshape(sequence_count, block, HEADS * head_size)
        )
        dk_low = (
            rotate(travel[0], cosine, -sine)
            .astype(jnp.bfloat16)
            .reshape(sequence_count, block, kv_heads * head_size)
        )
        dv_low = travel[1].astype(jnp.bfloat16).reshape(sequence_count, block, kv_heads * head_size)
        grad_query = outer_sum(normed_low, dq_low)
        grad_key = outer_sum(normed_low, dk_low)
        grad_value = outer_sum(normed_low, dv_low)
        normed_gradient = (
            project_back(dq_low, query_full)
            + project_back(dk_low, key_full)
            + project_back(dv_low, value_full)
        )
        unused, pull_first = jax.vjp(rms_norm, hidden, first_gain.astype(jnp.float32))
        d_hidden, grad_first = pull_first(normed_gradient)
        grad_in = grad_mid + d_hidden
        return (
            grad_in,
            (
                grad_query,
                grad_key,
                grad_value,
                grad_out_proj,
                grad_gate,
                grad_up,
                grad_down,
                grad_first,
                grad_second,
            ),
        )

    fast = cycle_size == 4 and lax.axis_size("fsdp") == 8
    heads_width = HEADS * head_size
    kv_width = kv_heads * head_size
    packs = [
        jnp.stack(
            [
                jnp.concatenate(
                    [query_weight[i], key_matrix[i], value_weight[i], out_weight[i]], axis=1
                ),
                gate_weight[i],
                up_weight[i],
                fold_down(down_weight[i]),
            ]
        )
        for i in range(LAYERS)
    ]
    gains = lax.all_gather(jnp.concatenate([attn_gain, mlp_gain]), "fsdp", axis=1, tiled=True)
    if fast:
        own_first = packs[0][:1]
        own_second = jnp.concatenate([packs[0][1:], packs[1][:1]])
        first_line = gather_line(own_first)
        second_line = gather_line(tied(own_second, first_line))
        third = gather_plain(tied(packs[1][1:], second_line))
        first = gather_rest(own_first, first_line)
        whole = [(first[0], None, None, None), (None, third[0], third[1], third[2])]
    else:
        third = [gather_plain(packs[i]) for i in range(LAYERS)]
        whole = [tuple(third[i][m] for m in range(4)) for i in range(LAYERS)]

    def attention_weights(i):
        attn = whole[i][0]
        ends = (heads_width, heads_width + kv_width, heads_width + 2 * kv_width)
        return (
            attn[:, : ends[0]],
            attn[:, ends[0] : ends[1]],
            attn[:, ends[1] : ends[2]],
            attn[:, ends[2] :],
        )

    def mlp_weights(i):
        _, gate_full, up_full, folded = whole[i]
        fsdp = lax.axis_size("fsdp")
        down_full = unfold_down(folded.reshape(fsdp, -1, folded.shape[1])).reshape(-1, width)
        return (gate_full, up_full, down_full)

    fulls = []
    hidden = tokens.astype(jnp.float32)
    saved = []
    for index in range(LAYERS):
        (
            forward_query_full,
            forward_key_full,
            forward_value_full,
            forward_out_full,
        ) = attention_weights(index)
        forward_first_gain, forward_second_gain = gains[index], gains[LAYERS + index]
        forward_normed_low = rms_norm(hidden, forward_first_gain.astype(jnp.float32)).astype(
            jnp.bfloat16
        )
        query_pre = project(forward_normed_low, forward_query_full)
        key_pre = project(forward_normed_low, forward_key_full)
        forward_value_low = low(project(forward_normed_low, forward_value_full))[0]
        forward_queries = rotate(
            query_pre.reshape(sequence_count, block, HEADS, head_size), cosine, sine
        )
        forward_queries = low(forward_queries * (0.125 * log_two_e)).reshape(block, -1)
        forward_key_rows = rotate(
            key_pre.reshape(sequence_count, block, kv_heads, head_size), cosine, sine
        )
        forward_key_rows = low(forward_key_rows).reshape(block, -1)
        pair = jnp.concatenate([forward_key_rows, forward_value_low], axis=1)
        kvs = [pair] + [flip(pair, "ctx", k) for k in range(1, cycle_size)]
        if fast and index == 0:
            second = gather_rest(own_second, tied(second_line, kvs))
            whole = [(first[0], *second[:3]), (second[3], *third)]
        forward_attn_low, lse = attend(forward_queries, doc_start, kvs)
        forward_attn_low = forward_attn_low[None]
        forward_gate_full, forward_up_full, forward_down_full = mlp_weights(index)
        fulls.append(
            (
                forward_query_full,
                forward_key_full,
                forward_value_full,
                forward_out_full,
                forward_gate_full,
                forward_up_full,
                forward_down_full,
                forward_first_gain,
                forward_second_gain,
            )
        )
        forward_middle = hidden + project(forward_attn_low, forward_out_full)
        forward_mixed_low = rms_norm(
            forward_middle, forward_second_gain.astype(jnp.float32)
        ).astype(jnp.bfloat16)
        forward_gate = project(forward_mixed_low, forward_gate_full)
        forward_upward = project(forward_mixed_low, forward_up_full)
        forward_inner = (jax.nn.silu(forward_gate) * forward_upward).astype(jnp.bfloat16)
        output = forward_middle + project(forward_inner, forward_down_full)
        forward_kept = (
            hidden,
            forward_normed_low,
            forward_queries,
            kvs,
            lse,
            forward_attn_low,
            forward_middle,
            forward_mixed_low,
            forward_gate,
            forward_upward,
            forward_inner,
        )
        hidden = output
        kept = forward_kept
        saved.append(kept)
    layer_out = swap_halves(low(hidden))
    grad = wide(swap_halves(tied(cotangent, saved[0][0])))
    matrix_grads = [None] * LAYERS
    gain_grads = [None] * LAYERS
    fsdp = lax.axis_size("fsdp")
    gain_rows = attn_gain.shape[1]
    for index in reversed(range(LAYERS)):
        grad, tree = backward_layer(grad, fulls[index], saved[index])
        gain_grads[index] = (tree[7], tree[8])
        down_rows = low(tree[6]).reshape(fsdp, -1, width)
        folded = jax.vmap(fold_down)(down_rows).reshape(width, -1)
        attn = jnp.concatenate([low(part) for part in tree[:4]], axis=1)
        rest = (low(tree[4]), low(tree[5]), folded)
        if fast and index == 0:
            by_shard = lambda x: x.reshape(fsdp, gain_rows, -1)
            rest_piece = reduce_fast(jnp.stack([by_shard(part) for part in rest]))
            rest_grads = spread_fast(rest_piece)
            gain_parts = jnp.stack([gain_grads[i][m] for m in range(2) for i in range(LAYERS)])
            gain_parts = low(gain_parts).reshape(2 * LAYERS, fsdp, gain_rows).transpose(1, 0, 2)
            gain_parts = gain_parts.reshape(fsdp, 1, -1)
            gain_parts = jnp.pad(gain_parts, ((0, 0), (0, 7), (0, PIECE - gain_parts.shape[2])))
            last = jnp.concatenate([by_shard(attn), jnp.tile(gain_parts, (1, 1, 4))], axis=1)
            attn_piece = reduce_fast(last[None])
            all_gains = attn_piece[0, gain_rows, : 2 * LAYERS * gain_rows]
            all_gains = all_gains.reshape(2 * LAYERS, gain_rows)
            attn_grads = spread_fast(attn_piece[:, :gain_rows])
            matrix_grads[index] = jnp.concatenate([attn_grads, rest_grads])
        elif fast:
            rest_piece = reduce_line(jnp.concatenate(rest, axis=1))
            attn_piece = reduce_line(attn)
            matrix_grads[index] = spread_fast(jnp.concatenate([attn_piece, rest_piece]))
        else:
            matrix_grads[index] = reduce_plain(jnp.stack([attn, *rest]))
    if not fast:
        all_gains = jnp.stack([gain_grads[i][m] for m in range(2) for i in range(LAYERS)])
        all_gains = lax.psum(all_gains, ("ctx", "fsdp"))
        all_gains = lax.dynamic_slice_in_dim(
            all_gains, lax.axis_index("fsdp") * gain_rows, gain_rows, axis=1
        )
    grad = wide(swap_halves(low(grad)))
    stacked = jnp.stack(matrix_grads)
    ends = (heads_width, heads_width + kv_width, heads_width + 2 * kv_width)
    results = (
        stacked[:, 0, :, : ends[0]],
        stacked[:, 0, :, ends[0] : ends[1]],
        stacked[:, 0, :, ends[1] : ends[2]],
        stacked[:, 0, :, ends[2] :],
        stacked[:, 1],
        stacked[:, 2],
        unfold_down(stacked[:, 3]),
        all_gains[:LAYERS],
        all_gains[LAYERS:],
    )
    return (
        layer_out,
        grad,
        results[0],
        results[1],
        results[2],
        results[3],
        results[4],
        results[5],
        results[6],
        results[7],
        results[8],
    )


def solution(mesh):
    return jax.shard_map(
        body,
        mesh=mesh,
        in_specs=(
            P("fsdp", "ctx", None),
            P("fsdp", "ctx"),
            P(None, "fsdp", None),
            P(None, "fsdp", None),
            P(None, "fsdp", None),
            P(None, "fsdp", None),
            P(None, "fsdp", None),
            P(None, "fsdp", None),
            P(None, "fsdp", None),
            P(None, "fsdp"),
            P(None, "fsdp"),
            P("fsdp", "ctx", None),
        ),
        out_specs=(
            P("fsdp", "ctx", None),
            P("fsdp", "ctx", None),
            P(None, "fsdp", None),
            P(None, "fsdp", None),
            P(None, "fsdp", None),
            P(None, "fsdp", None),
            P(None, "fsdp", None),
            P(None, "fsdp", None),
            P(None, "fsdp", None),
            P(None, "fsdp"),
            P(None, "fsdp"),
        ),
        check_vma=False,
    )
```

time: 1110 us -> 565 us (0.51)
  waiting for transfers between devices: 524 us -> 86.4 us
  matrix products: 241 us -> 69.7 us
  blocking collectives: 160 us -> 12 us
  Pallas kernels: 0 us -> 97 us
  local copies, waits for them, and re-layouts: 51 us -> 137 us
  starting transfers between devices: 59 us -> 81.1 us
    reduce_scatter x10 -> x2, waiting for transfers between devices: 241 us -> 0.01 us  [reduce_line(): part = lax.psum_scatter(whole, 'fsdp', scatter_dimension=0, tiled=True)]
    dot_general x54 -> x0, matrix products: 147 us -> none  [the longest x8 35.3 us: contrib(): jnp.einsum('sqgjd,skgd->sgjqk', d_numer, value_in, preferred_element_type...]
    unnamed x26 -> x3, waiting for transfers between devices: 132 us -> 0.05 us
    all_gather x8 -> x1, blocking collectives: 127 us -> 12 us  [body(): lax.all_gather(jnp.concatenate([attn_gain, mlp_gain]), 'fsdp', axis=1, ti...]
    psum x2 -> x0, waiting for transfers between devices: 107 us -> none  [the longest x1 65.8 us: body(): lax.psum(lax.psum_scatter(gradient_tree[0].astype(jnp.bfloat16), 'fsdp',...]
    pallas_call x0 -> x8, Pallas kernels: none -> 97 us  [the longest x2 47.4 us: attend_back(): pl.pallas_call(lambda *refs: attend_back_kernel(slots, *refs), out_shape=...]
    ppermute x40 -> x66, waiting for transfers between devices: 45 us -> 86.4 us  [flip(): return lax.ppermute(block, axis, route)]
    unnamed x2 -> x0, blocking collectives: 33 us -> none
  transfers between devices with their start and end apart: 62 -> 69, of which waited for: 34 -> 21; matrix products, arithmetic and copies ran while one was open for 23% -> 34% of each run, Pallas kernels for 0% -> 13%
where the time goes in v1:
time: 565 us; the launch traced here: 557 us
  local copies, waits for them, and re-layouts  137 us (24%)
  Pallas kernels  97 us (17%)
  waiting for transfers between devices  86.4 us (15%)
  starting transfers between devices  81.1 us (14%)
  matrix products  69.7 us (12%)
  other arithmetic  57.3 us (10%)
  between operations  16.6 us (3%)
  blocking collectives  12 us (2%)
    ppermute x66, waiting for transfers between devices, flip(): return lax.ppermute(block, axis, route)  86.4 us
    ppermute x66, starting transfers between devices, flip(): return lax.ppermute(block, axis, route)  80.4 us
    unnamed x349, local copies, waits for them, and re-layouts  52.6 us
    pallas_call x2, Pallas kernels, attend_back(): pl.pallas_call(lambda *refs: attend_back_kernel(slots, *refs), out_shape=...  47.4 us
    pallas_call x2, Pallas kernels, attend(): pl.pallas_call(lambda *refs: attend_kernel(slots, *refs), out_shape=(jax....  36.3 us
    dot_general x14, matrix products, project_back(): jnp.einsum('qzy,gy->qzg', gradient_tree, weight_matrix, preferred_element...  24.3 us
    dot_general x14, matrix products, outer_sum(): jnp.einsum('cwu,cwf->uf', input_tokens, gradient_tree, preferred_element_...  23.1 us
    dot_general x14, matrix products, project(): jnp.einsum('vnk,kp->vnp', input_tokens, weight_matrix, preferred_element_...  22.3 us
  transfers between devices with their start and end apart: 69, of which 21 were waited for; matrix products, arithmetic and copies ran while one was open for 34% of the time, Pallas kernels for 13%

profile of v1, /device:TPU:0, one launch (start us, length us, event | category | flops | bytes accessed | tf_op | source)
XLA Modules:
  0.0 557.3 jit_solution(1895309586457175748)
XLA Ops:
  10.6 3.0 collective-permute-start.2
  13.6 2.6 collective-permute-start.3
  17.2 2.7 collective-permute-start
  21.4 12.0 %all-gather = bf16[8,72,4]{1,2,0:T(4,128)(2,1)S(1)} all-gather(bf16[1,72,4]{1,2,0:T(4,128)(2,1)S(1)} %maximum_bitcast_fusion.6), channel_id=1, replica_groups=mesh['ctx'=4,'fsdp'=8] {'fsdp'}, dimensions={0}, use_global_device_ids=true | all-gather | bytes 5184 | tf_op jit(solution)/shard_map/all_gather | solution.py:646
  65.4 4.4 collective-permute-start.17
  71.8 12.5 %collective-permute-done.16 = bf16[4,72,384]{2,1,0:T(8,128)(2,1)S(1)} collective-permute-done((bf16[4,72,384]{2,1,0:T(8,128)(2,1)}, bf16[4,72,384]{2,1,0:T(8,128)(2,1)S(1)}, u32[]{:S(2)}, u32[]{:S(2)}) %collective-permute-start.16) | collective-permute-done | bytes 221216 | tf_op jit(solution)/shard_map/ppermute | solution.py:22
  96.7 12.1 %collective-permute-done.18 = bf16[3,4,72,384]{3,2,1,0:T(8,128)(2,1)} collective-permute-done((bf16[3,4,72,384]{3,2,1,0:T(8,128)(2,1)}, bf16[3,4,72,384]{3,2,1,0:T(8,128)(2,1)}, u32[]{:S(2)}, u32[]{:S(2)}) %collective-permute-start.18) | collective-permute-done | bytes 663584 | tf_op jit(solution)/shard_map/ppermute | solution.py:22
  112.5 2.3 copy.120
  135.1 17.5 %attend.2 = (bf16[512,576]{1,0:T(8,128)(2,1)S(1)}, f32[16,512]{1,0:T(8,128)S(1)}) custom-call(bf16[512,576]{1,0:T(8,128)(2,1)S(1)} %copy-done.4, s32[1,512]{1,0:T(1,128)S(1)} %add_subtract_fusion.refs_1_.refs_4_, bf16[512,384]{1,0:T(8,128)(2,1)S(1)} %copy-done.11, bf16[512,384]{1,0:T(8,128)(2,1)S(1)} %copy-done.16, bf16[512,384]{1,0:T(8,128)(2,1)S(1)} %copy-done.19, ...), custom_call_target="tpu_custom_call" | custom-call | flops 15000000512 | bytes 4000000 | tf_op jit(solution)/shard_map/attend/pallas_call | solution.py:321
  155.0 6.0 %assemble.3 = bf16[4,8,72,1536]{3,2,1,0:T(8,128)(2,1)} custom-call(bf16[4,72,1536]{2,1,0:T(8,128)(2,1)S(1)} %pad_maximum_fusion.17.refs_0_, bf16[4,72,1536]{2,1,0:T(8,128)(2,1)S(1)} %collective-permute-done.14.refs_1_, bf16[12,4,72,384]{3,2,1,0:T(8,128)(2,1)} %constant_dynamic-update-slice_fusion.7.refs_2_, ...), custom_call_target="tpu_custom_call" | custom-call | tf_op jit(solution)/shard_map/assemble/pallas_call | solution.py:95
  161.0 5.7 %fusion.136 = (bf16[1,8,72,1536]{3,2,1,0:T(8,128)(2,1)S(1)}, bf16[8,72,1536]{2,1,0:T(8,128)(2,1)}, bf16[1,8,72,1536]{3,2,1,0:T(8,128)(2,1)}, bf16[1,8,72,1536]{3,2,1,0:T(8,128)(2,1)}) fusion(bf16[4,8,72,1536]{3,2,1,0:T(8,128)(2,1)} %assemble.3), kind=kLoop, calls=%fused_computation.388 | loop fusion | bytes 14155776 | tf_op jit(solution)/shard_map/slice | solution.py:704
  175.8 3.5 multiply_convert_fusion.3
  191.3 2.3 copy.125
  198.7 7.7 %collective-permute-done.24.refs_4_.refs_7_ = bf16[512,384]{1,0:T(8,128)(2,1)} collective-permute-done((bf16[512,384]{1,0:T(8,128)(2,1)S(1)}, bf16[512,384]{1,0:T(8,128)(2,1)}, u32[]{:S(2)}, u32[]{:S(2)}) %collective-permute-start.24) | collective-permute-done | bytes 393248 | tf_op jit(solution)/shard_map/ppermute | solution.py:22
  207.4 18.8 %attend.3 = (bf16[512,576]{1,0:T(8,128)(2,1)S(1)}, f32[16,512]{1,0:T(8,128)S(1)}) custom-call(bf16[512,576]{1,0:T(8,128)(2,1)S(1)} %copy.129.refs_0_, s32[1,512]{1,0:T(1,128)S(1)} %add_subtract_fusion.refs_1_.refs_4_, bf16[512,384]{1,0:T(8,128)(2,1)S(1)} %pad_maximum_fusion.30.refs_2_.refs_5_, bf16[512,384]{1,0:T(8,128)(2,1)S(1)} %copy-done.25, ...), custom_call_target="tpu_custom_call" | custom-call | flops 15000000512 | bytes 4000000 | tf_op jit(solution)/shard_map/attend/pallas_call | solution.py:321
  237.6 4.7 multiply_convert_fusion.1
  255.9 24.3 %attend_back.2 = (f32[512,576]{1,0:T(8,128)}, f32[512,384]{1,0:T(8,128)S(1)}, bf16[512,384]{1,0:T(8,128)(2,1)S(1)}, bf16[512,384]{1,0:T(8,128)(2,1)S(1)}, bf16[512,384]{1,0:T(8,128)(2,1)S(1)}) custom-call(bf16[512,576]{1,0:T(8,128)(2,1)S(1)} %copy-done.7, bf16[512,576]{1,0:T(8,128)(2,1)S(1)} %get-tuple-element.35.refs_1_, bf16[512,576]{1,0:T(8,128)(2,1)S(1)} %copy-done.9, ...), custom_call_target="tpu_custom_call" | custom-call | flops 20000000000 | bytes 4000000 | tf_op jit(solution)/shard_map/attend_back/pallas_call | solution.py:443
  282.5 2.8 copy.132
  294.2 3.3 collective-permute-done.28
  297.5 7.5 %collective-permute-done.29 = bf16[512,384]{1,0:T(8,128)(2,1)S(1)} collective-permute-done((bf16[512,384]{1,0:T(8,128)(2,1)}, bf16[512,384]{1,0:T(8,128)(2,1)S(1)}, u32[]{:S(2)}, u32[]{:S(2)}) %collective-permute-start.29) | collective-permute-done | bytes 393248 | tf_op jit(solution)/shard_map/ppermute | solution.py:22
  311.7 3.9 concatenate.365
  315.7 2.7 convolution_convert_fusion
  318.4 2.4 copy.149
  320.8 2.6 slice.633
  324.1 3.3 fusion.38
  333.7 2.8 pad_maximum_fusion.1
  339.7 2.8 multiply_reduce_fusion.2
  344.3 2.9 fusion.10
  355.7 2.3 convolution_convert_fusion.1
  365.3 23.1 %attend_back.3 = (f32[512,576]{1,0:T(8,128)}, f32[512,384]{1,0:T(8,128)S(1)}, bf16[512,384]{1,0:T(8,128)(2,1)}, bf16[512,384]{1,0:T(8,128)(2,1)S(1)}, bf16[512,384]{1,0:T(8,128)(2,1)S(1)}) custom-call(bf16[512,576]{1,0:T(8,128)(2,1)S(1)} %copy-done.5, bf16[512,576]{1,0:T(8,128)(2,1)S(1)} %copy-done.3, bf16[512,576]{1,0:T(8,128)(2,1)S(1)} %copy-done.8, ...), custom_call_target="tpu_custom_call" | custom-call | flops 20000000000 | bytes 4000000 | tf_op jit(solution)/shard_map/attend_back/pallas_call | solution.py:443
  389.9 2.8 copy.136
  399.4 3.9 copy.146
  405.5 3.9 convolution_convert_fusion.5
  411.7 3.3 fusion.26
  429.9 2.6 concatenate.357
  436.5 2.9 pad_maximum_fusion.whole
  439.4 4.9 cut.3
  450.7 5.8 %collective-permute-done.36 = bf16[2,2,1,80,384]{4,3,1,2,0:T(8,128)(2,1)S(1)} collective-permute-done((bf16[2,2,1,80,384]{4,3,1,2,0:T(8,128)(2,1)S(1)}, bf16[2,2,1,80,384]{4,3,1,2,0:T(8,128)(2,1)S(1)}, u32[]{:S(2)}, u32[]{:S(2)}) %collective-permute-start.36) | collective-permute-done | bytes 245792 | tf_op jit(solution)/shard_map/ppermute | solution.py:22
  461.0 2.7 collective-permute-done.40
  463.7 3.0 collective-permute-start.41
  470.0 4.8 convert_add_fusion
  477.2 2.4 collective-permute-start.38
  487.4 4.7 collective-permute-done.47
  506.6 3.0 collective-permute-start.52
  512.1 5.6 %collective-permute-done.52 = bf16[3,72,384]{2,1,0:T(8,128)(2,1)S(1)} collective-permute-done((bf16[3,72,384]{2,1,0:T(8,128)(2,1)S(1)}, bf16[3,72,384]{2,1,0:T(8,128)(2,1)S(1)}, u32[]{:S(2)}, u32[]{:S(2)}) %collective-permute-start.52) | collective-permute-done | bytes 165920 | tf_op jit(solution)/shard_map/ppermute | solution.py:22
  528.0 2.7 collective-permute-done.60
  530.7 5.9 %collective-permute-done.61 = bf16[3,72,384]{2,1,0:T(8,128)(2,1)S(1)} collective-permute-done((bf16[3,72,384]{2,1,0:T(8,128)(2,1)S(1)}, bf16[3,72,384]{2,1,0:T(8,128)(2,1)S(1)}, u32[]{:S(2)}, u32[]{:S(2)}) %collective-permute-start.61) | collective-permute-done | bytes 165920 | tf_op jit(solution)/shard_map/ppermute | solution.py:22
  540.4 3.4 collective-permute-done.63
  (670 shorter events, 268.3 us)
Async XLA Ops:
  7.2 223.4 %all-gather.3.cloned.1.call-start = ((), (), s32[]{:S(2)}) async-start(), calls=%async_computation.2 | async-start | bytes 5971968 | tf_op jit(solution)/shard_map/all_gather | solution.py:125
  10.6 25.3 %collective-permute-start.2 = (bf16[1,72,384]{2,1,0:T(8,128)(2,1)}, bf16[1,72,384]{2,1,0:T(8,128)(2,1)S(1)}, u32[]{:S(2)}, u32[]{:S(2)}) collective-permute-start(bf16[1,72,384]{2,1,0:T(8,128)(2,1)} %dynamic-slice_bitcast_fusion.15), channel_id=1, source_target_pairs={{0,2},{1,3},{2,0},{3,1},{4,6},{5,7},{6,4},{7,5},{8,10},{9,11},{10,... | collective-permute-start | bytes 165896 | tf_op jit(solution)/shard_map/ppermute | solution.py:22
  13.6 23.0 %collective-permute-start.3 = (bf16[1,72,384]{2,1,0:T(8,128)(2,1)}, bf16[1,72,384]{2,1,0:T(8,128)(2,1)}, u32[]{:S(2)}, u32[]{:S(2)}) collective-permute-start(bf16[1,72,384]{2,1,0:T(8,128)(2,1)} %dynamic-slice_bitcast_fusion.15), channel_id=1, source_target_pairs={{0,4},{1,5},{2,6},{3,7},{4,0},{5,1},{6,2},{7,3},{8,12},{9,13},{10,... | collective-permute-start | bytes 165896 | tf_op jit(solution)/shard_map/ppermute | solution.py:22
  16.2 20.5 %collective-permute-start.4 = (bf16[1,72,384]{2,1,0:T(8,128)(2,1)}, bf16[1,72,384]{2,1,0:T(8,128)(2,1)}, u32[]{:S(2)}, u32[]{:S(2)}) collective-permute-start(bf16[1,72,384]{2,1,0:T(8,128)(2,1)} %dynamic-slice_bitcast_fusion.15), channel_id=1, source_target_pairs={{0,6},{1,7},{2,4},{3,5},{4,2},{5,3},{6,0},{7,1},{8,14},{9,15},{10,... | collective-permute-start | bytes 165896 | tf_op jit(solution)/shard_map/ppermute | solution.py:22
  16.3 35.9 %collective-permute-start.1 = (bf16[1,72,1536]{2,1,0:T(8,128)(2,1)S(1)}, bf16[1,72,1536]{2,1,0:T(8,128)(2,1)S(1)}, u32[]{:S(2)}, u32[]{:S(2)}) collective-permute-start(bf16[1,72,1536]{2,1,0:T(8,128)(2,1)S(1)} %bitcast.324), channel_id=1, source_target_pairs={{0,1},{1,0},{2,3},{3,2},{4,5},{5,4},{6,7},{7,6},{8,9},{9,8},{10,11... | collective-permute-start | bytes 663560 | tf_op jit(solution)/shard_map/ppermute | solution.py:22
  17.2 34.8 %collective-permute-start = (bf16[1,256,576]{1,2,0:T(8,128)(2,1)}, bf16[1,256,576]{1,2,0:T(8,128)(2,1)S(1)}, u32[]{:S(2)}, u32[]{:S(2)}) collective-permute-start(bf16[1,256,576]{1,2,0:T(8,128)(2,1)} %get-tuple-element.153), channel_id=1, source_target_pairs={{0,24},{8,16},{16,8},{24,0},{1,25},{9,17},{17,9},{25,1},{2,26},{10... | collective-permute-start | bytes 884744 | tf_op jit(solution)/shard_map/ppermute | solution.py:22
  36.2 13.5 %collective-permute-start.10 = (s32[1,256]{1,0:T(1,128)S(1)}, s32[1,256]{1,0:T(1,128)S(1)}, u32[]{:S(2)}, u32[]{:S(2)}) collective-permute-start(s32[1,256]{1,0:T(1,128)S(1)} %copy-done.154), channel_id=1, source_target_pairs={{0,24},{8,16},{16,8},{24,0},{1,25},{9,17},{17,9},{25,1},{2,26},{10... | collective-permute-start | bytes 3080 | tf_op jit(solution)/shard_map/ppermute | solution.py:22
  52.0 13.4 %collective-permute-start.15 = (bf16[4,72,384]{2,1,0:T(8,128)(2,1)}, bf16[4,72,384]{2,1,0:T(8,128)(2,1)}, u32[]{:S(2)}, u32[]{:S(2)}) collective-permute-start(bf16[4,72,384]{2,1,0:T(8,128)(2,1)} %constant_dynamic-slice_fusion), channel_id=1, source_target_pairs={{0,2},{1,3},{2,0},{3,1},{4,6},{5,7},{6,4},{7,5},{8,10},{9,11},{10,... | collective-permute-start | bytes 663560 | tf_op jit(solution)/shard_map/ppermute | solution.py:22
  61.8 25.9 %collective-permute-start.11 = (bf16[512,384]{1,0:T(8,128)(2,1)S(1)}, bf16[512,384]{1,0:T(8,128)(2,1)S(1)}, u32[]{:S(2)}, u32[]{:S(2)}) collective-permute-start(bf16[512,384]{1,0:T(8,128)(2,1)S(1)} %pad_maximum_fusion.29.refs_2_.refs_5_), channel_id=1, source_target_pairs={{0,8},{8,0},{16,24},{24,16},{1,9},{9,1},{17,25},{25,17},{2,10},{10... | collective-permute-start | bytes 1179656 | tf_op jit(solution)/shard_map/ppermute | solution.py:22
  63.3 25.1 %collective-permute-start.12 = (bf16[512,384]{1,0:T(8,128)(2,1)S(1)}, bf16[512,384]{1,0:T(8,128)(2,1)S(1)}, u32[]{:S(2)}, u32[]{:S(2)}) collective-permute-start(bf16[512,384]{1,0:T(8,128)(2,1)S(1)} %pad_maximum_fusion.29.refs_2_.refs_5_), channel_id=1, source_target_pairs={{0,16},{8,24},{16,0},{24,8},{1,17},{9,25},{17,1},{25,9},{2,18},{10... | collective-permute-start | bytes 1179656 | tf_op jit(solution)/shard_map/ppermute | solution.py:22
  63.9 25.3 %collective-permute-start.13 = (bf16[512,384]{1,0:T(8,128)(2,1)S(1)}, bf16[512,384]{1,0:T(8,128)(2,1)S(1)}, u32[]{:S(2)}, u32[]{:S(2)}) collective-permute-start(bf16[512,384]{1,0:T(8,128)(2,1)S(1)} %pad_maximum_fusion.29.refs_2_.refs_5_), channel_id=1, source_target_pairs={{0,24},{8,16},{16,8},{24,0},{1,25},{9,17},{17,9},{25,1},{2,26},{10... | collective-permute-start | bytes 1179656 | tf_op jit(solution)/shard_map/ppermute | solution.py:22
  65.3 19.0 %collective-permute-start.16 = (bf16[4,72,384]{2,1,0:T(8,128)(2,1)}, bf16[4,72,384]{2,1,0:T(8,128)(2,1)S(1)}, u32[]{:S(2)}, u32[]{:S(2)}) collective-permute-start(bf16[4,72,384]{2,1,0:T(8,128)(2,1)} %constant_dynamic-slice_fusion), channel_id=1, source_target_pairs={{0,4},{1,5},{2,6},{3,7},{4,0},{5,1},{6,2},{7,3},{8,12},{9,13},{10,... | collective-permute-start | bytes 663560 | tf_op jit(solution)/shard_map/ppermute | solution.py:22
  65.4 18.9 %collective-permute-start.17 = (bf16[4,72,384]{2,1,0:T(8,128)(2,1)}, bf16[4,72,384]{2,1,0:T(8,128)(2,1)S(1)}, u32[]{:S(2)}, u32[]{:S(2)}) collective-permute-start(bf16[4,72,384]{2,1,0:T(8,128)(2,1)} %constant_dynamic-slice_fusion), channel_id=1, source_target_pairs={{0,6},{1,7},{2,4},{3,5},{4,2},{5,3},{6,0},{7,1},{8,14},{9,15},{10,... | collective-permute-start | bytes 663560 | tf_op jit(solution)/shard_map/ppermute | solution.py:22
  84.3 70.7 %collective-permute-start.14 = (bf16[4,72,1536]{2,1,0:T(8,128)(2,1)S(1)}, bf16[4,72,1536]{2,1,0:T(8,128)(2,1)S(1)}, u32[]{:S(2)}, u32[]{:S(2)}) collective-permute-start(bf16[4,72,1536]{2,1,0:T(8,128)(2,1)S(1)} %pad_maximum_fusion.17.refs_0_), channel_id=1, source_target_pairs={{0,1},{1,0},{2,3},{3,2},{4,5},{5,4},{6,7},{7,6},{8,9},{9,8},{10,11... | collective-permute-start | bytes 2654216 | tf_op jit(solution)/shard_map/ppermute | solution.py:22
  84.3 153.3 %collective-permute-start.27 = (bf16[1,256,576]{1,2,0:T(8,128)(2,1)}, bf16[1,256,576]{1,2,0:T(8,128)(2,1)}, u32[]{:S(2)}, u32[]{:S(2)}) collective-permute-start(bf16[1,256,576]{1,2,0:T(8,128)(2,1)} %get-tuple-element.148), channel_id=1, source_target_pairs={{0,24},{8,16},{16,8},{24,0},{1,25},{9,17},{17,9},{25,1},{2,26},{10... | collective-permute-start | bytes 884744 | tf_op jit(solution)/shard_map/ppermute | solution.py:22
  89.9 18.8 %collective-permute-start.18 = (bf16[3,4,72,384]{3,2,1,0:T(8,128)(2,1)}, bf16[3,4,72,384]{3,2,1,0:T(8,128)(2,1)}, u32[]{:S(2)}, u32[]{:S(2)}) collective-permute-start(bf16[3,4,72,384]{3,2,1,0:T(8,128)(2,1)} %pad_maximum_fusion.18), channel_id=1, source_target_pairs={{0,8},{8,0},{16,24},{24,16},{1,9},{9,1},{17,25},{25,17},{2,10},{10... | collective-permute-start | bytes 1990664 | tf_op jit(solution)/shard_map/ppermute | solution.py:22
  93.9 22.9 %collective-permute-start.19 = (bf16[3,4,72,384]{3,2,1,0:T(8,128)(2,1)}, bf16[3,4,72,384]{3,2,1,0:T(8,128)(2,1)}, u32[]{:S(2)}, u32[]{:S(2)}) collective-permute-start(bf16[3,4,72,384]{3,2,1,0:T(8,128)(2,1)} %pad_maximum_fusion.18), channel_id=1, source_target_pairs={{0,16},{8,24},{16,0},{24,8},{1,17},{9,25},{17,1},{25,9},{2,18},{10... | collective-permute-start | bytes 1990664 | tf_op jit(solution)/shard_map/ppermute | solution.py:22
  96.1 404.5 %reduce-scatter.3.cloned.1.call-start = ((), (), s32[]{:S(2)}) async-start(), calls=%async_computation.3 | async-start | bytes 1990656 | tf_op jit(solution)/shard_map/reduce_scatter | solution.py:192
  110.6 12.8 %collective-permute-start.20 = (bf16[2,4,72,384]{3,2,1,0:T(8,128)(2,1)}, bf16[2,4,72,384]{3,2,1,0:T(8,128)(2,1)}, u32[]{:S(2)}, u32[]{:S(2)}) collective-permute-start(bf16[2,4,72,384]{3,2,1,0:T(8,128)(2,1)} %slice.567), channel_id=1, source_target_pairs={{0,16},{8,24},{16,0},{24,8},{1,17},{9,25},{17,1},{25,9},{2,18},{10... | collective-permute-start | bytes 1327112 | tf_op jit(solution)/shard_map/ppermute | solution.py:22
  125.9 29.1 %collective-permute-start.22 = (bf16[12,4,72,384]{3,2,1,0:T(8,128)(2,1)}, bf16[12,4,72,384]{3,2,1,0:T(8,128)(2,1)}, u32[]{:S(2)}, u32[]{:S(2)}) collective-permute-start(bf16[12,4,72,384]{3,2,1,0:T(8,128)(2,1)} %constant_dynamic-update-slice_fusion.7.refs_2_), channel_id=1, source_target_pairs={{0,1},{1,0},{2,3},{3,2},{4,5},{5,4},{6,7},{7,6},{8,9},{9,8},{10,11... | collective-permute-start | bytes 7962632 | tf_op jit(solution)/shard_map/ppermute | solution.py:22
  185.7 12.2 %collective-permute-start.23 = (bf16[512,384]{1,0:T(8,128)(2,1)S(1)}, bf16[512,384]{1,0:T(8,128)(2,1)S(1)}, u32[]{:S(2)}, u32[]{:S(2)}) collective-permute-start(bf16[512,384]{1,0:T(8,128)(2,1)S(1)} %pad_maximum_fusion.30.refs_2_.refs_5_), channel_id=1, source_target_pairs={{0,8},{8,0},{16,24},{24,16},{1,9},{9,1},{17,25},{25,17},{2,10},{10... | collective-permute-start | bytes 1179656 | tf_op jit(solution)/shard_map/ppermute | solution.py:22
  186.6 19.8 %collective-permute-start.24 = (bf16[512,384]{1,0:T(8,128)(2,1)S(1)}, bf16[512,384]{1,0:T(8,128)(2,1)}, u32[]{:S(2)}, u32[]{:S(2)}) collective-permute-start(bf16[512,384]{1,0:T(8,128)(2,1)S(1)} %pad_maximum_fusion.30.refs_2_.refs_5_), channel_id=1, source_target_pairs={{0,16},{8,24},{16,0},{24,8},{1,17},{9,25},{17,1},{25,9},{2,18},{10... | collective-permute-start | bytes 1179656 | tf_op jit(solution)/shard_map/ppermute | solution.py:22
  187.6 18.8 %collective-permute-start.25 = (bf16[512,384]{1,0:T(8,128)(2,1)S(1)}, bf16[512,384]{1,0:T(8,128)(2,1)}, u32[]{:S(2)}, u32[]{:S(2)}) collective-permute-start(bf16[512,384]{1,0:T(8,128)(2,1)S(1)} %pad_maximum_fusion.30.refs_2_.refs_5_), channel_id=1, source_target_pairs={{0,24},{8,16},{16,8},{24,0},{1,25},{9,17},{17,9},{25,1},{2,26},{10... | collective-permute-start | bytes 1179656 | tf_op jit(solution)/shard_map/ppermute | solution.py:22
  285.3 12.3 %collective-permute-start.28 = (bf16[512,384]{1,0:T(8,128)(2,1)}, bf16[512,384]{1,0:T(8,128)(2,1)S(1)}, u32[]{:S(2)}, u32[]{:S(2)}) collective-permute-start(bf16[512,384]{1,0:T(8,128)(2,1)} %copy-done.33), channel_id=1, source_target_pairs={{0,8},{8,0},{16,24},{24,16},{1,9},{9,1},{17,25},{25,17},{2,10},{10... | collective-permute-start | bytes 1179656 | tf_op jit(solution)/shard_map/ppermute | solution.py:22
  286.4 18.6 %collective-permute-start.29 = (bf16[512,384]{1,0:T(8,128)(2,1)}, bf16[512,384]{1,0:T(8,128)(2,1)S(1)}, u32[]{:S(2)}, u32[]{:S(2)}) collective-permute-start(bf16[512,384]{1,0:T(8,128)(2,1)} %copy-done.32), channel_id=1, source_target_pairs={{0,16},{8,24},{16,0},{24,8},{1,17},{9,25},{17,1},{25,9},{2,18},{10... | collective-permute-start | bytes 1179656 | tf_op jit(solution)/shard_map/ppermute | solution.py:22
  287.0 18.0 %collective-permute-start.30 = (bf16[512,384]{1,0:T(8,128)(2,1)}, bf16[512,384]{1,0:T(8,128)(2,1)S(1)}, u32[]{:S(2)}, u32[]{:S(2)}) collective-permute-start(bf16[512,384]{1,0:T(8,128)(2,1)} %copy-done.31), channel_id=1, source_target_pairs={{0,24},{8,16},{16,8},{24,0},{1,25},{9,17},{17,9},{25,1},{2,26},{10... | collective-permute-start | bytes 1179656 | tf_op jit(solution)/shard_map/ppermute | solution.py:22
  315.6 207.2 %reduce-scatter.5.cloned.1.call-start = ((), (), s32[]{:S(2)}) async-start(), calls=%async_computation.4 | async-start | bytes 5971968 | tf_op jit(solution)/shard_map/reduce_scatter | solution.py:192
  328.3 116.2 %collective-permute-start.26 = (bf16[1,256,576]{1,2,0:T(8,128)(2,1)}, bf16[1,256,576]{1,2,0:T(8,128)(2,1)}, u32[]{:S(2)}, u32[]{:S(2)}) collective-permute-start(bf16[1,256,576]{1,2,0:T(8,128)(2,1)} %get-tuple-element.151), channel_id=1, source_target_pairs={{0,24},{8,16},{16,8},{24,0},{1,25},{9,17},{17,9},{25,1},{2,26},{10... | collective-permute-start | bytes 884744 | tf_op jit(solution)/shard_map/ppermute | solution.py:22
  395.9 19.2 %collective-permute-start.31 = (bf16[512,384]{1,0:T(8,128)(2,1)}, bf16[512,384]{1,0:T(8,128)(2,1)}, u32[]{:S(2)}, u32[]{:S(2)}) collective-permute-start(bf16[512,384]{1,0:T(8,128)(2,1)} %get-tuple-element.46), channel_id=1, source_target_pairs={{0,8},{8,0},{16,24},{24,16},{1,9},{9,1},{17,25},{25,17},{2,10},{10... | collective-permute-start | bytes 1179656 | tf_op jit(solution)/shard_map/ppermute | solution.py:22
  396.9 18.2 %collective-permute-start.32 = (bf16[512,384]{1,0:T(8,128)(2,1)S(1)}, bf16[512,384]{1,0:T(8,128)(2,1)}, u32[]{:S(2)}, u32[]{:S(2)}) collective-permute-start(bf16[512,384]{1,0:T(8,128)(2,1)S(1)} %copy-done.30), channel_id=1, source_target_pairs={{0,16},{8,24},{16,0},{24,8},{1,17},{9,25},{17,1},{25,9},{2,18},{10... | collective-permute-start | bytes 1179656 | tf_op jit(solution)/shard_map/ppermute | solution.py:22
  397.9 17.2 %collective-permute-start.33 = (bf16[512,384]{1,0:T(8,128)(2,1)S(1)}, bf16[512,384]{1,0:T(8,128)(2,1)}, u32[]{:S(2)}, u32[]{:S(2)}) collective-permute-start(bf16[512,384]{1,0:T(8,128)(2,1)S(1)} %copy-done.28), channel_id=1, source_target_pairs={{0,24},{8,16},{16,8},{24,0},{1,25},{9,17},{17,9},{25,1},{2,26},{10... | collective-permute-start | bytes 1179656 | tf_op jit(solution)/shard_map/ppermute | solution.py:22
  434.1 12.3 %collective-permute-start.35 = (bf16[4,4,1,80,384]{4,3,1,2,0:T(8,128)(2,1)}, bf16[4,4,1,80,384]{4,3,1,2,0:T(8,128)(2,1)}, u32[]{:S(2)}, u32[]{:S(2)}) collective-permute-start(bf16[4,4,1,80,384]{4,3,1,2,0:T(8,128)(2,1)} %bitcast.76), channel_id=1, source_target_pairs={{0,1},{1,0},{2,3},{3,2},{4,5},{5,4},{6,7},{7,6},{8,9},{9,8},{10,11... | collective-permute-start | bytes 2949128 | tf_op jit(solution)/shard_map/ppermute | solution.py:22
  444.3 25.7 %collective-permute-start.46 = (bf16[4,4,3,72,384]{4,3,2,1,0:T(8,128)(2,1)}, bf16[4,4,3,72,384]{4,3,2,1,0:T(8,128)(2,1)}, u32[]{:S(2)}, u32[]{:S(2)}) collective-permute-start(bf16[4,4,3,72,384]{4,3,2,1,0:T(8,128)(2,1)} %get-tuple-element.52), channel_id=1, source_target_pairs={{0,1},{1,0},{2,3},{3,2},{4,5},{5,4},{6,7},{7,6},{8,9},{9,8},{10,11... | collective-permute-start | bytes 7962632 | tf_op jit(solution)/shard_map/ppermute | solution.py:22
  458.5 18.7 %collective-permute-start.34 = (bf16[1,256,576]{1,2,0:T(8,128)(2,1)S(1)}, bf16[1,256,576]{1,2,0:T(8,128)(2,1)S(1)}, u32[]{:S(2)}, u32[]{:S(2)}) collective-permute-start(bf16[1,256,576]{1,2,0:T(8,128)(2,1)S(1)} %get-tuple-element.146), channel_id=1, source_target_pairs={{0,24},{8,16},{16,8},{24,0},{1,25},{9,17},{17,9},{25,1},{2,26},{10... | collective-permute-start | bytes 884744 | tf_op jit(solution)/shard_map/ppermute | solution.py:22
  460.0 10.0 %collective-permute-start.37 = (bf16[2,1,80,384]{3,2,1,0:T(8,128)(2,1)S(1)}, bf16[2,1,80,384]{3,2,1,0:T(8,128)(2,1)S(1)}, u32[]{:S(2)}, u32[]{:S(2)}) collective-permute-start(bf16[2,1,80,384]{3,2,1,0:T(8,128)(2,1)S(1)} %get-tuple-element.89), channel_id=1, source_target_pairs={{0,16},{8,24},{16,0},{24,8},{1,17},{9,25},{17,1},{25,9},{2,18},{10... | collective-permute-start | bytes 368648 | tf_op jit(solution)/shard_map/ppermute | solution.py:22
  463.7 17.1 %collective-permute-start.41 = (bf16[1,80,384]{2,1,0:T(8,128)(2,1)S(1)}, bf16[1,80,384]{2,1,0:T(8,128)(2,1)S(1)}, u32[]{:S(2)}, u32[]{:S(2)}) collective-permute-start(bf16[1,80,384]{2,1,0:T(8,128)(2,1)S(1)} %get-tuple-element.190), channel_id=1, source_target_pairs={{0,4},{1,5},{2,6},{3,7},{4,0},{5,1},{6,2},{7,3},{8,12},{9,13},{10,... | collective-permute-start | bytes 184328 | tf_op jit(solution)/shard_map/ppermute | solution.py:22
  466.7 14.1 %collective-permute-start.42 = (bf16[1,80,384]{2,1,0:T(8,128)(2,1)S(1)}, bf16[1,80,384]{2,1,0:T(8,128)(2,1)S(1)}, u32[]{:S(2)}, u32[]{:S(2)}) collective-permute-start(bf16[1,80,384]{2,1,0:T(8,128)(2,1)S(1)} %get-tuple-element.191), channel_id=1, source_target_pairs={{0,6},{1,7},{2,4},{3,5},{4,2},{5,3},{6,0},{7,1},{8,14},{9,15},{10,... | collective-permute-start | bytes 184328 | tf_op jit(solution)/shard_map/ppermute | solution.py:22
  475.1 17.0 %collective-permute-start.47 = (bf16[2,2,3,72,384]{4,3,2,1,0:T(8,128)(2,1)S(1)}, bf16[2,2,3,72,384]{4,3,2,1,0:T(8,128)(2,1)S(1)}, u32[]{:S(2)}, u32[]{:S(2)}) collective-permute-start(bf16[2,2,3,72,384]{4,3,2,1,0:T(8,128)(2,1)S(1)} %pad_maximum_fusion.20), channel_id=1, source_target_pairs={{0,8},{8,0},{16,24},{24,16},{1,9},{9,1},{17,25},{25,17},{2,10},{10... | collective-permute-start | bytes 1990664 | tf_op jit(solution)/shard_map/ppermute | solution.py:22
  476.1 17.2 %collective-permute-start.50 = (bf16[2,2,3,72,384]{4,3,2,1,0:T(8,128)(2,1)S(1)}, bf16[2,2,3,72,384]{4,3,2,1,0:T(8,128)(2,1)S(1)}, u32[]{:S(2)}, u32[]{:S(2)}) collective-permute-start(bf16[2,2,3,72,384]{4,3,2,1,0:T(8,128)(2,1)S(1)} %stack.185), channel_id=1, source_target_pairs={{0,16},{8,24},{16,0},{24,8},{1,17},{9,25},{17,1},{25,9},{2,18},{10... | collective-permute-start | bytes 1990664 | tf_op jit(solution)/shard_map/ppermute | solution.py:22
  482.5 15.3 %collective-permute-start.43 = (bf16[1,72,384]{2,1,0:T(8,128)(2,1)}, bf16[1,72,384]{2,1,0:T(8,128)(2,1)S(1)}, u32[]{:S(2)}, u32[]{:S(2)}) collective-permute-start(bf16[1,72,384]{2,1,0:T(8,128)(2,1)} %slice.819), channel_id=1, source_target_pairs={{0,24},{8,16},{16,8},{24,0},{1,25},{9,17},{17,9},{25,1},{2,26},{10... | collective-permute-start | bytes 165896 | tf_op jit(solution)/shard_map/ppermute | solution.py:22
  483.9 13.9 %collective-permute-start.44 = (bf16[1,72,384]{2,1,0:T(8,128)(2,1)}, bf16[1,72,384]{2,1,0:T(8,128)(2,1)S(1)}, u32[]{:S(2)}, u32[]{:S(2)}) collective-permute-start(bf16[1,72,384]{2,1,0:T(8,128)(2,1)} %slice.819), channel_id=1, source_target_pairs={{0,16},{8,24},{16,0},{24,8},{1,17},{9,25},{17,1},{25,9},{2,18},{10... | collective-permute-start | bytes 165896 | tf_op jit(solution)/shard_map/ppermute | solution.py:22
  484.6 14.5 %collective-permute-start.45 = (bf16[1,72,384]{2,1,0:T(8,128)(2,1)}, bf16[1,72,384]{2,1,0:T(8,128)(2,1)}, u32[]{:S(2)}, u32[]{:S(2)}) collective-permute-start(bf16[1,72,384]{2,1,0:T(8,128)(2,1)} %slice.819), channel_id=1, source_target_pairs={{0,8},{8,0},{16,24},{24,16},{1,9},{9,1},{17,25},{25,17},{2,10},{10... | collective-permute-start | bytes 165896 | tf_op jit(solution)/shard_map/ppermute | solution.py:22
  495.7 9.4 %collective-permute-start.48 = (bf16[2,3,72,384]{3,2,1,0:T(8,128)(2,1)}, bf16[2,3,72,384]{3,2,1,0:T(8,128)(2,1)S(1)}, u32[]{:S(2)}, u32[]{:S(2)}) collective-permute-start(bf16[2,3,72,384]{3,2,1,0:T(8,128)(2,1)} %get-tuple-element.79), channel_id=1, source_target_pairs={{0,16},{8,24},{16,0},{24,8},{1,17},{9,25},{17,1},{25,9},{2,18},{10... | collective-permute-start | bytes 995336 | tf_op jit(solution)/shard_map/ppermute | solution.py:22
  501.5 9.6 %collective-permute-start.57 = (bf16[1,72,384]{2,1,0:T(8,128)(2,1)S(1)}, bf16[1,72,384]{2,1,0:T(8,128)(2,1)S(1)}, u32[]{:S(2)}, u32[]{:S(2)}) collective-permute-start(bf16[1,72,384]{2,1,0:T(8,128)(2,1)S(1)} %get-tuple-element.179), channel_id=1, source_target_pairs={{0,8},{8,0},{16,24},{24,16},{1,9},{9,1},{17,25},{25,17},{2,10},{10... | collective-permute-start | bytes 165896 | tf_op jit(solution)/shard_map/ppermute | solution.py:22
  502.7 8.5 %collective-permute-start.58 = (bf16[1,72,384]{2,1,0:T(8,128)(2,1)S(1)}, bf16[1,72,384]{2,1,0:T(8,128)(2,1)S(1)}, u32[]{:S(2)}, u32[]{:S(2)}) collective-permute-start(bf16[1,72,384]{2,1,0:T(8,128)(2,1)S(1)} %get-tuple-element.181), channel_id=1, source_target_pairs={{0,16},{8,24},{16,0},{24,8},{1,17},{9,25},{17,1},{25,9},{2,18},{10... | collective-permute-start | bytes 165896 | tf_op jit(solution)/shard_map/ppermute | solution.py:22
  506.6 11.0 %collective-permute-start.52 = (bf16[3,72,384]{2,1,0:T(8,128)(2,1)S(1)}, bf16[3,72,384]{2,1,0:T(8,128)(2,1)S(1)}, u32[]{:S(2)}, u32[]{:S(2)}) collective-permute-start(bf16[3,72,384]{2,1,0:T(8,128)(2,1)S(1)} %get-tuple-element.169), channel_id=1, source_target_pairs={{0,4},{1,5},{2,6},{3,7},{4,0},{5,1},{6,2},{7,3},{8,12},{9,13},{10,... | collective-permute-start | bytes 497672 | tf_op jit(solution)/shard_map/ppermute | solution.py:22
  525.5 11.1 %collective-permute-start.61 = (bf16[3,72,384]{2,1,0:T(8,128)(2,1)S(1)}, bf16[3,72,384]{2,1,0:T(8,128)(2,1)S(1)}, u32[]{:S(2)}, u32[]{:S(2)}) collective-permute-start(bf16[3,72,384]{2,1,0:T(8,128)(2,1)S(1)} %pad_maximum_fusion.45), channel_id=1, source_target_pairs={{0,16},{8,24},{16,0},{24,8},{1,17},{9,25},{17,1},{25,9},{2,18},{10... | collective-permute-start | bytes 497672 | tf_op jit(solution)/shard_map/ppermute | solution.py:22
  526.3 10.3 %collective-permute-start.62 = (bf16[3,72,384]{2,1,0:T(8,128)(2,1)S(1)}, bf16[3,72,384]{2,1,0:T(8,128)(2,1)S(1)}, u32[]{:S(2)}, u32[]{:S(2)}) collective-permute-start(bf16[3,72,384]{2,1,0:T(8,128)(2,1)S(1)} %pad_maximum_fusion.46), channel_id=1, source_target_pairs={{0,24},{8,16},{16,8},{24,0},{1,25},{9,17},{17,9},{25,1},{2,26},{10... | collective-permute-start | bytes 497672 | tf_op jit(solution)/shard_map/ppermute | solution.py:22
  (191 other events, 968.7 us)
Sparse Core Ops, SparseCore 0:
  96.2 57.2 all-gather.2
  315.8 34.6 reduce-scatter.2
  352.7 58.8 reduce-scatter.4

commit v2 on v1

v2 whole, which is shorter than its diff:
```python
import jax
import jax.numpy as jnp
from jax import lax
from jax.experimental import pallas as pl
from jax.experimental.pallas import tpu as pltpu
from jax.sharding import PartitionSpec as P

HEADS = 9
KV_HEADS = 3
HD = 64
LAYERS = 2


epsilon = 1e-05
theta = 100000.0
log_two_e = 1.4426950408889634
mask_filler = -1e30


def flip(block, axis, mask):
    route = [(i, i ^ mask) for i in range(lax.axis_size(axis))]
    return lax.ppermute(block, axis, route)


def swap_halves(x):
    half = x.shape[1] // 2
    return jnp.concatenate(
        [x[:, :half], flip(x[:, half:], "ctx", lax.axis_size("ctx") - 1)], axis=1
    )


def tied(first, *then):
    return lax.optimization_barrier((first, then))[0]


def low(x):
    return x.astype(jnp.bfloat16)


def wide(x):
    return x.astype(jnp.float32)


PIECE = 384
VMEM_LIMIT = 48 * 1024 * 1024


def fold_down(shard):
    step = shard.shape[0] // 4
    pieces = []
    for j in range(4):
        rows = shard[j * step : (j + 1) * step]
        rest = rows[:, PIECE:]
        rest = jnp.concatenate([rest[: step // 2], rest[step // 2 :]], axis=1)
        pieces.append(jnp.concatenate([rows[:, :PIECE], rest], axis=0))
    return jnp.concatenate(pieces, axis=1)


def unfold_down(folded):
    step = folded.shape[-2] * 2 // 3
    pieces = []
    for piece in jnp.split(folded, 4, axis=-1):
        rest = piece[..., step:, :]
        rest = jnp.concatenate(jnp.split(rest, 2, axis=-1), axis=-2)
        pieces.append(jnp.concatenate([piece[..., :step, :], rest], axis=-1))
    return jnp.concatenate(pieces, axis=-2)


def assemble_kernel(rows, own, own_flip, mine, theirs, out, *rest):
    sems = rest[-1]
    j = lax.axis_index("ctx")
    f = lax.axis_index("fsdp")
    copies = []

    def copy(src, dst):
        made = pltpu.make_async_copy(src, dst, sems.at[len(copies)])
        made.start()
        copies.append(made)

    for core, shard in ((0, own), (1, own_flip)):
        copy(shard.at[:, :rows], out.at[:, f ^ core])
        if len(rest) > 1:
            copy(shard.at[0, rows:, :PIECE], rest[0].at[f ^ core])
    for core, pieces in ((0, mine), (1, theirs)):
        for jrel in range(4):
            for zrel in range(1, 4):
                row = f ^ (core + 2 * zrel)
                column = pl.multiple_of((j ^ jrel) * PIECE, 128)
                piece = pieces.at[jrel * 3 + zrel - 1]
                copy(piece.at[:, :rows], out.at[:, row, :, pl.ds(column, PIECE)])
                if jrel == 0 and len(rest) > 1:
                    copy(piece.at[0, rows:], rest[0].at[row])
    for made in copies:
        made.wait()


def assemble(rows, own, own_flip, mine, theirs):
    count, all_rows, columns = own.shape
    fsdp = lax.axis_size("fsdp")
    shapes = [jax.ShapeDtypeStruct((count, fsdp, rows, columns), own.dtype)]
    if all_rows > rows:
        shapes.append(jax.ShapeDtypeStruct((fsdp, all_rows - rows, PIECE), own.dtype))
    return pl.pallas_call(
        lambda *refs: assemble_kernel(rows, *refs),
        out_shape=tuple(shapes),
        in_specs=[pl.BlockSpec(memory_space=pl.ANY)] * 4,
        out_specs=[pl.BlockSpec(memory_space=pltpu.VMEM)] * len(shapes),
        scratch_shapes=[pltpu.SemaphoreType.DMA((34,))],
        compiler_params=pltpu.CompilerParams(vmem_limit_bytes=VMEM_LIMIT),
        name="assemble",
    )(own, own_flip, mine, theirs)


def gather_line(own):
    j = lax.axis_index("ctx")
    piece = lax.dynamic_slice_in_dim(own, j * PIECE, PIECE, axis=2)
    return jnp.stack([flip(piece, "fsdp", 2 * k) for k in (1, 2, 3)])


def gather_sides(line):
    return flip(line, "ctx", 1), flip(line, "ctx", 2)


def gather_rest(rows, own, own_flip, line, sides):
    by_x, by_y = sides
    diag = jnp.concatenate([flip(by_x[:2], "ctx", 2), flip(by_y[2:], "ctx", 1)])
    mine = jnp.concatenate([line, by_x, by_y, diag])
    theirs = flip(mine, "fsdp", 1)
    return assemble(rows, own, own_flip, mine, theirs), mine


def gather_plain(own):
    return lax.all_gather(own, "fsdp", axis=1, tiled=True)


def scatter_kernel(whole, keep, send, sems):
    j = lax.axis_index("ctx")
    f = lax.axis_index("fsdp")
    copies = []
    for core, pieces in ((0, keep), (1, send)):
        for jrel in range(4):
            for zrel in range(4):
                row = f ^ (core + 2 * zrel)
                column = pl.multiple_of((j ^ jrel) * PIECE, 128)
                made = pltpu.make_async_copy(
                    whole.at[row, :, :, pl.ds(column, PIECE)],
                    pieces.at[jrel, zrel],
                    sems.at[len(copies)],
                )
                made.start()
                copies.append(made)
    for made in copies:
        made.wait()


def cut(whole):
    fsdp, count, rows, columns = whole.shape
    piece = jax.ShapeDtypeStruct((4, 4, count, rows, PIECE), whole.dtype)
    return pl.pallas_call(
        scatter_kernel,
        out_shape=(piece, piece),
        in_specs=[pl.BlockSpec(memory_space=pltpu.VMEM)],
        out_specs=[pl.BlockSpec(memory_space=pl.ANY)] * 2,
        scratch_shapes=[pltpu.SemaphoreType.DMA((32,))],
        compiler_params=pltpu.CompilerParams(vmem_limit_bytes=VMEM_LIMIT),
        name="cut",
    )(whole)


def reduce_begin(whole):
    keep, send = cut(whole)
    total = wide(keep) + wide(flip(send, "fsdp", 1))
    a = total[:, :2]
    b = total[:, 2:]
    return (a[0], a[2], b[0], b[1]), (low(jnp.stack([a[1], a[3]])), low(jnp.stack([b[2], b[3]])))


def reduce_sides(sends):
    return flip(sends[0], "ctx", 1), flip(sends[1], "ctx", 2)


def reduce_end(sums, sides):
    a0, a2, b0, b1 = sums
    x1, y1 = wide(sides[0]), wide(sides[1])
    a0, a2 = a0 + x1[0], a2 + x1[1]
    b0, b1 = b0 + y1[0], b1 + y1[1]
    a0 = a0 + wide(flip(low(a2), "ctx", 2))
    b0 = b0 + wide(flip(low(b1), "ctx", 1))
    return (
        a0[0]
        + wide(flip(low(a0[1]), "fsdp", 2))
        + wide(flip(low(b0[0]), "fsdp", 4))
        + wide(flip(low(b0[1]), "fsdp", 6))
    )


def spread_fast(piece):
    j = lax.axis_index("ctx")
    own = low(piece)
    parts = [own] + [flip(own, "ctx", k) for k in (1, 2, 3)]
    for bit in (1, 2):
        odd = (j & bit) != 0
        parts = [jnp.where(odd, parts[i ^ bit], parts[i]) for i in range(4)]
    return wide(jnp.concatenate(parts, axis=2))


def line_pieces(whole):
    part = lax.psum_scatter(whole, "fsdp", scatter_dimension=0, tiled=True)[0]
    j = lax.axis_index("ctx")
    return [
        lax.dynamic_slice_in_dim(part, (j ^ k) * PIECE, PIECE, axis=2) for k in range(4)
    ]


def line_sum(pieces):
    return sum(
        (wide(flip(pieces[k], "ctx", k)) for k in (1, 2, 3)), wide(pieces[0])
    )


def reduce_plain(whole, dim):
    part = lax.psum_scatter(whole, "fsdp", scatter_dimension=dim, tiled=True)
    return wide(lax.psum(part, "ctx"))


def dot_nn(a, b):
    return jnp.dot(a, b, preferred_element_type=jnp.float32)


def dot_nt(a, b):
    return lax.dot_general(a, b, (((1,), (1,)), ((), ())), preferred_element_type=jnp.float32)


def dot_tn(a, b):
    return lax.dot_general(a, b, (((0,), (0,)), ((), ())), preferred_element_type=jnp.float32)


def run_kernel(body, inputs, outputs, scratch=(), cost=0, name=None):
    count = len(inputs)

    def kernel(*refs):
        sources = refs[:count]
        outs = refs[count : count + len(outputs)]
        rest = refs[count + len(outputs) :]
        buffers, extra, sems = rest[:count], rest[count:-1], rest[-1]
        copies = [
            pltpu.make_async_copy(source, buffer, sems.at[i])
            for i, (source, buffer) in enumerate(zip(sources, buffers))
        ]
        for copy in copies:
            copy.start()
        waited = set()

        def get(i):
            if i not in waited:
                waited.add(i)
                copies[i].wait()
            return buffers[i]

        body(get, outs, extra)
        for i in range(count):
            get(i)

    return pl.pallas_call(
        kernel,
        out_shape=tuple(outputs),
        in_specs=[pl.BlockSpec(memory_space=pl.ANY)] * count,
        out_specs=[pl.BlockSpec(memory_space=pltpu.VMEM)] * len(outputs),
        scratch_shapes=[
            *[pltpu.VMEM(x.shape, x.dtype) for x in inputs],
            *scratch,
            pltpu.SemaphoreType.DMA((count,)),
        ],
        compiler_params=pltpu.CompilerParams(vmem_limit_bytes=VMEM_LIMIT),
        cost_estimate=pl.CostEstimate(flops=cost, bytes_accessed=4_000_000, transcendentals=0),
        name=name,
    )(*inputs)


def like(shape, kind):
    return jax.ShapeDtypeStruct(shape, kind)


def chunks_of(source, slots):
    return (2 * source, 2 * slots - 1 - 2 * source)


def stack_heads(ref, dst, half):
    group = HEADS // KV_HEADS
    for g in range(KV_HEADS):
        for part in range(2):
            for i in range(group):
                h = g * group + i
                dst[g, part, i * half : (i + 1) * half] = ref[
                    part * half : (part + 1) * half, h * HD : (h + 1) * HD
                ]


def thrice(row):
    return jnp.concatenate([row] * (HEADS // KV_HEADS), axis=1)


def attend_kernel(slots, *refs):
    q_ref, start_ref = refs[:2]
    kv_refs = refs[2 : 2 + slots]
    o_ref, lse_ref, qs, ks, vt, top_s, acc_s, ot = refs[2 + slots :]
    rank = lax.axis_index("ctx")
    half = q_ref.shape[0] // 2
    group = HEADS // KV_HEADS
    wide_cols = group * half
    stack_heads(q_ref, qs, half)
    ones = jnp.ones((16, half), jnp.bfloat16)
    for k in range(slots):
        values_t = low(jnp.transpose(wide(kv_refs[k][:, 128:])))
        for g in range(KV_HEADS):
            row = KV_HEADS * HD - 128 + g * HD
            for part in range(2):
                rows = slice(part * half, (part + 1) * half)
                ks[k, g, part] = kv_refs[k][rows, g * HD : (g + 1) * HD]
                vt[k, g, part, :HD] = values_t[row : row + HD, rows]
                vt[k, g, part, HD:] = ones
    lse_ref[...] = jnp.zeros_like(lse_ref)
    mine = chunks_of(rank, slots)

    def one_group(g, carry):
        for part in range(2):
            cols = slice(part * half, (part + 1) * half)
            start = thrice(start_ref[:, cols])
            q = qs[g, part]

            def scores(k, other, first):
                s = dot_nt(ks[k, g, other], q)
                key = lax.broadcasted_iota(jnp.int32, s.shape, 0)
                visible = key >= start - first
                return s, key, visible

            s, key, visible = scores(0, part, mine[part] * half)
            query = thrice(lax.broadcasted_iota(jnp.int32, (half, half), 1))
            s = jnp.where(visible & (key <= query), s, mask_filler)
            top = jnp.floor(jnp.max(s, axis=0, keepdims=True))
            top_s[...] = top
            acc_s[...] = dot_nn(vt[0, g, part], low(jnp.exp2(s - top)))

            def tile(k, other, chunk):
                @pl.when(chunk < mine[part])
                def _():
                    s, _, visible = scores(k, other, chunk * half)
                    s = jnp.where(visible, s, mask_filler)
                    old = top_s[...]
                    top = jnp.maximum(old, jnp.floor(jnp.max(s, axis=0, keepdims=True)))
                    top_s[...] = top
                    acc_s[...] = acc_s[...] * jnp.exp2(old - top) + dot_nn(
                        vt[k, g, other], low(jnp.exp2(s - top))
                    )

            tile(0, 1 - part, mine[1 - part])

            def slot(k, carry):
                theirs = chunks_of(rank ^ k, slots)
                for other in range(2):
                    tile(k, other, theirs[other])
                return carry

            lax.fori_loop(1, slots, slot, 0)
            total = acc_s[HD : HD + 1]
            out = acc_s[:HD] / total
            level = top_s[...] + jnp.log2(total)
            for i in range(group):
                inner = slice(i * half, (i + 1) * half)
                ot[g, i, :, cols] = out[:, inner]
                lse_ref[pl.ds(g * group + i, 1), cols] = level[:, inner]
        return carry

    lax.fori_loop(0, KV_HEADS, one_group, 0)
    o_ref[...] = low(jnp.transpose(ot[...].reshape(HEADS * HD, 2 * half)))


def attend(q, start, kvs):
    block = q.shape[0]
    half = block // 2
    slots = len(kvs)
    group = HEADS // KV_HEADS
    inputs = (q, start, *kvs)

    def body(get, outs, extra):
        attend_kernel(slots, *[get(i) for i in range(len(inputs))], *outs, *extra)

    return run_kernel(
        body,
        inputs,
        (like((block, HEADS * HD), jnp.bfloat16), like((16, block), jnp.float32)),
        scratch=(
            pltpu.VMEM((KV_HEADS, 2, group * half, HD), jnp.bfloat16),
            pltpu.VMEM((slots, KV_HEADS, 2, half, HD), jnp.bfloat16),
            pltpu.VMEM((slots, KV_HEADS, 2, HD + 16, half), jnp.bfloat16),
            pltpu.VMEM((1, group * half), jnp.float32),
            pltpu.VMEM((HD + 16, group * half), jnp.float32),
            pltpu.VMEM((KV_HEADS, group, HD, block), jnp.float32),
        ),
        cost=15_000_000_000,
        name="attend",
    )


def attend_back_kernel(slots, *refs):
    q_ref, o_ref, do_ref, lse_ref, start_ref = refs[:5]
    kv_refs = refs[5 : 5 + slots]
    dq_ref = refs[5 + slots]
    dkv_refs = refs[6 + slots : 6 + 2 * slots]
    qs, dos, ks, kt, vs, dk_s, dv_s, dqt_s, delta_s, dqt_all = refs[6 + 2 * slots :]
    rank = lax.axis_index("ctx")
    half = q_ref.shape[0] // 2
    group = HEADS // KV_HEADS
    stack_heads(q_ref, qs, half)
    stack_heads(do_ref, dos, half)
    for k in range(slots):
        keys_t = low(jnp.transpose(wide(kv_refs[k][:, : 2 * 128])))
        for g in range(KV_HEADS):
            for part in range(2):
                rows = slice(part * half, (part + 1) * half)
                ks[k, g, part] = kv_refs[k][rows, g * HD : (g + 1) * HD]
                kt[k, g, part] = keys_t[g * HD : (g + 1) * HD, rows]
                vs[k, g, part] = kv_refs[k][rows, (KV_HEADS + g) * HD : (KV_HEADS + g + 1) * HD]
    product = wide(do_ref[...]) * wide(o_ref[...])
    coarse = low(product)
    fine = low(product - wide(coarse))
    shape = (16, HEADS * HD)
    owner = lax.div(lax.broadcasted_iota(jnp.int32, shape, 1), HD)
    pick = jnp.where(owner == lax.broadcasted_iota(jnp.int32, shape, 0), 1.0, 0.0)
    pick = pick.astype(jnp.bfloat16)
    delta_s[...] = dot_nt(pick, coarse) + dot_nt(pick, fine)
    dk_s[...] = jnp.zeros_like(dk_s)
    dv_s[...] = jnp.zeros_like(dv_s)
    mine = chunks_of(rank, slots)

    def one_group(g, carry):
        for part in range(2):
            cols = slice(part * half, (part + 1) * half)
            start = thrice(start_ref[:, cols])
            heads = [pl.ds(g * group + i, 1) for i in range(group)]
            lse = jnp.concatenate([lse_ref[h, cols] for h in heads], axis=1)
            delta = jnp.concatenate([delta_s[h, cols] for h in heads], axis=1)

            def tile(k, other, first, diagonal):
                q = qs[g, part]
                do = dos[g, part]
                s = dot_nt(ks[k, g, other], q)
                key = lax.broadcasted_iota(jnp.int32, s.shape, 0)
                visible = key >= start - first
                if diagonal:
                    query = thrice(lax.broadcasted_iota(jnp.int32, (half, half), 1))
                    visible = visible & (key <= query)
                p = jnp.where(visible, jnp.exp2(s - lse), 0.0)
                dv = dot_nn(low(p), do)
                dp = dot_nt(vs[k, g, other], do)
                ds = low(p * (dp - delta))
                dk_s[k, g, other] += dot_nn(ds, q)
                dv_s[k, g, other] += dv
                dq = dot_nn(kt[k, g, other], ds)
                if diagonal:
                    dqt_s[...] = dq
                else:
                    dqt_s[...] += dq

            tile(0, part, mine[part] * half, True)

            @pl.when(mine[1 - part] < mine[part])
            def _():
                tile(0, 1 - part, mine[1 - part] * half, False)

            def slot(k, carry):
                theirs = chunks_of(rank ^ k, slots)
                for other in range(2):

                    @pl.when(theirs[other] < mine[part])
                    def _():
                        tile(k, other, theirs[other] * half, False)

                return carry

            lax.fori_loop(1, slots, slot, 0)
            for i in range(group):
                dqt_all[g, i, :, cols] = dqt_s[:, i * half : (i + 1) * half]
        return carry

    lax.fori_loop(0, KV_HEADS, one_group, 0)
    dq_ref[...] = jnp.transpose(dqt_all[...].reshape(HEADS * HD, 2 * half)) * 0.125
    for k in range(slots):
        for part in range(2):
            dkv = jnp.concatenate(
                [dk_s[k, g, part] * (1.0 / log_two_e) for g in range(KV_HEADS)]
                + [dv_s[k, g, part] for g in range(KV_HEADS)],
                axis=1,
            )
            dkv_refs[k][part * half : (part + 1) * half] = dkv.astype(dkv_refs[k].dtype)


def attend_back(q, o, do, lse, start_row, kvs):
    block = q.shape[0]
    half = block // 2
    slots = len(kvs)
    group = HEADS // KV_HEADS
    inputs = (q, o, do, lse, start_row, *kvs)
    pair = lambda kind: like((block, 2 * KV_HEADS * HD), kind)

    def body(get, outs, extra):
        attend_back_kernel(slots, *[get(i) for i in range(len(inputs))], *outs, *extra)

    return run_kernel(
        body,
        inputs,
        (
            like((block, HEADS * HD), jnp.float32),
            pair(jnp.float32),
            *[pair(jnp.bfloat16)] * (slots - 1),
        ),
        scratch=(
            pltpu.VMEM((KV_HEADS, 2, group * half, HD), jnp.bfloat16),
            pltpu.VMEM((KV_HEADS, 2, group * half, HD), jnp.bfloat16),
            pltpu.VMEM((slots, KV_HEADS, 2, half, HD), jnp.bfloat16),
            pltpu.VMEM((slots, KV_HEADS, 2, HD, half), jnp.bfloat16),
            pltpu.VMEM((slots, KV_HEADS, 2, half, HD), jnp.bfloat16),
            pltpu.VMEM((slots, KV_HEADS, 2, half, HD), jnp.float32),
            pltpu.VMEM((slots, KV_HEADS, 2, half, HD), jnp.float32),
            pltpu.VMEM((HD, group * half), jnp.float32),
            pltpu.VMEM((16, block), jnp.float32),
            pltpu.VMEM((KV_HEADS, group, HD, block), jnp.float32),
        ),
        cost=20_000_000_000,
        name="attend_back",
    )


def scale_of(x):
    return lax.rsqrt(jnp.mean(x * x, axis=1, keepdims=True) + epsilon)


def tiled_lanes(table, columns):
    full = [table] * (columns // 128)
    if columns % 128:
        full.append(table[:, : columns % 128])
    return jnp.concatenate(full, axis=1)


def swapped(x):
    columns = x.shape[1]
    row = lax.broadcasted_iota(jnp.int32, (columns, columns), 0)
    col = lax.broadcasted_iota(jnp.int32, (columns, columns), 1)
    partner = jnp.where((col & (HD - 1)) < HD // 2, col + HD // 2, col - HD // 2)
    exchange = jnp.where(row == partner, 1.0, 0.0).astype(jnp.bfloat16)
    coarse = low(x)
    rest = x - wide(coarse)
    fine = low(rest)
    return dot_nn(coarse, exchange) + dot_nn(fine, exchange)


def turned(x, cosine, sine, sign):
    columns = x.shape[1]
    return x * tiled_lanes(cosine, columns) + swapped(x) * (sign * tiled_lanes(sine, columns))


QUERY = HEADS * HD
KVW = KV_HEADS * HD
QKV = QUERY + 2 * KVW


def project_in(hidden, gains, which, weights, cosine, sine):
    tokens, width = hidden.shape

    def body(get, outs, extra):
        normed_ref, q_ref, pair_ref = outs
        h = get(0)[...]
        normed = low(h * scale_of(h) * get(1)[which : which + 1])
        normed_ref[...] = normed
        out = dot_nn(normed, get(2)[:, :QKV])
        cos, sin = get(3)[...], get(4)[...]
        q_ref[...] = low(turned(out[:, :QUERY], cos, sin, 1.0) * (0.125 * log_two_e))
        keys = turned(out[:, QUERY : QUERY + KVW], cos, sin, 1.0)
        pair_ref[...] = low(jnp.concatenate([keys, out[:, QUERY + KVW :]], axis=1))

    return run_kernel(
        body,
        (hidden, gains, weights, cosine, sine),
        (
            like((tokens, width), jnp.bfloat16),
            like((tokens, QUERY), jnp.bfloat16),
            like((tokens, 2 * KVW), jnp.bfloat16),
        ),
        cost=4_000_000_000,
        name="project_in",
    )


def down_scratch(hidden):
    return (
        pltpu.VMEM((hidden, PIECE), jnp.bfloat16),
        pltpu.VMEM((hidden, PIECE // 2), jnp.bfloat16),
        pltpu.VMEM((hidden, PIECE // 2), jnp.float32),
    )


def open_down(down, left, right, wide_right):
    if len(down.shape) == 2:
        left[...] = down[:, :PIECE]
        right[...] = down[:, PIECE:]
        return
    shards, rows, columns = down.shape
    step = rows * 2 // 3
    for f in range(shards):
        for j in range(columns // PIECE):
            at = (f * (columns // PIECE) + j) * step
            lanes = slice(j * PIECE, (j + 1) * PIECE)
            left[at : at + step] = down[f, :step, lanes]
            rest = wide(down[f, step:, lanes])
            wide_right[at : at + step // 2] = rest[:, : PIECE // 2]
            wide_right[at + step // 2 : at + step] = rest[:, PIECE // 2 :]
    right[...] = low(wide_right[...])


def mlp(hidden, attention, gains, which, attn_weights, gate_w, up_w, down_w):
    tokens, width = hidden.shape
    ff = gate_w.shape[1]
    chunk = 512

    def body(get, outs, extra):
        middle_ref, mixed_ref, gate_ref, up_ref, inner_ref, out_ref = outs
        left, right, wide_right = extra
        middle = get(0)[...] + dot_nn(get(1)[...], get(3)[:, QKV:])
        middle_ref[...] = middle
        mixed = low(middle * scale_of(middle) * get(2)[which : which + 1])
        mixed_ref[...] = mixed
        open_down(get(6), left, right, wide_right)
        gate_weight, up_weight = get(4), get(5)
        sums = [0.0, 0.0]
        for c in range(ff // chunk):
            cols = slice(c * chunk, (c + 1) * chunk)
            gate = dot_nn(mixed, gate_weight[:, cols])
            up = dot_nn(mixed, up_weight[:, cols])
            gate_ref[:, cols] = low(gate)
            up_ref[:, cols] = low(up)
            inner = low(gate * jax.nn.sigmoid(gate) * up)
            inner_ref[:, cols] = inner
            sums[0] = sums[0] + dot_nn(inner, left[cols])
            sums[1] = sums[1] + dot_nn(inner, right[cols])
        out_ref[...] = middle + jnp.concatenate(sums, axis=1)

    return run_kernel(
        body,
        (hidden, attention, gains, attn_weights, gate_w, up_w, down_w),
        (
            like((tokens, width), jnp.float32),
            like((tokens, width), jnp.bfloat16),
            like((tokens, ff), jnp.bfloat16),
            like((tokens, ff), jnp.bfloat16),
            like((tokens, ff), jnp.bfloat16),
            like((tokens, width), jnp.float32),
        ),
        scratch=down_scratch(ff),
        cost=8_000_000_000,
        name="mlp",
    )


def norm_back(x, gain, grad):
    scale = scale_of(x)
    unit = x * scale
    e = grad * gain
    dx = scale * (e - unit * jnp.mean(e * unit, axis=1, keepdims=True))
    return dx, jnp.sum(grad * unit, axis=0, keepdims=True)


def put_rows(ref, index, value, shards):
    if shards is None:
        ref[index] = low(value)
        return
    rows = value.shape[0] // shards
    for f in range(shards):
        ref[f, index] = low(value[f * rows : (f + 1) * rows])


def mlp_back(grad, kept, gains, which, attn_weights, gate_w, up_w, down_w, shards):
    middle, mixed, gate, up, inner, attention = kept
    tokens, width = grad.shape
    ff = gate_w.shape[1]
    chunk = 512

    def body(get, outs, extra):
        datt_ref, mid_ref, gain_ref, out_grad_ref, weights_ref = outs[:5]
        left, right, wide_right, grad_s, total = extra
        open_down(get(11), left, right, wide_right)
        grad = get(0)[...]
        grad_low = low(grad)
        mixed = get(2)[...]
        d_mixed = 0.0
        for c in range(ff // chunk):
            cols = slice(c * chunk, (c + 1) * chunk)
            d_inner = dot_nt(grad_low[:, :PIECE], left[cols]) + dot_nt(
                grad_low[:, PIECE:], right[cols]
            )
            g = wide(get(3)[:, cols])
            sig = jax.nn.sigmoid(g)
            d_gate = low(d_inner * wide(get(4)[:, cols]) * (sig * (1.0 + g * (1.0 - sig))))
            d_up = low(d_inner * (g * sig))
            grad_s[0, :, cols] = dot_tn(mixed, d_gate)
            grad_s[1, :, cols] = dot_tn(mixed, d_up)
            part = dot_nt(d_gate, get(9)[:, cols]) + dot_nt(d_up, get(10)[:, cols])
            d_mixed = part + d_mixed
            d_down = dot_tn(get(5)[:, cols], grad_low)
            if shards is None:
                outs[5][cols] = low(d_down)
            else:
                total[cols] = d_down
        for index in range(2):
            put_rows(weights_ref, index, grad_s[index], shards)
        if shards is not None:
            rows = width // shards
            step = rows * 2 // 3
            for f in range(shards):
                for j in range(ff // PIECE):
                    at = (f * (ff // PIECE) + j) * step
                    rest = total[at : at + step, PIECE:]
                    value = jnp.concatenate(
                        [
                            total[at : at + step, :PIECE],
                            jnp.concatenate([rest[: step // 2], rest[step // 2 :]], axis=1),
                        ],
                        axis=0,
                    )
                    weights_ref[f, 2, :, j * PIECE : (j + 1) * PIECE] = low(value)
        dx, gain_grad = norm_back(get(1)[...], get(7)[which : which + 1], d_mixed)
        gain_ref[...] = jnp.broadcast_to(gain_grad, gain_ref.shape)
        mid = grad + dx
        mid_ref[...] = mid
        mid_low = low(mid)
        out_grad_ref[...] = low(dot_tn(get(6)[...], mid_low))
        datt_ref[...] = low(dot_nt(mid_low, get(8)[:, QKV:]))

    if shards is None:
        weight_outs = (like((2, width, ff), jnp.bfloat16), like((ff, width), jnp.bfloat16))
    else:
        weight_outs = (like((shards, 3, width // shards, ff), jnp.bfloat16),)
    return run_kernel(
        body,
        (
            grad, middle, mixed, gate, up, inner, attention, gains,
            attn_weights, gate_w, up_w, down_w,
        ),
        (
            like((tokens, width), jnp.bfloat16),
            like((tokens, width), jnp.float32),
            like((8, width), jnp.float32),
            like((width, width), jnp.bfloat16),
            *weight_outs,
        ),
        scratch=(
            *down_scratch(ff),
            pltpu.VMEM((2, width, ff), jnp.float32),
            pltpu.VMEM((ff, width), jnp.float32),
        ),
        cost=15_000_000_000,
        name="mlp_back",
    )


def project_back(d_query, pairs, cosine, sine, kept, gains, which, weights, out_grad, mid, shards, riders):
    hidden, normed = kept
    tokens, width = hidden.shape
    count = len(pairs)
    columns = weights.shape[1]
    extra_rows = 0 if riders is None else 8

    def body(get, outs, extra):
        grad_ref, gain_ref, weights_ref = outs
        cos, sin = get(1)[...], get(2)[...]
        dq = turned(get(0)[...], cos, sin, -1.0)
        pair = get(9)[...]
        for k in range(1, count):
            pair = pair + wide(get(9 + k)[...])
        dk = turned(pair[:, :KVW], cos, sin, -1.0)
        d_all = low(jnp.concatenate([dq, dk, pair[:, KVW:]], axis=1))
        normed_grad = dot_nt(d_all, get(6)[:, :QKV])
        dx, gain_grad = norm_back(get(3)[...], get(5)[which : which + 1], normed_grad)
        gain_ref[...] = jnp.broadcast_to(gain_grad, gain_ref.shape)
        grad_ref[...] = get(8)[...] + dx
        d_weights = dot_tn(get(4)[...], d_all)
        value = jnp.concatenate([d_weights, wide(get(7)[...])], axis=1)
        if riders is None:
            put_rows(weights_ref, 0, value, shards)
        else:
            rows = width // shards
            lines = [get(9 + count)[...], gain_grad]
            lines.append(jnp.zeros((8 - 1 - lines[0].shape[0], width), jnp.float32))
            ride = jnp.concatenate(lines, axis=0)
            ride = jnp.concatenate(
                [ride, jnp.zeros((8, columns - width), jnp.float32)], axis=1
            )
            for f in range(shards):
                weights_ref[f, 0] = low(
                    jnp.concatenate([value[f * rows : (f + 1) * rows], ride], axis=0)
                )

    if shards is None:
        shape = (1, width, columns)
    else:
        shape = (shards, 1, width // shards + extra_rows, columns)
    inputs = (d_query, cosine, sine, hidden, normed, gains, weights, out_grad, mid, *pairs)
    if riders is not None:
        inputs = (*inputs, riders)
    return run_kernel(
        body,
        inputs,
        (
            like((tokens, width), jnp.float32),
            like((8, width), jnp.float32),
            like(shape, jnp.bfloat16),
        ),
        cost=6_000_000_000,
        name="project_back",
    )


def rope_tables(positions, head_size):
    half = head_size // 2
    freq = theta ** (-(jnp.arange(half, dtype=jnp.float32) * 2.0 / head_size))
    angle = positions.astype(jnp.float32)[..., None] * freq
    return (jnp.cos(angle), jnp.sin(angle))


def body(
    tokens,
    positions,
    query_weight,
    key_matrix,
    value_weight,
    out_weight,
    gate_weight,
    up_weight,
    down_weight,
    attn_gain,
    mlp_gain,
    cotangent,
):
    slots = lax.axis_size("ctx")
    rank = lax.axis_index("ctx")
    shard = lax.axis_index("fsdp")
    shards = lax.axis_size("fsdp")
    fast = slots == 4 and shards == 8
    tokens = swap_halves(tokens)
    positions = swap_halves(positions)
    half = tokens.shape[1] // 2
    rows = attn_gain.shape[1]
    gain_count = 2 * LAYERS
    own_gains = jnp.concatenate([attn_gain, mlp_gain])
    attn_own = [
        jnp.concatenate([query_weight[i], key_matrix[i], value_weight[i], out_weight[i]], axis=1)
        for i in range(LAYERS)
    ]
    mlp_own = [[gate_weight[i], up_weight[i]] for i in range(LAYERS)]
    if fast:
        for i in range(LAYERS):
            mlp_own[i].append(fold_down(down_weight[i]))
        ride = jnp.pad(own_gains, ((0, 8 - gain_count), (0, PIECE - rows)))
        own_first = jnp.concatenate([attn_own[0], jnp.tile(ride, (1, 4))], axis=0)[None]
        own_second = jnp.stack([*mlp_own[0], attn_own[1]])
        own_third = jnp.stack(mlp_own[1])
        first_line = gather_line(own_first)
        second_line = gather_line(tied(own_second, first_line))
        third = gather_plain(tied(own_third, second_line))
        third = third.reshape(3, shards, rows, -1)
        first_sides = gather_sides(first_line)
        first_flip = flip(own_first, "fsdp", 1)
        (first, gains), first_mine = gather_rest(
            rows, own_first, first_flip, first_line, first_sides
        )
        gains = wide(gains[:, :gain_count, :rows]).transpose(1, 0, 2).reshape(gain_count, -1)
        second_flip = flip(tied(own_second, first_mine), "fsdp", 1)
        second_line = tied(second_line, first_mine)
        second_sides = gather_sides(second_line)
        merge = lambda x: x.reshape(-1, x.shape[-1])
        attn_full = [merge(first[0]), None]
        mlp_full = [None, (merge(third[0]), merge(third[1]), third[2])]
    else:
        gains = wide(lax.all_gather(own_gains, "fsdp", axis=1, tiled=True))
        gather = lambda x: lax.all_gather(x, "fsdp", axis=0, tiled=True)
        attn_full = [gather(x) for x in attn_own]
        mlp_full = [
            (gather(gate_weight[i]), gather(up_weight[i]), gather(down_weight[i]))
            for i in range(LAYERS)
        ]
    gains = jnp.pad(gains, ((0, 8 - gain_count), (0, 0)))
    cosine, sine = rope_tables(positions[0], HD)
    cosine = jnp.concatenate([cosine] * 4, axis=1)
    sine = jnp.concatenate([-sine, sine] * 2, axis=1)
    first_row, second_row = chunks_of(rank, slots)
    offsets = jnp.arange(half, dtype=jnp.int32)
    row_index = jnp.concatenate([first_row * half + offsets, second_row * half + offsets])
    doc_start = row_index[None, :] - positions

    hidden = wide(tokens[0])
    saved = []
    for i in range(LAYERS):
        normed, q, pair = project_in(hidden, gains, i, attn_full[i], cosine, sine)
        kvs = [pair] + [flip(pair, "ctx", k) for k in range(1, slots)]
        attention, lse = attend(q, doc_start, kvs)
        if fast and i == 0:
            second_sides, cotangent = tied((second_sides, cotangent), attention)
            (second,), _ = gather_rest(
                rows, own_second, second_flip, second_line, second_sides
            )
            mlp_full[0] = (merge(second[0]), merge(second[1]), second[2])
            attn_full[1] = merge(second[3])
        middle, mixed, gate, up, inner, out = mlp(
            hidden, attention, gains, LAYERS + i, attn_full[i], *mlp_full[i]
        )
        saved.append((hidden, normed, q, kvs, attention, lse, middle, mixed, gate, up, inner))
        hidden = out
    layer_out = swap_halves(low(hidden)[None])
    grad = wide(swap_halves(cotangent)[0])

    gain_grads = {}
    mlp_grads = [None] * LAYERS
    attn_grads = [None] * LAYERS
    by_shard = shards if fast else None
    for i in reversed(range(LAYERS)):
        hidden, normed, q, kvs, attention, lse, middle, mixed, gate, up, inner = saved[i]
        d_attention, mid, gain_grads[LAYERS + i], out_grad, *weight_grads = mlp_back(
            grad,
            (middle, mixed, gate, up, inner, attention),
            gains,
            LAYERS + i,
            attn_full[i],
            *mlp_full[i],
            by_shard,
        )
        if fast and i == 0:
            sums, sends = reduce_begin(weight_grads[0])
            d_attention, sends, pieces = lax.optimization_barrier(
                (d_attention, sends, mlp_grads[1])
            )
            sides = reduce_sides(sends)
            moved = [pieces[0]] + [flip(pieces[k], "ctx", k) for k in (1, 2, 3)]
        elif fast:
            mlp_grads[i] = line_pieces(weight_grads[0])
        else:
            mlp_grads[i] = (
                reduce_plain(weight_grads[0], 1),
                reduce_plain(weight_grads[1], 0),
            )
        d_query, *pairs = attend_back(q, attention, d_attention, lse, doc_start, kvs)
        pairs = [pairs[0]] + [flip(pairs[k], "ctx", k) for k in range(1, slots)]
        riders = None
        if fast and i == 0:
            riders = jnp.concatenate([gain_grads[v][:1] for v in (1, 2, 3)])
        grad, gain_grads[i], attn_grad = project_back(
            d_query,
            pairs,
            cosine,
            sine,
            (hidden, normed),
            gains,
            i,
            attn_full[i],
            out_grad,
            mid,
            by_shard,
            riders,
        )
        if fast and i == 0:
            sides, moved, pieces = tied((sides, moved, attn_grads[1]), pairs)
            mlp_sum = sum((wide(part) for part in moved[1:]), wide(moved[0]))
            early = jnp.concatenate([mlp_sum, line_sum(pieces)])
            early = spread_fast(early)
            rest = spread_fast(reduce_end(sums, sides))
            sums, sends = reduce_begin(attn_grad)
            last = reduce_end(sums, reduce_sides(sends))
            last = spread_fast(last)
            all_gains = lax.dynamic_slice_in_dim(last[0, rows:], shard * rows, rows, axis=1)
            order = (3, 0, 1, 2)
            all_gains = jnp.stack([all_gains[v] for v in order])
            attn_rows = jnp.stack([last[0, :rows], early[3]])
            gate_rows = jnp.stack([rest[0], early[0]])
            up_rows = jnp.stack([rest[1], early[1]])
            down_rows = unfold_down(jnp.stack([rest[2], early[2]]))
        elif fast:
            attn_grads[i] = line_pieces(attn_grad)
        else:
            attn_grads[i] = reduce_plain(attn_grad[0], 0)
    if not fast:
        attn_rows = jnp.stack(attn_grads)
        gate_rows = jnp.stack([part[0][0] for part in mlp_grads])
        up_rows = jnp.stack([part[0][1] for part in mlp_grads])
        down_rows = jnp.stack([part[1] for part in mlp_grads])
        all_gains = jnp.concatenate([gain_grads[v][:1] for v in range(gain_count)])
        all_gains = lax.psum(all_gains, ("ctx", "fsdp"))
        all_gains = lax.dynamic_slice_in_dim(all_gains, shard * rows, rows, axis=1)
    far = wide(flip(low(grad[half:]), "ctx", slots - 1))
    grad = jnp.concatenate([grad[:half], far])[None]
    return (
        layer_out,
        grad,
        attn_rows[..., :QUERY],
        attn_rows[..., QUERY : QUERY + KVW],
        attn_rows[..., QUERY + KVW : QKV],
        attn_rows[..., QKV:],
        gate_rows,
        up_rows,
        down_rows,
        all_gains[:LAYERS],
        all_gains[LAYERS:],
    )


def solution(mesh):
    return jax.shard_map(
        body,
        mesh=mesh,
        in_specs=(
            P("fsdp", "ctx", None),
            P("fsdp", "ctx"),
            P(None, "fsdp", None),
            P(None, "fsdp", None),
            P(None, "fsdp", None),
            P(None, "fsdp", None),
            P(None, "fsdp", None),
            P(None, "fsdp", None),
            P(None, "fsdp", None),
            P(None, "fsdp"),
            P(None, "fsdp"),
            P("fsdp", "ctx", None),
        ),
        out_specs=(
            P("fsdp", "ctx", None),
            P("fsdp", "ctx", None),
            P(None, "fsdp", None),
            P(None, "fsdp", None),
            P(None, "fsdp", None),
            P(None, "fsdp", None),
            P(None, "fsdp", None),
            P(None, "fsdp", None),
            P(None, "fsdp", None),
            P(None, "fsdp"),
            P(None, "fsdp"),
        ),
        check_vma=False,
    )
```

time: 565 us -> 507 us (0.90)
  Pallas kernels: 97 us -> 181 us
  local copies, waits for them, and re-layouts: 137 us -> 58.6 us
  matrix products: 69.7 us -> 0 us
  waiting for transfers between devices: 86.4 us -> 135 us
  other arithmetic: 57.3 us -> 34.1 us
  blocking collectives: 12 us -> 0 us
    pallas_call x6 -> x14, Pallas kernels: 90.7 us -> 176 us  [the longest x12 168 us: run_kernel(): pl.pallas_call(kernel, out_shape=tuple(outputs), in_specs=[pl.BlockSpec(m...]
    dot_general x42 -> x0, matrix products: 69.7 us -> none  [the longest x14 24.3 us: project_back(): jnp.einsum('qzy,gy->qzg', gradient_tree, weight_matrix, preferred_element...]
    ppermute x66, waiting for transfers between devices: 86.4 us -> 135 us  [flip(): return lax.ppermute(block, axis, route)]
    convert_element_type x18 -> x5, local copies, waits for them, and re-layouts: 19.8 us -> 0.08 us  [low(): return x.astype(jnp.bfloat16)]
    unnamed x349 -> x146, local copies, waits for them, and re-layouts: 52.6 us -> 34.9 us
    dot_general x8 -> x0, local copies, waits for them, and re-layouts: 13 us -> none  [project(): jnp.einsum('vnk,kp->vnp', input_tokens, weight_matrix, preferred_element_...]
    all_gather x1 -> x0, blocking collectives: 12 us -> none  [body(): lax.all_gather(jnp.concatenate([attn_gain, mlp_gain]), 'fsdp', axis=1, ti...]
    concatenate x4 -> x0, local copies, waits for them, and re-layouts: 9.34 us -> none  [the longest x2 6.44 us: body(): attn = jnp.concatenate([low(part) for part in tree[:4]], axis=1)]
  transfers between devices with their start and end apart: 69 -> 69, of which waited for: 21 -> 37; matrix products, arithmetic and copies ran while one was open for 34% -> 11% of each run, Pallas kernels for 13% -> 30%
where the time goes in v2:
time: 507 us; the launch traced here: 502 us
  Pallas kernels  181 us (36%)
  waiting for transfers between devices  135 us (27%)
  starting transfers between devices  78.2 us (15%)
  local copies, waits for them, and re-layouts  58.6 us (12%)
  other arithmetic  34.1 us (7%)
  between operations  15.3 us (3%)
    pallas_call x12, Pallas kernels, run_kernel(): pl.pallas_call(kernel, out_shape=tuple(outputs), in_specs=[pl.BlockSpec(m...  168 us
    ppermute x66, waiting for transfers between devices, flip(): return lax.ppermute(block, axis, route)  135 us
    ppermute x66, starting transfers between devices, flip(): return lax.ppermute(block, axis, route)  77.9 us
    unnamed x146, local copies, waits for them, and re-layouts  34.9 us
  transfers between devices with their start and end apart: 69, of which 37 were waited for; matrix products, arithmetic and copies ran while one was open for 11% of the time, Pallas kernels for 30%

profile of v2, /device:TPU:0, one launch (start us, length us, event | category | flops | bytes accessed | tf_op | source)
XLA Modules:
  0.0 502.0 jit_solution(14387729029654435181)
XLA Ops:
  11.4 3.0 collective-permute-start.2
  14.4 2.6 collective-permute-start.3
  17.9 2.7 collective-permute-start
  24.6 3.5 collective-permute-done.10
  41.8 3.6 collective-permute-start.17
  48.4 3.6 collective-permute-done.17
  52.0 11.9 %collective-permute-done.16 = bf16[4,72,384]{2,1,0:T(8,128)(2,1)S(1)} collective-permute-done((bf16[4,72,384]{2,1,0:T(8,128)(2,1)S(1)}, bf16[4,72,384]{2,1,0:T(8,128)(2,1)S(1)}, u32[]{:S(2)}, u32[]{:S(2)}) %collective-permute-start.16) | collective-permute-done | bytes 221216 | tf_op jit(solution)/shard_map/ppermute | solution.py:22
  72.3 3.8 project_in.2
  81.9 7.0 %collective-permute-done.11.refs_3_.refs_6_ = bf16[512,384]{1,0:T(8,128)(2,1)S(1)} collective-permute-done((bf16[512,384]{1,0:T(8,128)(2,1)S(1)}, bf16[512,384]{1,0:T(8,128)(2,1)S(1)}, u32[]{:S(2)}, u32[]{:S(2)}) %collective-permute-start.11) | collective-permute-done | bytes 393248 | tf_op jit(solution)/shard_map/ppermute | solution.py:22
  88.9 7.8 %collective-permute-done.12.refs_4_.refs_7_ = bf16[512,384]{1,0:T(8,128)(2,1)S(1)} collective-permute-done((bf16[512,384]{1,0:T(8,128)(2,1)S(1)}, bf16[512,384]{1,0:T(8,128)(2,1)S(1)}, u32[]{:S(2)}, u32[]{:S(2)}) %collective-permute-start.12) | collective-permute-done | bytes 393248 | tf_op jit(solution)/shard_map/ppermute | solution.py:22
  98.3 18.6 %attend.2 = (bf16[512,576]{1,0:T(8,128)(2,1)S(1)}, f32[16,512]{1,0:T(8,128)S(1)}) custom-call(bf16[512,576]{1,0:T(8,128)(2,1)S(1)} %get-tuple-element.90.refs_0_, s32[1,512]{1,0:T(1,128)S(1)} %get-tuple-element.300.refs_1_.refs_4_, bf16[512,384]{1,0:T(8,128)(2,1)S(1)} %get-tuple-element.91.refs_2_.refs_5_, ...), custom_call_target="tpu_custom_call" | custom-call | flops 15000000512 | bytes 4000000 | tf_op jit(solution)/shard_map/attend/pallas_call | solution.py:264
  118.5 2.2 collective-permute-start.21
  120.9 6.7 %collective-permute-done.20 = bf16[2,4,72,384]{3,2,1,0:T(8,128)(2,1)S(1)} collective-permute-done((bf16[2,4,72,384]{3,2,1,0:T(8,128)(2,1)S(1)}, bf16[2,4,72,384]{3,2,1,0:T(8,128)(2,1)S(1)}, u32[]{:S(2)}, u32[]{:S(2)}) %collective-permute-start.20) | collective-permute-done | bytes 442400 | tf_op jit(solution)/shard_map/ppermute | solution.py:22
  128.3 2.1 copy.41
  134.1 5.4 %assemble.3 = bf16[4,8,72,1536]{3,2,1,0:T(8,128)(2,1)} custom-call(bf16[4,72,1536]{2,1,0:T(8,128)(2,1)S(1)} %pad_maximum_fusion.refs_0_, bf16[4,72,1536]{2,1,0:T(8,128)(2,1)} %collective-permute-done.14.refs_1_, bf16[12,4,72,384]{3,2,1,0:T(8,128)(2,1)S(1)} %constant_dynamic-update-slice_fusion.7.refs_2_, bf16[12,4,72,384]{3,2,1,0:T(8,128)(2,1)} %collective-permute-done.22.refs_3_), custom_call_target="tpu_custom_call" | custom-call | tf_op jit(solution)/shard_map/assemble/pallas_call | solution.py:103
  139.5 5.6 %fusion.65 = (bf16[1,8,72,1536]{3,2,1,0:T(8,128)(2,1)S(1)}, bf16[8,72,1536]{2,1,0:T(8,128)(2,1)}, bf16[1,8,72,1536]{3,2,1,0:T(8,128)(2,1)}, bf16[1,8,72,1536]{3,2,1,0:T(8,128)(2,1)}) fusion(bf16[4,8,72,1536]{3,2,1,0:T(8,128)(2,1)} %assemble.3), kind=kLoop, calls=%fused_computation.229 | loop fusion | bytes 14155776 | tf_op jit(solution)/shard_map/slice | solution.py:911
  145.2 9.7 %mlp.2 = (f32[512,576]{1,0:T(8,128)S(1)}, bf16[512,576]{1,0:T(8,128)(2,1)S(1)}, bf16[512,1536]{1,0:T(8,128)(2,1)}, bf16[512,1536]{1,0:T(8,128)(2,1)}, bf16[512,1536]{1,0:T(8,128)(2,1)}, /*index=5*/f32[512,576]{1,0:T(8,128)S(1)}) custom-call(f32[512,576]{1,0:T(8,128)S(1)} %copy-done.3, bf16[512,576]{1,0:T(8,128)(2,1)S(1)} %copy-done.44, ...), custom_call_target="tpu_custom_call" | custom-call | flops 8000000000 | bytes 4000000 | tf_op jit(solution)/shard_map/mlp/pallas_call | solution.py:264
  155.0 3.8 project_in.3
  160.9 2.3 collective-permute-start.25
  163.3 8.4 %collective-permute-done.23.refs_3_.refs_6_ = bf16[512,384]{1,0:T(8,128)(2,1)S(1)} collective-permute-done((bf16[512,384]{1,0:T(8,128)(2,1)S(1)}, bf16[512,384]{1,0:T(8,128)(2,1)S(1)}, u32[]{:S(2)}, u32[]{:S(2)}) %collective-permute-start.23) | collective-permute-done | bytes 393248 | tf_op jit(solution)/shard_map/ppermute | solution.py:22
  171.6 7.9 %collective-permute-done.24.refs_4_.refs_7_ = bf16[512,384]{1,0:T(8,128)(2,1)S(1)} collective-permute-done((bf16[512,384]{1,0:T(8,128)(2,1)S(1)}, bf16[512,384]{1,0:T(8,128)(2,1)S(1)}, u32[]{:S(2)}, u32[]{:S(2)}) %collective-permute-start.24) | collective-permute-done | bytes 393248 | tf_op jit(solution)/shard_map/ppermute | solution.py:22
  179.5 19.0 %attend.3 = (bf16[512,576]{1,0:T(8,128)(2,1)S(1)}, f32[16,512]{1,0:T(8,128)S(1)}) custom-call(bf16[512,576]{1,0:T(8,128)(2,1)S(1)} %get-tuple-element.99.refs_0_, s32[1,512]{1,0:T(1,128)S(1)} %get-tuple-element.300.refs_1_.refs_4_, bf16[512,384]{1,0:T(8,128)(2,1)S(1)} %get-tuple-element.100.refs_2_.refs_5_, ...), custom_call_target="tpu_custom_call" | custom-call | flops 15000000512 | bytes 4000000 | tf_op jit(solution)/shard_map/attend/pallas_call | solution.py:264
  200.2 5.1 %fusion.66 = (bf16[1,576,1536]{2,1,0:T(8,128)(2,1)}, bf16[576,1536]{1,0:T(8,128)(2,1)}, bf16[576,1536]{1,0:T(8,128)(2,1)}) fusion(bf16[3,576,1536]{2,1,0:T(8,128)(2,1)} %all-gather.2.cloned.1.call-done), kind=kLoop, calls=%fused_computation.230 | loop fusion | bytes 10616832 | tf_op jit(solution)/shard_map/slice | solution.py:881
  205.3 9.3 %mlp.3 = (f32[512,576]{1,0:T(8,128)S(1)}, bf16[512,576]{1,0:T(8,128)(2,1)S(1)}, bf16[512,1536]{1,0:T(8,128)(2,1)}, bf16[512,1536]{1,0:T(8,128)(2,1)}, bf16[512,1536]{1,0:T(8,128)(2,1)}, /*index=5*/f32[512,576]{1,0:T(8,128)S(1)}) custom-call(f32[512,576]{1,0:T(8,128)S(1)} %copy-done.24, bf16[512,576]{1,0:T(8,128)(2,1)S(1)} %copy-done.50, ...), custom_call_target="tpu_custom_call" | custom-call | flops 8000000000 | bytes 4000000 | tf_op jit(solution)/shard_map/mlp/pallas_call | solution.py:264
  216.7 18.9 %mlp_back.2 = (bf16[512,576]{1,0:T(8,128)(2,1)S(1)}, f32[512,576]{1,0:T(8,128)S(1)}, f32[8,576]{1,0:T(8,128)S(1)}, bf16[576,576]{1,0:T(8,128)(2,1)S(1)}, bf16[8,3,72,1536]{3,2,1,0:T(8,128)(2,1)}) custom-call(f32[512,576]{1,0:T(8,128)S(1)} %fusion.11.refs_0_, f32[512,576]{1,0:T(8,128)} %copy-done.42, bf16[512,576]{1,0:T(8,128)(2,1)S(1)} %get-tuple-element.106.refs_2_, ...), custom_call_target="tpu_custom_call" | custom-call | flops 15000000512 | bytes 4000000 | tf_op jit(solution)/shard_map/mlp_back/pallas_call | solution.py:264
  241.8 24.6 %attend_back.2 = (f32[512,576]{1,0:T(8,128)}, f32[512,384]{1,0:T(8,128)S(1)}, bf16[512,384]{1,0:T(8,128)(2,1)S(1)}, bf16[512,384]{1,0:T(8,128)(2,1)S(1)}, bf16[512,384]{1,0:T(8,128)(2,1)S(1)}) custom-call(bf16[512,576]{1,0:T(8,128)(2,1)S(1)} %copy-done.34, bf16[512,576]{1,0:T(8,128)(2,1)S(1)} %copy-done.51, bf16[512,576]{1,0:T(8,128)(2,1)S(1)} %copy-done.55, ...), custom_call_target="tpu_custom_call" | custom-call | flops 20000000000 | bytes 4000000 | tf_op jit(solution)/shard_map/attend_back/pallas_call | solution.py:264
  270.0 8.6 %collective-permute-done.28.refs_10_ = bf16[512,384]{1,0:T(8,128)(2,1)S(1)} collective-permute-done((bf16[512,384]{1,0:T(8,128)(2,1)S(1)}, bf16[512,384]{1,0:T(8,128)(2,1)S(1)}, u32[]{:S(2)}, u32[]{:S(2)}) %collective-permute-start.28) | collective-permute-done | bytes 393248 | tf_op jit(solution)/shard_map/ppermute | solution.py:22
  278.6 5.7 %collective-permute-done.29.refs_11_ = bf16[512,384]{1,0:T(8,128)(2,1)S(1)} collective-permute-done((bf16[512,384]{1,0:T(8,128)(2,1)S(1)}, bf16[512,384]{1,0:T(8,128)(2,1)S(1)}, u32[]{:S(2)}, u32[]{:S(2)}) %collective-permute-start.29) | collective-permute-done | bytes 393248 | tf_op jit(solution)/shard_map/ppermute | solution.py:22
  285.8 8.2 %project_back.2 = (f32[512,576]{1,0:T(8,128)S(1)}, f32[8,576]{1,0:T(8,128)S(1)}, bf16[8,1,72,1536]{3,2,1,0:T(8,128)(2,1)}) custom-call(f32[512,576]{1,0:T(8,128)} %get-tuple-element.112.refs_0_, f32[512,128]{1,0:T(8,128)S(1)} %copy-done.6, f32[512,128]{1,0:T(8,128)S(1)} %copy-done.8, f32[512,576]{1,0:T(8,128)} %copy-done.23, ...), custom_call_target="tpu_custom_call" | custom-call | flops 6000000000 | bytes 4000000 | tf_op jit(solution)/shard_map/project_back/pallas_call | solution.py:264
  294.1 19.0 %mlp_back.3 = (bf16[512,576]{1,0:T(8,128)(2,1)S(1)}, f32[512,576]{1,0:T(8,128)S(1)}, f32[8,576]{1,0:T(8,128)S(1)}, bf16[576,576]{1,0:T(8,128)(2,1)S(1)}, bf16[8,3,72,1536]{3,2,1,0:T(8,128)(2,1)}) custom-call(f32[512,576]{1,0:T(8,128)S(1)} %get-tuple-element.120.refs_0_, f32[512,576]{1,0:T(8,128)} %copy-done.41, bf16[512,576]{1,0:T(8,128)(2,1)S(1)} %copy-done.48, ...), custom_call_target="tpu_custom_call" | custom-call | flops 15000000512 | bytes 4000000 | tf_op jit(solution)/shard_map/mlp_back/pallas_call | solution.py:264
  315.1 4.8 cut.2
  325.3 4.8 convert_add_fusion
  337.2 24.8 %attend_back.3 = (f32[512,576]{1,0:T(8,128)}, f32[512,384]{1,0:T(8,128)S(1)}, bf16[512,384]{1,0:T(8,128)(2,1)}, bf16[512,384]{1,0:T(8,128)(2,1)S(1)}, bf16[512,384]{1,0:T(8,128)(2,1)S(1)}) custom-call(bf16[512,576]{1,0:T(8,128)(2,1)S(1)} %copy-done.30, bf16[512,576]{1,0:T(8,128)(2,1)S(1)} %copy-done.46, bf16[512,576]{1,0:T(8,128)(2,1)S(1)} %copy-done.53, ...), custom_call_target="tpu_custom_call" | custom-call | flops 20000000000 | bytes 4000000 | tf_op jit(solution)/shard_map/attend_back/pallas_call | solution.py:264
  376.1 8.3 %collective-permute-done.33.refs_11_ = bf16[512,384]{1,0:T(8,128)(2,1)S(1)} collective-permute-done((bf16[512,384]{1,0:T(8,128)(2,1)S(1)}, bf16[512,384]{1,0:T(8,128)(2,1)S(1)}, u32[]{:S(2)}, u32[]{:S(2)}) %collective-permute-start.33) | collective-permute-done | bytes 393248 | tf_op jit(solution)/shard_map/ppermute | solution.py:22
  390.0 8.5 %project_back.3 = (f32[512,576]{1,0:T(8,128)S(1)}, f32[8,576]{1,0:T(8,128)}, bf16[8,1,80,1536]{3,2,1,0:T(8,128)(2,1)}) custom-call(f32[512,576]{1,0:T(8,128)} %get-tuple-element.133.refs_0_, f32[512,128]{1,0:T(8,128)S(1)} %copy-done.6, f32[512,128]{1,0:T(8,128)S(1)} %copy-done.8, f32[512,576]{1,0:T(8,128)} %copy-done.2, bf16[512,576]{1,0:T(8,128)(2,1)S(1)} %copy-done.28, ...), custom_call_target="tpu_custom_call" | custom-call | flops 6000000000 | bytes 4000000 | tf_op jit(solution)/shard_map/project_back/pallas_call | solution.py:264
  403.2 7.8 %collective-permute-done.50 = bf16[3,72,384]{2,1,0:T(8,128)(2,1)S(1)} collective-permute-done((bf16[3,72,384]{2,1,0:T(8,128)(2,1)}, bf16[3,72,384]{2,1,0:T(8,128)(2,1)S(1)}, u32[]{:S(2)}, u32[]{:S(2)}) %collective-permute-start.50) | collective-permute-done | bytes 165920 | tf_op jit(solution)/shard_map/ppermute | solution.py:22
  411.1 3.0 collective-permute-start.53
  420.1 2.4 collective-permute-start.55
  424.3 2.3 fusion.14
  430.0 2.7 copy.51
  437.8 2.2 collective-permute-start.62
  440.0 2.3 collective-permute-start.59
  442.5 4.3 collective-permute-done.62
  446.8 5.7 %collective-permute-done.61 = bf16[3,72,384]{2,1,0:T(8,128)(2,1)S(1)} collective-permute-done((bf16[3,72,384]{2,1,0:T(8,128)(2,1)S(1)}, bf16[3,72,384]{2,1,0:T(8,128)(2,1)S(1)}, u32[]{:S(2)}, u32[]{:S(2)}) %collective-permute-start.61) | collective-permute-done | bytes 165920 | tf_op jit(solution)/shard_map/ppermute | solution.py:22
  456.3 4.4 collective-permute-done.63
  467.4 5.8 %collective-permute-done.40 = bf16[2,2,1,80,384]{4,3,1,2,0:T(8,128)(2,1)S(1)} collective-permute-done((bf16[2,2,1,80,384]{4,3,1,2,0:T(8,128)(2,1)S(1)}, bf16[2,2,1,80,384]{4,3,1,2,0:T(8,128)(2,1)S(1)}, u32[]{:S(2)}, u32[]{:S(2)}) %collective-permute-start.40) | collective-permute-done | bytes 245792 | tf_op jit(solution)/shard_map/ppermute | solution.py:22
  475.3 2.9 collective-permute-done.41
  480.3 2.5 collective-permute-start.39
  (369 shorter events, 146.6 us)
Async XLA Ops:
  7.2 193.0 %all-gather.2.cloned.1.call-start = ((), (), s32[]{:S(2)}) async-start(), calls=%async_computation.2 | async-start | bytes 5971968 | tf_op jit(solution)/shard_map/all_gather | solution.py:133
  11.4 16.7 %collective-permute-start.2 = (bf16[1,80,384]{2,1,0:T(8,128)(2,1)}, bf16[1,80,384]{2,1,0:T(8,128)(2,1)S(1)}, u32[]{:S(2)}, u32[]{:S(2)}) collective-permute-start(bf16[1,80,384]{2,1,0:T(8,128)(2,1)} %fusion.44), channel_id=1, source_target_pairs={{0,2},{1,3},{2,0},{3,1},{4,6},{5,7},{6,4},{7,5},{8,10},{9,11},{10,... | collective-permute-start | bytes 184328 | tf_op jit(solution)/shard_map/ppermute | solution.py:22
  14.4 13.7 %collective-permute-start.3 = (bf16[1,80,384]{2,1,0:T(8,128)(2,1)}, bf16[1,80,384]{2,1,0:T(8,128)(2,1)S(1)}, u32[]{:S(2)}, u32[]{:S(2)}) collective-permute-start(bf16[1,80,384]{2,1,0:T(8,128)(2,1)} %fusion.44), channel_id=1, source_target_pairs={{0,4},{1,5},{2,6},{3,7},{4,0},{5,1},{6,2},{7,3},{8,12},{9,13},{10,... | collective-permute-start | bytes 184328 | tf_op jit(solution)/shard_map/ppermute | solution.py:22
  17.0 11.1 %collective-permute-start.4 = (bf16[1,80,384]{2,1,0:T(8,128)(2,1)}, bf16[1,80,384]{2,1,0:T(8,128)(2,1)}, u32[]{:S(2)}, u32[]{:S(2)}) collective-permute-start(bf16[1,80,384]{2,1,0:T(8,128)(2,1)} %fusion.44), channel_id=1, source_target_pairs={{0,6},{1,7},{2,4},{3,5},{4,2},{5,3},{6,0},{7,1},{8,14},{9,15},{10,... | collective-permute-start | bytes 184328 | tf_op jit(solution)/shard_map/ppermute | solution.py:22
  17.9 47.2 %collective-permute-start = (bf16[1,256,576]{2,1,0:T(8,128)(2,1)}, bf16[1,256,576]{2,1,0:T(8,128)(2,1)}, u32[]{:S(2)}, u32[]{:S(2)}) collective-permute-start(bf16[1,256,576]{2,1,0:T(8,128)(2,1)} %copy.53), channel_id=1, source_target_pairs={{0,24},{8,16},{16,8},{24,0},{1,25},{9,17},{17,9},{25,1},{2,26},{10... | collective-permute-start | bytes 884744 | tf_op jit(solution)/shard_map/ppermute | solution.py:22
  41.7 24.7 %collective-permute-start.9 = (bf16[12,1,80,384]{3,2,1,0:T(8,128)(2,1)S(1)}, bf16[12,1,80,384]{3,2,1,0:T(8,128)(2,1)}, u32[]{:S(2)}, u32[]{:S(2)}) collective-permute-start(bf16[12,1,80,384]{3,2,1,0:T(8,128)(2,1)S(1)} %constant_dynamic-update-slice_fusion.refs_2_), channel_id=1, source_target_pairs={{0,1},{1,0},{2,3},{3,2},{4,5},{5,4},{6,7},{7,6},{8,9},{9,8},{10,11... | collective-permute-start | bytes 2211848 | tf_op jit(solution)/shard_map/ppermute | solution.py:22
  41.8 10.2 %collective-permute-start.17 = (bf16[4,72,384]{2,1,0:T(8,128)(2,1)S(1)}, bf16[4,72,384]{2,1,0:T(8,128)(2,1)S(1)}, u32[]{:S(2)}, u32[]{:S(2)}) collective-permute-start(bf16[4,72,384]{2,1,0:T(8,128)(2,1)S(1)} %constant_dynamic-slice_fusion), channel_id=1, source_target_pairs={{0,6},{1,7},{2,4},{3,5},{4,2},{5,3},{6,0},{7,1},{8,14},{9,15},{10,... | collective-permute-start | bytes 663560 | tf_op jit(solution)/shard_map/ppermute | solution.py:22
  45.4 18.5 %collective-permute-start.16 = (bf16[4,72,384]{2,1,0:T(8,128)(2,1)S(1)}, bf16[4,72,384]{2,1,0:T(8,128)(2,1)S(1)}, u32[]{:S(2)}, u32[]{:S(2)}) collective-permute-start(bf16[4,72,384]{2,1,0:T(8,128)(2,1)S(1)} %constant_dynamic-slice_fusion), channel_id=1, source_target_pairs={{0,4},{1,5},{2,6},{3,7},{4,0},{5,1},{6,2},{7,3},{8,12},{9,13},{10,... | collective-permute-start | bytes 663560 | tf_op jit(solution)/shard_map/ppermute | solution.py:22
  45.4 18.5 %collective-permute-start.15 = (bf16[4,72,384]{2,1,0:T(8,128)(2,1)S(1)}, bf16[4,72,384]{2,1,0:T(8,128)(2,1)S(1)}, u32[]{:S(2)}, u32[]{:S(2)}) collective-permute-start(bf16[4,72,384]{2,1,0:T(8,128)(2,1)S(1)} %constant_dynamic-slice_fusion), channel_id=1, source_target_pairs={{0,2},{1,3},{2,0},{3,1},{4,6},{5,7},{6,4},{7,5},{8,10},{9,11},{10,... | collective-permute-start | bytes 663560 | tf_op jit(solution)/shard_map/ppermute | solution.py:22
  52.0 14.3 %collective-permute-start.1 = (bf16[1,80,1536]{2,1,0:T(8,128)(2,1)S(1)}, bf16[1,80,1536]{2,1,0:T(8,128)(2,1)}, u32[]{:S(2)}, u32[]{:S(2)}) collective-permute-start(bf16[1,80,1536]{2,1,0:T(8,128)(2,1)S(1)} %fusion.19.refs_0_), channel_id=1, source_target_pairs={{0,1},{1,0},{2,3},{3,2},{4,5},{5,4},{6,7},{7,6},{8,9},{9,8},{10,11... | collective-permute-start | bytes 737288 | tf_op jit(solution)/shard_map/ppermute | solution.py:22
  64.9 267.1 %reduce-scatter.3.cloned.1.call-start = ((), (), s32[]{:S(2)}) async-start(), calls=%async_computation.3 | async-start | bytes 5971968 | tf_op jit(solution)/shard_map/reduce_scatter | solution.py:208
  76.9 12.0 %collective-permute-start.11 = (bf16[512,384]{1,0:T(8,128)(2,1)S(1)}, bf16[512,384]{1,0:T(8,128)(2,1)S(1)}, u32[]{:S(2)}, u32[]{:S(2)}) collective-permute-start(bf16[512,384]{1,0:T(8,128)(2,1)S(1)} %get-tuple-element.91.refs_2_.refs_5_), channel_id=1, source_target_pairs={{0,8},{8,0},{16,24},{24,16},{1,9},{9,1},{17,25},{25,17},{2,10},{10... | collective-permute-start | bytes 1179656 | tf_op jit(solution)/shard_map/ppermute | solution.py:22
  77.1 19.7 %collective-permute-start.12 = (bf16[512,384]{1,0:T(8,128)(2,1)S(1)}, bf16[512,384]{1,0:T(8,128)(2,1)S(1)}, u32[]{:S(2)}, u32[]{:S(2)}) collective-permute-start(bf16[512,384]{1,0:T(8,128)(2,1)S(1)} %get-tuple-element.91.refs_2_.refs_5_), channel_id=1, source_target_pairs={{0,16},{8,24},{16,0},{24,8},{1,17},{9,25},{17,1},{25,9},{2,18},{10... | collective-permute-start | bytes 1179656 | tf_op jit(solution)/shard_map/ppermute | solution.py:22
  78.4 19.9 %collective-permute-start.13 = (bf16[512,384]{1,0:T(8,128)(2,1)S(1)}, bf16[512,384]{1,0:T(8,128)(2,1)S(1)}, u32[]{:S(2)}, u32[]{:S(2)}) collective-permute-start(bf16[512,384]{1,0:T(8,128)(2,1)S(1)} %get-tuple-element.91.refs_2_.refs_5_), channel_id=1, source_target_pairs={{0,24},{8,16},{16,8},{24,0},{1,25},{9,17},{17,9},{25,1},{2,26},{10... | collective-permute-start | bytes 1179656 | tf_op jit(solution)/shard_map/ppermute | solution.py:22
  80.4 36.6 %collective-permute-start.18 = (bf16[3,4,72,384]{3,2,1,0:T(8,128)(2,1)S(1)}, bf16[3,4,72,384]{3,2,1,0:T(8,128)(2,1)S(1)}, u32[]{:S(2)}, u32[]{:S(2)}) collective-permute-start(bf16[3,4,72,384]{3,2,1,0:T(8,128)(2,1)S(1)} %copy-done.60), channel_id=1, source_target_pairs={{0,8},{8,0},{16,24},{24,16},{1,9},{9,1},{17,25},{25,17},{2,10},{10... | collective-permute-start | bytes 1990664 | tf_op jit(solution)/shard_map/ppermute | solution.py:22
  80.6 36.5 %collective-permute-start.19 = (bf16[3,4,72,384]{3,2,1,0:T(8,128)(2,1)S(1)}, bf16[3,4,72,384]{3,2,1,0:T(8,128)(2,1)S(1)}, u32[]{:S(2)}, u32[]{:S(2)}) collective-permute-start(bf16[3,4,72,384]{3,2,1,0:T(8,128)(2,1)S(1)} %copy-done.60), channel_id=1, source_target_pairs={{0,16},{8,24},{16,0},{24,8},{1,17},{9,25},{17,1},{25,9},{2,18},{10... | collective-permute-start | bytes 1990664 | tf_op jit(solution)/shard_map/ppermute | solution.py:22
  117.9 9.7 %collective-permute-start.20 = (bf16[2,4,72,384]{3,2,1,0:T(8,128)(2,1)S(1)}, bf16[2,4,72,384]{3,2,1,0:T(8,128)(2,1)S(1)}, u32[]{:S(2)}, u32[]{:S(2)}) collective-permute-start(bf16[2,4,72,384]{3,2,1,0:T(8,128)(2,1)S(1)} %slice.527), channel_id=1, source_target_pairs={{0,16},{8,24},{16,0},{24,8},{1,17},{9,25},{17,1},{25,9},{2,18},{10... | collective-permute-start | bytes 1327112 | tf_op jit(solution)/shard_map/ppermute | solution.py:22
  118.5 9.1 %collective-permute-start.21 = (bf16[1,4,72,384]{3,2,1,0:T(8,128)(2,1)S(1)}, bf16[1,4,72,384]{3,2,1,0:T(8,128)(2,1)S(1)}, u32[]{:S(2)}, u32[]{:S(2)}) collective-permute-start(bf16[1,4,72,384]{3,2,1,0:T(8,128)(2,1)S(1)} %slice.528), channel_id=1, source_target_pairs={{0,8},{8,0},{16,24},{24,16},{1,9},{9,1},{17,25},{25,17},{2,10},{10... | collective-permute-start | bytes 663560 | tf_op jit(solution)/shard_map/ppermute | solution.py:22
  131.6 31.6 %collective-permute-start.27 = (bf16[1,256,576]{2,1,0:T(8,128)(2,1)S(1)}, bf16[1,256,576]{2,1,0:T(8,128)(2,1)S(1)}, u32[]{:S(2)}, u32[]{:S(2)}) collective-permute-start(bf16[1,256,576]{2,1,0:T(8,128)(2,1)S(1)} %get-tuple-element.242), channel_id=1, source_target_pairs={{0,24},{8,16},{16,8},{24,0},{1,25},{9,17},{17,9},{25,1},{2,26},{10... | collective-permute-start | bytes 884744 | tf_op jit(solution)/shard_map/ppermute | solution.py:22
  159.7 12.0 %collective-permute-start.23 = (bf16[512,384]{1,0:T(8,128)(2,1)S(1)}, bf16[512,384]{1,0:T(8,128)(2,1)S(1)}, u32[]{:S(2)}, u32[]{:S(2)}) collective-permute-start(bf16[512,384]{1,0:T(8,128)(2,1)S(1)} %get-tuple-element.100.refs_2_.refs_5_), channel_id=1, source_target_pairs={{0,8},{8,0},{16,24},{24,16},{1,9},{9,1},{17,25},{25,17},{2,10},{10... | collective-permute-start | bytes 1179656 | tf_op jit(solution)/shard_map/ppermute | solution.py:22
  160.2 19.3 %collective-permute-start.24 = (bf16[512,384]{1,0:T(8,128)(2,1)S(1)}, bf16[512,384]{1,0:T(8,128)(2,1)S(1)}, u32[]{:S(2)}, u32[]{:S(2)}) collective-permute-start(bf16[512,384]{1,0:T(8,128)(2,1)S(1)} %get-tuple-element.100.refs_2_.refs_5_), channel_id=1, source_target_pairs={{0,16},{8,24},{16,0},{24,8},{1,17},{9,25},{17,1},{25,9},{2,18},{10... | collective-permute-start | bytes 1179656 | tf_op jit(solution)/shard_map/ppermute | solution.py:22
  160.9 18.6 %collective-permute-start.25 = (bf16[512,384]{1,0:T(8,128)(2,1)S(1)}, bf16[512,384]{1,0:T(8,128)(2,1)S(1)}, u32[]{:S(2)}, u32[]{:S(2)}) collective-permute-start(bf16[512,384]{1,0:T(8,128)(2,1)S(1)} %get-tuple-element.100.refs_2_.refs_5_), channel_id=1, source_target_pairs={{0,24},{8,16},{16,8},{24,0},{1,25},{9,17},{17,9},{25,1},{2,26},{10... | collective-permute-start | bytes 1179656 | tf_op jit(solution)/shard_map/ppermute | solution.py:22
  238.4 134.6 %reduce-scatter.5.cloned.1.call-start = ((), (), s32[]{:S(2)}) async-start(), calls=%async_computation.4 | async-start | bytes 1990656 | tf_op jit(solution)/shard_map/reduce_scatter | solution.py:208
  266.4 12.1 %collective-permute-start.28 = (bf16[512,384]{1,0:T(8,128)(2,1)S(1)}, bf16[512,384]{1,0:T(8,128)(2,1)S(1)}, u32[]{:S(2)}, u32[]{:S(2)}) collective-permute-start(bf16[512,384]{1,0:T(8,128)(2,1)S(1)} %get-tuple-element.117), channel_id=1, source_target_pairs={{0,8},{8,0},{16,24},{24,16},{1,9},{9,1},{17,25},{25,17},{2,10},{10... | collective-permute-start | bytes 1179656 | tf_op jit(solution)/shard_map/ppermute | solution.py:22
  268.0 16.3 %collective-permute-start.29 = (bf16[512,384]{1,0:T(8,128)(2,1)S(1)}, bf16[512,384]{1,0:T(8,128)(2,1)S(1)}, u32[]{:S(2)}, u32[]{:S(2)}) collective-permute-start(bf16[512,384]{1,0:T(8,128)(2,1)S(1)} %get-tuple-element.118), channel_id=1, source_target_pairs={{0,16},{8,24},{16,0},{24,8},{1,17},{9,25},{17,1},{25,9},{2,18},{10... | collective-permute-start | bytes 1179656 | tf_op jit(solution)/shard_map/ppermute | solution.py:22
  268.4 17.4 %collective-permute-start.30 = (bf16[512,384]{1,0:T(8,128)(2,1)S(1)}, bf16[512,384]{1,0:T(8,128)(2,1)S(1)}, u32[]{:S(2)}, u32[]{:S(2)}) collective-permute-start(bf16[512,384]{1,0:T(8,128)(2,1)S(1)} %get-tuple-element.119), channel_id=1, source_target_pairs={{0,24},{8,16},{16,8},{24,0},{1,25},{9,17},{17,9},{25,1},{2,26},{10... | collective-permute-start | bytes 1179656 | tf_op jit(solution)/shard_map/ppermute | solution.py:22
  322.3 44.1 %collective-permute-start.26 = (bf16[1,256,576]{2,1,0:T(8,128)(2,1)}, bf16[1,256,576]{2,1,0:T(8,128)(2,1)}, u32[]{:S(2)}, u32[]{:S(2)}) collective-permute-start(bf16[1,256,576]{2,1,0:T(8,128)(2,1)} %get-tuple-element.244), channel_id=1, source_target_pairs={{0,24},{8,16},{16,8},{24,0},{1,25},{9,17},{17,9},{25,1},{2,26},{10... | collective-permute-start | bytes 884744 | tf_op jit(solution)/shard_map/ppermute | solution.py:22
  362.9 12.2 %collective-permute-start.32 = (bf16[512,384]{1,0:T(8,128)(2,1)}, bf16[512,384]{1,0:T(8,128)(2,1)S(1)}, u32[]{:S(2)}, u32[]{:S(2)}) collective-permute-start(bf16[512,384]{1,0:T(8,128)(2,1)} %get-tuple-element.138), channel_id=1, source_target_pairs={{0,8},{8,0},{16,24},{24,16},{1,9},{9,1},{17,25},{25,17},{2,10},{10... | collective-permute-start | bytes 1179656 | tf_op jit(solution)/shard_map/ppermute | solution.py:22
  363.9 20.4 %collective-permute-start.33 = (bf16[512,384]{1,0:T(8,128)(2,1)S(1)}, bf16[512,384]{1,0:T(8,128)(2,1)S(1)}, u32[]{:S(2)}, u32[]{:S(2)}) collective-permute-start(bf16[512,384]{1,0:T(8,128)(2,1)S(1)} %get-tuple-element.139), channel_id=1, source_target_pairs={{0,16},{8,24},{16,0},{24,8},{1,17},{9,25},{17,1},{25,9},{2,18},{10... | collective-permute-start | bytes 1179656 | tf_op jit(solution)/shard_map/ppermute | solution.py:22
  365.4 20.4 %collective-permute-start.34 = (bf16[512,384]{1,0:T(8,128)(2,1)S(1)}, bf16[512,384]{1,0:T(8,128)(2,1)S(1)}, u32[]{:S(2)}, u32[]{:S(2)}) collective-permute-start(bf16[512,384]{1,0:T(8,128)(2,1)S(1)} %get-tuple-element.140), channel_id=1, source_target_pairs={{0,24},{8,16},{16,8},{24,0},{1,25},{9,17},{17,9},{25,1},{2,26},{10... | collective-permute-start | bytes 1179656 | tf_op jit(solution)/shard_map/ppermute | solution.py:22
  370.5 40.5 %collective-permute-start.47 = (bf16[2,2,3,72,384]{4,3,2,1,0:T(8,128)(2,1)}, bf16[2,2,3,72,384]{4,3,2,1,0:T(8,128)(2,1)}, u32[]{:S(2)}, u32[]{:S(2)}) collective-permute-start(bf16[2,2,3,72,384]{4,3,2,1,0:T(8,128)(2,1)} %pad_maximum_fusion.5), channel_id=1, source_target_pairs={{0,8},{8,0},{16,24},{24,16},{1,9},{9,1},{17,25},{25,17},{2,10},{10... | collective-permute-start | bytes 1990664 | tf_op jit(solution)/shard_map/ppermute | solution.py:22
  371.6 39.4 %collective-permute-start.48 = (bf16[2,2,3,72,384]{4,3,2,1,0:T(8,128)(2,1)}, bf16[2,2,3,72,384]{4,3,2,1,0:T(8,128)(2,1)}, u32[]{:S(2)}, u32[]{:S(2)}) collective-permute-start(bf16[2,2,3,72,384]{4,3,2,1,0:T(8,128)(2,1)} %stack.92), channel_id=1, source_target_pairs={{0,16},{8,24},{16,0},{24,8},{1,17},{9,25},{17,1},{25,9},{2,18},{10... | collective-permute-start | bytes 1990664 | tf_op jit(solution)/shard_map/ppermute | solution.py:22
  375.1 26.2 %collective-permute-start.49 = (bf16[3,72,384]{2,1,0:T(8,128)(2,1)}, bf16[3,72,384]{2,1,0:T(8,128)(2,1)S(1)}, u32[]{:S(2)}, u32[]{:S(2)}) collective-permute-start(bf16[3,72,384]{2,1,0:T(8,128)(2,1)} %get-tuple-element.151), channel_id=1, source_target_pairs={{0,8},{8,0},{16,24},{24,16},{1,9},{9,1},{17,25},{25,17},{2,10},{10... | collective-permute-start | bytes 497672 | tf_op jit(solution)/shard_map/ppermute | solution.py:22
  384.3 26.7 %collective-permute-start.50 = (bf16[3,72,384]{2,1,0:T(8,128)(2,1)}, bf16[3,72,384]{2,1,0:T(8,128)(2,1)S(1)}, u32[]{:S(2)}, u32[]{:S(2)}) collective-permute-start(bf16[3,72,384]{2,1,0:T(8,128)(2,1)} %get-tuple-element.152), channel_id=1, source_target_pairs={{0,16},{8,24},{16,0},{24,8},{1,17},{9,25},{17,1},{25,9},{2,18},{10... | collective-permute-start | bytes 497672 | tf_op jit(solution)/shard_map/ppermute | solution.py:22
  385.8 25.2 %collective-permute-start.51 = (bf16[3,72,384]{2,1,0:T(8,128)(2,1)S(1)}, bf16[3,72,384]{2,1,0:T(8,128)(2,1)S(1)}, u32[]{:S(2)}, u32[]{:S(2)}) collective-permute-start(bf16[3,72,384]{2,1,0:T(8,128)(2,1)S(1)} %get-tuple-element.153), channel_id=1, source_target_pairs={{0,24},{8,16},{16,8},{24,0},{1,25},{9,17},{17,9},{25,1},{2,26},{10... | collective-permute-start | bytes 497672 | tf_op jit(solution)/shard_map/ppermute | solution.py:22
  401.3 27.3 %collective-permute-start.35 = (bf16[256,576]{1,0:T(8,128)(2,1)S(1)}, bf16[256,576]{1,0:T(8,128)(2,1)S(1)}, u32[]{:S(2)}, u32[]{:S(2)}) collective-permute-start(bf16[256,576]{1,0:T(8,128)(2,1)S(1)} %slice.865), channel_id=1, source_target_pairs={{0,24},{8,16},{16,8},{24,0},{1,25},{9,17},{17,9},{25,1},{2,26},{10... | collective-permute-start | bytes 884744 | tf_op jit(solution)/shard_map/ppermute | solution.py:22
  420.1 12.7 %collective-permute-start.55 = (bf16[4,72,384]{2,1,0:T(8,128)(2,1)}, bf16[4,72,384]{2,1,0:T(8,128)(2,1)}, u32[]{:S(2)}, u32[]{:S(2)}) collective-permute-start(bf16[4,72,384]{2,1,0:T(8,128)(2,1)} %pad_maximum_fusion.12), channel_id=1, source_target_pairs={{0,24},{8,16},{16,8},{24,0},{1,25},{9,17},{17,9},{25,1},{2,26},{10... | collective-permute-start | bytes 663560 | tf_op jit(solution)/shard_map/ppermute | solution.py:22
  422.5 10.3 %collective-permute-start.56 = (bf16[4,72,384]{2,1,0:T(8,128)(2,1)}, bf16[4,72,384]{2,1,0:T(8,128)(2,1)}, u32[]{:S(2)}, u32[]{:S(2)}) collective-permute-start(bf16[4,72,384]{2,1,0:T(8,128)(2,1)} %pad_maximum_fusion.12), channel_id=1, source_target_pairs={{0,16},{8,24},{16,0},{24,8},{1,17},{9,25},{17,1},{25,9},{2,18},{10... | collective-permute-start | bytes 663560 | tf_op jit(solution)/shard_map/ppermute | solution.py:22
  424.3 8.5 %collective-permute-start.57 = (bf16[4,72,384]{2,1,0:T(8,128)(2,1)}, bf16[4,72,384]{2,1,0:T(8,128)(2,1)}, u32[]{:S(2)}, u32[]{:S(2)}) collective-permute-start(bf16[4,72,384]{2,1,0:T(8,128)(2,1)} %pad_maximum_fusion.12), channel_id=1, source_target_pairs={{0,8},{8,0},{16,24},{24,16},{1,9},{9,1},{17,25},{25,17},{2,10},{10... | collective-permute-start | bytes 663560 | tf_op jit(solution)/shard_map/ppermute | solution.py:22
  426.6 8.3 %collective-permute-start.60 = (bf16[2,3,72,384]{3,2,1,0:T(8,128)(2,1)}, bf16[2,3,72,384]{3,2,1,0:T(8,128)(2,1)}, u32[]{:S(2)}, u32[]{:S(2)}) collective-permute-start(bf16[2,3,72,384]{3,2,1,0:T(8,128)(2,1)} %get-tuple-element.193), channel_id=1, source_target_pairs={{0,8},{8,0},{16,24},{24,16},{1,9},{9,1},{17,25},{25,17},{2,10},{10... | collective-permute-start | bytes 995336 | tf_op jit(solution)/shard_map/ppermute | solution.py:22
  432.8 32.4 %collective-permute-start.36 = (bf16[4,4,1,80,384]{4,3,2,1,0:T(8,128)(2,1)S(1)}, bf16[4,4,1,80,384]{4,3,2,1,0:T(8,128)(2,1)S(1)}, u32[]{:S(2)}, u32[]{:S(2)}) collective-permute-start(bf16[4,4,1,80,384]{4,3,2,1,0:T(8,128)(2,1)S(1)} %get-tuple-element.147), channel_id=1, source_target_pairs={{0,1},{1,0},{2,3},{3,2},{4,5},{5,4},{6,7},{7,6},{8,9},{9,8},{10,11... | collective-permute-start | bytes 2949128 | tf_op jit(solution)/shard_map/ppermute | solution.py:22
  437.8 9.0 %collective-permute-start.62 = (bf16[3,72,384]{2,1,0:T(8,128)(2,1)S(1)}, bf16[3,72,384]{2,1,0:T(8,128)(2,1)S(1)}, u32[]{:S(2)}, u32[]{:S(2)}) collective-permute-start(bf16[3,72,384]{2,1,0:T(8,128)(2,1)S(1)} %get-tuple-element.260), channel_id=1, source_target_pairs={{0,6},{1,7},{2,4},{3,5},{4,2},{5,3},{6,0},{7,1},{8,14},{9,15},{10,... | collective-permute-start | bytes 497672 | tf_op jit(solution)/shard_map/ppermute | solution.py:22
  439.9 12.6 %collective-permute-start.61 = (bf16[3,72,384]{2,1,0:T(8,128)(2,1)S(1)}, bf16[3,72,384]{2,1,0:T(8,128)(2,1)S(1)}, u32[]{:S(2)}, u32[]{:S(2)}) collective-permute-start(bf16[3,72,384]{2,1,0:T(8,128)(2,1)S(1)} %get-tuple-element.259), channel_id=1, source_target_pairs={{0,4},{1,5},{2,6},{3,7},{4,0},{5,1},{6,2},{7,3},{8,12},{9,13},{10,... | collective-permute-start | bytes 497672 | tf_op jit(solution)/shard_map/ppermute | solution.py:22
  440.0 12.6 %collective-permute-start.59 = (bf16[3,72,384]{2,1,0:T(8,128)(2,1)S(1)}, bf16[3,72,384]{2,1,0:T(8,128)(2,1)S(1)}, u32[]{:S(2)}, u32[]{:S(2)}) collective-permute-start(bf16[3,72,384]{2,1,0:T(8,128)(2,1)S(1)} %fusion.28), channel_id=1, source_target_pairs={{0,2},{1,3},{2,0},{3,1},{4,6},{5,7},{6,4},{7,5},{8,10},{9,11},{10,... | collective-permute-start | bytes 497672 | tf_op jit(solution)/shard_map/ppermute | solution.py:22
  452.6 8.1 %collective-permute-start.63 = (bf16[3,72,384]{2,1,0:T(8,128)(2,1)S(1)}, bf16[3,72,384]{2,1,0:T(8,128)(2,1)S(1)}, u32[]{:S(2)}, u32[]{:S(2)}) collective-permute-start(bf16[3,72,384]{2,1,0:T(8,128)(2,1)S(1)} %fusion.18), channel_id=1, source_target_pairs={{0,24},{8,16},{16,8},{24,0},{1,25},{9,17},{17,9},{25,1},{2,26},{10... | collective-permute-start | bytes 497672 | tf_op jit(solution)/shard_map/ppermute | solution.py:22
  453.4 9.1 %collective-permute-start.64 = (bf16[3,72,384]{2,1,0:T(8,128)(2,1)S(1)}, bf16[3,72,384]{2,1,0:T(8,128)(2,1)S(1)}, u32[]{:S(2)}, u32[]{:S(2)}) collective-permute-start(bf16[3,72,384]{2,1,0:T(8,128)(2,1)S(1)} %fusion.18), channel_id=1, source_target_pairs={{0,16},{8,24},{16,0},{24,8},{1,17},{9,25},{17,1},{25,9},{2,18},{10... | collective-permute-start | bytes 497672 | tf_op jit(solution)/shard_map/ppermute | solution.py:22
  454.2 8.6 %collective-permute-start.65 = (bf16[3,72,384]{2,1,0:T(8,128)(2,1)S(1)}, bf16[3,72,384]{2,1,0:T(8,128)(2,1)S(1)}, u32[]{:S(2)}, u32[]{:S(2)}) collective-permute-start(bf16[3,72,384]{2,1,0:T(8,128)(2,1)S(1)} %fusion.18), channel_id=1, source_target_pairs={{0,8},{8,0},{16,24},{24,16},{1,9},{9,1},{17,25},{25,17},{2,10},{10... | collective-permute-start | bytes 497672 | tf_op jit(solution)/shard_map/ppermute | solution.py:22
  466.4 7.6 %collective-permute-start.37 = (bf16[2,2,1,80,384]{4,3,1,2,0:T(8,128)(2,1)S(1)}, bf16[2,2,1,80,384]{4,3,1,2,0:T(8,128)(2,1)S(1)}, u32[]{:S(2)}, u32[]{:S(2)}) collective-permute-start(bf16[2,2,1,80,384]{4,3,1,2,0:T(8,128)(2,1)S(1)} %pad_maximum_fusion.11), channel_id=1, source_target_pairs={{0,8},{8,0},{16,24},{24,16},{1,9},{9,1},{17,25},{25,17},{2,10},{10... | collective-permute-start | bytes 737288 | tf_op jit(solution)/shard_map/ppermute | solution.py:22
  (87 other events, 612.8 us)
Sparse Core Ops, SparseCore 0:
  65.0 55.7 all-gather.1
  238.6 59.4 reduce-scatter.2
  320.2 34.4 reduce-scatter.4

commit v3 on v2

--- a/solution.py
+++ b/solution.py
@@ -133,65 +133,79 @@
     return lax.all_gather(own, "fsdp", axis=1, tiled=True)
 
 
-def scatter_kernel(whole, keep, send, sems):
+def scatter_kernel(count, *refs):
+    wholes, (keep, send, sems) = refs[:count], refs[count:]
     j = lax.axis_index("ctx")
     f = lax.axis_index("fsdp")
     copies = []
     for core, pieces in ((0, keep), (1, send)):
         for jrel in range(4):
             for zrel in range(4):
-                row = f ^ (core + 2 * zrel)
-                column = pl.multiple_of((j ^ jrel) * PIECE, 128)
-                made = pltpu.make_async_copy(
-                    whole.at[row, :, :, pl.ds(column, PIECE)],
-                    pieces.at[jrel, zrel],
-                    sems.at[len(copies)],
-                )
-                made.start()
-                copies.append(made)
+                row = (f ^ (core + 2 * zrel)) * 4 + (j ^ jrel)
+                at = 0
+                for whole in wholes:
+                    made = pltpu.make_async_copy(
+                        whole.at[row],
+                        pieces.at[jrel, zrel, at : at + whole.shape[1]],
+                        sems.at[len(copies)],
+                    )
+                    made.start()
+                    copies.append(made)
+                    at += whole.shape[1]
     for made in copies:
         made.wait()
 
 
-def cut(whole):
-    fsdp, count, rows, columns = whole.shape
-    piece = jax.ShapeDtypeStruct((4, 4, count, rows, PIECE), whole.dtype)
+def cut(wholes):
+    rows = wholes[0].shape[2]
+    total = sum(whole.shape[1] for whole in wholes)
+    piece = jax.ShapeDtypeStruct((4, 4, total, rows, PIECE), wholes[0].dtype)
     return pl.pallas_call(
-        scatter_kernel,
+        lambda *refs: scatter_kernel(len(wholes), *refs),
         out_shape=(piece, piece),
-        in_specs=[pl.BlockSpec(memory_space=pltpu.VMEM)],
+        in_specs=[pl.BlockSpec(memory_space=pltpu.VMEM)] * len(wholes),
         out_specs=[pl.BlockSpec(memory_space=pl.ANY)] * 2,
-        scratch_shapes=[pltpu.SemaphoreType.DMA((32,))],
+        scratch_shapes=[pltpu.SemaphoreType.DMA((32 * len(wholes),))],
         compiler_params=pltpu.CompilerParams(vmem_limit_bytes=VMEM_LIMIT),
         name="cut",
-    )(whole)
-
-
-def reduce_begin(whole):
-    keep, send = cut(whole)
-    total = wide(keep) + wide(flip(send, "fsdp", 1))
-    a = total[:, :2]
-    b = total[:, 2:]
-    return (a[0], a[2], b[0], b[1]), (low(jnp.stack([a[1], a[3]])), low(jnp.stack([b[2], b[3]])))
+    )(*wholes)
+
+
+def reduce_begin(*wholes):
+    keep, send = cut(wholes)
+    other = flip(send, "fsdp", 1)
+    total = wide(keep) + wide(other)
+    a = low(total[:, :2])
+    b = low(total[:, 2:])
+    return (a[0], a[2], b[0], b[1]), (jnp.stack([a[1], a[3]]), jnp.stack([b[2], b[3]]))
 
 
 def reduce_sides(sends):
     return flip(sends[0], "ctx", 1), flip(sends[1], "ctx", 2)
 
 
-def reduce_end(sums, sides):
-    a0, a2, b0, b1 = sums
+def reduce_middle(sums, sides):
+    a0, a2, b0, b1 = (wide(part) for part in sums)
     x1, y1 = wide(sides[0]), wide(sides[1])
-    a0, a2 = a0 + x1[0], a2 + x1[1]
-    b0, b1 = b0 + y1[0], b1 + y1[1]
-    a0 = a0 + wide(flip(low(a2), "ctx", 2))
-    b0 = b0 + wide(flip(low(b1), "ctx", 1))
-    return (
-        a0[0]
-        + wide(flip(low(a0[1]), "fsdp", 2))
-        + wide(flip(low(b0[0]), "fsdp", 4))
-        + wide(flip(low(b0[1]), "fsdp", 6))
-    )
+    return (a0 + x1[0], b0 + y1[0]), (low(a2 + x1[1]), low(b1 + y1[1]))
+
+
+def reduce_across(sends):
+    return flip(sends[0], "ctx", 2), flip(sends[1], "ctx", 1)
+
+
+def reduce_turn(sums, across):
+    a0 = sums[0] + wide(across[0])
+    b0 = sums[1] + wide(across[1])
+    return a0[0], (low(a0[1]), low(b0[0]), low(b0[1]))
+
+
+def reduce_line(sends):
+    return [flip(part, "fsdp", 2 * k + 2) for k, part in enumerate(sends)]
+
+
+def reduce_end(line):
+    return line[0] + sum(wide(part) for part in line[1:])
 
 
 def spread_fast(piece):
@@ -204,20 +218,6 @@
     return wide(jnp.concatenate(parts, axis=2))
 
 
-def line_pieces(whole):
-    part = lax.psum_scatter(whole, "fsdp", scatter_dimension=0, tiled=True)[0]
-    j = lax.axis_index("ctx")
-    return [
-        lax.dynamic_slice_in_dim(part, (j ^ k) * PIECE, PIECE, axis=2) for k in range(4)
-    ]
-
-
-def line_sum(pieces):
-    return sum(
-        (wide(flip(pieces[k], "ctx", k)) for k in (1, 2, 3)), wide(pieces[0])
-    )
-
-
 def reduce_plain(whole, dim):
     part = lax.psum_scatter(whole, "fsdp", scatter_dimension=dim, tiled=True)
     return wide(lax.psum(part, "ctx"))
@@ -235,8 +235,13 @@
     return lax.dot_general(a, b, (((0,), (0,)), ((), ())), preferred_element_type=jnp.float32)
 
 
+def shape_of(x):
+    return x[0].shape[1:] if isinstance(x, tuple) else x.shape
+
+
 def run_kernel(body, inputs, outputs, scratch=(), cost=0, name=None):
     count = len(inputs)
+    arrays = [x[0] if isinstance(x, tuple) else x for x in inputs]
 
     def kernel(*refs):
         sources = refs[:count]
@@ -244,8 +249,10 @@
         rest = refs[count + len(outputs) :]
         buffers, extra, sems = rest[:count], rest[count:-1], rest[-1]
         copies = [
-            pltpu.make_async_copy(source, buffer, sems.at[i])
-            for i, (source, buffer) in enumerate(zip(sources, buffers))
+            pltpu.make_async_copy(
+                source.at[x[1]] if isinstance(x, tuple) else source, buffer, sems.at[i]
+            )
+            for i, (x, source, buffer) in enumerate(zip(inputs, sources, buffers))
         ]
         for copy in copies:
             copy.start()
@@ -267,14 +274,14 @@
         in_specs=[pl.BlockSpec(memory_space=pl.ANY)] * count,
         out_specs=[pl.BlockSpec(memory_space=pltpu.VMEM)] * len(outputs),
         scratch_shapes=[
-            *[pltpu.VMEM(x.shape, x.dtype) for x in inputs],
+            *[pltpu.VMEM(shape_of(x), array.dtype) for x, array in zip(inputs, arrays)],
             *scratch,
             pltpu.SemaphoreType.DMA((count,)),
         ],
         compiler_params=pltpu.CompilerParams(vmem_limit_bytes=VMEM_LIMIT),
         cost_estimate=pl.CostEstimate(flops=cost, bytes_accessed=4_000_000, transcendentals=0),
         name=name,
-    )(*inputs)
+    )(*arrays)
 
 
 def like(shape, kind):
@@ -285,9 +292,9 @@
     return (2 * source, 2 * slots - 1 - 2 * source)
 
 
-def stack_heads(ref, dst, half):
+def stack_heads(ref, dst, half, groups=range(KV_HEADS)):
     group = HEADS // KV_HEADS
-    for g in range(KV_HEADS):
+    for g in groups:
         for part in range(2):
             for i in range(group):
                 h = g * group + i
@@ -402,7 +409,7 @@
     )
 
 
-def attend_back_kernel(slots, *refs):
+def attend_back_kernel(slots, groups, *refs):
     q_ref, o_ref, do_ref, lse_ref, start_ref = refs[:5]
     kv_refs = refs[5 : 5 + slots]
     dq_ref = refs[5 + slots]
@@ -411,11 +418,11 @@
     rank = lax.axis_index("ctx")
     half = q_ref.shape[0] // 2
     group = HEADS // KV_HEADS
-    stack_heads(q_ref, qs, half)
-    stack_heads(do_ref, dos, half)
+    stack_heads(q_ref, qs, half, groups)
+    stack_heads(do_ref, dos, half, groups)
     for k in range(slots):
         keys_t = low(jnp.transpose(wide(kv_refs[k][:, : 2 * 128])))
-        for g in range(KV_HEADS):
+        for g in groups:
             for part in range(2):
                 rows = slice(part * half, (part + 1) * half)
                 ks[k, g, part] = kv_refs[k][rows, g * HD : (g + 1) * HD]
@@ -483,34 +490,38 @@
                 dqt_all[g, i, :, cols] = dqt_s[:, i * half : (i + 1) * half]
         return carry
 
-    lax.fori_loop(0, KV_HEADS, one_group, 0)
-    dq_ref[...] = jnp.transpose(dqt_all[...].reshape(HEADS * HD, 2 * half)) * 0.125
+    lax.fori_loop(groups.start, groups.stop, one_group, 0)
+    dqt = dqt_all[groups.start : groups.stop]
+    dq_ref[...] = jnp.transpose(dqt.reshape(len(groups) * group * HD, 2 * half)) * 0.125
     for k in range(slots):
         for part in range(2):
             dkv = jnp.concatenate(
-                [dk_s[k, g, part] * (1.0 / log_two_e) for g in range(KV_HEADS)]
-                + [dv_s[k, g, part] for g in range(KV_HEADS)],
+                [
+                    x
+                    for g in groups
+                    for x in (dk_s[k, g, part] * (1.0 / log_two_e), dv_s[k, g, part])
+                ],
                 axis=1,
             )
             dkv_refs[k][part * half : (part + 1) * half] = dkv.astype(dkv_refs[k].dtype)
 
 
-def attend_back(q, o, do, lse, start_row, kvs):
+def attend_back(q, o, do, lse, start_row, kvs, groups):
     block = q.shape[0]
     half = block // 2
     slots = len(kvs)
     group = HEADS // KV_HEADS
     inputs = (q, o, do, lse, start_row, *kvs)
-    pair = lambda kind: like((block, 2 * KV_HEADS * HD), kind)
+    pair = lambda kind: like((block, 2 * len(groups) * HD), kind)
 
     def body(get, outs, extra):
-        attend_back_kernel(slots, *[get(i) for i in range(len(inputs))], *outs, *extra)
+        attend_back_kernel(slots, groups, *[get(i) for i in range(len(inputs))], *outs, *extra)
 
     return run_kernel(
         body,
         inputs,
         (
-            like((block, HEADS * HD), jnp.float32),
+            like((block, len(groups) * group * HD), jnp.float32),
             pair(jnp.float32),
             *[pair(jnp.bfloat16)] * (slots - 1),
         ),
@@ -526,7 +537,7 @@
             pltpu.VMEM((16, block), jnp.float32),
             pltpu.VMEM((KV_HEADS, group, HD, block), jnp.float32),
         ),
-        cost=20_000_000_000,
+        cost=7_000_000_000 * len(groups),
         name="attend_back",
     )
 
@@ -619,7 +630,7 @@
 
 def mlp(hidden, attention, gains, which, attn_weights, gate_w, up_w, down_w):
     tokens, width = hidden.shape
-    ff = gate_w.shape[1]
+    ff = shape_of(gate_w)[1]
     chunk = 512
 
     def body(get, outs, extra):
@@ -674,14 +685,18 @@
         ref[index] = low(value)
         return
     rows = value.shape[0] // shards
-    for f in range(shards):
-        ref[f, index] = low(value[f * rows : (f + 1) * rows])
+    ranks = value.shape[1] // PIECE
+    for j in range(ranks):
+        for f in range(shards):
+            ref[f * ranks + j, index] = low(
+                value[f * rows : (f + 1) * rows, j * PIECE : (j + 1) * PIECE]
+            )
 
 
 def mlp_back(grad, kept, gains, which, attn_weights, gate_w, up_w, down_w, shards):
     middle, mixed, gate, up, inner, attention = kept
     tokens, width = grad.shape
-    ff = gate_w.shape[1]
+    ff = shape_of(gate_w)[1]
     chunk = 512
 
     def body(get, outs, extra):
@@ -715,9 +730,10 @@
         if shards is not None:
             rows = width // shards
             step = rows * 2 // 3
+            ranks = ff // PIECE
             for f in range(shards):
-                for j in range(ff // PIECE):
-                    at = (f * (ff // PIECE) + j) * step
+                for j in range(ranks):
+                    at = (f * ranks + j) * step
                     rest = total[at : at + step, PIECE:]
                     value = jnp.concatenate(
                         [
@@ -726,7 +742,7 @@
                         ],
                         axis=0,
                     )
-                    weights_ref[f, 2, :, j * PIECE : (j + 1) * PIECE] = low(value)
+                    weights_ref[f * ranks + j, 2] = low(value)
         dx, gain_grad = norm_back(get(1)[...], get(7)[which : which + 1], d_mixed)
         gain_ref[...] = jnp.broadcast_to(gain_grad, gain_ref.shape)
         mid = grad + dx
@@ -738,7 +754,7 @@
     if shards is None:
         weight_outs = (like((2, width, ff), jnp.bfloat16), like((ff, width), jnp.bfloat16))
     else:
-        weight_outs = (like((shards, 3, width // shards, ff), jnp.bfloat16),)
+        weight_outs = (like((ff // PIECE * shards, 3, width // shards, PIECE), jnp.bfloat16),)
     return run_kernel(
         body,
         (
@@ -762,48 +778,63 @@
     )
 
 
-def project_back(d_query, pairs, cosine, sine, kept, gains, which, weights, out_grad, mid, shards, riders):
+def project_back(d_queries, pairs, cosine, sine, kept, gains, which, weights, out_grad, mid, shards, riders):
     hidden, normed = kept
     tokens, width = hidden.shape
-    count = len(pairs)
-    columns = weights.shape[1]
+    parts = len(d_queries)
+    slots = len(pairs[0])
+    fixed = 8 + parts
+    pair_at = lambda part, k: fixed + part * slots + k
+    columns = shape_of(weights)[1]
     extra_rows = 0 if riders is None else 8
 
     def body(get, outs, extra):
         grad_ref, gain_ref, weights_ref = outs
-        cos, sin = get(1)[...], get(2)[...]
-        dq = turned(get(0)[...], cos, sin, -1.0)
-        pair = get(9)[...]
-        for k in range(1, count):
-            pair = pair + wide(get(9 + k)[...])
-        dk = turned(pair[:, :KVW], cos, sin, -1.0)
-        d_all = low(jnp.concatenate([dq, dk, pair[:, KVW:]], axis=1))
-        normed_grad = dot_nt(d_all, get(6)[:, :QKV])
-        dx, gain_grad = norm_back(get(3)[...], get(5)[which : which + 1], normed_grad)
+        cos, sin = get(0)[...], get(1)[...]
+        d_query = jnp.concatenate([get(8 + part)[...] for part in range(parts)], axis=1)
+        dq = turned(d_query, cos, sin, -1.0)
+        keys, values = [], []
+        for part in range(parts):
+            pair = get(pair_at(part, 0))[...]
+            for k in range(1, slots):
+                pair = pair + wide(get(pair_at(part, k))[...])
+            for at in range(0, pair.shape[1], 2 * HD):
+                keys.append(pair[:, at : at + HD])
+                values.append(pair[:, at + HD : at + 2 * HD])
+        dk = turned(jnp.concatenate(keys, axis=1), cos, sin, -1.0)
+        d_all = low(jnp.concatenate([dq, dk, *values], axis=1))
+        normed_grad = dot_nt(d_all, get(5)[:, :QKV])
+        dx, gain_grad = norm_back(get(2)[...], get(4)[which : which + 1], normed_grad)
         gain_ref[...] = jnp.broadcast_to(gain_grad, gain_ref.shape)
-        grad_ref[...] = get(8)[...] + dx
-        d_weights = dot_tn(get(4)[...], d_all)
-        value = jnp.concatenate([d_weights, wide(get(7)[...])], axis=1)
+        grad_ref[...] = get(7)[...] + dx
+        d_weights = dot_tn(get(3)[...], d_all)
+        value = jnp.concatenate([d_weights, wide(get(6)[...])], axis=1)
         if riders is None:
             put_rows(weights_ref, 0, value, shards)
         else:
             rows = width // shards
-            lines = [get(9 + count)[...], gain_grad]
+            lines = [get(fixed + parts * slots)[...], gain_grad]
             lines.append(jnp.zeros((8 - 1 - lines[0].shape[0], width), jnp.float32))
             ride = jnp.concatenate(lines, axis=0)
             ride = jnp.concatenate(
                 [ride, jnp.zeros((8, columns - width), jnp.float32)], axis=1
             )
-            for f in range(shards):
-                weights_ref[f, 0] = low(
-                    jnp.concatenate([value[f * rows : (f + 1) * rows], ride], axis=0)
-                )
+            ranks = columns // PIECE
+            for j in range(ranks):
+                cols = slice(j * PIECE, (j + 1) * PIECE)
+                for f in range(shards):
+                    weights_ref[f * ranks + j, 0] = low(
+                        jnp.concatenate(
+                            [value[f * rows : (f + 1) * rows, cols], ride[:, cols]], axis=0
+                        )
+                    )
 
     if shards is None:
         shape = (1, width, columns)
     else:
-        shape = (shards, 1, width // shards + extra_rows, columns)
-    inputs = (d_query, cosine, sine, hidden, normed, gains, weights, out_grad, mid, *pairs)
+        shape = (columns // PIECE * shards, 1, width // shards + extra_rows, PIECE)
+    inputs = (cosine, sine, hidden, normed, gains, weights, out_grad, mid, *d_queries)
+    inputs = (*inputs, *[x for pair in pairs for x in pair])
     if riders is not None:
         inputs = (*inputs, riders)
     return run_kernel(
@@ -864,9 +895,8 @@
         own_second = jnp.stack([*mlp_own[0], attn_own[1]])
         own_third = jnp.stack(mlp_own[1])
         first_line = gather_line(own_first)
-        second_line = gather_line(tied(own_second, first_line))
+        second_line = gather_line(own_second)
         third = gather_plain(tied(own_third, second_line))
-        third = third.reshape(3, shards, rows, -1)
         first_sides = gather_sides(first_line)
         first_flip = flip(own_first, "fsdp", 1)
         (first, gains), first_mine = gather_rest(
@@ -874,11 +904,10 @@
         )
         gains = wide(gains[:, :gain_count, :rows]).transpose(1, 0, 2).reshape(gain_count, -1)
         second_flip = flip(tied(own_second, first_mine), "fsdp", 1)
-        second_line = tied(second_line, first_mine)
-        second_sides = gather_sides(second_line)
-        merge = lambda x: x.reshape(-1, x.shape[-1])
-        attn_full = [merge(first[0]), None]
-        mlp_full = [None, (merge(third[0]), merge(third[1]), third[2])]
+        merge = lambda x: x.reshape(x.shape[0], -1, x.shape[-1])
+        attn_full = [(merge(first), 0), None]
+        by_row = third.reshape(3, shards, rows, -1)
+        mlp_full = [None, ((third, 0), (third, 1), (by_row, 2))]
     else:
         gains = wide(lax.all_gather(own_gains, "fsdp", axis=1, tiled=True))
         gather = lambda x: lax.all_gather(x, "fsdp", axis=0, tiled=True)
@@ -900,15 +929,20 @@
     saved = []
     for i in range(LAYERS):
         normed, q, pair = project_in(hidden, gains, i, attn_full[i], cosine, sine)
+        if fast and i == 0:
+            second_line, pair = lax.optimization_barrier((second_line, pair))
         kvs = [pair] + [flip(pair, "ctx", k) for k in range(1, slots)]
+        if fast and i == 0:
+            second_sides = gather_sides(second_line)
         attention, lse = attend(q, doc_start, kvs)
         if fast and i == 0:
             second_sides, cotangent = tied((second_sides, cotangent), attention)
             (second,), _ = gather_rest(
                 rows, own_second, second_flip, second_line, second_sides
             )
-            mlp_full[0] = (merge(second[0]), merge(second[1]), second[2])
-            attn_full[1] = merge(second[3])
+            merged = merge(second)
+            mlp_full[0] = ((merged, 0), (merged, 1), (second, 2))
+            attn_full[1] = (merged, 3)
         middle, mixed, gate, up, inner, out = mlp(
             hidden, attention, gains, LAYERS + i, attn_full[i], *mlp_full[i]
         )
@@ -933,26 +967,42 @@
             by_shard,
         )
         if fast and i == 0:
-            sums, sends = reduce_begin(weight_grads[0])
-            d_attention, sends, pieces = lax.optimization_barrier(
-                (d_attention, sends, mlp_grads[1])
+            sums, sends = reduce_begin(weight_grads[0], attn_grads[1])
+            d_attention, sends, early = lax.optimization_barrier((d_attention, sends, early))
+            sides = reduce_sides(sends)
+        elif fast:
+            early = lax.psum_scatter(
+                weight_grads[0], "fsdp", scatter_dimension=0, tiled=True
             )
-            sides = reduce_sides(sends)
-            moved = [pieces[0]] + [flip(pieces[k], "ctx", k) for k in (1, 2, 3)]
-        elif fast:
-            mlp_grads[i] = line_pieces(weight_grads[0])
         else:
             mlp_grads[i] = (
                 reduce_plain(weight_grads[0], 1),
                 reduce_plain(weight_grads[1], 0),
             )
-        d_query, *pairs = attend_back(q, attention, d_attention, lse, doc_start, kvs)
-        pairs = [pairs[0]] + [flip(pairs[k], "ctx", k) for k in range(1, slots)]
+        d_queries, pairs = [], []
+        for groups in (range(KV_HEADS - 1), range(KV_HEADS - 1, KV_HEADS)):
+            d_query, *pair = attend_back(
+                q, attention, d_attention, lse, doc_start, kvs, groups
+            )
+            d_queries.append(d_query)
+            if pairs:
+                pair, pairs = lax.optimization_barrier((pair, pairs))
+            d_attention, pair = lax.optimization_barrier((d_attention, pair))
+            pairs.append([pair[0]] + [flip(pair[k], "ctx", k) for k in range(1, slots)])
+            if fast and i == 0 and groups.start == 0:
+                sides = tied(sides, d_query)
+                sums, sends = reduce_middle(sums, sides)
+                d_attention, sends = lax.optimization_barrier((d_attention, sends))
+                across = reduce_across(sends)
+            elif fast and i == 0:
+                sums, sends = reduce_turn(sums, tied(across, d_query))
+                d_queries, sends = lax.optimization_barrier((d_queries, sends))
+                line = (sums, *reduce_line(sends))
         riders = None
         if fast and i == 0:
             riders = jnp.concatenate([gain_grads[v][:1] for v in (1, 2, 3)])
         grad, gain_grads[i], attn_grad = project_back(
-            d_query,
+            d_queries,
             pairs,
             cosine,
             sine,
@@ -966,23 +1016,29 @@
             riders,
         )
         if fast and i == 0:
-            sides, moved, pieces = tied((sides, moved, attn_grads[1]), pairs)
-            mlp_sum = sum((wide(part) for part in moved[1:]), wide(moved[0]))
-            early = jnp.concatenate([mlp_sum, line_sum(pieces)])
-            early = spread_fast(early)
-            rest = spread_fast(reduce_end(sums, sides))
+            moved = [
+                lax.dynamic_index_in_dim(early, rank ^ k, axis=0, keepdims=False)
+                for k in range(4)
+            ]
+            moved = [moved[0]] + [flip(moved[k], "ctx", k) for k in (1, 2, 3)]
             sums, sends = reduce_begin(attn_grad)
-            last = reduce_end(sums, reduce_sides(sends))
-            last = spread_fast(last)
+            line, sends, grad, moved = lax.optimization_barrier((line, sends, grad, moved))
+            early = low(sum((wide(part) for part in moved[1:]), wide(moved[0])))
+            sides = reduce_sides(sends)
+            rest = spread_fast(jnp.concatenate([low(reduce_end(line)), early]))
+            sums, sends = reduce_middle(sums, sides)
+            sums, sends = reduce_turn(sums, reduce_across(sends))
+            last = spread_fast(reduce_end((sums, *reduce_line(sends))))
+            early = rest[4:]
             all_gains = lax.dynamic_slice_in_dim(last[0, rows:], shard * rows, rows, axis=1)
             order = (3, 0, 1, 2)
             all_gains = jnp.stack([all_gains[v] for v in order])
-            attn_rows = jnp.stack([last[0, :rows], early[3]])
+            attn_rows = jnp.stack([last[0, :rows], rest[3]])
             gate_rows = jnp.stack([rest[0], early[0]])
             up_rows = jnp.stack([rest[1], early[1]])
             down_rows = unfold_down(jnp.stack([rest[2], early[2]]))
         elif fast:
-            attn_grads[i] = line_pieces(attn_grad)
+            attn_grads[i] = attn_grad
         else:
             attn_grads[i] = reduce_plain(attn_grad[0], 0)
     if not fast:

time: 507 us -> 494 us (0.974)
  waiting for transfers between devices: 135 us -> 122 us
  Pallas kernels: 181 us -> 193 us
  local copies, waits for them, and re-layouts: 58.6 us -> 52.2 us
  other arithmetic: 34.1 us -> 28.5 us
    ppermute x66, waiting for transfers between devices: 135 us -> 122 us  [flip(): return lax.ppermute(block, axis, route)]
    slice x3 -> x1, local copies, waits for them, and re-layouts: 10.8 us -> 0.03 us  [body(): attn_rows = jnp.stack([last[0, :rows], rest[3]])]
    pallas_call x2, Pallas kernels: 5.47 us -> 12.4 us  [cut(): pl.pallas_call(lambda *refs: scatter_kernel(len(wholes), *refs), out_shap...]
    unnamed x146 -> x170, local copies, waits for them, and re-layouts: 34.9 us -> 39.9 us
    pallas_call x12 -> x14, Pallas kernels: 168 us -> 173 us  [run_kernel(): pl.pallas_call(kernel, out_shape=tuple(outputs), in_specs=[pl.BlockSpec(m...]
  transfers between devices with their start and end apart: 69 -> 68, of which waited for: 37 -> 27; matrix products, arithmetic and copies ran while one was open for 11% -> 8% of each run, Pallas kernels for 30% -> 31%
where the time goes in v3:
time: 494 us; the launch traced here: 488 us
  Pallas kernels  193 us (39%)
  waiting for transfers between devices  122 us (25%)
  starting transfers between devices  77.4 us (16%)
  local copies, waits for them, and re-layouts  52.2 us (11%)
  other arithmetic  28.5 us (6%)
  between operations  15.7 us (3%)
    pallas_call x14, Pallas kernels, run_kernel(): pl.pallas_call(kernel, out_shape=tuple(outputs), in_specs=[pl.BlockSpec(m...  173 us
    ppermute x66, waiting for transfers between devices, flip(): return lax.ppermute(block, axis, route)  122 us
    ppermute x66, starting transfers between devices, flip(): return lax.ppermute(block, axis, route)  77.4 us
    unnamed x170, local copies, waits for them, and re-layouts  39.9 us
    pallas_call x2, Pallas kernels, cut(): pl.pallas_call(lambda *refs: scatter_kernel(len(wholes), *refs), out_shap...  12.4 us
  transfers between devices with their start and end apart: 68, of which 27 were waited for; matrix products, arithmetic and copies ran while one was open for 8% of the time, Pallas kernels for 31%

profile of v3, /device:TPU:0, one launch (start us, length us, event | category | flops | bytes accessed | tf_op | source)
XLA Modules:
  0.0 488.4 jit_solution(12104873167501768055)
XLA Ops:
  11.3 3.0 collective-permute-start.2
  14.4 2.6 collective-permute-start.3
  19.1 3.8 collective-permute-start.13
  29.3 2.3 collective-permute-done.5
  33.4 4.7 collective-permute-done.6
  41.2 5.6 %collective-permute-done.8 = bf16[1,1,80,384]{3,2,1,0:T(8,128)(2,1)S(1)} collective-permute-done((bf16[1,1,80,384]{3,2,1,0:T(8,128)(2,1)S(1)}, bf16[1,1,80,384]{3,2,1,0:T(8,128)(2,1)S(1)}, u32[]{:S(2)}, u32[]{:S(2)}) %collective-permute-start.8) | collective-permute-done | bytes 61472 | tf_op jit(solution)/shard_map/ppermute | solution.py:22
  47.7 2.0 pad_maximum_fusion.4
  54.8 2.0 assemble.2
  60.9 3.8 project_in.2
  66.0 2.3 collective-permute-start.16
  69.5 7.4 %collective-permute-done.14.refs_3_.refs_6_ = bf16[512,384]{1,0:T(8,128)(2,1)S(1)} collective-permute-done((bf16[512,384]{1,0:T(8,128)(2,1)S(1)}, bf16[512,384]{1,0:T(8,128)(2,1)S(1)}, u32[]{:S(2)}, u32[]{:S(2)}) %collective-permute-start.14) | collective-permute-done | bytes 393248 | tf_op jit(solution)/shard_map/ppermute | solution.py:22
  76.9 8.5 %collective-permute-done.15.refs_4_.refs_7_ = bf16[512,384]{1,0:T(8,128)(2,1)S(1)} collective-permute-done((bf16[512,384]{1,0:T(8,128)(2,1)S(1)}, bf16[512,384]{1,0:T(8,128)(2,1)S(1)}, u32[]{:S(2)}, u32[]{:S(2)}) %collective-permute-start.15) | collective-permute-done | bytes 393248 | tf_op jit(solution)/shard_map/ppermute | solution.py:22
  85.4 18.6 %attend.2 = (bf16[512,576]{1,0:T(8,128)(2,1)S(1)}, f32[16,512]{1,0:T(8,128)S(1)}) custom-call(bf16[512,576]{1,0:T(8,128)(2,1)S(1)} %get-tuple-element.144.refs_0_, s32[1,512]{1,0:T(1,128)S(1)} %get-tuple-element.388.refs_1_.refs_4_, bf16[512,384]{1,0:T(8,128)(2,1)S(1)} %get-tuple-element.146.refs_2_.refs_5_, ...), custom_call_target="tpu_custom_call" | custom-call | flops 15000000512 | bytes 4000000 | tf_op jit(solution)/shard_map/attend/pallas_call | solution.py:271
  107.7 6.0 %collective-permute-done.20 = bf16[2,4,72,384]{3,2,1,0:T(8,128)(2,1)S(1)} collective-permute-done((bf16[2,4,72,384]{3,2,1,0:T(8,128)(2,1)S(1)}, bf16[2,4,72,384]{3,2,1,0:T(8,128)(2,1)S(1)}, u32[]{:S(2)}, u32[]{:S(2)}) %collective-permute-start.20) | collective-permute-done | bytes 442400 | tf_op jit(solution)/shard_map/ppermute | solution.py:22
  114.4 2.1 copy.43
  117.7 2.5 collective-permute-start.27
  120.2 5.4 %assemble.3.refs_6_.refs_11_ = bf16[4,8,72,1536]{3,2,1,0:T(8,128)(2,1)} custom-call(bf16[4,72,1536]{2,1,0:T(8,128)(2,1)S(1)} %pad_maximum_fusion.refs_0_, bf16[4,72,1536]{2,1,0:T(8,128)(2,1)} %collective-permute-done.17.refs_1_, bf16[12,4,72,384]{3,2,1,0:T(8,128)(2,1)S(1)} %constant_dynamic-update-slice_fusion.7.refs_2_, ...), custom_call_target="tpu_custom_call" | custom-call | tf_op jit(solution)/shard_map/assemble/pallas_call | solution.py:103
  125.7 9.5 %mlp.2 = (f32[512,576]{1,0:T(8,128)S(1)}, bf16[512,576]{1,0:T(8,128)(2,1)S(1)}, bf16[512,1536]{1,0:T(8,128)(2,1)}, bf16[512,1536]{1,0:T(8,128)(2,1)}, bf16[512,1536]{1,0:T(8,128)(2,1)}, /*index=5*/f32[512,576]{1,0:T(8,128)S(1)}) custom-call(f32[512,576]{1,0:T(8,128)S(1)} %copy-done.3, bf16[512,576]{1,0:T(8,128)(2,1)S(1)} %copy-done.34, ...), custom_call_target="tpu_custom_call" | custom-call | flops 8000000000 | bytes 4000000 | tf_op jit(solution)/shard_map/mlp/pallas_call | solution.py:271
  137.1 4.9 %project_in.3 = (bf16[512,576]{1,0:T(8,128)(2,1)S(1)}, bf16[512,576]{1,0:T(8,128)(2,1)S(1)}, bf16[512,384]{1,0:T(8,128)(2,1)S(1)}) custom-call(f32[512,576]{1,0:T(8,128)S(1)} %get-tuple-element.152.refs_0_.refs_2_, f32[8,576]{1,0:T(8,128)S(1)} %copy-done.9, bf16[4,576,1536]{2,1,0:T(8,128)(2,1)} %bitcast.155, f32[512,128]{1,0:T(8,128)S(1)} %copy-done.5, ...), custom_call_target="tpu_custom_call" | custom-call | flops 4000000000 | bytes 4000000 | tf_op jit(solution)/shard_map/project_in/pallas_call | solution.py:271
  142.8 2.7 collective-permute-start.23
  147.2 8.3 %collective-permute-done.23.refs_3_.refs_6_ = bf16[512,384]{1,0:T(8,128)(2,1)S(1)} collective-permute-done((bf16[512,384]{1,0:T(8,128)(2,1)S(1)}, bf16[512,384]{1,0:T(8,128)(2,1)S(1)}, u32[]{:S(2)}, u32[]{:S(2)}) %collective-permute-start.23) | collective-permute-done | bytes 393248 | tf_op jit(solution)/shard_map/ppermute | solution.py:22
  155.5 9.4 %collective-permute-done.24.refs_4_.refs_7_ = bf16[512,384]{1,0:T(8,128)(2,1)S(1)} collective-permute-done((bf16[512,384]{1,0:T(8,128)(2,1)S(1)}, bf16[512,384]{1,0:T(8,128)(2,1)S(1)}, u32[]{:S(2)}, u32[]{:S(2)}) %collective-permute-start.24) | collective-permute-done | bytes 393248 | tf_op jit(solution)/shard_map/ppermute | solution.py:22
  164.9 19.0 %attend.3 = (bf16[512,576]{1,0:T(8,128)(2,1)S(1)}, f32[16,512]{1,0:T(8,128)S(1)}) custom-call(bf16[512,576]{1,0:T(8,128)(2,1)S(1)} %get-tuple-element.153.refs_0_, s32[1,512]{1,0:T(1,128)S(1)} %get-tuple-element.388.refs_1_.refs_4_, bf16[512,384]{1,0:T(8,128)(2,1)S(1)} %get-tuple-element.154.refs_2_.refs_5_, ...), custom_call_target="tpu_custom_call" | custom-call | flops 15000000512 | bytes 4000000 | tf_op jit(solution)/shard_map/attend/pallas_call | solution.py:271
  189.5 9.3 %mlp.3 = (f32[512,576]{1,0:T(8,128)S(1)}, bf16[512,576]{1,0:T(8,128)(2,1)S(1)}, bf16[512,1536]{1,0:T(8,128)(2,1)}, bf16[512,1536]{1,0:T(8,128)(2,1)}, bf16[512,1536]{1,0:T(8,128)(2,1)}, /*index=5*/f32[512,576]{1,0:T(8,128)S(1)}) custom-call(f32[512,576]{1,0:T(8,128)S(1)} %copy-done.31, bf16[512,576]{1,0:T(8,128)(2,1)S(1)} %copy-done.41, ...), custom_call_target="tpu_custom_call" | custom-call | flops 8000000000 | bytes 4000000 | tf_op jit(solution)/shard_map/mlp/pallas_call | solution.py:271
  199.9 18.8 %mlp_back.2 = (bf16[512,576]{1,0:T(8,128)(2,1)S(1)}, f32[512,576]{1,0:T(8,128)S(1)}, f32[8,576]{1,0:T(8,128)S(1)}, bf16[576,576]{1,0:T(8,128)(2,1)S(1)}, bf16[32,3,72,384]{3,2,1,0:T(8,128)(2,1)}) custom-call(f32[512,576]{1,0:T(8,128)S(1)} %fusion.11.refs_0_, f32[512,576]{1,0:T(8,128)} %copy-done.32, bf16[512,576]{1,0:T(8,128)(2,1)S(1)} %get-tuple-element.161.refs_2_, ...), custom_call_target="tpu_custom_call" | custom-call | flops 15000000512 | bytes 4000000 | tf_op jit(solution)/shard_map/mlp_back/pallas_call | solution.py:271
  227.0 16.9 %attend_back.4 = (f32[512,384]{1,0:T(8,128)S(1)}, f32[512,256]{1,0:T(8,128)S(1)}, bf16[512,256]{1,0:T(8,128)(2,1)S(1)}, bf16[512,256]{1,0:T(8,128)(2,1)S(1)}, bf16[512,256]{1,0:T(8,128)(2,1)S(1)}) custom-call(bf16[512,576]{1,0:T(8,128)(2,1)S(1)} %copy-done.49, bf16[512,576]{1,0:T(8,128)(2,1)S(1)} %copy-done.43, bf16[512,576]{1,0:T(8,128)(2,1)S(1)} %copy-done.62, ...), custom_call_target="tpu_custom_call" | custom-call | flops 14000000000 | bytes 4000000 | tf_op jit(solution)/shard_map/attend_back/pallas_call | solution.py:271
  247.5 9.2 %attend_back.5 = (f32[512,192]{1,0:T(8,128)S(1)}, f32[512,128]{1,0:T(8,128)S(1)}, bf16[512,128]{1,0:T(8,128)(2,1)S(1)}, bf16[512,128]{1,0:T(8,128)(2,1)S(1)}, bf16[512,128]{1,0:T(8,128)(2,1)S(1)}) custom-call(bf16[512,576]{1,0:T(8,128)(2,1)S(1)} %copy-done.49, bf16[512,576]{1,0:T(8,128)(2,1)S(1)} %copy-done.43, bf16[512,576]{1,0:T(8,128)(2,1)S(1)} %copy-done.63, ...), custom_call_target="tpu_custom_call" | custom-call | flops 7000000000 | bytes 4000000 | tf_op jit(solution)/shard_map/attend_back/pallas_call | solution.py:271
  260.4 2.7 collective-permute-done.31.refs_15_
  265.1 8.5 %project_back.2 = (f32[512,576]{1,0:T(8,128)}, f32[8,576]{1,0:T(8,128)S(1)}, bf16[32,1,72,384]{3,2,1,0:T(8,128)(2,1)}) custom-call(f32[512,128]{1,0:T(8,128)S(1)} %copy-done.5, f32[512,128]{1,0:T(8,128)S(1)} %copy-done.7, f32[512,576]{1,0:T(8,128)} %copy-done.30, bf16[512,576]{1,0:T(8,128)(2,1)S(1)} %copy-done.47, f32[8,576]{1,0:T(8,128)S(1)} %copy-done.10, ...), custom_call_target="tpu_custom_call" | custom-call | flops 6000000000 | bytes 4000000 | tf_op jit(solution)/shard_map/project_back/pallas_call | solution.py:271
  274.9 19.2 %mlp_back.3 = (bf16[512,576]{1,0:T(8,128)(2,1)S(1)}, f32[512,576]{1,0:T(8,128)S(1)}, f32[8,576]{1,0:T(8,128)S(1)}, bf16[576,576]{1,0:T(8,128)(2,1)S(1)}, bf16[32,3,72,384]{3,2,1,0:T(8,128)(2,1)}) custom-call(f32[512,576]{1,0:T(8,128)S(1)} %copy-done.45, f32[512,576]{1,0:T(8,128)} %copy-done.29, bf16[512,576]{1,0:T(8,128)(2,1)S(1)} %copy-done.39, ...), custom_call_target="tpu_custom_call" | custom-call | flops 15000000512 | bytes 4000000 | tf_op jit(solution)/shard_map/mlp_back/pallas_call | solution.py:271
  296.9 9.4 %cut.2 = (bf16[4,4,4,72,384]{4,3,2,1,0:T(8,128)(2,1)S(1)}, bf16[4,4,4,72,384]{4,3,2,1,0:T(8,128)(2,1)}) custom-call(bf16[32,3,72,384]{3,2,1,0:T(8,128)(2,1)} %get-tuple-element.202.refs_0_, bf16[32,1,72,384]{3,2,1,0:T(8,128)(2,1)S(1)} %copy-done.1), custom_call_target="tpu_custom_call" | custom-call | tf_op jit(solution)/shard_map/cut/pallas_call | solution.py:163
  307.3 5.5 %collective-permute-done.34 = bf16[4,4,4,72,384]{4,3,2,1,0:T(8,128)(2,1)S(1)} collective-permute-done((bf16[4,4,4,72,384]{4,3,2,1,0:T(8,128)(2,1)}, bf16[4,4,4,72,384]{4,3,2,1,0:T(8,128)(2,1)S(1)}, u32[]{:S(2)}, u32[]{:S(2)}) %collective-permute-start.34) | collective-permute-done | bytes 3538976 | tf_op jit(solution)/shard_map/ppermute | solution.py:22
  321.9 16.7 %attend_back.6 = (f32[512,384]{1,0:T(8,128)S(1)}, f32[512,256]{1,0:T(8,128)S(1)}, bf16[512,256]{1,0:T(8,128)(2,1)S(1)}, bf16[512,256]{1,0:T(8,128)(2,1)S(1)}, bf16[512,256]{1,0:T(8,128)(2,1)S(1)}) custom-call(bf16[512,576]{1,0:T(8,128)(2,1)S(1)} %copy-done.56, bf16[512,576]{1,0:T(8,128)(2,1)S(1)} %copy-done.36, bf16[512,576]{1,0:T(8,128)(2,1)S(1)} %copy-done.60, ...), custom_call_target="tpu_custom_call" | custom-call | flops 14000000000 | bytes 4000000 | tf_op jit(solution)/shard_map/attend_back/pallas_call | solution.py:271
  347.2 9.6 %attend_back.7 = (f32[512,192]{1,0:T(8,128)S(1)}, f32[512,128]{1,0:T(8,128)S(1)}, bf16[512,128]{1,0:T(8,128)(2,1)S(1)}, bf16[512,128]{1,0:T(8,128)(2,1)S(1)}, bf16[512,128]{1,0:T(8,128)(2,1)S(1)}) custom-call(bf16[512,576]{1,0:T(8,128)(2,1)S(1)} %copy-done.56, bf16[512,576]{1,0:T(8,128)(2,1)S(1)} %copy-done.37, bf16[512,576]{1,0:T(8,128)(2,1)S(1)} %copy-done.60, ...), custom_call_target="tpu_custom_call" | custom-call | flops 7000000000 | bytes 4000000 | tf_op jit(solution)/shard_map/attend_back/pallas_call | solution.py:271
  360.4 4.1 collective-permute-done.37
  366.3 2.2 collective-permute-done.46.refs_16_
  368.5 8.8 %project_back.3 = (f32[512,576]{1,0:T(8,128)}, f32[8,576]{1,0:T(8,128)}, bf16[32,1,80,384]{3,2,1,0:T(8,128)(2,1)}) custom-call(f32[512,128]{1,0:T(8,128)S(1)} %copy-done.5, f32[512,128]{1,0:T(8,128)S(1)} %copy-done.7, f32[512,576]{1,0:T(8,128)} %copy-done.2, bf16[512,576]{1,0:T(8,128)(2,1)S(1)} %copy-done.54, f32[8,576]{1,0:T(8,128)S(1)} %copy-done.10, ...), custom_call_target="tpu_custom_call" | custom-call | flops 6000000000 | bytes 4000000 | tf_op jit(solution)/shard_map/project_back/pallas_call | solution.py:271
  378.9 3.1 cut.3
  384.2 9.9 %collective-permute-done.26 = bf16[1,256,576]{2,1,0:T(8,128)(2,1)} collective-permute-done((bf16[1,256,576]{2,1,0:T(8,128)(2,1)}, bf16[1,256,576]{2,1,0:T(8,128)(2,1)}, u32[]{:S(2)}, u32[]{:S(2)}) %collective-permute-start.26) | collective-permute-done | bytes 294944 | tf_op jit(solution)/shard_map/ppermute | solution.py:22
  396.0 2.1 copy.54
  402.9 2.8 collective-permute-start.39
  410.3 3.1 collective-permute-done.39
  413.4 10.8 %collective-permute-done.40 = bf16[4,72,384]{2,1,0:T(8,128)(2,1)S(1)} collective-permute-done((bf16[4,72,384]{2,1,0:T(8,128)(2,1)}, bf16[4,72,384]{2,1,0:T(8,128)(2,1)S(1)}, u32[]{:S(2)}, u32[]{:S(2)}) %collective-permute-start.40) | collective-permute-done | bytes 221216 | tf_op jit(solution)/shard_map/ppermute | solution.py:22
  431.0 2.0 collective-permute-done.53
  435.3 5.8 %collective-permute-done.56 = bf16[2,2,1,80,384]{4,3,1,2,0:T(8,128)(2,1)S(1)} collective-permute-done((bf16[2,2,1,80,384]{4,3,1,2,0:T(8,128)(2,1)S(1)}, bf16[2,2,1,80,384]{4,3,1,2,0:T(8,128)(2,1)S(1)}, u32[]{:S(2)}, u32[]{:S(2)}) %collective-permute-start.56) | collective-permute-done | bytes 245792 | tf_op jit(solution)/shard_map/ppermute | solution.py:22
  441.8 13.1 %collective-permute-done.52 = bf16[256,576]{1,0:T(8,128)(2,1)S(1)} collective-permute-done((bf16[256,576]{1,0:T(8,128)(2,1)S(1)}, bf16[256,576]{1,0:T(8,128)(2,1)S(1)}, u32[]{:S(2)}, u32[]{:S(2)}) %collective-permute-start.52) | collective-permute-done | bytes 294944 | tf_op jit(solution)/shard_map/ppermute | solution.py:22
  457.0 3.1 collective-permute-done.57
  461.9 3.8 collective-permute-start.58
  (386 shorter events, 135.9 us)
Async XLA Ops:
  7.2 179.9 %all-gather.2.cloned.1.call-start = ((), (), s32[]{:S(2)}) async-start(), calls=%async_computation.1 | async-start | bytes 5971968 | tf_op jit(solution)/shard_map/all_gather | solution.py:133
  11.3 13.9 %collective-permute-start.2 = (bf16[1,80,384]{2,1,0:T(8,128)(2,1)}, bf16[1,80,384]{2,1,0:T(8,128)(2,1)S(1)}, u32[]{:S(2)}, u32[]{:S(2)}) collective-permute-start(bf16[1,80,384]{2,1,0:T(8,128)(2,1)} %fusion.38), channel_id=1, source_target_pairs={{0,2},{1,3},{2,0},{3,1},{4,6},{5,7},{6,4},{7,5},{8,10},{9,11},{10,... | collective-permute-start | bytes 184328 | tf_op jit(solution)/shard_map/ppermute | solution.py:22
  14.4 11.5 %collective-permute-start.3 = (bf16[1,80,384]{2,1,0:T(8,128)(2,1)}, bf16[1,80,384]{2,1,0:T(8,128)(2,1)S(1)}, u32[]{:S(2)}, u32[]{:S(2)}) collective-permute-start(bf16[1,80,384]{2,1,0:T(8,128)(2,1)} %fusion.38), channel_id=1, source_target_pairs={{0,4},{1,5},{2,6},{3,7},{4,0},{5,1},{6,2},{7,3},{8,12},{9,13},{10,... | collective-permute-start | bytes 184328 | tf_op jit(solution)/shard_map/ppermute | solution.py:22
  17.0 8.9 %collective-permute-start.4 = (bf16[1,80,384]{2,1,0:T(8,128)(2,1)}, bf16[1,80,384]{2,1,0:T(8,128)(2,1)S(1)}, u32[]{:S(2)}, u32[]{:S(2)}) collective-permute-start(bf16[1,80,384]{2,1,0:T(8,128)(2,1)} %fusion.38), channel_id=1, source_target_pairs={{0,6},{1,7},{2,4},{3,5},{4,2},{5,3},{6,0},{7,1},{8,14},{9,15},{10,... | collective-permute-start | bytes 184328 | tf_op jit(solution)/shard_map/ppermute | solution.py:22
  19.1 27.7 %collective-permute-start.13 = (bf16[4,72,384]{2,1,0:T(8,128)(2,1)}, bf16[4,72,384]{2,1,0:T(8,128)(2,1)}, u32[]{:S(2)}, u32[]{:S(2)}) collective-permute-start(bf16[4,72,384]{2,1,0:T(8,128)(2,1)} %constant_dynamic-slice_fusion), channel_id=1, source_target_pairs={{0,6},{1,7},{2,4},{3,5},{4,2},{5,3},{6,0},{7,1},{8,14},{9,15},{10,... | collective-permute-start | bytes 663560 | tf_op jit(solution)/shard_map/ppermute | solution.py:22
  22.9 24.6 %collective-permute-start.12 = (bf16[4,72,384]{2,1,0:T(8,128)(2,1)}, bf16[4,72,384]{2,1,0:T(8,128)(2,1)}, u32[]{:S(2)}, u32[]{:S(2)}) collective-permute-start(bf16[4,72,384]{2,1,0:T(8,128)(2,1)} %constant_dynamic-slice_fusion), channel_id=1, source_target_pairs={{0,4},{1,5},{2,6},{3,7},{4,0},{5,1},{6,2},{7,3},{8,12},{9,13},{10,... | collective-permute-start | bytes 663560 | tf_op jit(solution)/shard_map/ppermute | solution.py:22
  25.3 22.5 %collective-permute-start.11 = (bf16[4,72,384]{2,1,0:T(8,128)(2,1)}, bf16[4,72,384]{2,1,0:T(8,128)(2,1)S(1)}, u32[]{:S(2)}, u32[]{:S(2)}) collective-permute-start(bf16[4,72,384]{2,1,0:T(8,128)(2,1)} %constant_dynamic-slice_fusion), channel_id=1, source_target_pairs={{0,2},{1,3},{2,0},{3,1},{4,6},{5,7},{6,4},{7,5},{8,10},{9,11},{10,... | collective-permute-start | bytes 663560 | tf_op jit(solution)/shard_map/ppermute | solution.py:22
  27.7 10.4 %collective-permute-start.6 = (bf16[3,1,80,384]{3,2,1,0:T(8,128)(2,1)S(1)}, bf16[3,1,80,384]{3,2,1,0:T(8,128)(2,1)S(1)}, u32[]{:S(2)}, u32[]{:S(2)}) collective-permute-start(bf16[3,1,80,384]{3,2,1,0:T(8,128)(2,1)S(1)} %pad_maximum_fusion.13), channel_id=1, source_target_pairs={{0,16},{8,24},{16,0},{24,8},{1,17},{9,25},{17,1},{25,9},{2,18},{10... | collective-permute-start | bytes 552968 | tf_op jit(solution)/shard_map/ppermute | solution.py:22
  38.1 15.4 %collective-permute-start = (bf16[1,256,576]{2,1,0:T(8,128)(2,1)S(1)}, bf16[1,256,576]{2,1,0:T(8,128)(2,1)}, u32[]{:S(2)}, u32[]{:S(2)}) collective-permute-start(bf16[1,256,576]{2,1,0:T(8,128)(2,1)S(1)} %copy.57), channel_id=1, source_target_pairs={{0,24},{8,16},{16,8},{24,0},{1,25},{9,17},{17,9},{25,1},{2,26},{10... | collective-permute-start | bytes 884744 | tf_op jit(solution)/shard_map/ppermute | solution.py:22
  49.7 267.0 %reduce-scatter.2.cloned.1.call-start = ((), (), s32[]{:S(2)}) async-start(), calls=%async_computation.2 | async-start | bytes 5971968 | tf_op jit(solution)/shard_map/reduce_scatter | solution.py:974
  64.8 12.1 %collective-permute-start.14 = (bf16[512,384]{1,0:T(8,128)(2,1)S(1)}, bf16[512,384]{1,0:T(8,128)(2,1)S(1)}, u32[]{:S(2)}, u32[]{:S(2)}) collective-permute-start(bf16[512,384]{1,0:T(8,128)(2,1)S(1)} %get-tuple-element.146.refs_2_.refs_5_), channel_id=1, source_target_pairs={{0,8},{8,0},{16,24},{24,16},{1,9},{9,1},{17,25},{25,17},{2,10},{10... | collective-permute-start | bytes 1179656 | tf_op jit(solution)/shard_map/ppermute | solution.py:22
  64.9 20.5 %collective-permute-start.15 = (bf16[512,384]{1,0:T(8,128)(2,1)S(1)}, bf16[512,384]{1,0:T(8,128)(2,1)S(1)}, u32[]{:S(2)}, u32[]{:S(2)}) collective-permute-start(bf16[512,384]{1,0:T(8,128)(2,1)S(1)} %get-tuple-element.146.refs_2_.refs_5_), channel_id=1, source_target_pairs={{0,16},{8,24},{16,0},{24,8},{1,17},{9,25},{17,1},{25,9},{2,18},{10... | collective-permute-start | bytes 1179656 | tf_op jit(solution)/shard_map/ppermute | solution.py:22
  66.0 19.3 %collective-permute-start.16 = (bf16[512,384]{1,0:T(8,128)(2,1)S(1)}, bf16[512,384]{1,0:T(8,128)(2,1)S(1)}, u32[]{:S(2)}, u32[]{:S(2)}) collective-permute-start(bf16[512,384]{1,0:T(8,128)(2,1)S(1)} %get-tuple-element.146.refs_2_.refs_5_), channel_id=1, source_target_pairs={{0,24},{8,16},{16,8},{24,0},{1,25},{9,17},{17,9},{25,1},{2,26},{10... | collective-permute-start | bytes 1179656 | tf_op jit(solution)/shard_map/ppermute | solution.py:22
  68.3 35.8 %collective-permute-start.18 = (bf16[3,4,72,384]{3,2,1,0:T(8,128)(2,1)S(1)}, bf16[3,4,72,384]{3,2,1,0:T(8,128)(2,1)S(1)}, u32[]{:S(2)}, u32[]{:S(2)}) collective-permute-start(bf16[3,4,72,384]{3,2,1,0:T(8,128)(2,1)S(1)} %copy-done.68), channel_id=1, source_target_pairs={{0,8},{8,0},{16,24},{24,16},{1,9},{9,1},{17,25},{25,17},{2,10},{10... | collective-permute-start | bytes 1990664 | tf_op jit(solution)/shard_map/ppermute | solution.py:22
  68.4 35.7 %collective-permute-start.19 = (bf16[3,4,72,384]{3,2,1,0:T(8,128)(2,1)S(1)}, bf16[3,4,72,384]{3,2,1,0:T(8,128)(2,1)S(1)}, u32[]{:S(2)}, u32[]{:S(2)}) collective-permute-start(bf16[3,4,72,384]{3,2,1,0:T(8,128)(2,1)S(1)} %copy-done.68), channel_id=1, source_target_pairs={{0,16},{8,24},{16,0},{24,8},{1,17},{9,25},{17,1},{25,9},{2,18},{10... | collective-permute-start | bytes 1990664 | tf_op jit(solution)/shard_map/ppermute | solution.py:22
  117.7 29.4 %collective-permute-start.27 = (bf16[1,256,576]{2,1,0:T(8,128)(2,1)S(1)}, bf16[1,256,576]{2,1,0:T(8,128)(2,1)S(1)}, u32[]{:S(2)}, u32[]{:S(2)}) collective-permute-start(bf16[1,256,576]{2,1,0:T(8,128)(2,1)S(1)} %get-tuple-element.334), channel_id=1, source_target_pairs={{0,24},{8,16},{16,8},{24,0},{1,25},{9,17},{17,9},{25,1},{2,26},{10... | collective-permute-start | bytes 884744 | tf_op jit(solution)/shard_map/ppermute | solution.py:22
  142.8 12.6 %collective-permute-start.23 = (bf16[512,384]{1,0:T(8,128)(2,1)S(1)}, bf16[512,384]{1,0:T(8,128)(2,1)S(1)}, u32[]{:S(2)}, u32[]{:S(2)}) collective-permute-start(bf16[512,384]{1,0:T(8,128)(2,1)S(1)} %get-tuple-element.154.refs_2_.refs_5_), channel_id=1, source_target_pairs={{0,8},{8,0},{16,24},{24,16},{1,9},{9,1},{17,25},{25,17},{2,10},{10... | collective-permute-start | bytes 1179656 | tf_op jit(solution)/shard_map/ppermute | solution.py:22
  145.6 19.3 %collective-permute-start.24 = (bf16[512,384]{1,0:T(8,128)(2,1)S(1)}, bf16[512,384]{1,0:T(8,128)(2,1)S(1)}, u32[]{:S(2)}, u32[]{:S(2)}) collective-permute-start(bf16[512,384]{1,0:T(8,128)(2,1)S(1)} %get-tuple-element.154.refs_2_.refs_5_), channel_id=1, source_target_pairs={{0,16},{8,24},{16,0},{24,8},{1,17},{9,25},{17,1},{25,9},{2,18},{10... | collective-permute-start | bytes 1179656 | tf_op jit(solution)/shard_map/ppermute | solution.py:22
  145.9 19.0 %collective-permute-start.25 = (bf16[512,384]{1,0:T(8,128)(2,1)S(1)}, bf16[512,384]{1,0:T(8,128)(2,1)S(1)}, u32[]{:S(2)}, u32[]{:S(2)}) collective-permute-start(bf16[512,384]{1,0:T(8,128)(2,1)S(1)} %get-tuple-element.154.refs_2_.refs_5_), channel_id=1, source_target_pairs={{0,24},{8,16},{16,8},{24,0},{1,25},{9,17},{17,9},{25,1},{2,26},{10... | collective-permute-start | bytes 1179656 | tf_op jit(solution)/shard_map/ppermute | solution.py:22
  244.0 12.7 %collective-permute-start.28 = (bf16[512,256]{1,0:T(8,128)(2,1)S(1)}, bf16[512,256]{1,0:T(8,128)(2,1)S(1)}, u32[]{:S(2)}, u32[]{:S(2)}) collective-permute-start(bf16[512,256]{1,0:T(8,128)(2,1)S(1)} %get-tuple-element.181), channel_id=1, source_target_pairs={{0,8},{8,0},{16,24},{24,16},{1,9},{9,1},{17,25},{25,17},{2,10},{10... | collective-permute-start | bytes 786440 | tf_op jit(solution)/shard_map/ppermute | solution.py:22
  244.3 12.4 %collective-permute-start.29 = (bf16[512,256]{1,0:T(8,128)(2,1)S(1)}, bf16[512,256]{1,0:T(8,128)(2,1)S(1)}, u32[]{:S(2)}, u32[]{:S(2)}) collective-permute-start(bf16[512,256]{1,0:T(8,128)(2,1)S(1)} %get-tuple-element.182), channel_id=1, source_target_pairs={{0,16},{8,24},{16,0},{24,8},{1,17},{9,25},{17,1},{25,9},{2,18},{10... | collective-permute-start | bytes 786440 | tf_op jit(solution)/shard_map/ppermute | solution.py:22
  245.7 11.2 %collective-permute-start.30 = (bf16[512,256]{1,0:T(8,128)(2,1)S(1)}, bf16[512,256]{1,0:T(8,128)(2,1)S(1)}, u32[]{:S(2)}, u32[]{:S(2)}) collective-permute-start(bf16[512,256]{1,0:T(8,128)(2,1)S(1)} %get-tuple-element.183), channel_id=1, source_target_pairs={{0,24},{8,16},{16,8},{24,0},{1,25},{9,17},{17,9},{25,1},{2,26},{10... | collective-permute-start | bytes 786440 | tf_op jit(solution)/shard_map/ppermute | solution.py:22
  316.7 25.5 %collective-permute-start.35 = (bf16[2,2,4,72,384]{4,3,2,1,0:T(8,128)(2,1)}, bf16[2,2,4,72,384]{4,3,2,1,0:T(8,128)(2,1)S(1)}, u32[]{:S(2)}, u32[]{:S(2)}) collective-permute-start(bf16[2,2,4,72,384]{4,3,2,1,0:T(8,128)(2,1)} %pad_maximum_fusion.1), channel_id=1, source_target_pairs={{0,8},{8,0},{16,24},{24,16},{1,9},{9,1},{17,25},{25,17},{2,10},{10... | collective-permute-start | bytes 2654216 | tf_op jit(solution)/shard_map/ppermute | solution.py:22
  318.1 24.1 %collective-permute-start.36 = (bf16[2,2,4,72,384]{4,3,2,1,0:T(8,128)(2,1)S(1)}, bf16[2,2,4,72,384]{4,3,2,1,0:T(8,128)(2,1)S(1)}, u32[]{:S(2)}, u32[]{:S(2)}) collective-permute-start(bf16[2,2,4,72,384]{4,3,2,1,0:T(8,128)(2,1)S(1)} %stack.91), channel_id=1, source_target_pairs={{0,16},{8,24},{16,0},{24,8},{1,17},{9,25},{17,1},{25,9},{2,18},{10... | collective-permute-start | bytes 2654216 | tf_op jit(solution)/shard_map/ppermute | solution.py:22
  338.6 18.1 %collective-permute-start.42 = (bf16[512,256]{1,0:T(8,128)(2,1)S(1)}, bf16[512,256]{1,0:T(8,128)(2,1)S(1)}, u32[]{:S(2)}, u32[]{:S(2)}) collective-permute-start(bf16[512,256]{1,0:T(8,128)(2,1)S(1)} %get-tuple-element.239), channel_id=1, source_target_pairs={{0,8},{8,0},{16,24},{24,16},{1,9},{9,1},{17,25},{25,17},{2,10},{10... | collective-permute-start | bytes 786440 | tf_op jit(solution)/shard_map/ppermute | solution.py:22
  340.2 16.6 %collective-permute-start.43 = (bf16[512,256]{1,0:T(8,128)(2,1)S(1)}, bf16[512,256]{1,0:T(8,128)(2,1)S(1)}, u32[]{:S(2)}, u32[]{:S(2)}) collective-permute-start(bf16[512,256]{1,0:T(8,128)(2,1)S(1)} %get-tuple-element.240), channel_id=1, source_target_pairs={{0,16},{8,24},{16,0},{24,8},{1,17},{9,25},{17,1},{25,9},{2,18},{10... | collective-permute-start | bytes 786440 | tf_op jit(solution)/shard_map/ppermute | solution.py:22
  340.8 16.0 %collective-permute-start.44 = (bf16[512,256]{1,0:T(8,128)(2,1)S(1)}, bf16[512,256]{1,0:T(8,128)(2,1)S(1)}, u32[]{:S(2)}, u32[]{:S(2)}) collective-permute-start(bf16[512,256]{1,0:T(8,128)(2,1)S(1)} %get-tuple-element.241), channel_id=1, source_target_pairs={{0,24},{8,16},{16,8},{24,0},{1,25},{9,17},{17,9},{25,1},{2,26},{10... | collective-permute-start | bytes 786440 | tf_op jit(solution)/shard_map/ppermute | solution.py:22
  345.2 19.3 %collective-permute-start.37 = (bf16[2,4,72,384]{3,2,1,0:T(8,128)(2,1)}, bf16[2,4,72,384]{3,2,1,0:T(8,128)(2,1)S(1)}, u32[]{:S(2)}, u32[]{:S(2)}) collective-permute-start(bf16[2,4,72,384]{3,2,1,0:T(8,128)(2,1)} %get-tuple-element.220), channel_id=1, source_target_pairs={{0,16},{8,24},{16,0},{24,8},{1,17},{9,25},{17,1},{25,9},{2,18},{10... | collective-permute-start | bytes 1327112 | tf_op jit(solution)/shard_map/ppermute | solution.py:22
  346.6 17.8 %collective-permute-start.38 = (bf16[2,4,72,384]{3,2,1,0:T(8,128)(2,1)S(1)}, bf16[2,4,72,384]{3,2,1,0:T(8,128)(2,1)S(1)}, u32[]{:S(2)}, u32[]{:S(2)}) collective-permute-start(bf16[2,4,72,384]{3,2,1,0:T(8,128)(2,1)S(1)} %get-tuple-element.221), channel_id=1, source_target_pairs={{0,8},{8,0},{16,24},{24,16},{1,9},{9,1},{17,25},{25,17},{2,10},{10... | collective-permute-start | bytes 1327112 | tf_op jit(solution)/shard_map/ppermute | solution.py:22
  356.8 9.4 %collective-permute-start.45 = (bf16[512,128]{1,0:T(8,128)(2,1)S(1)}, bf16[512,128]{1,0:T(8,128)(2,1)S(1)}, u32[]{:S(2)}, u32[]{:S(2)}) collective-permute-start(bf16[512,128]{1,0:T(8,128)(2,1)S(1)} %get-tuple-element.251), channel_id=1, source_target_pairs={{0,8},{8,0},{16,24},{24,16},{1,9},{9,1},{17,25},{25,17},{2,10},{10... | collective-permute-start | bytes 393224 | tf_op jit(solution)/shard_map/ppermute | solution.py:22
  358.3 10.1 %collective-permute-start.46 = (bf16[512,128]{1,0:T(8,128)(2,1)S(1)}, bf16[512,128]{1,0:T(8,128)(2,1)S(1)}, u32[]{:S(2)}, u32[]{:S(2)}) collective-permute-start(bf16[512,128]{1,0:T(8,128)(2,1)S(1)} %get-tuple-element.252), channel_id=1, source_target_pairs={{0,16},{8,24},{16,0},{24,8},{1,17},{9,25},{17,1},{25,9},{2,18},{10... | collective-permute-start | bytes 393224 | tf_op jit(solution)/shard_map/ppermute | solution.py:22
  358.9 9.6 %collective-permute-start.47 = (bf16[512,128]{1,0:T(8,128)(2,1)S(1)}, bf16[512,128]{1,0:T(8,128)(2,1)S(1)}, u32[]{:S(2)}, u32[]{:S(2)}) collective-permute-start(bf16[512,128]{1,0:T(8,128)(2,1)S(1)} %get-tuple-element.253), channel_id=1, source_target_pairs={{0,24},{8,16},{16,8},{24,0},{1,25},{9,17},{17,9},{25,1},{2,26},{10... | collective-permute-start | bytes 393224 | tf_op jit(solution)/shard_map/ppermute | solution.py:22
  381.9 23.8 %collective-permute-start.48 = (bf16[4,4,1,80,384]{4,3,2,1,0:T(8,128)(2,1)S(1)}, bf16[4,4,1,80,384]{4,3,2,1,0:T(8,128)(2,1)}, u32[]{:S(2)}, u32[]{:S(2)}) collective-permute-start(bf16[4,4,1,80,384]{4,3,2,1,0:T(8,128)(2,1)S(1)} %get-tuple-element.259), channel_id=1, source_target_pairs={{0,1},{1,0},{2,3},{3,2},{4,5},{5,4},{6,7},{7,6},{8,9},{9,8},{10,11... | collective-permute-start | bytes 2949128 | tf_op jit(solution)/shard_map/ppermute | solution.py:22
  382.8 11.3 %collective-permute-start.26 = (bf16[1,256,576]{2,1,0:T(8,128)(2,1)}, bf16[1,256,576]{2,1,0:T(8,128)(2,1)}, u32[]{:S(2)}, u32[]{:S(2)}) collective-permute-start(bf16[1,256,576]{2,1,0:T(8,128)(2,1)} %get-tuple-element.336), channel_id=1, source_target_pairs={{0,24},{8,16},{16,8},{24,0},{1,25},{9,17},{17,9},{25,1},{2,26},{10... | collective-permute-start | bytes 884744 | tf_op jit(solution)/shard_map/ppermute | solution.py:22
  399.4 9.3 %collective-permute-start.49 = (bf16[3,72,384]{2,1,0:T(8,128)(2,1)S(1)}, bf16[3,72,384]{2,1,0:T(8,128)(2,1)S(1)}, u32[]{:S(2)}, u32[]{:S(2)}) collective-permute-start(bf16[3,72,384]{2,1,0:T(8,128)(2,1)S(1)} %get-tuple-element.331), channel_id=1, source_target_pairs={{0,8},{8,0},{16,24},{24,16},{1,9},{9,1},{17,25},{25,17},{2,10},{10... | collective-permute-start | bytes 497672 | tf_op jit(solution)/shard_map/ppermute | solution.py:22
  399.9 10.4 %collective-permute-start.50 = (bf16[3,72,384]{2,1,0:T(8,128)(2,1)S(1)}, bf16[3,72,384]{2,1,0:T(8,128)(2,1)S(1)}, u32[]{:S(2)}, u32[]{:S(2)}) collective-permute-start(bf16[3,72,384]{2,1,0:T(8,128)(2,1)S(1)} %get-tuple-element.330), channel_id=1, source_target_pairs={{0,16},{8,24},{16,0},{24,8},{1,17},{9,25},{17,1},{25,9},{2,18},{10... | collective-permute-start | bytes 497672 | tf_op jit(solution)/shard_map/ppermute | solution.py:22
  401.4 8.9 %collective-permute-start.51 = (bf16[3,72,384]{2,1,0:T(8,128)(2,1)S(1)}, bf16[3,72,384]{2,1,0:T(8,128)(2,1)S(1)}, u32[]{:S(2)}, u32[]{:S(2)}) collective-permute-start(bf16[3,72,384]{2,1,0:T(8,128)(2,1)S(1)} %get-tuple-element.329), channel_id=1, source_target_pairs={{0,24},{8,16},{16,8},{24,0},{1,25},{9,17},{17,9},{25,1},{2,26},{10... | collective-permute-start | bytes 497672 | tf_op jit(solution)/shard_map/ppermute | solution.py:22
  402.9 10.5 %collective-permute-start.39 = (bf16[4,72,384]{2,1,0:T(8,128)(2,1)}, bf16[4,72,384]{2,1,0:T(8,128)(2,1)S(1)}, u32[]{:S(2)}, u32[]{:S(2)}) collective-permute-start(bf16[4,72,384]{2,1,0:T(8,128)(2,1)} %fusion.24), channel_id=1, source_target_pairs={{0,2},{1,3},{2,0},{3,1},{4,6},{5,7},{6,4},{7,5},{8,10},{9,11},{10,... | collective-permute-start | bytes 663560 | tf_op jit(solution)/shard_map/ppermute | solution.py:22
  405.7 18.4 %collective-permute-start.40 = (bf16[4,72,384]{2,1,0:T(8,128)(2,1)}, bf16[4,72,384]{2,1,0:T(8,128)(2,1)S(1)}, u32[]{:S(2)}, u32[]{:S(2)}) collective-permute-start(bf16[4,72,384]{2,1,0:T(8,128)(2,1)} %get-tuple-element.227), channel_id=1, source_target_pairs={{0,4},{1,5},{2,6},{3,7},{4,0},{5,1},{6,2},{7,3},{8,12},{9,13},{10,... | collective-permute-start | bytes 663560 | tf_op jit(solution)/shard_map/ppermute | solution.py:22
  408.7 15.5 %collective-permute-start.41 = (bf16[4,72,384]{2,1,0:T(8,128)(2,1)S(1)}, bf16[4,72,384]{2,1,0:T(8,128)(2,1)S(1)}, u32[]{:S(2)}, u32[]{:S(2)}) collective-permute-start(bf16[4,72,384]{2,1,0:T(8,128)(2,1)S(1)} %copy-done.76), channel_id=1, source_target_pairs={{0,6},{1,7},{2,4},{3,5},{4,2},{5,3},{6,0},{7,1},{8,14},{9,15},{10,... | collective-permute-start | bytes 663560 | tf_op jit(solution)/shard_map/ppermute | solution.py:22
  424.8 16.3 %collective-permute-start.56 = (bf16[2,2,1,80,384]{4,3,1,2,0:T(8,128)(2,1)S(1)}, bf16[2,2,1,80,384]{4,3,1,2,0:T(8,128)(2,1)S(1)}, u32[]{:S(2)}, u32[]{:S(2)}) collective-permute-start(bf16[2,2,1,80,384]{4,3,1,2,0:T(8,128)(2,1)S(1)} %stack.92), channel_id=1, source_target_pairs={{0,16},{8,24},{16,0},{24,8},{1,17},{9,25},{17,1},{25,9},{2,18},{10... | collective-permute-start | bytes 737288 | tf_op jit(solution)/shard_map/ppermute | solution.py:22
  427.5 39.2 %collective-permute-start.63 = (bf16[7,72,384]{2,1,0:T(8,128)(2,1)}, bf16[7,72,384]{2,1,0:T(8,128)(2,1)}, u32[]{:S(2)}, u32[]{:S(2)}) collective-permute-start(bf16[7,72,384]{2,1,0:T(8,128)(2,1)} %pad_maximum_fusion.7), channel_id=1, source_target_pairs={{0,24},{8,16},{16,8},{24,0},{1,25},{9,17},{17,9},{25,1},{2,26},{10... | collective-permute-start | bytes 1161224 | tf_op jit(solution)/shard_map/ppermute | solution.py:22
  428.9 37.9 %collective-permute-start.64 = (bf16[7,72,384]{2,1,0:T(8,128)(2,1)}, bf16[7,72,384]{2,1,0:T(8,128)(2,1)}, u32[]{:S(2)}, u32[]{:S(2)}) collective-permute-start(bf16[7,72,384]{2,1,0:T(8,128)(2,1)} %pad_maximum_fusion.7), channel_id=1, source_target_pairs={{0,16},{8,24},{16,0},{24,8},{1,17},{9,25},{17,1},{25,9},{2,18},{10... | collective-permute-start | bytes 1161224 | tf_op jit(solution)/shard_map/ppermute | solution.py:22
  429.6 37.2 %collective-permute-start.65 = (bf16[7,72,384]{2,1,0:T(8,128)(2,1)}, bf16[7,72,384]{2,1,0:T(8,128)(2,1)}, u32[]{:S(2)}, u32[]{:S(2)}) collective-permute-start(bf16[7,72,384]{2,1,0:T(8,128)(2,1)} %pad_maximum_fusion.7), channel_id=1, source_target_pairs={{0,8},{8,0},{16,24},{24,16},{1,9},{9,1},{17,25},{25,17},{2,10},{10... | collective-permute-start | bytes 1161224 | tf_op jit(solution)/shard_map/ppermute | solution.py:22
  433.0 21.9 %collective-permute-start.52 = (bf16[256,576]{1,0:T(8,128)(2,1)S(1)}, bf16[256,576]{1,0:T(8,128)(2,1)S(1)}, u32[]{:S(2)}, u32[]{:S(2)}) collective-permute-start(bf16[256,576]{1,0:T(8,128)(2,1)S(1)} %slice.804), channel_id=1, source_target_pairs={{0,24},{8,16},{16,8},{24,0},{1,25},{9,17},{17,9},{25,1},{2,26},{10... | collective-permute-start | bytes 884744 | tf_op jit(solution)/shard_map/ppermute | solution.py:22
  441.1 20.8 %collective-permute-start.54 = (bf16[2,1,80,384]{3,2,1,0:T(8,128)(2,1)}, bf16[2,1,80,384]{3,2,1,0:T(8,128)(2,1)}, u32[]{:S(2)}, u32[]{:S(2)}) collective-permute-start(bf16[2,1,80,384]{3,2,1,0:T(8,128)(2,1)} %fusion.31), channel_id=1, source_target_pairs={{0,16},{8,24},{16,0},{24,8},{1,17},{9,25},{17,1},{25,9},{2,18},{10... | collective-permute-start | bytes 368648 | tf_op jit(solution)/shard_map/ppermute | solution.py:22
  461.1 9.9 %collective-permute-start.59 = (bf16[1,80,384]{2,1,0:T(8,128)(2,1)S(1)}, bf16[1,80,384]{2,1,0:T(8,128)(2,1)S(1)}, u32[]{:S(2)}, u32[]{:S(2)}) collective-permute-start(bf16[1,80,384]{2,1,0:T(8,128)(2,1)S(1)} %slice_bitcast_fusion.9), channel_id=1, source_target_pairs={{0,6},{1,7},{2,4},{3,5},{4,2},{5,3},{6,0},{7,1},{8,14},{9,15},{10,... | collective-permute-start | bytes 184328 | tf_op jit(solution)/shard_map/ppermute | solution.py:22
  461.9 9.1 %collective-permute-start.58 = (bf16[1,80,384]{2,1,0:T(8,128)(2,1)S(1)}, bf16[1,80,384]{2,1,0:T(8,128)(2,1)S(1)}, u32[]{:S(2)}, u32[]{:S(2)}) collective-permute-start(bf16[1,80,384]{2,1,0:T(8,128)(2,1)S(1)} %slice_bitcast_fusion.10), channel_id=1, source_target_pairs={{0,4},{1,5},{2,6},{3,7},{4,0},{5,1},{6,2},{7,3},{8,12},{9,13},{10,... | collective-permute-start | bytes 184328 | tf_op jit(solution)/shard_map/ppermute | solution.py:22
  (98 other events, 710.8 us)
Sparse Core Ops, SparseCore 0:
  49.8 57.6 all-gather.1
  221.7 60.4 reduce-scatter.1

commit v4 on v3

--- a/solution.py
+++ b/solution.py
@@ -133,48 +133,13 @@
     return lax.all_gather(own, "fsdp", axis=1, tiled=True)
 
 
-def scatter_kernel(count, *refs):
-    wholes, (keep, send, sems) = refs[:count], refs[count:]
-    j = lax.axis_index("ctx")
-    f = lax.axis_index("fsdp")
-    copies = []
-    for core, pieces in ((0, keep), (1, send)):
-        for jrel in range(4):
-            for zrel in range(4):
-                row = (f ^ (core + 2 * zrel)) * 4 + (j ^ jrel)
-                at = 0
-                for whole in wholes:
-                    made = pltpu.make_async_copy(
-                        whole.at[row],
-                        pieces.at[jrel, zrel, at : at + whole.shape[1]],
-                        sems.at[len(copies)],
-                    )
-                    made.start()
-                    copies.append(made)
-                    at += whole.shape[1]
-    for made in copies:
-        made.wait()
-
-
-def cut(wholes):
-    rows = wholes[0].shape[2]
-    total = sum(whole.shape[1] for whole in wholes)
-    piece = jax.ShapeDtypeStruct((4, 4, total, rows, PIECE), wholes[0].dtype)
-    return pl.pallas_call(
-        lambda *refs: scatter_kernel(len(wholes), *refs),
-        out_shape=(piece, piece),
-        in_specs=[pl.BlockSpec(memory_space=pltpu.VMEM)] * len(wholes),
-        out_specs=[pl.BlockSpec(memory_space=pl.ANY)] * 2,
-        scratch_shapes=[pltpu.SemaphoreType.DMA((32 * len(wholes),))],
-        compiler_params=pltpu.CompilerParams(vmem_limit_bytes=VMEM_LIMIT),
-        name="cut",
-    )(*wholes)
-
-
-def reduce_begin(*wholes):
-    keep, send = cut(wholes)
-    other = flip(send, "fsdp", 1)
-    total = wide(keep) + wide(other)
+def reduce_start(whole):
+    by_core = whole.reshape(2, 4, 4, *whole.shape[1:])
+    return by_core[0], flip(by_core[1], "fsdp", 1)
+
+
+def reduce_begin(*halves):
+    total = jnp.concatenate([wide(keep) + wide(other) for keep, other in halves], axis=2)
     a = low(total[:, :2])
     b = low(total[:, 2:])
     return (a[0], a[2], b[0], b[1]), (jnp.stack([a[1], a[3]]), jnp.stack([b[2], b[3]]))
@@ -680,7 +645,19 @@
     return dx, jnp.sum(grad * unit, axis=0, keepdims=True)
 
 
-def put_rows(ref, index, value, shards):
+def place_of(relative, ranks, shards):
+    if not relative:
+        return lambda f, j: f * ranks + j
+    me, rank = lax.axis_index("fsdp"), lax.axis_index("ctx")
+
+    def place(f, j):
+        apart = f ^ me
+        return (apart & 1) * (ranks * shards // 2) + (j ^ rank) * (shards // 2) + (apart >> 1)
+
+    return place
+
+
+def put_rows(ref, index, value, shards, place):
     if shards is None:
         ref[index] = low(value)
         return
@@ -688,12 +665,12 @@
     ranks = value.shape[1] // PIECE
     for j in range(ranks):
         for f in range(shards):
-            ref[f * ranks + j, index] = low(
+            ref[place(f, j), index] = low(
                 value[f * rows : (f + 1) * rows, j * PIECE : (j + 1) * PIECE]
             )
 
 
-def mlp_back(grad, kept, gains, which, attn_weights, gate_w, up_w, down_w, shards):
+def mlp_back(grad, kept, gains, which, attn_weights, gate_w, up_w, down_w, shards, relative):
     middle, mixed, gate, up, inner, attention = kept
     tokens, width = grad.shape
     ff = shape_of(gate_w)[1]
@@ -702,10 +679,11 @@
     def body(get, outs, extra):
         datt_ref, mid_ref, gain_ref, out_grad_ref, weights_ref = outs[:5]
         left, right, wide_right, grad_s, total = extra
+        place = None if shards is None else place_of(relative, ff // PIECE, shards)
         open_down(get(11), left, right, wide_right)
         grad = get(0)[...]
         grad_low = low(grad)
-        mixed = get(2)[...]
+        mixed_t = low(jnp.transpose(wide(get(2)[...])))
         d_mixed = 0.0
         for c in range(ff // chunk):
             cols = slice(c * chunk, (c + 1) * chunk)
@@ -716,8 +694,8 @@
             sig = jax.nn.sigmoid(g)
             d_gate = low(d_inner * wide(get(4)[:, cols]) * (sig * (1.0 + g * (1.0 - sig))))
             d_up = low(d_inner * (g * sig))
-            grad_s[0, :, cols] = dot_tn(mixed, d_gate)
-            grad_s[1, :, cols] = dot_tn(mixed, d_up)
+            grad_s[0, :, cols] = dot_nn(mixed_t, d_gate)
+            grad_s[1, :, cols] = dot_nn(mixed_t, d_up)
             part = dot_nt(d_gate, get(9)[:, cols]) + dot_nt(d_up, get(10)[:, cols])
             d_mixed = part + d_mixed
             d_down = dot_tn(get(5)[:, cols], grad_low)
@@ -726,7 +704,7 @@
             else:
                 total[cols] = d_down
         for index in range(2):
-            put_rows(weights_ref, index, grad_s[index], shards)
+            put_rows(weights_ref, index, grad_s[index], shards, place)
         if shards is not None:
             rows = width // shards
             step = rows * 2 // 3
@@ -742,7 +720,7 @@
                         ],
                         axis=0,
                     )
-                    weights_ref[f * ranks + j, 2] = low(value)
+                    weights_ref[place(f, j), 2] = low(value)
         dx, gain_grad = norm_back(get(1)[...], get(7)[which : which + 1], d_mixed)
         gain_ref[...] = jnp.broadcast_to(gain_grad, gain_ref.shape)
         mid = grad + dx
@@ -778,7 +756,7 @@
     )
 
 
-def project_back(d_queries, pairs, cosine, sine, kept, gains, which, weights, out_grad, mid, shards, riders):
+def project_back(d_queries, pairs, cosine, sine, kept, gains, which, weights, out_grad, mid, shards, riders, relative):
     hidden, normed = kept
     tokens, width = hidden.shape
     parts = len(d_queries)
@@ -810,7 +788,8 @@
         d_weights = dot_tn(get(3)[...], d_all)
         value = jnp.concatenate([d_weights, wide(get(6)[...])], axis=1)
         if riders is None:
-            put_rows(weights_ref, 0, value, shards)
+            place = None if shards is None else place_of(relative, columns // PIECE, shards)
+            put_rows(weights_ref, 0, value, shards, place)
         else:
             rows = width // shards
             lines = [get(fixed + parts * slots)[...], gain_grad]
@@ -820,10 +799,11 @@
                 [ride, jnp.zeros((8, columns - width), jnp.float32)], axis=1
             )
             ranks = columns // PIECE
+            place = place_of(relative, ranks, shards)
             for j in range(ranks):
                 cols = slice(j * PIECE, (j + 1) * PIECE)
                 for f in range(shards):
-                    weights_ref[f * ranks + j, 0] = low(
+                    weights_ref[place(f, j), 0] = low(
                         jnp.concatenate(
                             [value[f * rows : (f + 1) * rows, cols], ride[:, cols]], axis=0
                         )
@@ -965,9 +945,18 @@
             attn_full[i],
             *mlp_full[i],
             by_shard,
+            i == 0,
         )
         if fast and i == 0:
-            sums, sends = reduce_begin(weight_grads[0], attn_grads[1])
+            moved = [
+                lax.dynamic_index_in_dim(early, rank ^ k, axis=0, keepdims=False)
+                for k in range(4)
+            ]
+            weight_grads[0], moved = lax.optimization_barrier((weight_grads[0], moved))
+            begun = reduce_start(weight_grads[0])
+            moved = [moved[0]] + [flip(moved[k], "ctx", k) for k in (1, 2, 3)]
+            early = low(sum((wide(part) for part in moved[1:]), wide(moved[0])))
+            sums, sends = reduce_begin(begun, attn_begun)
             d_attention, sends, early = lax.optimization_barrier((d_attention, sends, early))
             sides = reduce_sides(sends)
         elif fast:
@@ -1014,22 +1003,21 @@
             mid,
             by_shard,
             riders,
+            True,
         )
         if fast and i == 0:
-            moved = [
-                lax.dynamic_index_in_dim(early, rank ^ k, axis=0, keepdims=False)
-                for k in range(4)
-            ]
-            moved = [moved[0]] + [flip(moved[k], "ctx", k) for k in (1, 2, 3)]
-            sums, sends = reduce_begin(attn_grad)
-            line, sends, grad, moved = lax.optimization_barrier((line, sends, grad, moved))
-            early = low(sum((wide(part) for part in moved[1:]), wide(moved[0])))
+            sums, sends = reduce_begin(reduce_start(attn_grad))
+            line, sends, grad, early = lax.optimization_barrier((line, sends, grad, early))
             sides = reduce_sides(sends)
-            rest = spread_fast(jnp.concatenate([low(reduce_end(line)), early]))
+            rest = low(reduce_end(line))
             sums, sends = reduce_middle(sums, sides)
-            sums, sends = reduce_turn(sums, reduce_across(sends))
+            sends, rest, early = lax.optimization_barrier((sends, rest, early))
+            across = reduce_across(sends)
+            rest = spread_fast(rest)
+            sums, sends = reduce_turn(sums, across)
             last = spread_fast(reduce_end((sums, *reduce_line(sends))))
-            early = rest[4:]
+            early = spread_fast(early)
+            far = tied(flip(low(grad[half:]), "ctx", slots - 1), last)
             all_gains = lax.dynamic_slice_in_dim(last[0, rows:], shard * rows, rows, axis=1)
             order = (3, 0, 1, 2)
             all_gains = jnp.stack([all_gains[v] for v in order])
@@ -1038,7 +1026,8 @@
             up_rows = jnp.stack([rest[1], early[1]])
             down_rows = unfold_down(jnp.stack([rest[2], early[2]]))
         elif fast:
-            attn_grads[i] = attn_grad
+            attn_begun = reduce_start(attn_grad)
+            grad, layer_out = lax.optimization_barrier((grad, layer_out))
         else:
             attn_grads[i] = reduce_plain(attn_grad[0], 0)
     if not fast:
@@ -1049,8 +1038,9 @@
         all_gains = jnp.concatenate([gain_grads[v][:1] for v in range(gain_count)])
         all_gains = lax.psum(all_gains, ("ctx", "fsdp"))
         all_gains = lax.dynamic_slice_in_dim(all_gains, shard * rows, rows, axis=1)
-    far = wide(flip(low(grad[half:]), "ctx", slots - 1))
-    grad = jnp.concatenate([grad[:half], far])[None]
+    if not fast:
+        far = flip(low(grad[half:]), "ctx", slots - 1)
+    grad = jnp.concatenate([grad[:half], wide(far)])[None]
     return (
         layer_out,
         grad,

time: 494 us -> 475 us (0.962)
  Pallas kernels: 193 us -> 181 us
  other arithmetic: 28.5 us -> 21.5 us
  starting transfers between devices: 77.4 us -> 84.1 us
    pallas_call x2 -> x0, Pallas kernels: 12.4 us -> none  [cut(): pl.pallas_call(lambda *refs: scatter_kernel(len(wholes), *refs), out_shap...]
    unnamed x170 -> x176, local copies, waits for them, and re-layouts: 39.9 us -> 32.3 us
    slice x2 -> x6, local copies, waits for them, and re-layouts: 0.08 us -> 7.35 us  [the longest x3 5.09 us: reduce_start(): return (by_core[0], flip(by_core[1], 'fsdp', 1))]
    ppermute x66 -> x70, starting transfers between devices: 77.4 us -> 84.1 us  [flip(): return lax.ppermute(block, axis, route)]
    ppermute x66 -> x70, waiting for transfers between devices: 122 us -> 119 us  [flip(): return lax.ppermute(block, axis, route)]
  transfers between devices with their start and end apart: 68 -> 72, of which waited for: 27 -> 31; matrix products, arithmetic and copies ran while one was open for 8% -> 6% of each run, Pallas kernels for 31% -> 31%
where the time goes in v4:
time: 475 us; the launch traced here: 470 us
  Pallas kernels  181 us (38%)
  waiting for transfers between devices  119 us (25%)
  starting transfers between devices  84.1 us (18%)
  local copies, waits for them, and re-layouts  49.1 us (10%)
  other arithmetic  21.5 us (5%)
  between operations  15.8 us (3%)
    pallas_call x14, Pallas kernels, run_kernel(): pl.pallas_call(kernel, out_shape=tuple(outputs), in_specs=[pl.BlockSpec(m...  173 us
    ppermute x70, waiting for transfers between devices, flip(): return lax.ppermute(block, axis, route)  119 us
    ppermute x70, starting transfers between devices, flip(): return lax.ppermute(block, axis, route)  84.1 us
    unnamed x176, local copies, waits for them, and re-layouts  32.3 us
  transfers between devices with their start and end apart: 72, of which 31 were waited for; matrix products, arithmetic and copies ran while one was open for 6% of the time, Pallas kernels for 31%

profile of v4, /device:TPU:0, one launch (start us, length us, event | category | flops | bytes accessed | tf_op | source)
XLA Modules:
  0.0 470.4 jit_solution(11341801878814013137)
XLA Ops:
  10.8 3.1 collective-permute-start.11
  13.8 2.6 collective-permute-start.12
  18.5 3.9 collective-permute-start.5
  25.9 2.6 collective-permute-start.13
  28.5 7.5 %collective-permute-done.4 = bf16[1,80,384]{2,1,0:T(8,128)(2,1)S(1)} collective-permute-done((bf16[1,80,384]{2,1,0:T(8,128)(2,1)}, bf16[1,80,384]{2,1,0:T(8,128)(2,1)S(1)}, u32[]{:S(2)}, u32[]{:S(2)}) %collective-permute-start.4) | collective-permute-done | bytes 61472 | tf_op jit(solution)/shard_map/ppermute | solution.py:22
  39.1 2.5 collective-permute-done.6
  43.4 3.2 collective-permute-done.8
  48.1 2.7 collective-permute-done.9
  50.8 2.4 collective-permute-start
  53.8 2.0 pad_maximum_fusion.4
  58.1 3.5 collective-permute-done.1
  62.8 2.2 assemble.2
  68.8 3.8 project_in.2
  73.9 2.3 collective-permute-start.16
  77.4 7.3 %collective-permute-done.14.refs_3_.refs_6_ = bf16[512,384]{1,0:T(8,128)(2,1)S(1)} collective-permute-done((bf16[512,384]{1,0:T(8,128)(2,1)S(1)}, bf16[512,384]{1,0:T(8,128)(2,1)S(1)}, u32[]{:S(2)}, u32[]{:S(2)}) %collective-permute-start.14) | collective-permute-done | bytes 393248 | tf_op jit(solution)/shard_map/ppermute | solution.py:22
  84.8 8.9 %collective-permute-done.15.refs_4_.refs_7_ = bf16[512,384]{1,0:T(8,128)(2,1)S(1)} collective-permute-done((bf16[512,384]{1,0:T(8,128)(2,1)S(1)}, bf16[512,384]{1,0:T(8,128)(2,1)S(1)}, u32[]{:S(2)}, u32[]{:S(2)}) %collective-permute-start.15) | collective-permute-done | bytes 393248 | tf_op jit(solution)/shard_map/ppermute | solution.py:22
  93.7 18.6 %attend.2 = (bf16[512,576]{1,0:T(8,128)(2,1)S(1)}, f32[16,512]{1,0:T(8,128)S(1)}) custom-call(bf16[512,576]{1,0:T(8,128)(2,1)S(1)} %get-tuple-element.149.refs_0_, s32[1,512]{1,0:T(1,128)S(1)} %get-tuple-element.412.refs_1_.refs_4_, bf16[512,384]{1,0:T(8,128)(2,1)S(1)} %get-tuple-element.151.refs_2_.refs_5_, ...), custom_call_target="tpu_custom_call" | custom-call | flops 15000000512 | bytes 4000000 | tf_op jit(solution)/shard_map/attend/pallas_call | solution.py:236
  115.7 5.9 %collective-permute-done.20 = bf16[2,4,72,384]{3,2,1,0:T(8,128)(2,1)S(1)} collective-permute-done((bf16[2,4,72,384]{3,2,1,0:T(8,128)(2,1)S(1)}, bf16[2,4,72,384]{3,2,1,0:T(8,128)(2,1)S(1)}, u32[]{:S(2)}, u32[]{:S(2)}) %collective-permute-start.20) | collective-permute-done | bytes 442400 | tf_op jit(solution)/shard_map/ppermute | solution.py:22
  122.3 2.1 copy.40
  128.1 5.3 %assemble.3.refs_6_.refs_11_ = bf16[4,8,72,1536]{3,2,1,0:T(8,128)(2,1)} custom-call(bf16[4,72,1536]{2,1,0:T(8,128)(2,1)S(1)} %pad_maximum_fusion.refs_0_, bf16[4,72,1536]{2,1,0:T(8,128)(2,1)} %collective-permute-done.17.refs_1_, bf16[12,4,72,384]{3,2,1,0:T(8,128)(2,1)S(1)} %constant_dynamic-update-slice_fusion.7.refs_2_, ...), custom_call_target="tpu_custom_call" | custom-call | tf_op jit(solution)/shard_map/assemble/pallas_call | solution.py:103
  133.4 9.4 %mlp.2 = (f32[512,576]{1,0:T(8,128)S(1)}, bf16[512,576]{1,0:T(8,128)(2,1)S(1)}, bf16[512,1536]{1,0:T(8,128)(2,1)}, bf16[512,1536]{1,0:T(8,128)(2,1)}, bf16[512,1536]{1,0:T(8,128)(2,1)}, /*index=5*/f32[512,576]{1,0:T(8,128)S(1)}) custom-call(f32[512,576]{1,0:T(8,128)S(1)} %copy-done.1, bf16[512,576]{1,0:T(8,128)(2,1)S(1)} %copy-done.32, ...), custom_call_target="tpu_custom_call" | custom-call | flops 8000000000 | bytes 4000000 | tf_op jit(solution)/shard_map/mlp/pallas_call | solution.py:236
  144.0 5.2 %project_in.3 = (bf16[512,576]{1,0:T(8,128)(2,1)S(1)}, bf16[512,576]{1,0:T(8,128)(2,1)S(1)}, bf16[512,384]{1,0:T(8,128)(2,1)S(1)}) custom-call(f32[512,576]{1,0:T(8,128)S(1)} %get-tuple-element.157.refs_0_.refs_2_, f32[8,576]{1,0:T(8,128)S(1)} %copy-done.7, bf16[4,576,1536]{2,1,0:T(8,128)(2,1)} %bitcast.171, f32[512,128]{1,0:T(8,128)S(1)} %copy-done.3, ...), custom_call_target="tpu_custom_call" | custom-call | flops 4000000000 | bytes 4000000 | tf_op jit(solution)/shard_map/project_in/pallas_call | solution.py:236
  152.9 8.4 %collective-permute-done.24.refs_3_.refs_6_ = bf16[512,384]{1,0:T(8,128)(2,1)S(1)} collective-permute-done((bf16[512,384]{1,0:T(8,128)(2,1)S(1)}, bf16[512,384]{1,0:T(8,128)(2,1)S(1)}, u32[]{:S(2)}, u32[]{:S(2)}) %collective-permute-start.24) | collective-permute-done | bytes 393248 | tf_op jit(solution)/shard_map/ppermute | solution.py:22
  161.2 8.8 %collective-permute-done.25.refs_4_.refs_7_ = bf16[512,384]{1,0:T(8,128)(2,1)S(1)} collective-permute-done((bf16[512,384]{1,0:T(8,128)(2,1)S(1)}, bf16[512,384]{1,0:T(8,128)(2,1)S(1)}, u32[]{:S(2)}, u32[]{:S(2)}) %collective-permute-start.25) | collective-permute-done | bytes 393248 | tf_op jit(solution)/shard_map/ppermute | solution.py:22
  170.1 19.0 %attend.3 = (bf16[512,576]{1,0:T(8,128)(2,1)S(1)}, f32[16,512]{1,0:T(8,128)S(1)}) custom-call(bf16[512,576]{1,0:T(8,128)(2,1)S(1)} %get-tuple-element.160.refs_0_, s32[1,512]{1,0:T(1,128)S(1)} %get-tuple-element.412.refs_1_.refs_4_, bf16[512,384]{1,0:T(8,128)(2,1)S(1)} %get-tuple-element.161.refs_2_.refs_5_, ...), custom_call_target="tpu_custom_call" | custom-call | flops 15000000512 | bytes 4000000 | tf_op jit(solution)/shard_map/attend/pallas_call | solution.py:236
  194.6 9.2 %mlp.3 = (f32[512,576]{1,0:T(8,128)S(1)}, bf16[512,576]{1,0:T(8,128)(2,1)S(1)}, bf16[512,1536]{1,0:T(8,128)(2,1)}, bf16[512,1536]{1,0:T(8,128)(2,1)}, bf16[512,1536]{1,0:T(8,128)(2,1)}, /*index=5*/f32[512,576]{1,0:T(8,128)S(1)}) custom-call(f32[512,576]{1,0:T(8,128)S(1)} %copy-done.29, bf16[512,576]{1,0:T(8,128)(2,1)S(1)} %copy-done.37, ...), custom_call_target="tpu_custom_call" | custom-call | flops 8000000000 | bytes 4000000 | tf_op jit(solution)/shard_map/mlp/pallas_call | solution.py:236
  205.0 18.8 %mlp_back.2 = (bf16[512,576]{1,0:T(8,128)(2,1)S(1)}, f32[512,576]{1,0:T(8,128)S(1)}, f32[8,576]{1,0:T(8,128)S(1)}, bf16[576,576]{1,0:T(8,128)(2,1)S(1)}, bf16[32,3,72,384]{3,2,1,0:T(8,128)(2,1)}) custom-call(f32[512,576]{1,0:T(8,128)S(1)} %fusion.12.refs_0_, f32[512,576]{1,0:T(8,128)} %copy-done.30, bf16[512,576]{1,0:T(8,128)(2,1)S(1)} %get-tuple-element.165.refs_2_, ...), custom_call_target="tpu_custom_call" | custom-call | flops 15000000512 | bytes 4000000 | tf_op jit(solution)/shard_map/mlp_back/pallas_call | solution.py:236
  228.5 16.7 %attend_back.4 = (f32[512,384]{1,0:T(8,128)S(1)}, f32[512,256]{1,0:T(8,128)S(1)}, bf16[512,256]{1,0:T(8,128)(2,1)S(1)}, bf16[512,256]{1,0:T(8,128)(2,1)S(1)}, bf16[512,256]{1,0:T(8,128)(2,1)S(1)}) custom-call(bf16[512,576]{1,0:T(8,128)(2,1)S(1)} %copy-done.45, bf16[512,576]{1,0:T(8,128)(2,1)S(1)} %copy-done.39, bf16[512,576]{1,0:T(8,128)(2,1)S(1)} %copy-done.64, ...), custom_call_target="tpu_custom_call" | custom-call | flops 14000000000 | bytes 4000000 | tf_op jit(solution)/shard_map/attend_back/pallas_call | solution.py:236
  249.6 9.6 %attend_back.5 = (f32[512,192]{1,0:T(8,128)S(1)}, f32[512,128]{1,0:T(8,128)S(1)}, bf16[512,128]{1,0:T(8,128)(2,1)S(1)}, bf16[512,128]{1,0:T(8,128)(2,1)S(1)}, bf16[512,128]{1,0:T(8,128)(2,1)S(1)}) custom-call(bf16[512,576]{1,0:T(8,128)(2,1)S(1)} %copy-done.45, bf16[512,576]{1,0:T(8,128)(2,1)S(1)} %copy-done.39, bf16[512,576]{1,0:T(8,128)(2,1)S(1)} %copy-done.65, ...), custom_call_target="tpu_custom_call" | custom-call | flops 7000000000 | bytes 4000000 | tf_op jit(solution)/shard_map/attend_back/pallas_call | solution.py:236
  274.9 8.7 %project_back.2 = (f32[512,576]{1,0:T(8,128)}, f32[8,576]{1,0:T(8,128)S(1)}, bf16[32,1,72,384]{3,2,1,0:T(8,128)(2,1)}) custom-call(f32[512,128]{1,0:T(8,128)S(1)} %copy-done.3, f32[512,128]{1,0:T(8,128)S(1)} %copy-done.5, f32[512,576]{1,0:T(8,128)} %copy-done.28, bf16[512,576]{1,0:T(8,128)(2,1)S(1)} %copy-done.43, f32[8,576]{1,0:T(8,128)S(1)} %copy-done.8, ...), custom_call_target="tpu_custom_call" | custom-call | flops 6000000000 | bytes 4000000 | tf_op jit(solution)/shard_map/project_back/pallas_call | solution.py:236
  285.0 19.2 %mlp_back.3 = (bf16[512,576]{1,0:T(8,128)(2,1)S(1)}, f32[512,576]{1,0:T(8,128)S(1)}, f32[8,576]{1,0:T(8,128)S(1)}, bf16[576,576]{1,0:T(8,128)(2,1)S(1)}, bf16[32,3,72,384]{3,2,1,0:T(8,128)(2,1)}) custom-call(f32[512,576]{1,0:T(8,128)S(1)} %copy-done.41, f32[512,576]{1,0:T(8,128)} %copy-done.27, bf16[512,576]{1,0:T(8,128)(2,1)S(1)} %copy-done.35, ...), custom_call_target="tpu_custom_call" | custom-call | flops 15000000512 | bytes 4000000 | tf_op jit(solution)/shard_map/mlp_back/pallas_call | solution.py:236
  307.4 3.2 fusion.54
  315.0 1.9 collective-permute-done.35
  318.6 3.1 collective-permute-done.37
  326.6 16.5 %attend_back.6 = (f32[512,384]{1,0:T(8,128)S(1)}, f32[512,256]{1,0:T(8,128)S(1)}, bf16[512,256]{1,0:T(8,128)(2,1)S(1)}, bf16[512,256]{1,0:T(8,128)(2,1)S(1)}, bf16[512,256]{1,0:T(8,128)(2,1)S(1)}) custom-call(bf16[512,576]{1,0:T(8,128)(2,1)S(1)} %copy-done.58, bf16[512,576]{1,0:T(8,128)(2,1)S(1)} %copy-done.33, bf16[512,576]{1,0:T(8,128)(2,1)S(1)} %copy-done.62, ...), custom_call_target="tpu_custom_call" | custom-call | flops 14000000000 | bytes 4000000 | tf_op jit(solution)/shard_map/attend_back/pallas_call | solution.py:236
  350.0 9.3 %attend_back.7 = (f32[512,192]{1,0:T(8,128)S(1)}, f32[512,128]{1,0:T(8,128)S(1)}, bf16[512,128]{1,0:T(8,128)(2,1)S(1)}, bf16[512,128]{1,0:T(8,128)(2,1)S(1)}, bf16[512,128]{1,0:T(8,128)(2,1)S(1)}) custom-call(bf16[512,576]{1,0:T(8,128)(2,1)S(1)} %copy-done.58, bf16[512,576]{1,0:T(8,128)(2,1)S(1)} %copy-done.33, bf16[512,576]{1,0:T(8,128)(2,1)S(1)} %copy-done.62, ...), custom_call_target="tpu_custom_call" | custom-call | flops 7000000000 | bytes 4000000 | tf_op jit(solution)/shard_map/attend_back/pallas_call | solution.py:236
  363.1 6.2 %collective-permute-done.41 = bf16[2,4,72,384]{3,2,1,0:T(8,128)(2,1)} collective-permute-done((bf16[2,4,72,384]{3,2,1,0:T(8,128)(2,1)}, bf16[2,4,72,384]{3,2,1,0:T(8,128)(2,1)}, u32[]{:S(2)}, u32[]{:S(2)}) %collective-permute-start.41) | collective-permute-done | bytes 442400 | tf_op jit(solution)/shard_map/ppermute | solution.py:22
  369.3 1.7 fusion.6
  372.6 8.9 %project_back.3 = (f32[512,576]{1,0:T(8,128)}, f32[8,576]{1,0:T(8,128)}, bf16[32,1,80,384]{3,2,1,0:T(8,128)(2,1)}) custom-call(f32[512,128]{1,0:T(8,128)S(1)} %copy-done.3, f32[512,128]{1,0:T(8,128)S(1)} %copy-done.5, f32[512,576]{1,0:T(8,128)} %copy-done, bf16[512,576]{1,0:T(8,128)(2,1)S(1)} %copy-done.56, f32[8,576]{1,0:T(8,128)S(1)} %copy-done.8, ...), custom_call_target="tpu_custom_call" | custom-call | flops 6000000000 | bytes 4000000 | tf_op jit(solution)/shard_map/project_back/pallas_call | solution.py:236
  383.2 1.8 collective-permute-start.43
  385.1 1.7 collective-permute-start.44
  388.6 7.1 %collective-permute-done.43 = bf16[4,72,384]{2,1,0:T(8,128)(2,1)S(1)} collective-permute-done((bf16[4,72,384]{2,1,0:T(8,128)(2,1)S(1)}, bf16[4,72,384]{2,1,0:T(8,128)(2,1)S(1)}, u32[]{:S(2)}, u32[]{:S(2)}) %collective-permute-start.43) | collective-permute-done | bytes 221216 | tf_op jit(solution)/shard_map/ppermute | solution.py:22
  395.7 8.1 %collective-permute-done.44 = bf16[4,72,384]{2,1,0:T(8,128)(2,1)S(1)} collective-permute-done((bf16[4,72,384]{2,1,0:T(8,128)(2,1)S(1)}, bf16[4,72,384]{2,1,0:T(8,128)(2,1)S(1)}, u32[]{:S(2)}, u32[]{:S(2)}) %collective-permute-start.44) | collective-permute-done | bytes 221216 | tf_op jit(solution)/shard_map/ppermute | solution.py:22
  405.7 5.2 %collective-permute-done.54 = bf16[2,2,1,80,384]{4,3,1,2,0:T(8,128)(2,1)S(1)} collective-permute-done((bf16[2,2,1,80,384]{4,3,1,2,0:T(8,128)(2,1)S(1)}, bf16[2,2,1,80,384]{4,3,1,2,0:T(8,128)(2,1)S(1)}, u32[]{:S(2)}, u32[]{:S(2)}) %collective-permute-start.54) | collective-permute-done | bytes 245792 | tf_op jit(solution)/shard_map/ppermute | solution.py:22
  421.8 12.5 %collective-permute-done.56 = bf16[2,1,80,384]{3,2,1,0:T(8,128)(2,1)S(1)} collective-permute-done((bf16[2,1,80,384]{3,2,1,0:T(8,128)(2,1)S(1)}, bf16[2,1,80,384]{3,2,1,0:T(8,128)(2,1)S(1)}, u32[]{:S(2)}, u32[]{:S(2)}) %collective-permute-start.56) | collective-permute-done | bytes 122912 | tf_op jit(solution)/shard_map/ppermute | solution.py:22
  435.7 6.2 %collective-permute-start.59 = (bf16[1,80,384]{2,1,0:T(8,128)(2,1)S(1)}, bf16[1,80,384]{2,1,0:T(8,128)(2,1)S(1)}, u32[]{:S(2)}, u32[]{:S(2)}) collective-permute-start(bf16[1,80,384]{2,1,0:T(8,128)(2,1)S(1)} %get-tuple-element.383), channel_id=1, source_target_pairs={{0,4},{1,5},{2,6},{3,7},{4,0},{5,1},{6,2},{7,3},{8,12},{9,13},{10,... | collective-permute-start | bytes 184328 | tf_op jit(solution)/shard_map/ppermute | solution.py:22
  443.0 2.7 collective-permute-done.59
  453.0 2.1 collective-permute-done.66
  (404 shorter events, 130.6 us)
Async XLA Ops:
  7.2 185.0 %all-gather.2.cloned.1.call-start = ((), (), s32[]{:S(2)}) async-start(), calls=%async_computation.1 | async-start | bytes 5971968 | tf_op jit(solution)/shard_map/all_gather | solution.py:133
  10.8 42.5 %collective-permute-start.11 = (bf16[4,72,384]{2,1,0:T(8,128)(2,1)S(1)}, bf16[4,72,384]{2,1,0:T(8,128)(2,1)}, u32[]{:S(2)}, u32[]{:S(2)}) collective-permute-start(bf16[4,72,384]{2,1,0:T(8,128)(2,1)S(1)} %constant_dynamic-slice_fusion.1), channel_id=1, source_target_pairs={{0,2},{1,3},{2,0},{3,1},{4,6},{5,7},{6,4},{7,5},{8,10},{9,11},{10,... | collective-permute-start | bytes 663560 | tf_op jit(solution)/shard_map/ppermute | solution.py:22
  13.8 40.0 %collective-permute-start.12 = (bf16[4,72,384]{2,1,0:T(8,128)(2,1)S(1)}, bf16[4,72,384]{2,1,0:T(8,128)(2,1)}, u32[]{:S(2)}, u32[]{:S(2)}) collective-permute-start(bf16[4,72,384]{2,1,0:T(8,128)(2,1)S(1)} %constant_dynamic-slice_fusion.1), channel_id=1, source_target_pairs={{0,4},{1,5},{2,6},{3,7},{4,0},{5,1},{6,2},{7,3},{8,12},{9,13},{10,... | collective-permute-start | bytes 663560 | tf_op jit(solution)/shard_map/ppermute | solution.py:22
  18.5 17.5 %collective-permute-start.4 = (bf16[1,80,384]{2,1,0:T(8,128)(2,1)}, bf16[1,80,384]{2,1,0:T(8,128)(2,1)S(1)}, u32[]{:S(2)}, u32[]{:S(2)}) collective-permute-start(bf16[1,80,384]{2,1,0:T(8,128)(2,1)} %fusion.39), channel_id=1, source_target_pairs={{0,4},{1,5},{2,6},{3,7},{4,0},{5,1},{6,2},{7,3},{8,12},{9,13},{10,... | collective-permute-start | bytes 184328 | tf_op jit(solution)/shard_map/ppermute | solution.py:22
  18.5 17.5 %collective-permute-start.5 = (bf16[1,80,384]{2,1,0:T(8,128)(2,1)}, bf16[1,80,384]{2,1,0:T(8,128)(2,1)S(1)}, u32[]{:S(2)}, u32[]{:S(2)}) collective-permute-start(bf16[1,80,384]{2,1,0:T(8,128)(2,1)} %fusion.39), channel_id=1, source_target_pairs={{0,6},{1,7},{2,4},{3,5},{4,2},{5,3},{6,0},{7,1},{8,14},{9,15},{10,... | collective-permute-start | bytes 184328 | tf_op jit(solution)/shard_map/ppermute | solution.py:22
  25.9 27.9 %collective-permute-start.13 = (bf16[4,72,384]{2,1,0:T(8,128)(2,1)S(1)}, bf16[4,72,384]{2,1,0:T(8,128)(2,1)S(1)}, u32[]{:S(2)}, u32[]{:S(2)}) collective-permute-start(bf16[4,72,384]{2,1,0:T(8,128)(2,1)S(1)} %constant_dynamic-slice_fusion.1), channel_id=1, source_target_pairs={{0,6},{1,7},{2,4},{3,5},{4,2},{5,3},{6,0},{7,1},{8,14},{9,15},{10,... | collective-permute-start | bytes 663560 | tf_op jit(solution)/shard_map/ppermute | solution.py:22
  43.3 19.5 %collective-permute-start.2 = (bf16[1,80,1536]{2,1,0:T(8,128)(2,1)S(1)}, bf16[1,80,1536]{2,1,0:T(8,128)(2,1)}, u32[]{:S(2)}, u32[]{:S(2)}) collective-permute-start(bf16[1,80,1536]{2,1,0:T(8,128)(2,1)S(1)} %fusion.16.refs_0_), channel_id=1, source_target_pairs={{0,1},{1,0},{2,3},{3,2},{4,5},{5,4},{6,7},{7,6},{8,9},{9,8},{10,11... | collective-permute-start | bytes 737288 | tf_op jit(solution)/shard_map/ppermute | solution.py:22
  53.3 8.4 %collective-permute-start.1 = (bf16[1,256,576]{2,1,0:T(8,128)(2,1)}, bf16[1,256,576]{2,1,0:T(8,128)(2,1)}, u32[]{:S(2)}, u32[]{:S(2)}) collective-permute-start(bf16[1,256,576]{2,1,0:T(8,128)(2,1)} %copy.51), channel_id=1, source_target_pairs={{0,24},{8,16},{16,8},{24,0},{1,25},{9,17},{17,9},{25,1},{2,26},{10... | collective-permute-start | bytes 884744 | tf_op jit(solution)/shard_map/ppermute | solution.py:22
  53.8 9.0 %collective-permute-start.10 = (bf16[12,1,80,384]{3,2,1,0:T(8,128)(2,1)S(1)}, bf16[12,1,80,384]{3,2,1,0:T(8,128)(2,1)}, u32[]{:S(2)}, u32[]{:S(2)}) collective-permute-start(bf16[12,1,80,384]{3,2,1,0:T(8,128)(2,1)S(1)} %constant_dynamic-update-slice_fusion.refs_2_), channel_id=1, source_target_pairs={{0,1},{1,0},{2,3},{3,2},{4,5},{5,4},{6,7},{7,6},{8,9},{9,8},{10,11... | collective-permute-start | bytes 2211848 | tf_op jit(solution)/shard_map/ppermute | solution.py:22
  55.8 250.3 %reduce-scatter.2.cloned.1.call-start = ((), (), s32[]{:S(2)}) async-start(), calls=%async_computation.2 | async-start | bytes 5971968 | tf_op jit(solution)/shard_map/reduce_scatter | solution.py:963
  72.6 12.1 %collective-permute-start.14 = (bf16[512,384]{1,0:T(8,128)(2,1)S(1)}, bf16[512,384]{1,0:T(8,128)(2,1)S(1)}, u32[]{:S(2)}, u32[]{:S(2)}) collective-permute-start(bf16[512,384]{1,0:T(8,128)(2,1)S(1)} %get-tuple-element.151.refs_2_.refs_5_), channel_id=1, source_target_pairs={{0,8},{8,0},{16,24},{24,16},{1,9},{9,1},{17,25},{25,17},{2,10},{10... | collective-permute-start | bytes 1179656 | tf_op jit(solution)/shard_map/ppermute | solution.py:22
  73.2 20.5 %collective-permute-start.15 = (bf16[512,384]{1,0:T(8,128)(2,1)S(1)}, bf16[512,384]{1,0:T(8,128)(2,1)S(1)}, u32[]{:S(2)}, u32[]{:S(2)}) collective-permute-start(bf16[512,384]{1,0:T(8,128)(2,1)S(1)} %get-tuple-element.151.refs_2_.refs_5_), channel_id=1, source_target_pairs={{0,16},{8,24},{16,0},{24,8},{1,17},{9,25},{17,1},{25,9},{2,18},{10... | collective-permute-start | bytes 1179656 | tf_op jit(solution)/shard_map/ppermute | solution.py:22
  73.9 19.8 %collective-permute-start.16 = (bf16[512,384]{1,0:T(8,128)(2,1)S(1)}, bf16[512,384]{1,0:T(8,128)(2,1)S(1)}, u32[]{:S(2)}, u32[]{:S(2)}) collective-permute-start(bf16[512,384]{1,0:T(8,128)(2,1)S(1)} %get-tuple-element.151.refs_2_.refs_5_), channel_id=1, source_target_pairs={{0,24},{8,16},{16,8},{24,0},{1,25},{9,17},{17,9},{25,1},{2,26},{10... | collective-permute-start | bytes 1179656 | tf_op jit(solution)/shard_map/ppermute | solution.py:22
  76.2 36.2 %collective-permute-start.18 = (bf16[3,4,72,384]{3,2,1,0:T(8,128)(2,1)S(1)}, bf16[3,4,72,384]{3,2,1,0:T(8,128)(2,1)S(1)}, u32[]{:S(2)}, u32[]{:S(2)}) collective-permute-start(bf16[3,4,72,384]{3,2,1,0:T(8,128)(2,1)S(1)} %copy-done.69), channel_id=1, source_target_pairs={{0,8},{8,0},{16,24},{24,16},{1,9},{9,1},{17,25},{25,17},{2,10},{10... | collective-permute-start | bytes 1990664 | tf_op jit(solution)/shard_map/ppermute | solution.py:22
  76.7 35.7 %collective-permute-start.19 = (bf16[3,4,72,384]{3,2,1,0:T(8,128)(2,1)S(1)}, bf16[3,4,72,384]{3,2,1,0:T(8,128)(2,1)S(1)}, u32[]{:S(2)}, u32[]{:S(2)}) collective-permute-start(bf16[3,4,72,384]{3,2,1,0:T(8,128)(2,1)S(1)} %copy-done.69), channel_id=1, source_target_pairs={{0,16},{8,24},{16,0},{24,8},{1,17},{9,25},{17,1},{25,9},{2,18},{10... | collective-permute-start | bytes 1990664 | tf_op jit(solution)/shard_map/ppermute | solution.py:22
  125.6 27.2 %collective-permute-start.23 = (bf16[1,256,576]{2,1,0:T(8,128)(2,1)S(1)}, bf16[1,256,576]{2,1,0:T(8,128)(2,1)S(1)}, u32[]{:S(2)}, u32[]{:S(2)}) collective-permute-start(bf16[1,256,576]{2,1,0:T(8,128)(2,1)S(1)} %get-tuple-element.358), channel_id=1, source_target_pairs={{0,24},{8,16},{16,8},{24,0},{1,25},{9,17},{17,9},{25,1},{2,26},{10... | collective-permute-start | bytes 884744 | tf_op jit(solution)/shard_map/ppermute | solution.py:22
  149.2 12.0 %collective-permute-start.24 = (bf16[512,384]{1,0:T(8,128)(2,1)S(1)}, bf16[512,384]{1,0:T(8,128)(2,1)S(1)}, u32[]{:S(2)}, u32[]{:S(2)}) collective-permute-start(bf16[512,384]{1,0:T(8,128)(2,1)S(1)} %get-tuple-element.161.refs_2_.refs_5_), channel_id=1, source_target_pairs={{0,8},{8,0},{16,24},{24,16},{1,9},{9,1},{17,25},{25,17},{2,10},{10... | collective-permute-start | bytes 1179656 | tf_op jit(solution)/shard_map/ppermute | solution.py:22
  150.7 19.3 %collective-permute-start.25 = (bf16[512,384]{1,0:T(8,128)(2,1)S(1)}, bf16[512,384]{1,0:T(8,128)(2,1)S(1)}, u32[]{:S(2)}, u32[]{:S(2)}) collective-permute-start(bf16[512,384]{1,0:T(8,128)(2,1)S(1)} %get-tuple-element.161.refs_2_.refs_5_), channel_id=1, source_target_pairs={{0,16},{8,24},{16,0},{24,8},{1,17},{9,25},{17,1},{25,9},{2,18},{10... | collective-permute-start | bytes 1179656 | tf_op jit(solution)/shard_map/ppermute | solution.py:22
  151.3 18.8 %collective-permute-start.26 = (bf16[512,384]{1,0:T(8,128)(2,1)S(1)}, bf16[512,384]{1,0:T(8,128)(2,1)S(1)}, u32[]{:S(2)}, u32[]{:S(2)}) collective-permute-start(bf16[512,384]{1,0:T(8,128)(2,1)S(1)} %get-tuple-element.161.refs_2_.refs_5_), channel_id=1, source_target_pairs={{0,24},{8,16},{16,8},{24,0},{1,25},{9,17},{17,9},{25,1},{2,26},{10... | collective-permute-start | bytes 1179656 | tf_op jit(solution)/shard_map/ppermute | solution.py:22
  226.8 37.5 %collective-permute-start.33 = (bf16[1,256,576]{2,1,0:T(8,128)(2,1)S(1)}, bf16[1,256,576]{2,1,0:T(8,128)(2,1)S(1)}, u32[]{:S(2)}, u32[]{:S(2)}) collective-permute-start(bf16[1,256,576]{2,1,0:T(8,128)(2,1)S(1)} %get-tuple-element.356), channel_id=1, source_target_pairs={{0,24},{8,16},{16,8},{24,0},{1,25},{9,17},{17,9},{25,1},{2,26},{10... | collective-permute-start | bytes 884744 | tf_op jit(solution)/shard_map/ppermute | solution.py:22
  246.1 14.6 %collective-permute-start.27 = (bf16[512,256]{1,0:T(8,128)(2,1)S(1)}, bf16[512,256]{1,0:T(8,128)(2,1)S(1)}, u32[]{:S(2)}, u32[]{:S(2)}) collective-permute-start(bf16[512,256]{1,0:T(8,128)(2,1)S(1)} %get-tuple-element.185), channel_id=1, source_target_pairs={{0,8},{8,0},{16,24},{24,16},{1,9},{9,1},{17,25},{25,17},{2,10},{10... | collective-permute-start | bytes 786440 | tf_op jit(solution)/shard_map/ppermute | solution.py:22
  246.7 14.1 %collective-permute-start.28 = (bf16[512,256]{1,0:T(8,128)(2,1)S(1)}, bf16[512,256]{1,0:T(8,128)(2,1)S(1)}, u32[]{:S(2)}, u32[]{:S(2)}) collective-permute-start(bf16[512,256]{1,0:T(8,128)(2,1)S(1)} %get-tuple-element.186), channel_id=1, source_target_pairs={{0,16},{8,24},{16,0},{24,8},{1,17},{9,25},{17,1},{25,9},{2,18},{10... | collective-permute-start | bytes 786440 | tf_op jit(solution)/shard_map/ppermute | solution.py:22
  248.0 12.7 %collective-permute-start.29 = (bf16[512,256]{1,0:T(8,128)(2,1)S(1)}, bf16[512,256]{1,0:T(8,128)(2,1)S(1)}, u32[]{:S(2)}, u32[]{:S(2)}) collective-permute-start(bf16[512,256]{1,0:T(8,128)(2,1)S(1)} %get-tuple-element.187), channel_id=1, source_target_pairs={{0,24},{8,16},{16,8},{24,0},{1,25},{9,17},{17,9},{25,1},{2,26},{10... | collective-permute-start | bytes 786440 | tf_op jit(solution)/shard_map/ppermute | solution.py:22
  310.6 11.9 %collective-permute-start.34 = (bf16[4,4,3,72,384]{4,3,2,1,0:T(8,128)(2,1)S(1)}, bf16[4,4,3,72,384]{4,3,2,1,0:T(8,128)(2,1)S(1)}, u32[]{:S(2)}, u32[]{:S(2)}) collective-permute-start(bf16[4,4,3,72,384]{4,3,2,1,0:T(8,128)(2,1)S(1)} %bitcast.179), channel_id=1, source_target_pairs={{0,1},{1,0},{2,3},{3,2},{4,5},{5,4},{6,7},{7,6},{8,9},{9,8},{10,11... | collective-permute-start | bytes 7962632 | tf_op jit(solution)/shard_map/ppermute | solution.py:22
  312.3 9.5 %collective-permute-start.37 = (bf16[3,72,384]{2,1,0:T(8,128)(2,1)S(1)}, bf16[3,72,384]{2,1,0:T(8,128)(2,1)S(1)}, u32[]{:S(2)}, u32[]{:S(2)}) collective-permute-start(bf16[3,72,384]{2,1,0:T(8,128)(2,1)S(1)} %get-tuple-element.216), channel_id=1, source_target_pairs={{0,16},{8,24},{16,0},{24,8},{1,17},{9,25},{17,1},{25,9},{2,18},{10... | collective-permute-start | bytes 497672 | tf_op jit(solution)/shard_map/ppermute | solution.py:22
  324.5 22.2 %collective-permute-start.39 = (bf16[2,2,4,72,384]{4,3,2,1,0:T(8,128)(2,1)S(1)}, bf16[2,2,4,72,384]{4,3,2,1,0:T(8,128)(2,1)S(1)}, u32[]{:S(2)}, u32[]{:S(2)}) collective-permute-start(bf16[2,2,4,72,384]{4,3,2,1,0:T(8,128)(2,1)S(1)} %pad_maximum_fusion.1), channel_id=1, source_target_pairs={{0,8},{8,0},{16,24},{24,16},{1,9},{9,1},{17,25},{25,17},{2,10},{10... | collective-permute-start | bytes 2654216 | tf_op jit(solution)/shard_map/ppermute | solution.py:22
  325.8 21.3 %collective-permute-start.40 = (bf16[2,2,4,72,384]{4,3,2,1,0:T(8,128)(2,1)S(1)}, bf16[2,2,4,72,384]{4,3,2,1,0:T(8,128)(2,1)S(1)}, u32[]{:S(2)}, u32[]{:S(2)}) collective-permute-start(bf16[2,2,4,72,384]{4,3,2,1,0:T(8,128)(2,1)S(1)} %stack.91), channel_id=1, source_target_pairs={{0,16},{8,24},{16,0},{24,8},{1,17},{9,25},{17,1},{25,9},{2,18},{10... | collective-permute-start | bytes 2654216 | tf_op jit(solution)/shard_map/ppermute | solution.py:22
  343.1 16.2 %collective-permute-start.46 = (bf16[512,256]{1,0:T(8,128)(2,1)S(1)}, bf16[512,256]{1,0:T(8,128)(2,1)S(1)}, u32[]{:S(2)}, u32[]{:S(2)}) collective-permute-start(bf16[512,256]{1,0:T(8,128)(2,1)S(1)} %get-tuple-element.249), channel_id=1, source_target_pairs={{0,8},{8,0},{16,24},{24,16},{1,9},{9,1},{17,25},{25,17},{2,10},{10... | collective-permute-start | bytes 786440 | tf_op jit(solution)/shard_map/ppermute | solution.py:22
  344.7 14.9 %collective-permute-start.47 = (bf16[512,256]{1,0:T(8,128)(2,1)S(1)}, bf16[512,256]{1,0:T(8,128)(2,1)S(1)}, u32[]{:S(2)}, u32[]{:S(2)}) collective-permute-start(bf16[512,256]{1,0:T(8,128)(2,1)S(1)} %get-tuple-element.250), channel_id=1, source_target_pairs={{0,16},{8,24},{16,0},{24,8},{1,17},{9,25},{17,1},{25,9},{2,18},{10... | collective-permute-start | bytes 786440 | tf_op jit(solution)/shard_map/ppermute | solution.py:22
  345.2 14.4 %collective-permute-start.48 = (bf16[512,256]{1,0:T(8,128)(2,1)S(1)}, bf16[512,256]{1,0:T(8,128)(2,1)S(1)}, u32[]{:S(2)}, u32[]{:S(2)}) collective-permute-start(bf16[512,256]{1,0:T(8,128)(2,1)S(1)} %get-tuple-element.251), channel_id=1, source_target_pairs={{0,24},{8,16},{16,8},{24,0},{1,25},{9,17},{17,9},{25,1},{2,26},{10... | collective-permute-start | bytes 786440 | tf_op jit(solution)/shard_map/ppermute | solution.py:22
  348.4 20.8 %collective-permute-start.41 = (bf16[2,4,72,384]{3,2,1,0:T(8,128)(2,1)}, bf16[2,4,72,384]{3,2,1,0:T(8,128)(2,1)}, u32[]{:S(2)}, u32[]{:S(2)}) collective-permute-start(bf16[2,4,72,384]{3,2,1,0:T(8,128)(2,1)} %get-tuple-element.230), channel_id=1, source_target_pairs={{0,16},{8,24},{16,0},{24,8},{1,17},{9,25},{17,1},{25,9},{2,18},{10... | collective-permute-start | bytes 1327112 | tf_op jit(solution)/shard_map/ppermute | solution.py:22
  349.2 20.0 %collective-permute-start.42 = (bf16[2,4,72,384]{3,2,1,0:T(8,128)(2,1)S(1)}, bf16[2,4,72,384]{3,2,1,0:T(8,128)(2,1)}, u32[]{:S(2)}, u32[]{:S(2)}) collective-permute-start(bf16[2,4,72,384]{3,2,1,0:T(8,128)(2,1)S(1)} %get-tuple-element.231), channel_id=1, source_target_pairs={{0,8},{8,0},{16,24},{24,16},{1,9},{9,1},{17,25},{25,17},{2,10},{10... | collective-permute-start | bytes 1327112 | tf_op jit(solution)/shard_map/ppermute | solution.py:22
  359.6 11.5 %collective-permute-start.49 = (bf16[512,128]{1,0:T(8,128)(2,1)S(1)}, bf16[512,128]{1,0:T(8,128)(2,1)S(1)}, u32[]{:S(2)}, u32[]{:S(2)}) collective-permute-start(bf16[512,128]{1,0:T(8,128)(2,1)S(1)} %get-tuple-element.261), channel_id=1, source_target_pairs={{0,8},{8,0},{16,24},{24,16},{1,9},{9,1},{17,25},{25,17},{2,10},{10... | collective-permute-start | bytes 393224 | tf_op jit(solution)/shard_map/ppermute | solution.py:22
  360.7 11.9 %collective-permute-start.50 = (bf16[512,128]{1,0:T(8,128)(2,1)S(1)}, bf16[512,128]{1,0:T(8,128)(2,1)S(1)}, u32[]{:S(2)}, u32[]{:S(2)}) collective-permute-start(bf16[512,128]{1,0:T(8,128)(2,1)S(1)} %get-tuple-element.262), channel_id=1, source_target_pairs={{0,16},{8,24},{16,0},{24,8},{1,17},{9,25},{17,1},{25,9},{2,18},{10... | collective-permute-start | bytes 393224 | tf_op jit(solution)/shard_map/ppermute | solution.py:22
  361.9 10.6 %collective-permute-start.51 = (bf16[512,128]{1,0:T(8,128)(2,1)S(1)}, bf16[512,128]{1,0:T(8,128)(2,1)S(1)}, u32[]{:S(2)}, u32[]{:S(2)}) collective-permute-start(bf16[512,128]{1,0:T(8,128)(2,1)S(1)} %get-tuple-element.263), channel_id=1, source_target_pairs={{0,24},{8,16},{16,8},{24,0},{1,25},{9,17},{17,9},{25,1},{2,26},{10... | collective-permute-start | bytes 393224 | tf_op jit(solution)/shard_map/ppermute | solution.py:22
  383.2 12.5 %collective-permute-start.43 = (bf16[4,72,384]{2,1,0:T(8,128)(2,1)S(1)}, bf16[4,72,384]{2,1,0:T(8,128)(2,1)S(1)}, u32[]{:S(2)}, u32[]{:S(2)}) collective-permute-start(bf16[4,72,384]{2,1,0:T(8,128)(2,1)S(1)} %fusion.25), channel_id=1, source_target_pairs={{0,2},{1,3},{2,0},{3,1},{4,6},{5,7},{6,4},{7,5},{8,10},{9,11},{10,... | collective-permute-start | bytes 663560 | tf_op jit(solution)/shard_map/ppermute | solution.py:22
  385.1 18.7 %collective-permute-start.44 = (bf16[4,72,384]{2,1,0:T(8,128)(2,1)S(1)}, bf16[4,72,384]{2,1,0:T(8,128)(2,1)S(1)}, u32[]{:S(2)}, u32[]{:S(2)}) collective-permute-start(bf16[4,72,384]{2,1,0:T(8,128)(2,1)S(1)} %get-tuple-element.237), channel_id=1, source_target_pairs={{0,4},{1,5},{2,6},{3,7},{4,0},{5,1},{6,2},{7,3},{8,12},{9,13},{10,... | collective-permute-start | bytes 663560 | tf_op jit(solution)/shard_map/ppermute | solution.py:22
  386.8 17.0 %collective-permute-start.45 = (bf16[4,72,384]{2,1,0:T(8,128)(2,1)S(1)}, bf16[4,72,384]{2,1,0:T(8,128)(2,1)S(1)}, u32[]{:S(2)}, u32[]{:S(2)}) collective-permute-start(bf16[4,72,384]{2,1,0:T(8,128)(2,1)S(1)} %get-tuple-element.238), channel_id=1, source_target_pairs={{0,6},{1,7},{2,4},{3,5},{4,2},{5,3},{6,0},{7,1},{8,14},{9,15},{10,... | collective-permute-start | bytes 663560 | tf_op jit(solution)/shard_map/ppermute | solution.py:22
  411.3 9.7 %collective-permute-start.58 = (bf16[2,1,80,384]{3,2,0,1:T(8,128)(2,1)S(1)}, bf16[2,1,80,384]{3,2,0,1:T(8,128)(2,1)S(1)}, u32[]{:S(2)}, u32[]{:S(2)}) collective-permute-start(bf16[2,1,80,384]{3,2,0,1:T(8,128)(2,1)S(1)} %get-tuple-element.279), channel_id=1, source_target_pairs={{0,8},{8,0},{16,24},{24,16},{1,9},{9,1},{17,25},{25,17},{2,10},{10... | collective-permute-start | bytes 368648 | tf_op jit(solution)/shard_map/ppermute | solution.py:22
  416.2 44.4 %collective-permute-start.53 = (bf16[256,576]{1,0:T(8,128)(2,1)S(1)}, bf16[256,576]{1,0:T(8,128)(2,1)S(1)}, u32[]{:S(2)}, u32[]{:S(2)}) collective-permute-start(bf16[256,576]{1,0:T(8,128)(2,1)S(1)} %slice.821), channel_id=1, source_target_pairs={{0,24},{8,16},{16,8},{24,0},{1,25},{9,17},{17,9},{25,1},{2,26},{10... | collective-permute-start | bytes 884744 | tf_op jit(solution)/shard_map/ppermute | solution.py:22
  417.5 18.2 %collective-permute-start.67 = (bf16[3,72,384]{2,1,0:T(8,128)(2,1)S(1)}, bf16[3,72,384]{2,1,0:T(8,128)(2,1)S(1)}, u32[]{:S(2)}, u32[]{:S(2)}) collective-permute-start(bf16[3,72,384]{2,1,0:T(8,128)(2,1)S(1)} %copy-done.72), channel_id=1, source_target_pairs={{0,24},{8,16},{16,8},{24,0},{1,25},{9,17},{17,9},{25,1},{2,26},{10... | collective-permute-start | bytes 497672 | tf_op jit(solution)/shard_map/ppermute | solution.py:22
  419.2 22.8 %collective-permute-start.68 = (bf16[3,72,384]{2,1,0:T(8,128)(2,1)S(1)}, bf16[3,72,384]{2,1,0:T(8,128)(2,1)S(1)}, u32[]{:S(2)}, u32[]{:S(2)}) collective-permute-start(bf16[3,72,384]{2,1,0:T(8,128)(2,1)S(1)} %copy-done.72), channel_id=1, source_target_pairs={{0,16},{8,24},{16,0},{24,8},{1,17},{9,25},{17,1},{25,9},{2,18},{10... | collective-permute-start | bytes 497672 | tf_op jit(solution)/shard_map/ppermute | solution.py:22
  419.7 23.0 %collective-permute-start.69 = (bf16[3,72,384]{2,1,0:T(8,128)(2,1)S(1)}, bf16[3,72,384]{2,1,0:T(8,128)(2,1)S(1)}, u32[]{:S(2)}, u32[]{:S(2)}) collective-permute-start(bf16[3,72,384]{2,1,0:T(8,128)(2,1)S(1)} %copy-done.72), channel_id=1, source_target_pairs={{0,8},{8,0},{16,24},{24,16},{1,9},{9,1},{17,25},{25,17},{2,10},{10... | collective-permute-start | bytes 497672 | tf_op jit(solution)/shard_map/ppermute | solution.py:22
  421.0 13.3 %collective-permute-start.56 = (bf16[2,1,80,384]{3,2,1,0:T(8,128)(2,1)S(1)}, bf16[2,1,80,384]{3,2,1,0:T(8,128)(2,1)S(1)}, u32[]{:S(2)}, u32[]{:S(2)}) collective-permute-start(bf16[2,1,80,384]{3,2,1,0:T(8,128)(2,1)S(1)} %get-tuple-element.278), channel_id=1, source_target_pairs={{0,16},{8,24},{16,0},{24,8},{1,17},{9,25},{17,1},{25,9},{2,18},{10... | collective-permute-start | bytes 368648 | tf_op jit(solution)/shard_map/ppermute | solution.py:22
  434.4 16.0 %collective-permute-start.64 = (bf16[4,72,384]{2,1,0:T(8,128)(2,1)S(1)}, bf16[4,72,384]{2,1,0:T(8,128)(2,1)S(1)}, u32[]{:S(2)}, u32[]{:S(2)}) collective-permute-start(bf16[4,72,384]{2,1,0:T(8,128)(2,1)S(1)} %add_convert_fusion), channel_id=1, source_target_pairs={{0,24},{8,16},{16,8},{24,0},{1,25},{9,17},{17,9},{25,1},{2,26},{10... | collective-permute-start | bytes 663560 | tf_op jit(solution)/shard_map/ppermute | solution.py:22
  435.7 10.0 %collective-permute-start.59 = (bf16[1,80,384]{2,1,0:T(8,128)(2,1)S(1)}, bf16[1,80,384]{2,1,0:T(8,128)(2,1)S(1)}, u32[]{:S(2)}, u32[]{:S(2)}) collective-permute-start(bf16[1,80,384]{2,1,0:T(8,128)(2,1)S(1)} %get-tuple-element.383), channel_id=1, source_target_pairs={{0,4},{1,5},{2,6},{3,7},{4,0},{5,1},{6,2},{7,3},{8,12},{9,13},{10,... | collective-permute-start | bytes 184328 | tf_op jit(solution)/shard_map/ppermute | solution.py:22
  448.7 9.9 %collective-permute-start.61 = (bf16[1,80,384]{2,1,0:T(8,128)(2,1)S(1)}, bf16[1,80,384]{2,1,0:T(8,128)(2,1)S(1)}, u32[]{:S(2)}, u32[]{:S(2)}) collective-permute-start(bf16[1,80,384]{2,1,0:T(8,128)(2,1)S(1)} %fusion.35), channel_id=1, source_target_pairs={{0,24},{8,16},{16,8},{24,0},{1,25},{9,17},{17,9},{25,1},{2,26},{10... | collective-permute-start | bytes 184328 | tf_op jit(solution)/shard_map/ppermute | solution.py:22
  450.4 8.3 %collective-permute-start.62 = (bf16[1,80,384]{2,1,0:T(8,128)(2,1)S(1)}, bf16[1,80,384]{2,1,0:T(8,128)(2,1)S(1)}, u32[]{:S(2)}, u32[]{:S(2)}) collective-permute-start(bf16[1,80,384]{2,1,0:T(8,128)(2,1)S(1)} %fusion.35), channel_id=1, source_target_pairs={{0,16},{8,24},{16,0},{24,8},{1,17},{9,25},{17,1},{25,9},{2,18},{10... | collective-permute-start | bytes 184328 | tf_op jit(solution)/shard_map/ppermute | solution.py:22
  (105 other events, 713.7 us)
Sparse Core Ops, SparseCore 0:
  56.0 57.7 all-gather.1
  226.7 60.3 reduce-scatter.1

commit v5 on v4

--- a/solution.py
+++ b/solution.py
@@ -875,7 +875,7 @@
         own_second = jnp.stack([*mlp_own[0], attn_own[1]])
         own_third = jnp.stack(mlp_own[1])
         first_line = gather_line(own_first)
-        second_line = gather_line(own_second)
+        second_line = gather_line(tied(own_second, first_line))
         third = gather_plain(tied(own_third, second_line))
         first_sides = gather_sides(first_line)
         first_flip = flip(own_first, "fsdp", 1)
@@ -1007,17 +1007,18 @@
         )
         if fast and i == 0:
             sums, sends = reduce_begin(reduce_start(attn_grad))
-            line, sends, grad, early = lax.optimization_barrier((line, sends, grad, early))
             sides = reduce_sides(sends)
-            rest = low(reduce_end(line))
+            line = tied(line, sends)
             sums, sends = reduce_middle(sums, sides)
-            sends, rest, early = lax.optimization_barrier((sends, rest, early))
             across = reduce_across(sends)
-            rest = spread_fast(rest)
+            across, early = lax.optimization_barrier((across, early))
+            far = flip(low(grad[half:]), "ctx", slots - 1)
+            line, across, far = lax.optimization_barrier((line, across, far))
+            rest = spread_fast(low(reduce_end(line)))
             sums, sends = reduce_turn(sums, across)
-            last = spread_fast(reduce_end((sums, *reduce_line(sends))))
+            last = reduce_end((sums, *reduce_line(sends)))
+            last = spread_fast(last)
             early = spread_fast(early)
-            far = tied(flip(low(grad[half:]), "ctx", slots - 1), last)
             all_gains = lax.dynamic_slice_in_dim(last[0, rows:], shard * rows, rows, axis=1)
             order = (3, 0, 1, 2)
             all_gains = jnp.stack([all_gains[v] for v in order])

time: 475 us -> 456 us (0.960)
  waiting for transfers between devices: 119 us -> 94.7 us
  local copies, waits for them, and re-layouts: 49.1 us -> 55.4 us
    ppermute x70, waiting for transfers between devices: 119 us -> 94.6 us  [flip(): return lax.ppermute(block, axis, route)]
    unnamed x176 -> x224, local copies, waits for them, and re-layouts: 32.3 us -> 32.5 us
  transfers between devices with their start and end apart: 72 -> 72, of which waited for: 31 -> 31; matrix products, arithmetic and copies ran while one was open for 6% -> 7% of each run, Pallas kernels for 31% -> 32%
where the time goes in v5:
time: 456 us; the launch traced here: 451 us
  Pallas kernels  181 us (40%)
  waiting for transfers between devices  94.7 us (21%)
  starting transfers between devices  82.3 us (18%)
  local copies, waits for them, and re-layouts  55.4 us (12%)
  other arithmetic  21.9 us (5%)
  between operations  16.1 us (4%)
    pallas_call x14, Pallas kernels, run_kernel(): pl.pallas_call(kernel, out_shape=tuple(outputs), in_specs=[pl.BlockSpec(m...  173 us
    ppermute x70, waiting for transfers between devices, flip(): return lax.ppermute(block, axis, route)  94.6 us
    ppermute x70, starting transfers between devices, flip(): return lax.ppermute(block, axis, route)  82.2 us
    unnamed x224, local copies, waits for them, and re-layouts  32.5 us
  transfers between devices with their start and end apart: 72, of which 31 were waited for; matrix products, arithmetic and copies ran while one was open for 7% of the time, Pallas kernels for 32%

profile of v5, /device:TPU:0, one launch (start us, length us, event | category | flops | bytes accessed | tf_op | source)
XLA Modules:
  0.0 450.9 jit_solution(8024158440875572068)
XLA Ops:
  11.4 3.0 collective-permute-start.3
  14.4 2.6 collective-permute-start.4
  29.4 3.5 collective-permute-start.12
  36.0 3.4 collective-permute-done.6
  41.3 3.0 collective-permute-done.8
  45.9 2.7 collective-permute-done.9
  48.6 2.5 collective-permute-start
  55.3 3.9 collective-permute-done.1
  60.4 2.2 assemble.2
  66.5 3.8 project_in.2
  71.3 2.6 collective-permute-start.16
  74.8 7.6 %collective-permute-done.14.refs_3_.refs_6_ = bf16[512,384]{1,0:T(8,128)(2,1)S(1)} collective-permute-done((bf16[512,384]{1,0:T(8,128)(2,1)S(1)}, bf16[512,384]{1,0:T(8,128)(2,1)S(1)}, u32[]{:S(2)}, u32[]{:S(2)}) %collective-permute-start.14) | collective-permute-done | bytes 393248 | tf_op jit(solution)/shard_map/ppermute | solution.py:22
  82.5 8.9 %collective-permute-done.15.refs_4_.refs_7_ = bf16[512,384]{1,0:T(8,128)(2,1)S(1)} collective-permute-done((bf16[512,384]{1,0:T(8,128)(2,1)S(1)}, bf16[512,384]{1,0:T(8,128)(2,1)S(1)}, u32[]{:S(2)}, u32[]{:S(2)}) %collective-permute-start.15) | collective-permute-done | bytes 393248 | tf_op jit(solution)/shard_map/ppermute | solution.py:22
  91.4 18.6 %attend.2 = (bf16[512,576]{1,0:T(8,128)(2,1)S(1)}, f32[16,512]{1,0:T(8,128)S(1)}) custom-call(bf16[512,576]{1,0:T(8,128)(2,1)S(1)} %get-tuple-element.151.refs_0_, s32[1,512]{1,0:T(1,128)S(1)} %get-tuple-element.416.refs_1_.refs_4_, bf16[512,384]{1,0:T(8,128)(2,1)S(1)} %get-tuple-element.154.refs_2_.refs_5_, ...), custom_call_target="tpu_custom_call" | custom-call | flops 15000000512 | bytes 4000000 | tf_op jit(solution)/shard_map/attend/pallas_call | solution.py:236
  113.3 5.9 %collective-permute-done.20 = bf16[2,4,72,384]{3,2,1,0:T(8,128)(2,1)S(1)} collective-permute-done((bf16[2,4,72,384]{3,2,1,0:T(8,128)(2,1)S(1)}, bf16[2,4,72,384]{3,2,1,0:T(8,128)(2,1)S(1)}, u32[]{:S(2)}, u32[]{:S(2)}) %collective-permute-start.20) | collective-permute-done | bytes 442400 | tf_op jit(solution)/shard_map/ppermute | solution.py:22
  119.9 2.1 copy.40
  125.8 5.3 %assemble.3.refs_6_.refs_11_ = bf16[4,8,72,1536]{3,2,1,0:T(8,128)(2,1)} custom-call(bf16[4,72,1536]{2,1,0:T(8,128)(2,1)S(1)} %pad_maximum_fusion.refs_0_, bf16[4,72,1536]{2,1,0:T(8,128)(2,1)} %collective-permute-done.17.refs_1_, bf16[12,4,72,384]{3,2,1,0:T(8,128)(2,1)S(1)} %constant_dynamic-update-slice_fusion.7.refs_2_, ...), custom_call_target="tpu_custom_call" | custom-call | tf_op jit(solution)/shard_map/assemble/pallas_call | solution.py:103
  131.1 9.4 %mlp.2 = (f32[512,576]{1,0:T(8,128)S(1)}, bf16[512,576]{1,0:T(8,128)(2,1)S(1)}, bf16[512,1536]{1,0:T(8,128)(2,1)}, bf16[512,1536]{1,0:T(8,128)(2,1)}, bf16[512,1536]{1,0:T(8,128)(2,1)}, /*index=5*/f32[512,576]{1,0:T(8,128)S(1)}) custom-call(f32[512,576]{1,0:T(8,128)S(1)} %copy-done.1, bf16[512,576]{1,0:T(8,128)(2,1)S(1)} %copy-done.32, ...), custom_call_target="tpu_custom_call" | custom-call | flops 8000000000 | bytes 4000000 | tf_op jit(solution)/shard_map/mlp/pallas_call | solution.py:236
  141.7 5.2 %project_in.3 = (bf16[512,576]{1,0:T(8,128)(2,1)S(1)}, bf16[512,576]{1,0:T(8,128)(2,1)S(1)}, bf16[512,384]{1,0:T(8,128)(2,1)S(1)}) custom-call(f32[512,576]{1,0:T(8,128)S(1)} %get-tuple-element.160.refs_0_.refs_2_, f32[8,576]{1,0:T(8,128)S(1)} %copy-done.7, bf16[4,576,1536]{2,1,0:T(8,128)(2,1)} %bitcast.171, f32[512,128]{1,0:T(8,128)S(1)} %copy-done.3, ...), custom_call_target="tpu_custom_call" | custom-call | flops 4000000000 | bytes 4000000 | tf_op jit(solution)/shard_map/project_in/pallas_call | solution.py:236
  150.6 8.4 %collective-permute-done.24.refs_3_.refs_6_ = bf16[512,384]{1,0:T(8,128)(2,1)S(1)} collective-permute-done((bf16[512,384]{1,0:T(8,128)(2,1)S(1)}, bf16[512,384]{1,0:T(8,128)(2,1)S(1)}, u32[]{:S(2)}, u32[]{:S(2)}) %collective-permute-start.24) | collective-permute-done | bytes 393248 | tf_op jit(solution)/shard_map/ppermute | solution.py:22
  158.9 8.9 %collective-permute-done.25.refs_4_.refs_7_ = bf16[512,384]{1,0:T(8,128)(2,1)S(1)} collective-permute-done((bf16[512,384]{1,0:T(8,128)(2,1)S(1)}, bf16[512,384]{1,0:T(8,128)(2,1)S(1)}, u32[]{:S(2)}, u32[]{:S(2)}) %collective-permute-start.25) | collective-permute-done | bytes 393248 | tf_op jit(solution)/shard_map/ppermute | solution.py:22
  167.8 19.0 %attend.3 = (bf16[512,576]{1,0:T(8,128)(2,1)S(1)}, f32[16,512]{1,0:T(8,128)S(1)}) custom-call(bf16[512,576]{1,0:T(8,128)(2,1)S(1)} %get-tuple-element.163.refs_0_, s32[1,512]{1,0:T(1,128)S(1)} %get-tuple-element.416.refs_1_.refs_4_, bf16[512,384]{1,0:T(8,128)(2,1)S(1)} %get-tuple-element.164.refs_2_.refs_5_, ...), custom_call_target="tpu_custom_call" | custom-call | flops 15000000512 | bytes 4000000 | tf_op jit(solution)/shard_map/attend/pallas_call | solution.py:236
  192.4 9.2 %mlp.3 = (f32[512,576]{1,0:T(8,128)S(1)}, bf16[512,576]{1,0:T(8,128)(2,1)S(1)}, bf16[512,1536]{1,0:T(8,128)(2,1)}, bf16[512,1536]{1,0:T(8,128)(2,1)}, bf16[512,1536]{1,0:T(8,128)(2,1)}, /*index=5*/f32[512,576]{1,0:T(8,128)S(1)}) custom-call(f32[512,576]{1,0:T(8,128)S(1)} %copy-done.29, bf16[512,576]{1,0:T(8,128)(2,1)S(1)} %copy-done.37, ...), custom_call_target="tpu_custom_call" | custom-call | flops 8000000000 | bytes 4000000 | tf_op jit(solution)/shard_map/mlp/pallas_call | solution.py:236
  202.6 18.8 %mlp_back.2 = (bf16[512,576]{1,0:T(8,128)(2,1)S(1)}, f32[512,576]{1,0:T(8,128)S(1)}, f32[8,576]{1,0:T(8,128)S(1)}, bf16[576,576]{1,0:T(8,128)(2,1)S(1)}, bf16[32,3,72,384]{3,2,1,0:T(8,128)(2,1)}) custom-call(f32[512,576]{1,0:T(8,128)S(1)} %fusion.12.refs_0_, f32[512,576]{1,0:T(8,128)} %copy-done.30, bf16[512,576]{1,0:T(8,128)(2,1)S(1)} %get-tuple-element.168.refs_2_, ...), custom_call_target="tpu_custom_call" | custom-call | flops 15000000512 | bytes 4000000 | tf_op jit(solution)/shard_map/mlp_back/pallas_call | solution.py:236
  226.2 16.7 %attend_back.4 = (f32[512,384]{1,0:T(8,128)S(1)}, f32[512,256]{1,0:T(8,128)S(1)}, bf16[512,256]{1,0:T(8,128)(2,1)S(1)}, bf16[512,256]{1,0:T(8,128)(2,1)S(1)}, bf16[512,256]{1,0:T(8,128)(2,1)S(1)}) custom-call(bf16[512,576]{1,0:T(8,128)(2,1)S(1)} %copy-done.45, bf16[512,576]{1,0:T(8,128)(2,1)S(1)} %copy-done.39, bf16[512,576]{1,0:T(8,128)(2,1)S(1)} %copy-done.64, ...), custom_call_target="tpu_custom_call" | custom-call | flops 14000000000 | bytes 4000000 | tf_op jit(solution)/shard_map/attend_back/pallas_call | solution.py:236
  247.3 9.6 %attend_back.5 = (f32[512,192]{1,0:T(8,128)S(1)}, f32[512,128]{1,0:T(8,128)S(1)}, bf16[512,128]{1,0:T(8,128)(2,1)S(1)}, bf16[512,128]{1,0:T(8,128)(2,1)S(1)}, bf16[512,128]{1,0:T(8,128)(2,1)S(1)}) custom-call(bf16[512,576]{1,0:T(8,128)(2,1)S(1)} %copy-done.45, bf16[512,576]{1,0:T(8,128)(2,1)S(1)} %copy-done.39, bf16[512,576]{1,0:T(8,128)(2,1)S(1)} %copy-done.65, ...), custom_call_target="tpu_custom_call" | custom-call | flops 7000000000 | bytes 4000000 | tf_op jit(solution)/shard_map/attend_back/pallas_call | solution.py:236
  272.6 8.8 %project_back.2 = (f32[512,576]{1,0:T(8,128)}, f32[8,576]{1,0:T(8,128)S(1)}, bf16[32,1,72,384]{3,2,1,0:T(8,128)(2,1)}) custom-call(f32[512,128]{1,0:T(8,128)S(1)} %copy-done.3, f32[512,128]{1,0:T(8,128)S(1)} %copy-done.5, f32[512,576]{1,0:T(8,128)} %copy-done.28, bf16[512,576]{1,0:T(8,128)(2,1)S(1)} %copy-done.43, f32[8,576]{1,0:T(8,128)S(1)} %copy-done.8, ...), custom_call_target="tpu_custom_call" | custom-call | flops 6000000000 | bytes 4000000 | tf_op jit(solution)/shard_map/project_back/pallas_call | solution.py:236
  282.8 19.2 %mlp_back.3 = (bf16[512,576]{1,0:T(8,128)(2,1)S(1)}, f32[512,576]{1,0:T(8,128)S(1)}, f32[8,576]{1,0:T(8,128)S(1)}, bf16[576,576]{1,0:T(8,128)(2,1)S(1)}, bf16[32,3,72,384]{3,2,1,0:T(8,128)(2,1)}) custom-call(f32[512,576]{1,0:T(8,128)S(1)} %copy-done.41, f32[512,576]{1,0:T(8,128)} %copy-done.27, bf16[512,576]{1,0:T(8,128)(2,1)S(1)} %copy-done.35, ...), custom_call_target="tpu_custom_call" | custom-call | flops 15000000512 | bytes 4000000 | tf_op jit(solution)/shard_map/mlp_back/pallas_call | solution.py:236
  305.1 3.2 fusion.58
  312.7 1.9 collective-permute-done.35
  316.4 3.0 collective-permute-done.37
  324.2 16.5 %attend_back.6 = (f32[512,384]{1,0:T(8,128)S(1)}, f32[512,256]{1,0:T(8,128)S(1)}, bf16[512,256]{1,0:T(8,128)(2,1)S(1)}, bf16[512,256]{1,0:T(8,128)(2,1)S(1)}, bf16[512,256]{1,0:T(8,128)(2,1)S(1)}) custom-call(bf16[512,576]{1,0:T(8,128)(2,1)S(1)} %copy-done.58, bf16[512,576]{1,0:T(8,128)(2,1)S(1)} %copy-done.33, bf16[512,576]{1,0:T(8,128)(2,1)S(1)} %copy-done.62, ...), custom_call_target="tpu_custom_call" | custom-call | flops 14000000000 | bytes 4000000 | tf_op jit(solution)/shard_map/attend_back/pallas_call | solution.py:236
  347.8 9.3 %attend_back.7 = (f32[512,192]{1,0:T(8,128)S(1)}, f32[512,128]{1,0:T(8,128)S(1)}, bf16[512,128]{1,0:T(8,128)(2,1)S(1)}, bf16[512,128]{1,0:T(8,128)(2,1)S(1)}, bf16[512,128]{1,0:T(8,128)(2,1)S(1)}) custom-call(bf16[512,576]{1,0:T(8,128)(2,1)S(1)} %copy-done.58, bf16[512,576]{1,0:T(8,128)(2,1)S(1)} %copy-done.33, bf16[512,576]{1,0:T(8,128)(2,1)S(1)} %copy-done.62, ...), custom_call_target="tpu_custom_call" | custom-call | flops 7000000000 | bytes 4000000 | tf_op jit(solution)/shard_map/attend_back/pallas_call | solution.py:236
  360.7 6.2 %collective-permute-done.41 = bf16[2,4,72,384]{3,2,1,0:T(8,128)(2,1)} collective-permute-done((bf16[2,4,72,384]{3,2,1,0:T(8,128)(2,1)}, bf16[2,4,72,384]{3,2,1,0:T(8,128)(2,1)}, u32[]{:S(2)}, u32[]{:S(2)}) %collective-permute-start.41) | collective-permute-done | bytes 442400 | tf_op jit(solution)/shard_map/ppermute | solution.py:22
  366.9 1.7 fusion.6
  370.2 9.0 %project_back.3 = (f32[512,576]{1,0:T(8,128)}, f32[8,576]{1,0:T(8,128)}, bf16[32,1,80,384]{3,2,1,0:T(8,128)(2,1)}) custom-call(f32[512,128]{1,0:T(8,128)S(1)} %copy-done.3, f32[512,128]{1,0:T(8,128)S(1)} %copy-done.5, f32[512,576]{1,0:T(8,128)} %copy-done, bf16[512,576]{1,0:T(8,128)(2,1)S(1)} %copy-done.56, f32[8,576]{1,0:T(8,128)S(1)} %copy-done.8, ...), custom_call_target="tpu_custom_call" | custom-call | flops 6000000000 | bytes 4000000 | tf_op jit(solution)/shard_map/project_back/pallas_call | solution.py:236
  381.0 2.6 collective-permute-done.52
  388.0 3.4 collective-permute-start.51
  392.5 1.7 collective-permute-start.57
  394.9 2.7 collective-permute-done.49
  398.4 7.8 %collective-permute-done.50 = bf16[4,72,384]{2,1,0:T(8,128)(2,1)S(1)} collective-permute-done((bf16[4,72,384]{2,1,0:T(8,128)(2,1)}, bf16[4,72,384]{2,1,0:T(8,128)(2,1)S(1)}, u32[]{:S(2)}, u32[]{:S(2)}) %collective-permute-start.50) | collective-permute-done | bytes 221216 | tf_op jit(solution)/shard_map/ppermute | solution.py:22
  406.2 1.7 collective-permute-start.67
  408.5 4.0 collective-permute-start.59
  412.5 2.0 collective-permute-start.60
  415.4 3.1 collective-permute-done.60
  428.0 3.2 collective-permute-start.65
  432.9 2.8 collective-permute-done.64
  435.7 1.8 collective-permute-done.65
  (451 shorter events, 132.6 us)
Async XLA Ops:
  7.2 182.8 %all-gather.2.cloned.1.call-start = ((), (), s32[]{:S(2)}) async-start(), calls=%async_computation.1 | async-start | bytes 5971968 | tf_op jit(solution)/shard_map/all_gather | solution.py:133
  11.4 17.0 %collective-permute-start.3 = (bf16[1,80,384]{2,1,0:T(8,128)(2,1)}, bf16[1,80,384]{2,1,0:T(8,128)(2,1)S(1)}, u32[]{:S(2)}, u32[]{:S(2)}) collective-permute-start(bf16[1,80,384]{2,1,0:T(8,128)(2,1)} %fusion.39), channel_id=1, source_target_pairs={{0,2},{1,3},{2,0},{3,1},{4,6},{5,7},{6,4},{7,5},{8,10},{9,11},{10,... | collective-permute-start | bytes 184328 | tf_op jit(solution)/shard_map/ppermute | solution.py:22
  14.4 14.0 %collective-permute-start.4 = (bf16[1,80,384]{2,1,0:T(8,128)(2,1)}, bf16[1,80,384]{2,1,0:T(8,128)(2,1)S(1)}, u32[]{:S(2)}, u32[]{:S(2)}) collective-permute-start(bf16[1,80,384]{2,1,0:T(8,128)(2,1)} %fusion.39), channel_id=1, source_target_pairs={{0,4},{1,5},{2,6},{3,7},{4,0},{5,1},{6,2},{7,3},{8,12},{9,13},{10,... | collective-permute-start | bytes 184328 | tf_op jit(solution)/shard_map/ppermute | solution.py:22
  17.0 11.4 %collective-permute-start.5 = (bf16[1,80,384]{2,1,0:T(8,128)(2,1)}, bf16[1,80,384]{2,1,0:T(8,128)(2,1)S(1)}, u32[]{:S(2)}, u32[]{:S(2)}) collective-permute-start(bf16[1,80,384]{2,1,0:T(8,128)(2,1)} %fusion.39), channel_id=1, source_target_pairs={{0,6},{1,7},{2,4},{3,5},{4,2},{5,3},{6,0},{7,1},{8,14},{9,15},{10,... | collective-permute-start | bytes 184328 | tf_op jit(solution)/shard_map/ppermute | solution.py:22
  17.0 43.4 %collective-permute-start.2 = (bf16[1,80,1536]{2,1,0:T(8,128)(2,1)S(1)}, bf16[1,80,1536]{2,1,0:T(8,128)(2,1)}, u32[]{:S(2)}, u32[]{:S(2)}) collective-permute-start(bf16[1,80,1536]{2,1,0:T(8,128)(2,1)S(1)} %fusion.16.refs_0_), channel_id=1, source_target_pairs={{0,1},{1,0},{2,3},{3,2},{4,5},{5,4},{6,7},{7,6},{8,9},{9,8},{10,11... | collective-permute-start | bytes 737288 | tf_op jit(solution)/shard_map/ppermute | solution.py:22
  28.5 22.6 %collective-permute-start.11 = (bf16[4,72,384]{2,1,0:T(8,128)(2,1)S(1)}, bf16[4,72,384]{2,1,0:T(8,128)(2,1)S(1)}, u32[]{:S(2)}, u32[]{:S(2)}) collective-permute-start(bf16[4,72,384]{2,1,0:T(8,128)(2,1)S(1)} %constant_dynamic-slice_fusion), channel_id=1, source_target_pairs={{0,2},{1,3},{2,0},{3,1},{4,6},{5,7},{6,4},{7,5},{8,10},{9,11},{10,... | collective-permute-start | bytes 663560 | tf_op jit(solution)/shard_map/ppermute | solution.py:22
  29.4 22.2 %collective-permute-start.12 = (bf16[4,72,384]{2,1,0:T(8,128)(2,1)S(1)}, bf16[4,72,384]{2,1,0:T(8,128)(2,1)S(1)}, u32[]{:S(2)}, u32[]{:S(2)}) collective-permute-start(bf16[4,72,384]{2,1,0:T(8,128)(2,1)S(1)} %constant_dynamic-slice_fusion), channel_id=1, source_target_pairs={{0,4},{1,5},{2,6},{3,7},{4,0},{5,1},{6,2},{7,3},{8,12},{9,13},{10,... | collective-permute-start | bytes 663560 | tf_op jit(solution)/shard_map/ppermute | solution.py:22
  41.0 10.6 %collective-permute-start.13 = (bf16[4,72,384]{2,1,0:T(8,128)(2,1)S(1)}, bf16[4,72,384]{2,1,0:T(8,128)(2,1)S(1)}, u32[]{:S(2)}, u32[]{:S(2)}) collective-permute-start(bf16[4,72,384]{2,1,0:T(8,128)(2,1)S(1)} %constant_dynamic-slice_fusion), channel_id=1, source_target_pairs={{0,6},{1,7},{2,4},{3,5},{4,2},{5,3},{6,0},{7,1},{8,14},{9,15},{10,... | collective-permute-start | bytes 663560 | tf_op jit(solution)/shard_map/ppermute | solution.py:22
  51.6 8.8 %collective-permute-start.10 = (bf16[12,1,80,384]{3,2,1,0:T(8,128)(2,1)S(1)}, bf16[12,1,80,384]{3,2,1,0:T(8,128)(2,1)}, u32[]{:S(2)}, u32[]{:S(2)}) collective-permute-start(bf16[12,1,80,384]{3,2,1,0:T(8,128)(2,1)S(1)} %constant_dynamic-update-slice_fusion.refs_2_), channel_id=1, source_target_pairs={{0,1},{1,0},{2,3},{3,2},{4,5},{5,4},{6,7},{7,6},{8,9},{9,8},{10,11... | collective-permute-start | bytes 2211848 | tf_op jit(solution)/shard_map/ppermute | solution.py:22
  52.5 251.3 %reduce-scatter.2.cloned.1.call-start = ((), (), s32[]{:S(2)}) async-start(), calls=%async_computation.2 | async-start | bytes 5971968 | tf_op jit(solution)/shard_map/reduce_scatter | solution.py:963
  70.4 12.1 %collective-permute-start.14 = (bf16[512,384]{1,0:T(8,128)(2,1)S(1)}, bf16[512,384]{1,0:T(8,128)(2,1)S(1)}, u32[]{:S(2)}, u32[]{:S(2)}) collective-permute-start(bf16[512,384]{1,0:T(8,128)(2,1)S(1)} %get-tuple-element.154.refs_2_.refs_5_), channel_id=1, source_target_pairs={{0,8},{8,0},{16,24},{24,16},{1,9},{9,1},{17,25},{25,17},{2,10},{10... | collective-permute-start | bytes 1179656 | tf_op jit(solution)/shard_map/ppermute | solution.py:22
  70.9 20.5 %collective-permute-start.15 = (bf16[512,384]{1,0:T(8,128)(2,1)S(1)}, bf16[512,384]{1,0:T(8,128)(2,1)S(1)}, u32[]{:S(2)}, u32[]{:S(2)}) collective-permute-start(bf16[512,384]{1,0:T(8,128)(2,1)S(1)} %get-tuple-element.154.refs_2_.refs_5_), channel_id=1, source_target_pairs={{0,16},{8,24},{16,0},{24,8},{1,17},{9,25},{17,1},{25,9},{2,18},{10... | collective-permute-start | bytes 1179656 | tf_op jit(solution)/shard_map/ppermute | solution.py:22
  71.3 20.0 %collective-permute-start.16 = (bf16[512,384]{1,0:T(8,128)(2,1)S(1)}, bf16[512,384]{1,0:T(8,128)(2,1)S(1)}, u32[]{:S(2)}, u32[]{:S(2)}) collective-permute-start(bf16[512,384]{1,0:T(8,128)(2,1)S(1)} %get-tuple-element.154.refs_2_.refs_5_), channel_id=1, source_target_pairs={{0,24},{8,16},{16,8},{24,0},{1,25},{9,17},{17,9},{25,1},{2,26},{10... | collective-permute-start | bytes 1179656 | tf_op jit(solution)/shard_map/ppermute | solution.py:22
  73.9 36.2 %collective-permute-start.18 = (bf16[3,4,72,384]{3,2,1,0:T(8,128)(2,1)S(1)}, bf16[3,4,72,384]{3,2,1,0:T(8,128)(2,1)S(1)}, u32[]{:S(2)}, u32[]{:S(2)}) collective-permute-start(bf16[3,4,72,384]{3,2,1,0:T(8,128)(2,1)S(1)} %copy-done.69), channel_id=1, source_target_pairs={{0,8},{8,0},{16,24},{24,16},{1,9},{9,1},{17,25},{25,17},{2,10},{10... | collective-permute-start | bytes 1990664 | tf_op jit(solution)/shard_map/ppermute | solution.py:22
  74.4 35.7 %collective-permute-start.19 = (bf16[3,4,72,384]{3,2,1,0:T(8,128)(2,1)S(1)}, bf16[3,4,72,384]{3,2,1,0:T(8,128)(2,1)S(1)}, u32[]{:S(2)}, u32[]{:S(2)}) collective-permute-start(bf16[3,4,72,384]{3,2,1,0:T(8,128)(2,1)S(1)} %copy-done.69), channel_id=1, source_target_pairs={{0,16},{8,24},{16,0},{24,8},{1,17},{9,25},{17,1},{25,9},{2,18},{10... | collective-permute-start | bytes 1990664 | tf_op jit(solution)/shard_map/ppermute | solution.py:22
  110.9 8.3 %collective-permute-start.20 = (bf16[2,4,72,384]{3,2,1,0:T(8,128)(2,1)S(1)}, bf16[2,4,72,384]{3,2,1,0:T(8,128)(2,1)S(1)}, u32[]{:S(2)}, u32[]{:S(2)}) collective-permute-start(bf16[2,4,72,384]{3,2,1,0:T(8,128)(2,1)S(1)} %slice.523), channel_id=1, source_target_pairs={{0,16},{8,24},{16,0},{24,8},{1,17},{9,25},{17,1},{25,9},{2,18},{10... | collective-permute-start | bytes 1327112 | tf_op jit(solution)/shard_map/ppermute | solution.py:22
  123.2 27.2 %collective-permute-start.23 = (bf16[1,256,576]{2,1,0:T(8,128)(2,1)S(1)}, bf16[1,256,576]{2,1,0:T(8,128)(2,1)S(1)}, u32[]{:S(2)}, u32[]{:S(2)}) collective-permute-start(bf16[1,256,576]{2,1,0:T(8,128)(2,1)S(1)} %get-tuple-element.362), channel_id=1, source_target_pairs={{0,24},{8,16},{16,8},{24,0},{1,25},{9,17},{17,9},{25,1},{2,26},{10... | collective-permute-start | bytes 884744 | tf_op jit(solution)/shard_map/ppermute | solution.py:22
  146.9 12.0 %collective-permute-start.24 = (bf16[512,384]{1,0:T(8,128)(2,1)S(1)}, bf16[512,384]{1,0:T(8,128)(2,1)S(1)}, u32[]{:S(2)}, u32[]{:S(2)}) collective-permute-start(bf16[512,384]{1,0:T(8,128)(2,1)S(1)} %get-tuple-element.164.refs_2_.refs_5_), channel_id=1, source_target_pairs={{0,8},{8,0},{16,24},{24,16},{1,9},{9,1},{17,25},{25,17},{2,10},{10... | collective-permute-start | bytes 1179656 | tf_op jit(solution)/shard_map/ppermute | solution.py:22
  148.5 19.3 %collective-permute-start.25 = (bf16[512,384]{1,0:T(8,128)(2,1)S(1)}, bf16[512,384]{1,0:T(8,128)(2,1)S(1)}, u32[]{:S(2)}, u32[]{:S(2)}) collective-permute-start(bf16[512,384]{1,0:T(8,128)(2,1)S(1)} %get-tuple-element.164.refs_2_.refs_5_), channel_id=1, source_target_pairs={{0,16},{8,24},{16,0},{24,8},{1,17},{9,25},{17,1},{25,9},{2,18},{10... | collective-permute-start | bytes 1179656 | tf_op jit(solution)/shard_map/ppermute | solution.py:22
  149.0 18.8 %collective-permute-start.26 = (bf16[512,384]{1,0:T(8,128)(2,1)S(1)}, bf16[512,384]{1,0:T(8,128)(2,1)S(1)}, u32[]{:S(2)}, u32[]{:S(2)}) collective-permute-start(bf16[512,384]{1,0:T(8,128)(2,1)S(1)} %get-tuple-element.164.refs_2_.refs_5_), channel_id=1, source_target_pairs={{0,24},{8,16},{16,8},{24,0},{1,25},{9,17},{17,9},{25,1},{2,26},{10... | collective-permute-start | bytes 1179656 | tf_op jit(solution)/shard_map/ppermute | solution.py:22
  224.5 37.5 %collective-permute-start.33 = (bf16[1,256,576]{2,1,0:T(8,128)(2,1)S(1)}, bf16[1,256,576]{2,1,0:T(8,128)(2,1)S(1)}, u32[]{:S(2)}, u32[]{:S(2)}) collective-permute-start(bf16[1,256,576]{2,1,0:T(8,128)(2,1)S(1)} %get-tuple-element.360), channel_id=1, source_target_pairs={{0,24},{8,16},{16,8},{24,0},{1,25},{9,17},{17,9},{25,1},{2,26},{10... | collective-permute-start | bytes 884744 | tf_op jit(solution)/shard_map/ppermute | solution.py:22
  243.8 14.6 %collective-permute-start.27 = (bf16[512,256]{1,0:T(8,128)(2,1)S(1)}, bf16[512,256]{1,0:T(8,128)(2,1)S(1)}, u32[]{:S(2)}, u32[]{:S(2)}) collective-permute-start(bf16[512,256]{1,0:T(8,128)(2,1)S(1)} %get-tuple-element.188), channel_id=1, source_target_pairs={{0,8},{8,0},{16,24},{24,16},{1,9},{9,1},{17,25},{25,17},{2,10},{10... | collective-permute-start | bytes 786440 | tf_op jit(solution)/shard_map/ppermute | solution.py:22
  244.3 14.1 %collective-permute-start.28 = (bf16[512,256]{1,0:T(8,128)(2,1)S(1)}, bf16[512,256]{1,0:T(8,128)(2,1)S(1)}, u32[]{:S(2)}, u32[]{:S(2)}) collective-permute-start(bf16[512,256]{1,0:T(8,128)(2,1)S(1)} %get-tuple-element.189), channel_id=1, source_target_pairs={{0,16},{8,24},{16,0},{24,8},{1,17},{9,25},{17,1},{25,9},{2,18},{10... | collective-permute-start | bytes 786440 | tf_op jit(solution)/shard_map/ppermute | solution.py:22
  245.7 12.7 %collective-permute-start.29 = (bf16[512,256]{1,0:T(8,128)(2,1)S(1)}, bf16[512,256]{1,0:T(8,128)(2,1)S(1)}, u32[]{:S(2)}, u32[]{:S(2)}) collective-permute-start(bf16[512,256]{1,0:T(8,128)(2,1)S(1)} %get-tuple-element.190), channel_id=1, source_target_pairs={{0,24},{8,16},{16,8},{24,0},{1,25},{9,17},{17,9},{25,1},{2,26},{10... | collective-permute-start | bytes 786440 | tf_op jit(solution)/shard_map/ppermute | solution.py:22
  308.3 11.8 %collective-permute-start.34 = (bf16[4,4,3,72,384]{4,3,2,1,0:T(8,128)(2,1)S(1)}, bf16[4,4,3,72,384]{4,3,2,1,0:T(8,128)(2,1)S(1)}, u32[]{:S(2)}, u32[]{:S(2)}) collective-permute-start(bf16[4,4,3,72,384]{4,3,2,1,0:T(8,128)(2,1)S(1)} %bitcast.179), channel_id=1, source_target_pairs={{0,1},{1,0},{2,3},{3,2},{4,5},{5,4},{6,7},{7,6},{8,9},{9,8},{10,11... | collective-permute-start | bytes 7962632 | tf_op jit(solution)/shard_map/ppermute | solution.py:22
  309.9 9.5 %collective-permute-start.37 = (bf16[3,72,384]{2,1,0:T(8,128)(2,1)S(1)}, bf16[3,72,384]{2,1,0:T(8,128)(2,1)S(1)}, u32[]{:S(2)}, u32[]{:S(2)}) collective-permute-start(bf16[3,72,384]{2,1,0:T(8,128)(2,1)S(1)} %get-tuple-element.222), channel_id=1, source_target_pairs={{0,16},{8,24},{16,0},{24,8},{1,17},{9,25},{17,1},{25,9},{2,18},{10... | collective-permute-start | bytes 497672 | tf_op jit(solution)/shard_map/ppermute | solution.py:22
  322.1 22.2 %collective-permute-start.39 = (bf16[2,2,4,72,384]{4,3,2,1,0:T(8,128)(2,1)S(1)}, bf16[2,2,4,72,384]{4,3,2,1,0:T(8,128)(2,1)S(1)}, u32[]{:S(2)}, u32[]{:S(2)}) collective-permute-start(bf16[2,2,4,72,384]{4,3,2,1,0:T(8,128)(2,1)S(1)} %pad_maximum_fusion.1), channel_id=1, source_target_pairs={{0,8},{8,0},{16,24},{24,16},{1,9},{9,1},{17,25},{25,17},{2,10},{10... | collective-permute-start | bytes 2654216 | tf_op jit(solution)/shard_map/ppermute | solution.py:22
  323.5 21.3 %collective-permute-start.40 = (bf16[2,2,4,72,384]{4,3,2,1,0:T(8,128)(2,1)S(1)}, bf16[2,2,4,72,384]{4,3,2,1,0:T(8,128)(2,1)S(1)}, u32[]{:S(2)}, u32[]{:S(2)}) collective-permute-start(bf16[2,2,4,72,384]{4,3,2,1,0:T(8,128)(2,1)S(1)} %stack.91), channel_id=1, source_target_pairs={{0,16},{8,24},{16,0},{24,8},{1,17},{9,25},{17,1},{25,9},{2,18},{10... | collective-permute-start | bytes 2654216 | tf_op jit(solution)/shard_map/ppermute | solution.py:22
  340.7 16.4 %collective-permute-start.43 = (bf16[512,256]{1,0:T(8,128)(2,1)S(1)}, bf16[512,256]{1,0:T(8,128)(2,1)S(1)}, u32[]{:S(2)}, u32[]{:S(2)}) collective-permute-start(bf16[512,256]{1,0:T(8,128)(2,1)S(1)} %get-tuple-element.249), channel_id=1, source_target_pairs={{0,8},{8,0},{16,24},{24,16},{1,9},{9,1},{17,25},{25,17},{2,10},{10... | collective-permute-start | bytes 786440 | tf_op jit(solution)/shard_map/ppermute | solution.py:22
  342.3 14.9 %collective-permute-start.44 = (bf16[512,256]{1,0:T(8,128)(2,1)S(1)}, bf16[512,256]{1,0:T(8,128)(2,1)S(1)}, u32[]{:S(2)}, u32[]{:S(2)}) collective-permute-start(bf16[512,256]{1,0:T(8,128)(2,1)S(1)} %get-tuple-element.250), channel_id=1, source_target_pairs={{0,16},{8,24},{16,0},{24,8},{1,17},{9,25},{17,1},{25,9},{2,18},{10... | collective-permute-start | bytes 786440 | tf_op jit(solution)/shard_map/ppermute | solution.py:22
  342.8 14.4 %collective-permute-start.45 = (bf16[512,256]{1,0:T(8,128)(2,1)S(1)}, bf16[512,256]{1,0:T(8,128)(2,1)S(1)}, u32[]{:S(2)}, u32[]{:S(2)}) collective-permute-start(bf16[512,256]{1,0:T(8,128)(2,1)S(1)} %get-tuple-element.251), channel_id=1, source_target_pairs={{0,24},{8,16},{16,8},{24,0},{1,25},{9,17},{17,9},{25,1},{2,26},{10... | collective-permute-start | bytes 786440 | tf_op jit(solution)/shard_map/ppermute | solution.py:22
  346.2 20.7 %collective-permute-start.41 = (bf16[2,4,72,384]{3,2,1,0:T(8,128)(2,1)}, bf16[2,4,72,384]{3,2,1,0:T(8,128)(2,1)}, u32[]{:S(2)}, u32[]{:S(2)}) collective-permute-start(bf16[2,4,72,384]{3,2,1,0:T(8,128)(2,1)} %get-tuple-element.238), channel_id=1, source_target_pairs={{0,16},{8,24},{16,0},{24,8},{1,17},{9,25},{17,1},{25,9},{2,18},{10... | collective-permute-start | bytes 1327112 | tf_op jit(solution)/shard_map/ppermute | solution.py:22
  347.0 19.9 %collective-permute-start.42 = (bf16[2,4,72,384]{3,2,1,0:T(8,128)(2,1)S(1)}, bf16[2,4,72,384]{3,2,1,0:T(8,128)(2,1)}, u32[]{:S(2)}, u32[]{:S(2)}) collective-permute-start(bf16[2,4,72,384]{3,2,1,0:T(8,128)(2,1)S(1)} %get-tuple-element.239), channel_id=1, source_target_pairs={{0,8},{8,0},{16,24},{24,16},{1,9},{9,1},{17,25},{25,17},{2,10},{10... | collective-permute-start | bytes 1327112 | tf_op jit(solution)/shard_map/ppermute | solution.py:22
  357.2 12.9 %collective-permute-start.46 = (bf16[512,128]{1,0:T(8,128)(2,1)S(1)}, bf16[512,128]{1,0:T(8,128)(2,1)S(1)}, u32[]{:S(2)}, u32[]{:S(2)}) collective-permute-start(bf16[512,128]{1,0:T(8,128)(2,1)S(1)} %get-tuple-element.261), channel_id=1, source_target_pairs={{0,8},{8,0},{16,24},{24,16},{1,9},{9,1},{17,25},{25,17},{2,10},{10... | collective-permute-start | bytes 393224 | tf_op jit(solution)/shard_map/ppermute | solution.py:22
  358.5 11.8 %collective-permute-start.47 = (bf16[512,128]{1,0:T(8,128)(2,1)S(1)}, bf16[512,128]{1,0:T(8,128)(2,1)S(1)}, u32[]{:S(2)}, u32[]{:S(2)}) collective-permute-start(bf16[512,128]{1,0:T(8,128)(2,1)S(1)} %get-tuple-element.262), channel_id=1, source_target_pairs={{0,16},{8,24},{16,0},{24,8},{1,17},{9,25},{17,1},{25,9},{2,18},{10... | collective-permute-start | bytes 393224 | tf_op jit(solution)/shard_map/ppermute | solution.py:22
  359.7 10.6 %collective-permute-start.48 = (bf16[512,128]{1,0:T(8,128)(2,1)S(1)}, bf16[512,128]{1,0:T(8,128)(2,1)S(1)}, u32[]{:S(2)}, u32[]{:S(2)}) collective-permute-start(bf16[512,128]{1,0:T(8,128)(2,1)S(1)} %get-tuple-element.263), channel_id=1, source_target_pairs={{0,24},{8,16},{16,8},{24,0},{1,25},{9,17},{17,9},{25,1},{2,26},{10... | collective-permute-start | bytes 393224 | tf_op jit(solution)/shard_map/ppermute | solution.py:22
  383.9 8.6 %collective-permute-start.53 = (bf16[2,2,1,80,384]{4,3,1,2,0:T(8,128)(2,1)S(1)}, bf16[2,2,1,80,384]{4,3,1,2,0:T(8,128)(2,1)S(1)}, u32[]{:S(2)}, u32[]{:S(2)}) collective-permute-start(bf16[2,2,1,80,384]{4,3,1,2,0:T(8,128)(2,1)S(1)} %pad_maximum_fusion.11), channel_id=1, source_target_pairs={{0,8},{8,0},{16,24},{24,16},{1,9},{9,1},{17,25},{25,17},{2,10},{10... | collective-permute-start | bytes 737288 | tf_op jit(solution)/shard_map/ppermute | solution.py:22
  384.4 9.8 %collective-permute-start.55 = (bf16[2,2,1,80,384]{4,3,1,2,0:T(8,128)(2,1)S(1)}, bf16[2,2,1,80,384]{4,3,1,2,0:T(8,128)(2,1)S(1)}, u32[]{:S(2)}, u32[]{:S(2)}) collective-permute-start(bf16[2,2,1,80,384]{4,3,1,2,0:T(8,128)(2,1)S(1)} %stack.92), channel_id=1, source_target_pairs={{0,16},{8,24},{16,0},{24,8},{1,17},{9,25},{17,1},{25,9},{2,18},{10... | collective-permute-start | bytes 737288 | tf_op jit(solution)/shard_map/ppermute | solution.py:22
  387.0 10.7 %collective-permute-start.49 = (bf16[4,72,384]{2,1,0:T(8,128)(2,1)}, bf16[4,72,384]{2,1,0:T(8,128)(2,1)S(1)}, u32[]{:S(2)}, u32[]{:S(2)}) collective-permute-start(bf16[4,72,384]{2,1,0:T(8,128)(2,1)} %fusion.25), channel_id=1, source_target_pairs={{0,2},{1,3},{2,0},{3,1},{4,6},{5,7},{6,4},{7,5},{8,10},{9,11},{10,... | collective-permute-start | bytes 663560 | tf_op jit(solution)/shard_map/ppermute | solution.py:22
  387.2 19.0 %collective-permute-start.50 = (bf16[4,72,384]{2,1,0:T(8,128)(2,1)}, bf16[4,72,384]{2,1,0:T(8,128)(2,1)S(1)}, u32[]{:S(2)}, u32[]{:S(2)}) collective-permute-start(bf16[4,72,384]{2,1,0:T(8,128)(2,1)} %get-tuple-element.269), channel_id=1, source_target_pairs={{0,4},{1,5},{2,6},{3,7},{4,0},{5,1},{6,2},{7,3},{8,12},{9,13},{10,... | collective-permute-start | bytes 663560 | tf_op jit(solution)/shard_map/ppermute | solution.py:22
  388.0 18.2 %collective-permute-start.51 = (bf16[4,72,384]{2,1,0:T(8,128)(2,1)}, bf16[4,72,384]{2,1,0:T(8,128)(2,1)S(1)}, u32[]{:S(2)}, u32[]{:S(2)}) collective-permute-start(bf16[4,72,384]{2,1,0:T(8,128)(2,1)} %get-tuple-element.270), channel_id=1, source_target_pairs={{0,6},{1,7},{2,4},{3,5},{4,2},{5,3},{6,0},{7,1},{8,14},{9,15},{10,... | collective-permute-start | bytes 663560 | tf_op jit(solution)/shard_map/ppermute | solution.py:22
  392.5 15.9 %collective-permute-start.57 = (bf16[256,576]{1,0:T(8,128)(2,1)S(1)}, bf16[256,576]{1,0:T(8,128)(2,1)S(1)}, u32[]{:S(2)}, u32[]{:S(2)}) collective-permute-start(bf16[256,576]{1,0:T(8,128)(2,1)S(1)} %slice.820), channel_id=1, source_target_pairs={{0,24},{8,16},{16,8},{24,0},{1,25},{9,17},{17,9},{25,1},{2,26},{10... | collective-permute-start | bytes 884744 | tf_op jit(solution)/shard_map/ppermute | solution.py:22
  394.4 11.8 %collective-permute-start.54 = (bf16[2,1,80,384]{3,2,1,0:T(8,128)(2,1)S(1)}, bf16[2,1,80,384]{3,2,1,0:T(8,128)(2,1)S(1)}, u32[]{:S(2)}, u32[]{:S(2)}) collective-permute-start(bf16[2,1,80,384]{3,2,1,0:T(8,128)(2,1)S(1)} %get-tuple-element.329), channel_id=1, source_target_pairs={{0,16},{8,24},{16,0},{24,8},{1,17},{9,25},{17,1},{25,9},{2,18},{10... | collective-permute-start | bytes 368648 | tf_op jit(solution)/shard_map/ppermute | solution.py:22
  397.6 8.5 %collective-permute-start.56 = (bf16[2,1,80,384]{3,2,0,1:T(8,128)(2,1)S(1)}, bf16[2,1,80,384]{3,2,0,1:T(8,128)(2,1)S(1)}, u32[]{:S(2)}, u32[]{:S(2)}) collective-permute-start(bf16[2,1,80,384]{3,2,0,1:T(8,128)(2,1)S(1)} %get-tuple-element.328), channel_id=1, source_target_pairs={{0,8},{8,0},{16,24},{24,16},{1,9},{9,1},{17,25},{25,17},{2,10},{10... | collective-permute-start | bytes 368648 | tf_op jit(solution)/shard_map/ppermute | solution.py:22
  406.2 26.4 %collective-permute-start.67 = (bf16[3,72,384]{2,1,0:T(8,128)(2,1)S(1)}, bf16[3,72,384]{2,1,0:T(8,128)(2,1)S(1)}, u32[]{:S(2)}, u32[]{:S(2)}) collective-permute-start(bf16[3,72,384]{2,1,0:T(8,128)(2,1)S(1)} %copy-done.73), channel_id=1, source_target_pairs={{0,24},{8,16},{16,8},{24,0},{1,25},{9,17},{17,9},{25,1},{2,26},{10... | collective-permute-start | bytes 497672 | tf_op jit(solution)/shard_map/ppermute | solution.py:22
  407.9 24.7 %collective-permute-start.68 = (bf16[3,72,384]{2,1,0:T(8,128)(2,1)S(1)}, bf16[3,72,384]{2,1,0:T(8,128)(2,1)S(1)}, u32[]{:S(2)}, u32[]{:S(2)}) collective-permute-start(bf16[3,72,384]{2,1,0:T(8,128)(2,1)S(1)} %copy-done.73), channel_id=1, source_target_pairs={{0,16},{8,24},{16,0},{24,8},{1,17},{9,25},{17,1},{25,9},{2,18},{10... | collective-permute-start | bytes 497672 | tf_op jit(solution)/shard_map/ppermute | solution.py:22
  426.4 9.4 %collective-permute-start.64 = (bf16[4,72,384]{2,1,0:T(8,128)(2,1)S(1)}, bf16[4,72,384]{2,1,0:T(8,128)(2,1)S(1)}, u32[]{:S(2)}, u32[]{:S(2)}) collective-permute-start(bf16[4,72,384]{2,1,0:T(8,128)(2,1)S(1)} %add_convert_fusion), channel_id=1, source_target_pairs={{0,24},{8,16},{16,8},{24,0},{1,25},{9,17},{17,9},{25,1},{2,26},{10... | collective-permute-start | bytes 663560 | tf_op jit(solution)/shard_map/ppermute | solution.py:22
  428.0 9.5 %collective-permute-start.65 = (bf16[4,72,384]{2,1,0:T(8,128)(2,1)S(1)}, bf16[4,72,384]{2,1,0:T(8,128)(2,1)S(1)}, u32[]{:S(2)}, u32[]{:S(2)}) collective-permute-start(bf16[4,72,384]{2,1,0:T(8,128)(2,1)S(1)} %add_convert_fusion), channel_id=1, source_target_pairs={{0,16},{8,24},{16,0},{24,8},{1,17},{9,25},{17,1},{25,9},{2,18},{10... | collective-permute-start | bytes 663560 | tf_op jit(solution)/shard_map/ppermute | solution.py:22
  (129 other events, 808.9 us)
Sparse Core Ops, SparseCore 0:
  52.7 57.0 all-gather.1
  224.4 57.4 reduce-scatter.1

commit v6 on v5

--- a/solution.py
+++ b/solution.py
@@ -875,9 +875,12 @@
         own_second = jnp.stack([*mlp_own[0], attn_own[1]])
         own_third = jnp.stack(mlp_own[1])
         first_line = gather_line(own_first)
-        second_line = gather_line(tied(own_second, first_line))
+        first_sides = gather_sides(first_line)
+        first_sides, tokens, positions = lax.optimization_barrier(
+            (first_sides, tokens, positions)
+        )
+        second_line = gather_line(tied(own_second, first_sides))
         third = gather_plain(tied(own_third, second_line))
-        first_sides = gather_sides(first_line)
         first_flip = flip(own_first, "fsdp", 1)
         (first, gains), first_mine = gather_rest(
             rows, own_first, first_flip, first_line, first_sides

time: 456 us -> 458 us (level)
  waiting for transfers between devices: 94.7 us -> 103 us
  local copies, waits for them, and re-layouts: 55.4 us -> 47.3 us
    ppermute x70, waiting for transfers between devices: 94.6 us -> 103 us  [flip(): return lax.ppermute(block, axis, route)]
    unnamed x224 -> x172, local copies, waits for them, and re-layouts: 32.5 us -> 31.7 us
  transfers between devices with their start and end apart: 72 -> 72, of which waited for: 31 -> 33; matrix products, arithmetic and copies ran while one was open for 7% -> 6% of each run, Pallas kernels for 32% -> 32%
where the time goes in v6:
time: 458 us; the launch traced here: 454 us
  Pallas kernels  181 us (40%)
  waiting for transfers between devices  103 us (22%)
  starting transfers between devices  84.9 us (19%)
  local copies, waits for them, and re-layouts  47.3 us (10%)
  other arithmetic  22.7 us (5%)
  between operations  15.8 us (3%)
    pallas_call x14, Pallas kernels, run_kernel(): pl.pallas_call(kernel, out_shape=tuple(outputs), in_specs=[pl.BlockSpec(m...  173 us
    ppermute x70, waiting for transfers between devices, flip(): return lax.ppermute(block, axis, route)  103 us
    ppermute x70, starting transfers between devices, flip(): return lax.ppermute(block, axis, route)  84.8 us
    unnamed x172, local copies, waits for them, and re-layouts  31.7 us
  transfers between devices with their start and end apart: 72, of which 33 were waited for; matrix products, arithmetic and copies ran while one was open for 6% of the time, Pallas kernels for 32%

profile of v6, /device:TPU:0, one launch (start us, length us, event | category | flops | bytes accessed | tf_op | source)
XLA Modules:
  0.0 453.8 jit_solution(12392913792675432066)
XLA Ops:
  10.1 3.1 collective-permute-start
  13.2 2.6 collective-permute-start.1
  16.8 2.7 collective-permute-start.5
  21.7 5.2 %collective-permute-done.6 = s32[1,256]{1,0:T(1,128)S(1)} collective-permute-done((s32[1,256]{1,0:T(1,128)S(1)}, s32[1,256]{1,0:T(1,128)S(1)}, u32[]{:S(2)}, u32[]{:S(2)}) %collective-permute-start.6) | collective-permute-done | bytes 1056 | tf_op jit(solution)/shard_map/ppermute | solution.py:22
  30.1 1.9 pad_maximum_fusion.6
  31.9 2.1 collective-permute-done.3
  36.0 3.5 collective-permute-start.12
  41.4 3.3 collective-permute-done.8
  45.3 3.7 collective-permute-done.9
  49.0 6.3 %collective-permute-done.12 = bf16[4,72,384]{2,1,0:T(8,128)(2,1)S(1)} collective-permute-done((bf16[4,72,384]{2,1,0:T(8,128)(2,1)S(1)}, bf16[4,72,384]{2,1,0:T(8,128)(2,1)S(1)}, u32[]{:S(2)}, u32[]{:S(2)}) %collective-permute-start.12) | collective-permute-done | bytes 221216 | tf_op jit(solution)/shard_map/ppermute | solution.py:22
  59.9 2.0 assemble.2
  65.9 3.8 project_in.2
  75.2 6.6 %collective-permute-done.14.refs_3_.refs_6_ = bf16[512,384]{1,0:T(8,128)(2,1)S(1)} collective-permute-done((bf16[512,384]{1,0:T(8,128)(2,1)S(1)}, bf16[512,384]{1,0:T(8,128)(2,1)S(1)}, u32[]{:S(2)}, u32[]{:S(2)}) %collective-permute-start.14) | collective-permute-done | bytes 393248 | tf_op jit(solution)/shard_map/ppermute | solution.py:22
  81.8 8.4 %collective-permute-done.15.refs_4_.refs_7_ = bf16[512,384]{1,0:T(8,128)(2,1)S(1)} collective-permute-done((bf16[512,384]{1,0:T(8,128)(2,1)S(1)}, bf16[512,384]{1,0:T(8,128)(2,1)S(1)}, u32[]{:S(2)}, u32[]{:S(2)}) %collective-permute-start.15) | collective-permute-done | bytes 393248 | tf_op jit(solution)/shard_map/ppermute | solution.py:22
  91.2 18.6 %attend.2 = (bf16[512,576]{1,0:T(8,128)(2,1)S(1)}, f32[16,512]{1,0:T(8,128)S(1)}) custom-call(bf16[512,576]{1,0:T(8,128)(2,1)S(1)} %get-tuple-element.159.refs_0_, s32[1,512]{1,0:T(1,128)S(1)} %get-tuple-element.424.refs_1_.refs_4_, bf16[512,384]{1,0:T(8,128)(2,1)S(1)} %get-tuple-element.162.refs_2_.refs_5_, ...), custom_call_target="tpu_custom_call" | custom-call | flops 15000000512 | bytes 4000000 | tf_op jit(solution)/shard_map/attend/pallas_call | solution.py:236
  113.1 5.9 %collective-permute-done.20 = bf16[2,4,72,384]{3,2,1,0:T(8,128)(2,1)S(1)} collective-permute-done((bf16[2,4,72,384]{3,2,1,0:T(8,128)(2,1)S(1)}, bf16[2,4,72,384]{3,2,1,0:T(8,128)(2,1)S(1)}, u32[]{:S(2)}, u32[]{:S(2)}) %collective-permute-start.20) | collective-permute-done | bytes 442400 | tf_op jit(solution)/shard_map/ppermute | solution.py:22
  119.7 2.1 copy.40
  125.6 5.3 %assemble.3.refs_6_.refs_11_ = bf16[4,8,72,1536]{3,2,1,0:T(8,128)(2,1)} custom-call(bf16[4,72,1536]{2,1,0:T(8,128)(2,1)S(1)} %pad_maximum_fusion.refs_0_, bf16[4,72,1536]{2,1,0:T(8,128)(2,1)} %collective-permute-done.17.refs_1_, bf16[12,4,72,384]{3,2,1,0:T(8,128)(2,1)S(1)} %constant_dynamic-update-slice_fusion.7.refs_2_, ...), custom_call_target="tpu_custom_call" | custom-call | tf_op jit(solution)/shard_map/assemble/pallas_call | solution.py:103
  130.9 9.4 %mlp.2 = (f32[512,576]{1,0:T(8,128)S(1)}, bf16[512,576]{1,0:T(8,128)(2,1)S(1)}, bf16[512,1536]{1,0:T(8,128)(2,1)}, bf16[512,1536]{1,0:T(8,128)(2,1)}, bf16[512,1536]{1,0:T(8,128)(2,1)}, /*index=5*/f32[512,576]{1,0:T(8,128)S(1)}) custom-call(f32[512,576]{1,0:T(8,128)S(1)} %copy-done.1, bf16[512,576]{1,0:T(8,128)(2,1)S(1)} %copy-done.32, ...), custom_call_target="tpu_custom_call" | custom-call | flops 8000000000 | bytes 4000000 | tf_op jit(solution)/shard_map/mlp/pallas_call | solution.py:236
  141.5 5.2 %project_in.3 = (bf16[512,576]{1,0:T(8,128)(2,1)S(1)}, bf16[512,576]{1,0:T(8,128)(2,1)S(1)}, bf16[512,384]{1,0:T(8,128)(2,1)S(1)}) custom-call(f32[512,576]{1,0:T(8,128)S(1)} %get-tuple-element.168.refs_0_.refs_2_, f32[8,576]{1,0:T(8,128)S(1)} %copy-done.7, bf16[4,576,1536]{2,1,0:T(8,128)(2,1)} %bitcast.168, f32[512,128]{1,0:T(8,128)S(1)} %copy-done.5, ...), custom_call_target="tpu_custom_call" | custom-call | flops 4000000000 | bytes 4000000 | tf_op jit(solution)/shard_map/project_in/pallas_call | solution.py:236
  150.3 8.4 %collective-permute-done.24.refs_3_.refs_6_ = bf16[512,384]{1,0:T(8,128)(2,1)S(1)} collective-permute-done((bf16[512,384]{1,0:T(8,128)(2,1)S(1)}, bf16[512,384]{1,0:T(8,128)(2,1)S(1)}, u32[]{:S(2)}, u32[]{:S(2)}) %collective-permute-start.24) | collective-permute-done | bytes 393248 | tf_op jit(solution)/shard_map/ppermute | solution.py:22
  158.7 8.3 %collective-permute-done.25.refs_4_.refs_7_ = bf16[512,384]{1,0:T(8,128)(2,1)S(1)} collective-permute-done((bf16[512,384]{1,0:T(8,128)(2,1)S(1)}, bf16[512,384]{1,0:T(8,128)(2,1)S(1)}, u32[]{:S(2)}, u32[]{:S(2)}) %collective-permute-start.25) | collective-permute-done | bytes 393248 | tf_op jit(solution)/shard_map/ppermute | solution.py:22
  167.0 19.0 %attend.3 = (bf16[512,576]{1,0:T(8,128)(2,1)S(1)}, f32[16,512]{1,0:T(8,128)S(1)}) custom-call(bf16[512,576]{1,0:T(8,128)(2,1)S(1)} %get-tuple-element.171.refs_0_, s32[1,512]{1,0:T(1,128)S(1)} %get-tuple-element.424.refs_1_.refs_4_, bf16[512,384]{1,0:T(8,128)(2,1)S(1)} %get-tuple-element.172.refs_2_.refs_5_, ...), custom_call_target="tpu_custom_call" | custom-call | flops 15000000512 | bytes 4000000 | tf_op jit(solution)/shard_map/attend/pallas_call | solution.py:236
  191.6 9.2 %mlp.3 = (f32[512,576]{1,0:T(8,128)S(1)}, bf16[512,576]{1,0:T(8,128)(2,1)S(1)}, bf16[512,1536]{1,0:T(8,128)(2,1)}, bf16[512,1536]{1,0:T(8,128)(2,1)}, bf16[512,1536]{1,0:T(8,128)(2,1)}, /*index=5*/f32[512,576]{1,0:T(8,128)S(1)}) custom-call(f32[512,576]{1,0:T(8,128)S(1)} %copy-done.29, bf16[512,576]{1,0:T(8,128)(2,1)S(1)} %copy-done.37, ...), custom_call_target="tpu_custom_call" | custom-call | flops 8000000000 | bytes 4000000 | tf_op jit(solution)/shard_map/mlp/pallas_call | solution.py:236
  202.0 18.8 %mlp_back.2 = (bf16[512,576]{1,0:T(8,128)(2,1)S(1)}, f32[512,576]{1,0:T(8,128)S(1)}, f32[8,576]{1,0:T(8,128)S(1)}, bf16[576,576]{1,0:T(8,128)(2,1)S(1)}, bf16[32,3,72,384]{3,2,1,0:T(8,128)(2,1)}) custom-call(f32[512,576]{1,0:T(8,128)S(1)} %fusion.11.refs_0_, f32[512,576]{1,0:T(8,128)} %copy-done.30, bf16[512,576]{1,0:T(8,128)(2,1)S(1)} %get-tuple-element.176.refs_2_, ...), custom_call_target="tpu_custom_call" | custom-call | flops 15000000512 | bytes 4000000 | tf_op jit(solution)/shard_map/mlp_back/pallas_call | solution.py:236
  225.6 16.7 %attend_back.4 = (f32[512,384]{1,0:T(8,128)S(1)}, f32[512,256]{1,0:T(8,128)S(1)}, bf16[512,256]{1,0:T(8,128)(2,1)S(1)}, bf16[512,256]{1,0:T(8,128)(2,1)S(1)}, bf16[512,256]{1,0:T(8,128)(2,1)S(1)}) custom-call(bf16[512,576]{1,0:T(8,128)(2,1)S(1)} %copy-done.45, bf16[512,576]{1,0:T(8,128)(2,1)S(1)} %copy-done.39, bf16[512,576]{1,0:T(8,128)(2,1)S(1)} %copy-done.64, ...), custom_call_target="tpu_custom_call" | custom-call | flops 14000000000 | bytes 4000000 | tf_op jit(solution)/shard_map/attend_back/pallas_call | solution.py:236
  246.7 9.6 %attend_back.5 = (f32[512,192]{1,0:T(8,128)S(1)}, f32[512,128]{1,0:T(8,128)S(1)}, bf16[512,128]{1,0:T(8,128)(2,1)S(1)}, bf16[512,128]{1,0:T(8,128)(2,1)S(1)}, bf16[512,128]{1,0:T(8,128)(2,1)S(1)}) custom-call(bf16[512,576]{1,0:T(8,128)(2,1)S(1)} %copy-done.45, bf16[512,576]{1,0:T(8,128)(2,1)S(1)} %copy-done.39, bf16[512,576]{1,0:T(8,128)(2,1)S(1)} %copy-done.65, ...), custom_call_target="tpu_custom_call" | custom-call | flops 7000000000 | bytes 4000000 | tf_op jit(solution)/shard_map/attend_back/pallas_call | solution.py:236
  272.0 8.7 %project_back.2 = (f32[512,576]{1,0:T(8,128)}, f32[8,576]{1,0:T(8,128)S(1)}, bf16[32,1,72,384]{3,2,1,0:T(8,128)(2,1)}) custom-call(f32[512,128]{1,0:T(8,128)S(1)} %copy-done.5, f32[512,128]{1,0:T(8,128)S(1)} %copy-done.3, f32[512,576]{1,0:T(8,128)} %copy-done.28, bf16[512,576]{1,0:T(8,128)(2,1)S(1)} %copy-done.43, f32[8,576]{1,0:T(8,128)S(1)} %copy-done.8, ...), custom_call_target="tpu_custom_call" | custom-call | flops 6000000000 | bytes 4000000 | tf_op jit(solution)/shard_map/project_back/pallas_call | solution.py:236
  282.0 19.3 %mlp_back.3 = (bf16[512,576]{1,0:T(8,128)(2,1)S(1)}, f32[512,576]{1,0:T(8,128)S(1)}, f32[8,576]{1,0:T(8,128)S(1)}, bf16[576,576]{1,0:T(8,128)(2,1)S(1)}, bf16[32,3,72,384]{3,2,1,0:T(8,128)(2,1)}) custom-call(f32[512,576]{1,0:T(8,128)S(1)} %copy-done.41, f32[512,576]{1,0:T(8,128)} %copy-done.27, bf16[512,576]{1,0:T(8,128)(2,1)S(1)} %copy-done.35, ...), custom_call_target="tpu_custom_call" | custom-call | flops 15000000512 | bytes 4000000 | tf_op jit(solution)/shard_map/mlp_back/pallas_call | solution.py:236
  304.5 3.2 fusion.56
  312.1 1.9 collective-permute-done.35
  315.7 3.5 collective-permute-done.37
  324.1 16.5 %attend_back.6 = (f32[512,384]{1,0:T(8,128)S(1)}, f32[512,256]{1,0:T(8,128)S(1)}, bf16[512,256]{1,0:T(8,128)(2,1)S(1)}, bf16[512,256]{1,0:T(8,128)(2,1)S(1)}, bf16[512,256]{1,0:T(8,128)(2,1)S(1)}) custom-call(bf16[512,576]{1,0:T(8,128)(2,1)S(1)} %copy-done.58, bf16[512,576]{1,0:T(8,128)(2,1)S(1)} %copy-done.33, bf16[512,576]{1,0:T(8,128)(2,1)S(1)} %copy-done.62, ...), custom_call_target="tpu_custom_call" | custom-call | flops 14000000000 | bytes 4000000 | tf_op jit(solution)/shard_map/attend_back/pallas_call | solution.py:236
  347.5 9.3 %attend_back.7 = (f32[512,192]{1,0:T(8,128)S(1)}, f32[512,128]{1,0:T(8,128)S(1)}, bf16[512,128]{1,0:T(8,128)(2,1)S(1)}, bf16[512,128]{1,0:T(8,128)(2,1)S(1)}, bf16[512,128]{1,0:T(8,128)(2,1)S(1)}) custom-call(bf16[512,576]{1,0:T(8,128)(2,1)S(1)} %copy-done.58, bf16[512,576]{1,0:T(8,128)(2,1)S(1)} %copy-done.33, bf16[512,576]{1,0:T(8,128)(2,1)S(1)} %copy-done.62, ...), custom_call_target="tpu_custom_call" | custom-call | flops 7000000000 | bytes 4000000 | tf_op jit(solution)/shard_map/attend_back/pallas_call | solution.py:236
  360.4 5.9 %collective-permute-done.41 = bf16[2,4,72,384]{3,2,1,0:T(8,128)(2,1)} collective-permute-done((bf16[2,4,72,384]{3,2,1,0:T(8,128)(2,1)}, bf16[2,4,72,384]{3,2,1,0:T(8,128)(2,1)}, u32[]{:S(2)}, u32[]{:S(2)}) %collective-permute-start.41) | collective-permute-done | bytes 442400 | tf_op jit(solution)/shard_map/ppermute | solution.py:22
  366.3 1.7 fusion.6
  369.6 8.9 %project_back.3 = (f32[512,576]{1,0:T(8,128)}, f32[8,576]{1,0:T(8,128)}, bf16[32,1,80,384]{3,2,1,0:T(8,128)(2,1)}) custom-call(f32[512,128]{1,0:T(8,128)S(1)} %copy-done.5, f32[512,128]{1,0:T(8,128)S(1)} %copy-done.3, f32[512,576]{1,0:T(8,128)} %copy-done, bf16[512,576]{1,0:T(8,128)(2,1)S(1)} %copy-done.56, f32[8,576]{1,0:T(8,128)S(1)} %copy-done.8, ...), custom_call_target="tpu_custom_call" | custom-call | flops 6000000000 | bytes 4000000 | tf_op jit(solution)/shard_map/project_back/pallas_call | solution.py:236
  378.6 1.7 fusion.57
  380.3 2.6 collective-permute-done.52
  386.3 3.9 collective-permute-start.49
  397.0 2.4 collective-permute-done.49
  401.0 8.2 %collective-permute-done.50 = bf16[4,72,384]{2,1,0:T(8,128)(2,1)S(1)} collective-permute-done((bf16[4,72,384]{2,1,0:T(8,128)(2,1)}, bf16[4,72,384]{2,1,0:T(8,128)(2,1)S(1)}, u32[]{:S(2)}, u32[]{:S(2)}) %collective-permute-start.50) | collective-permute-done | bytes 221216 | tf_op jit(solution)/shard_map/ppermute | solution.py:22
  409.2 1.7 collective-permute-start.67
  412.3 4.6 %collective-permute-start.59 = (bf16[1,80,384]{2,1,0:T(8,128)(2,1)S(1)}, bf16[1,80,384]{2,1,0:T(8,128)(2,1)S(1)}, u32[]{:S(2)}, u32[]{:S(2)}) collective-permute-start(bf16[1,80,384]{2,1,0:T(8,128)(2,1)S(1)} %get-tuple-element.395), channel_id=1, source_target_pairs={{0,4},{1,5},{2,6},{3,7},{4,0},{5,1},{6,2},{7,3},{8,12},{9,13},{10,... | collective-permute-start | bytes 184328 | tf_op jit(solution)/shard_map/ppermute | solution.py:22
  419.8 3.2 collective-permute-done.60
  430.9 1.9 collective-permute-start.64
  436.7 2.4 collective-permute-done.64
  439.2 1.9 collective-permute-done.65
  (403 shorter events, 133.2 us)
Async XLA Ops:
  7.2 182.0 %all-gather.2.cloned.1.call-start = ((), (), s32[]{:S(2)}) async-start(), calls=%async_computation.1 | async-start | bytes 5971968 | tf_op jit(solution)/shard_map/all_gather | solution.py:133
  10.1 16.8 %collective-permute-start = (bf16[1,80,384]{2,1,0:T(8,128)(2,1)S(1)}, bf16[1,80,384]{2,1,0:T(8,128)(2,1)S(1)}, u32[]{:S(2)}, u32[]{:S(2)}) collective-permute-start(bf16[1,80,384]{2,1,0:T(8,128)(2,1)S(1)} %fusion.38), channel_id=1, source_target_pairs={{0,2},{1,3},{2,0},{3,1},{4,6},{5,7},{6,4},{7,5},{8,10},{9,11},{10,... | collective-permute-start | bytes 184328 | tf_op jit(solution)/shard_map/ppermute | solution.py:22
  13.2 13.7 %collective-permute-start.1 = (bf16[1,80,384]{2,1,0:T(8,128)(2,1)S(1)}, bf16[1,80,384]{2,1,0:T(8,128)(2,1)S(1)}, u32[]{:S(2)}, u32[]{:S(2)}) collective-permute-start(bf16[1,80,384]{2,1,0:T(8,128)(2,1)S(1)} %fusion.38), channel_id=1, source_target_pairs={{0,4},{1,5},{2,6},{3,7},{4,0},{5,1},{6,2},{7,3},{8,12},{9,13},{10,... | collective-permute-start | bytes 184328 | tf_op jit(solution)/shard_map/ppermute | solution.py:22
  15.8 11.1 %collective-permute-start.2 = (bf16[1,80,384]{2,1,0:T(8,128)(2,1)S(1)}, bf16[1,80,384]{2,1,0:T(8,128)(2,1)S(1)}, u32[]{:S(2)}, u32[]{:S(2)}) collective-permute-start(bf16[1,80,384]{2,1,0:T(8,128)(2,1)S(1)} %fusion.38), channel_id=1, source_target_pairs={{0,6},{1,7},{2,4},{3,5},{4,2},{5,3},{6,0},{7,1},{8,14},{9,15},{10,... | collective-permute-start | bytes 184328 | tf_op jit(solution)/shard_map/ppermute | solution.py:22
  16.8 13.3 %collective-permute-start.5 = (bf16[1,256,576]{2,1,0:T(8,128)(2,1)}, bf16[1,256,576]{2,1,0:T(8,128)(2,1)}, u32[]{:S(2)}, u32[]{:S(2)}) collective-permute-start(bf16[1,256,576]{2,1,0:T(8,128)(2,1)} %copy.51), channel_id=1, source_target_pairs={{0,24},{8,16},{16,8},{24,0},{1,25},{9,17},{17,9},{25,1},{2,26},{10... | collective-permute-start | bytes 884744 | tf_op jit(solution)/shard_map/ppermute | solution.py:22
  26.9 33.0 %collective-permute-start.7 = (bf16[1,80,1536]{2,1,0:T(8,128)(2,1)S(1)}, bf16[1,80,1536]{2,1,0:T(8,128)(2,1)}, u32[]{:S(2)}, u32[]{:S(2)}) collective-permute-start(bf16[1,80,1536]{2,1,0:T(8,128)(2,1)S(1)} %fusion.15.refs_0_), channel_id=1, source_target_pairs={{0,1},{1,0},{2,3},{3,2},{4,5},{5,4},{6,7},{7,6},{8,9},{9,8},{10,11... | collective-permute-start | bytes 737288 | tf_op jit(solution)/shard_map/ppermute | solution.py:22
  35.3 13.7 %collective-permute-start.11 = (bf16[4,72,384]{2,1,0:T(8,128)(2,1)S(1)}, bf16[4,72,384]{2,1,0:T(8,128)(2,1)S(1)}, u32[]{:S(2)}, u32[]{:S(2)}) collective-permute-start(bf16[4,72,384]{2,1,0:T(8,128)(2,1)S(1)} %constant_dynamic-slice_fusion), channel_id=1, source_target_pairs={{0,2},{1,3},{2,0},{3,1},{4,6},{5,7},{6,4},{7,5},{8,10},{9,11},{10,... | collective-permute-start | bytes 663560 | tf_op jit(solution)/shard_map/ppermute | solution.py:22
  36.0 19.3 %collective-permute-start.12 = (bf16[4,72,384]{2,1,0:T(8,128)(2,1)S(1)}, bf16[4,72,384]{2,1,0:T(8,128)(2,1)S(1)}, u32[]{:S(2)}, u32[]{:S(2)}) collective-permute-start(bf16[4,72,384]{2,1,0:T(8,128)(2,1)S(1)} %constant_dynamic-slice_fusion), channel_id=1, source_target_pairs={{0,4},{1,5},{2,6},{3,7},{4,0},{5,1},{6,2},{7,3},{8,12},{9,13},{10,... | collective-permute-start | bytes 663560 | tf_op jit(solution)/shard_map/ppermute | solution.py:22
  39.5 15.8 %collective-permute-start.13 = (bf16[4,72,384]{2,1,0:T(8,128)(2,1)S(1)}, bf16[4,72,384]{2,1,0:T(8,128)(2,1)S(1)}, u32[]{:S(2)}, u32[]{:S(2)}) collective-permute-start(bf16[4,72,384]{2,1,0:T(8,128)(2,1)S(1)} %constant_dynamic-slice_fusion), channel_id=1, source_target_pairs={{0,6},{1,7},{2,4},{3,5},{4,2},{5,3},{6,0},{7,1},{8,14},{9,15},{10,... | collective-permute-start | bytes 663560 | tf_op jit(solution)/shard_map/ppermute | solution.py:22
  48.9 10.9 %collective-permute-start.10 = (bf16[12,1,80,384]{3,2,1,0:T(8,128)(2,1)S(1)}, bf16[12,1,80,384]{3,2,1,0:T(8,128)(2,1)}, u32[]{:S(2)}, u32[]{:S(2)}) collective-permute-start(bf16[12,1,80,384]{3,2,1,0:T(8,128)(2,1)S(1)} %constant_dynamic-update-slice_fusion.refs_2_), channel_id=1, source_target_pairs={{0,1},{1,0},{2,3},{3,2},{4,5},{5,4},{6,7},{7,6},{8,9},{9,8},{10,11... | collective-permute-start | bytes 2211848 | tf_op jit(solution)/shard_map/ppermute | solution.py:22
  56.2 247.0 %reduce-scatter.2.cloned.1.call-start = ((), (), s32[]{:S(2)}) async-start(), calls=%async_computation.2 | async-start | bytes 5971968 | tf_op jit(solution)/shard_map/reduce_scatter | solution.py:966
  69.7 12.1 %collective-permute-start.14 = (bf16[512,384]{1,0:T(8,128)(2,1)S(1)}, bf16[512,384]{1,0:T(8,128)(2,1)S(1)}, u32[]{:S(2)}, u32[]{:S(2)}) collective-permute-start(bf16[512,384]{1,0:T(8,128)(2,1)S(1)} %get-tuple-element.162.refs_2_.refs_5_), channel_id=1, source_target_pairs={{0,8},{8,0},{16,24},{24,16},{1,9},{9,1},{17,25},{25,17},{2,10},{10... | collective-permute-start | bytes 1179656 | tf_op jit(solution)/shard_map/ppermute | solution.py:22
  70.2 20.0 %collective-permute-start.15 = (bf16[512,384]{1,0:T(8,128)(2,1)S(1)}, bf16[512,384]{1,0:T(8,128)(2,1)S(1)}, u32[]{:S(2)}, u32[]{:S(2)}) collective-permute-start(bf16[512,384]{1,0:T(8,128)(2,1)S(1)} %get-tuple-element.162.refs_2_.refs_5_), channel_id=1, source_target_pairs={{0,16},{8,24},{16,0},{24,8},{1,17},{9,25},{17,1},{25,9},{2,18},{10... | collective-permute-start | bytes 1179656 | tf_op jit(solution)/shard_map/ppermute | solution.py:22
  71.7 19.4 %collective-permute-start.16 = (bf16[512,384]{1,0:T(8,128)(2,1)S(1)}, bf16[512,384]{1,0:T(8,128)(2,1)S(1)}, u32[]{:S(2)}, u32[]{:S(2)}) collective-permute-start(bf16[512,384]{1,0:T(8,128)(2,1)S(1)} %get-tuple-element.162.refs_2_.refs_5_), channel_id=1, source_target_pairs={{0,24},{8,16},{16,8},{24,0},{1,25},{9,17},{17,9},{25,1},{2,26},{10... | collective-permute-start | bytes 1179656 | tf_op jit(solution)/shard_map/ppermute | solution.py:22
  73.3 36.6 %collective-permute-start.18 = (bf16[3,4,72,384]{3,2,1,0:T(8,128)(2,1)S(1)}, bf16[3,4,72,384]{3,2,1,0:T(8,128)(2,1)S(1)}, u32[]{:S(2)}, u32[]{:S(2)}) collective-permute-start(bf16[3,4,72,384]{3,2,1,0:T(8,128)(2,1)S(1)} %copy-done.69), channel_id=1, source_target_pairs={{0,8},{8,0},{16,24},{24,16},{1,9},{9,1},{17,25},{25,17},{2,10},{10... | collective-permute-start | bytes 1990664 | tf_op jit(solution)/shard_map/ppermute | solution.py:22
  73.7 36.2 %collective-permute-start.19 = (bf16[3,4,72,384]{3,2,1,0:T(8,128)(2,1)S(1)}, bf16[3,4,72,384]{3,2,1,0:T(8,128)(2,1)S(1)}, u32[]{:S(2)}, u32[]{:S(2)}) collective-permute-start(bf16[3,4,72,384]{3,2,1,0:T(8,128)(2,1)S(1)} %copy-done.69), channel_id=1, source_target_pairs={{0,16},{8,24},{16,0},{24,8},{1,17},{9,25},{17,1},{25,9},{2,18},{10... | collective-permute-start | bytes 1990664 | tf_op jit(solution)/shard_map/ppermute | solution.py:22
  123.1 27.2 %collective-permute-start.23 = (bf16[1,256,576]{2,1,0:T(8,128)(2,1)S(1)}, bf16[1,256,576]{2,1,0:T(8,128)(2,1)S(1)}, u32[]{:S(2)}, u32[]{:S(2)}) collective-permute-start(bf16[1,256,576]{2,1,0:T(8,128)(2,1)S(1)} %get-tuple-element.370), channel_id=1, source_target_pairs={{0,24},{8,16},{16,8},{24,0},{1,25},{9,17},{17,9},{25,1},{2,26},{10... | collective-permute-start | bytes 884744 | tf_op jit(solution)/shard_map/ppermute | solution.py:22
  146.7 12.0 %collective-permute-start.24 = (bf16[512,384]{1,0:T(8,128)(2,1)S(1)}, bf16[512,384]{1,0:T(8,128)(2,1)S(1)}, u32[]{:S(2)}, u32[]{:S(2)}) collective-permute-start(bf16[512,384]{1,0:T(8,128)(2,1)S(1)} %get-tuple-element.172.refs_2_.refs_5_), channel_id=1, source_target_pairs={{0,8},{8,0},{16,24},{24,16},{1,9},{9,1},{17,25},{25,17},{2,10},{10... | collective-permute-start | bytes 1179656 | tf_op jit(solution)/shard_map/ppermute | solution.py:22
  147.7 19.3 %collective-permute-start.25 = (bf16[512,384]{1,0:T(8,128)(2,1)S(1)}, bf16[512,384]{1,0:T(8,128)(2,1)S(1)}, u32[]{:S(2)}, u32[]{:S(2)}) collective-permute-start(bf16[512,384]{1,0:T(8,128)(2,1)S(1)} %get-tuple-element.172.refs_2_.refs_5_), channel_id=1, source_target_pairs={{0,16},{8,24},{16,0},{24,8},{1,17},{9,25},{17,1},{25,9},{2,18},{10... | collective-permute-start | bytes 1179656 | tf_op jit(solution)/shard_map/ppermute | solution.py:22
  148.8 18.2 %collective-permute-start.26 = (bf16[512,384]{1,0:T(8,128)(2,1)S(1)}, bf16[512,384]{1,0:T(8,128)(2,1)S(1)}, u32[]{:S(2)}, u32[]{:S(2)}) collective-permute-start(bf16[512,384]{1,0:T(8,128)(2,1)S(1)} %get-tuple-element.172.refs_2_.refs_5_), channel_id=1, source_target_pairs={{0,24},{8,16},{16,8},{24,0},{1,25},{9,17},{17,9},{25,1},{2,26},{10... | collective-permute-start | bytes 1179656 | tf_op jit(solution)/shard_map/ppermute | solution.py:22
  223.9 37.5 %collective-permute-start.33 = (bf16[1,256,576]{2,1,0:T(8,128)(2,1)S(1)}, bf16[1,256,576]{2,1,0:T(8,128)(2,1)S(1)}, u32[]{:S(2)}, u32[]{:S(2)}) collective-permute-start(bf16[1,256,576]{2,1,0:T(8,128)(2,1)S(1)} %get-tuple-element.368), channel_id=1, source_target_pairs={{0,24},{8,16},{16,8},{24,0},{1,25},{9,17},{17,9},{25,1},{2,26},{10... | collective-permute-start | bytes 884744 | tf_op jit(solution)/shard_map/ppermute | solution.py:22
  243.2 14.6 %collective-permute-start.27 = (bf16[512,256]{1,0:T(8,128)(2,1)S(1)}, bf16[512,256]{1,0:T(8,128)(2,1)S(1)}, u32[]{:S(2)}, u32[]{:S(2)}) collective-permute-start(bf16[512,256]{1,0:T(8,128)(2,1)S(1)} %get-tuple-element.196), channel_id=1, source_target_pairs={{0,8},{8,0},{16,24},{24,16},{1,9},{9,1},{17,25},{25,17},{2,10},{10... | collective-permute-start | bytes 786440 | tf_op jit(solution)/shard_map/ppermute | solution.py:22
  244.2 13.5 %collective-permute-start.28 = (bf16[512,256]{1,0:T(8,128)(2,1)S(1)}, bf16[512,256]{1,0:T(8,128)(2,1)S(1)}, u32[]{:S(2)}, u32[]{:S(2)}) collective-permute-start(bf16[512,256]{1,0:T(8,128)(2,1)S(1)} %get-tuple-element.197), channel_id=1, source_target_pairs={{0,16},{8,24},{16,0},{24,8},{1,17},{9,25},{17,1},{25,9},{2,18},{10... | collective-permute-start | bytes 786440 | tf_op jit(solution)/shard_map/ppermute | solution.py:22
  245.1 12.7 %collective-permute-start.29 = (bf16[512,256]{1,0:T(8,128)(2,1)S(1)}, bf16[512,256]{1,0:T(8,128)(2,1)S(1)}, u32[]{:S(2)}, u32[]{:S(2)}) collective-permute-start(bf16[512,256]{1,0:T(8,128)(2,1)S(1)} %get-tuple-element.198), channel_id=1, source_target_pairs={{0,24},{8,16},{16,8},{24,0},{1,25},{9,17},{17,9},{25,1},{2,26},{10... | collective-permute-start | bytes 786440 | tf_op jit(solution)/shard_map/ppermute | solution.py:22
  307.7 12.3 %collective-permute-start.34 = (bf16[4,4,3,72,384]{4,3,2,1,0:T(8,128)(2,1)S(1)}, bf16[4,4,3,72,384]{4,3,2,1,0:T(8,128)(2,1)S(1)}, u32[]{:S(2)}, u32[]{:S(2)}) collective-permute-start(bf16[4,4,3,72,384]{4,3,2,1,0:T(8,128)(2,1)S(1)} %bitcast.176), channel_id=1, source_target_pairs={{0,1},{1,0},{2,3},{3,2},{4,5},{5,4},{6,7},{7,6},{8,9},{9,8},{10,11... | collective-permute-start | bytes 7962632 | tf_op jit(solution)/shard_map/ppermute | solution.py:22
  309.8 9.5 %collective-permute-start.37 = (bf16[3,72,384]{2,1,0:T(8,128)(2,1)S(1)}, bf16[3,72,384]{2,1,0:T(8,128)(2,1)S(1)}, u32[]{:S(2)}, u32[]{:S(2)}) collective-permute-start(bf16[3,72,384]{2,1,0:T(8,128)(2,1)S(1)} %get-tuple-element.230), channel_id=1, source_target_pairs={{0,16},{8,24},{16,0},{24,8},{1,17},{9,25},{17,1},{25,9},{2,18},{10... | collective-permute-start | bytes 497672 | tf_op jit(solution)/shard_map/ppermute | solution.py:22
  310.9 8.4 %collective-permute-start.38 = (bf16[3,72,384]{2,1,0:T(8,128)(2,1)S(1)}, bf16[3,72,384]{2,1,0:T(8,128)(2,1)S(1)}, u32[]{:S(2)}, u32[]{:S(2)}) collective-permute-start(bf16[3,72,384]{2,1,0:T(8,128)(2,1)S(1)} %get-tuple-element.231), channel_id=1, source_target_pairs={{0,24},{8,16},{16,8},{24,0},{1,25},{9,17},{17,9},{25,1},{2,26},{10... | collective-permute-start | bytes 497672 | tf_op jit(solution)/shard_map/ppermute | solution.py:22
  321.9 22.3 %collective-permute-start.39 = (bf16[2,2,4,72,384]{4,3,2,1,0:T(8,128)(2,1)S(1)}, bf16[2,2,4,72,384]{4,3,2,1,0:T(8,128)(2,1)S(1)}, u32[]{:S(2)}, u32[]{:S(2)}) collective-permute-start(bf16[2,2,4,72,384]{4,3,2,1,0:T(8,128)(2,1)S(1)} %pad_maximum_fusion.1), channel_id=1, source_target_pairs={{0,8},{8,0},{16,24},{24,16},{1,9},{9,1},{17,25},{25,17},{2,10},{10... | collective-permute-start | bytes 2654216 | tf_op jit(solution)/shard_map/ppermute | solution.py:22
  322.9 21.3 %collective-permute-start.40 = (bf16[2,2,4,72,384]{4,3,2,1,0:T(8,128)(2,1)S(1)}, bf16[2,2,4,72,384]{4,3,2,1,0:T(8,128)(2,1)S(1)}, u32[]{:S(2)}, u32[]{:S(2)}) collective-permute-start(bf16[2,2,4,72,384]{4,3,2,1,0:T(8,128)(2,1)S(1)} %stack.91), channel_id=1, source_target_pairs={{0,16},{8,24},{16,0},{24,8},{1,17},{9,25},{17,1},{25,9},{2,18},{10... | collective-permute-start | bytes 2654216 | tf_op jit(solution)/shard_map/ppermute | solution.py:22
  340.6 16.2 %collective-permute-start.43 = (bf16[512,256]{1,0:T(8,128)(2,1)S(1)}, bf16[512,256]{1,0:T(8,128)(2,1)S(1)}, u32[]{:S(2)}, u32[]{:S(2)}) collective-permute-start(bf16[512,256]{1,0:T(8,128)(2,1)S(1)} %get-tuple-element.257), channel_id=1, source_target_pairs={{0,8},{8,0},{16,24},{24,16},{1,9},{9,1},{17,25},{25,17},{2,10},{10... | collective-permute-start | bytes 786440 | tf_op jit(solution)/shard_map/ppermute | solution.py:22
  341.8 15.1 %collective-permute-start.44 = (bf16[512,256]{1,0:T(8,128)(2,1)S(1)}, bf16[512,256]{1,0:T(8,128)(2,1)S(1)}, u32[]{:S(2)}, u32[]{:S(2)}) collective-permute-start(bf16[512,256]{1,0:T(8,128)(2,1)S(1)} %get-tuple-element.258), channel_id=1, source_target_pairs={{0,16},{8,24},{16,0},{24,8},{1,17},{9,25},{17,1},{25,9},{2,18},{10... | collective-permute-start | bytes 786440 | tf_op jit(solution)/shard_map/ppermute | solution.py:22
  342.6 14.2 %collective-permute-start.45 = (bf16[512,256]{1,0:T(8,128)(2,1)S(1)}, bf16[512,256]{1,0:T(8,128)(2,1)S(1)}, u32[]{:S(2)}, u32[]{:S(2)}) collective-permute-start(bf16[512,256]{1,0:T(8,128)(2,1)S(1)} %get-tuple-element.259), channel_id=1, source_target_pairs={{0,24},{8,16},{16,8},{24,0},{1,25},{9,17},{17,9},{25,1},{2,26},{10... | collective-permute-start | bytes 786440 | tf_op jit(solution)/shard_map/ppermute | solution.py:22
  345.6 20.7 %collective-permute-start.41 = (bf16[2,4,72,384]{3,2,1,0:T(8,128)(2,1)}, bf16[2,4,72,384]{3,2,1,0:T(8,128)(2,1)}, u32[]{:S(2)}, u32[]{:S(2)}) collective-permute-start(bf16[2,4,72,384]{3,2,1,0:T(8,128)(2,1)} %get-tuple-element.246), channel_id=1, source_target_pairs={{0,16},{8,24},{16,0},{24,8},{1,17},{9,25},{17,1},{25,9},{2,18},{10... | collective-permute-start | bytes 1327112 | tf_op jit(solution)/shard_map/ppermute | solution.py:22
  346.4 19.9 %collective-permute-start.42 = (bf16[2,4,72,384]{3,2,1,0:T(8,128)(2,1)S(1)}, bf16[2,4,72,384]{3,2,1,0:T(8,128)(2,1)}, u32[]{:S(2)}, u32[]{:S(2)}) collective-permute-start(bf16[2,4,72,384]{3,2,1,0:T(8,128)(2,1)S(1)} %get-tuple-element.247), channel_id=1, source_target_pairs={{0,8},{8,0},{16,24},{24,16},{1,9},{9,1},{17,25},{25,17},{2,10},{10... | collective-permute-start | bytes 1327112 | tf_op jit(solution)/shard_map/ppermute | solution.py:22
  356.8 12.7 %collective-permute-start.46 = (bf16[512,128]{1,0:T(8,128)(2,1)S(1)}, bf16[512,128]{1,0:T(8,128)(2,1)S(1)}, u32[]{:S(2)}, u32[]{:S(2)}) collective-permute-start(bf16[512,128]{1,0:T(8,128)(2,1)S(1)} %get-tuple-element.269), channel_id=1, source_target_pairs={{0,8},{8,0},{16,24},{24,16},{1,9},{9,1},{17,25},{25,17},{2,10},{10... | collective-permute-start | bytes 393224 | tf_op jit(solution)/shard_map/ppermute | solution.py:22
  357.8 11.8 %collective-permute-start.47 = (bf16[512,128]{1,0:T(8,128)(2,1)S(1)}, bf16[512,128]{1,0:T(8,128)(2,1)S(1)}, u32[]{:S(2)}, u32[]{:S(2)}) collective-permute-start(bf16[512,128]{1,0:T(8,128)(2,1)S(1)} %get-tuple-element.270), channel_id=1, source_target_pairs={{0,16},{8,24},{16,0},{24,8},{1,17},{9,25},{17,1},{25,9},{2,18},{10... | collective-permute-start | bytes 393224 | tf_op jit(solution)/shard_map/ppermute | solution.py:22
  359.0 10.6 %collective-permute-start.48 = (bf16[512,128]{1,0:T(8,128)(2,1)S(1)}, bf16[512,128]{1,0:T(8,128)(2,1)S(1)}, u32[]{:S(2)}, u32[]{:S(2)}) collective-permute-start(bf16[512,128]{1,0:T(8,128)(2,1)S(1)} %get-tuple-element.271), channel_id=1, source_target_pairs={{0,24},{8,16},{16,8},{24,0},{1,25},{9,17},{17,9},{25,1},{2,26},{10... | collective-permute-start | bytes 393224 | tf_op jit(solution)/shard_map/ppermute | solution.py:22
  383.2 10.5 %collective-permute-start.53 = (bf16[2,2,1,80,384]{4,3,1,2,0:T(8,128)(2,1)S(1)}, bf16[2,2,1,80,384]{4,3,1,2,0:T(8,128)(2,1)S(1)}, u32[]{:S(2)}, u32[]{:S(2)}) collective-permute-start(bf16[2,2,1,80,384]{4,3,1,2,0:T(8,128)(2,1)S(1)} %pad_maximum_fusion.12), channel_id=1, source_target_pairs={{0,8},{8,0},{16,24},{24,16},{1,9},{9,1},{17,25},{25,17},{2,10},{10... | collective-permute-start | bytes 737288 | tf_op jit(solution)/shard_map/ppermute | solution.py:22
  384.3 11.1 %collective-permute-start.55 = (bf16[2,2,1,80,384]{4,3,1,2,0:T(8,128)(2,1)S(1)}, bf16[2,2,1,80,384]{4,3,1,2,0:T(8,128)(2,1)S(1)}, u32[]{:S(2)}, u32[]{:S(2)}) collective-permute-start(bf16[2,2,1,80,384]{4,3,1,2,0:T(8,128)(2,1)S(1)} %stack.92), channel_id=1, source_target_pairs={{0,16},{8,24},{16,0},{24,8},{1,17},{9,25},{17,1},{25,9},{2,18},{10... | collective-permute-start | bytes 737288 | tf_op jit(solution)/shard_map/ppermute | solution.py:22
  386.3 13.1 %collective-permute-start.49 = (bf16[4,72,384]{2,1,0:T(8,128)(2,1)}, bf16[4,72,384]{2,1,0:T(8,128)(2,1)S(1)}, u32[]{:S(2)}, u32[]{:S(2)}) collective-permute-start(bf16[4,72,384]{2,1,0:T(8,128)(2,1)} %fusion.24), channel_id=1, source_target_pairs={{0,2},{1,3},{2,0},{3,1},{4,6},{5,7},{6,4},{7,5},{8,10},{9,11},{10,... | collective-permute-start | bytes 663560 | tf_op jit(solution)/shard_map/ppermute | solution.py:22
  390.2 19.0 %collective-permute-start.50 = (bf16[4,72,384]{2,1,0:T(8,128)(2,1)}, bf16[4,72,384]{2,1,0:T(8,128)(2,1)S(1)}, u32[]{:S(2)}, u32[]{:S(2)}) collective-permute-start(bf16[4,72,384]{2,1,0:T(8,128)(2,1)} %get-tuple-element.277), channel_id=1, source_target_pairs={{0,4},{1,5},{2,6},{3,7},{4,0},{5,1},{6,2},{7,3},{8,12},{9,13},{10,... | collective-permute-start | bytes 663560 | tf_op jit(solution)/shard_map/ppermute | solution.py:22
  391.2 18.0 %collective-permute-start.51 = (bf16[4,72,384]{2,1,0:T(8,128)(2,1)}, bf16[4,72,384]{2,1,0:T(8,128)(2,1)S(1)}, u32[]{:S(2)}, u32[]{:S(2)}) collective-permute-start(bf16[4,72,384]{2,1,0:T(8,128)(2,1)} %get-tuple-element.278), channel_id=1, source_target_pairs={{0,6},{1,7},{2,4},{3,5},{4,2},{5,3},{6,0},{7,1},{8,14},{9,15},{10,... | collective-permute-start | bytes 663560 | tf_op jit(solution)/shard_map/ppermute | solution.py:22
  393.8 18.4 %collective-permute-start.57 = (bf16[256,576]{1,0:T(8,128)(2,1)S(1)}, bf16[256,576]{1,0:T(8,128)(2,1)S(1)}, u32[]{:S(2)}, u32[]{:S(2)}) collective-permute-start(bf16[256,576]{1,0:T(8,128)(2,1)S(1)} %slice.818), channel_id=1, source_target_pairs={{0,24},{8,16},{16,8},{24,0},{1,25},{9,17},{17,9},{25,1},{2,26},{10... | collective-permute-start | bytes 884744 | tf_op jit(solution)/shard_map/ppermute | solution.py:22
  395.6 13.6 %collective-permute-start.54 = (bf16[2,1,80,384]{3,2,1,0:T(8,128)(2,1)S(1)}, bf16[2,1,80,384]{3,2,1,0:T(8,128)(2,1)S(1)}, u32[]{:S(2)}, u32[]{:S(2)}) collective-permute-start(bf16[2,1,80,384]{3,2,1,0:T(8,128)(2,1)S(1)} %get-tuple-element.337), channel_id=1, source_target_pairs={{0,16},{8,24},{16,0},{24,8},{1,17},{9,25},{17,1},{25,9},{2,18},{10... | collective-permute-start | bytes 368648 | tf_op jit(solution)/shard_map/ppermute | solution.py:22
  399.4 9.8 %collective-permute-start.56 = (bf16[2,1,80,384]{3,2,0,1:T(8,128)(2,1)S(1)}, bf16[2,1,80,384]{3,2,0,1:T(8,128)(2,1)S(1)}, u32[]{:S(2)}, u32[]{:S(2)}) collective-permute-start(bf16[2,1,80,384]{3,2,0,1:T(8,128)(2,1)S(1)} %get-tuple-element.336), channel_id=1, source_target_pairs={{0,8},{8,0},{16,24},{24,16},{1,9},{9,1},{17,25},{25,17},{2,10},{10... | collective-permute-start | bytes 368648 | tf_op jit(solution)/shard_map/ppermute | solution.py:22
  409.2 25.0 %collective-permute-start.67 = (bf16[3,72,384]{2,1,0:T(8,128)(2,1)S(1)}, bf16[3,72,384]{2,1,0:T(8,128)(2,1)S(1)}, u32[]{:S(2)}, u32[]{:S(2)}) collective-permute-start(bf16[3,72,384]{2,1,0:T(8,128)(2,1)S(1)} %copy-done.73), channel_id=1, source_target_pairs={{0,24},{8,16},{16,8},{24,0},{1,25},{9,17},{17,9},{25,1},{2,26},{10... | collective-permute-start | bytes 497672 | tf_op jit(solution)/shard_map/ppermute | solution.py:22
  410.8 24.9 %collective-permute-start.68 = (bf16[3,72,384]{2,1,0:T(8,128)(2,1)S(1)}, bf16[3,72,384]{2,1,0:T(8,128)(2,1)S(1)}, u32[]{:S(2)}, u32[]{:S(2)}) collective-permute-start(bf16[3,72,384]{2,1,0:T(8,128)(2,1)S(1)} %copy-done.73), channel_id=1, source_target_pairs={{0,16},{8,24},{16,0},{24,8},{1,17},{9,25},{17,1},{25,9},{2,18},{10... | collective-permute-start | bytes 497672 | tf_op jit(solution)/shard_map/ppermute | solution.py:22
  432.7 8.3 %collective-permute-start.65 = (bf16[4,72,384]{2,1,0:T(8,128)(2,1)S(1)}, bf16[4,72,384]{2,1,0:T(8,128)(2,1)S(1)}, u32[]{:S(2)}, u32[]{:S(2)}) collective-permute-start(bf16[4,72,384]{2,1,0:T(8,128)(2,1)S(1)} %add_convert_fusion), channel_id=1, source_target_pairs={{0,16},{8,24},{16,0},{24,8},{1,17},{9,25},{17,1},{25,9},{2,18},{10... | collective-permute-start | bytes 663560 | tf_op jit(solution)/shard_map/ppermute | solution.py:22
  (103 other events, 716.0 us)
Sparse Core Ops, SparseCore 0:
  56.4 57.9 all-gather.1
  223.8 62.0 reduce-scatter.1
